TPU v7x, 32 devices: a whole 2x2x4 slice. The times are simulated.
32 devices in a mesh: dom: 2 (over y), row: 4 (over z), sub: 2 (over x), rep: 2 (over core).
Axes of the slice: x: 2, y: 2, z: 4, core: 2. Of those that a mesh axis runs over, the one named last changes fastest.
Arguments:
- vectors: bfloat16 [28672, 768], P(('dom', 'row', 'sub', 'rep')), parts along dimension 0, may hold values from -150 to 150
- rotation: bfloat16 [1536, 768], P('dom'), parts along dimension 0, may hold values from -0.21875 to 0.21875
- codebooks: float32 [96, 256, 16], P(('dom', 'sub')), parts along dimension 0, may hold values from -8 to 8
Outputs:
- reconstruction: bfloat16 [28672, 768], P(('dom', 'row', 'sub', 'rep')), parts along dimension 0
- new_codebooks: float32 [96, 256, 16], P(('dom', 'sub')), parts along dimension 0
- cross_cov: float32 [1536, 768], P(('dom', 'sub')), parts along dimension 0
There are 2 independent parts, one for each index of `dom`. A program takes and returns all parts, laid end to end along the dimension named above; each array names one. Nothing has to cross between parts.
All inputs are finite; a program needn't handle non-finite values.
Results may differ from a plain program's by a relative error of at most 0.012.
Values may be sent and summed in bfloat16 or wider, within the bound.
No kernel may reach another device: no remote copies, remote signals or barrier semaphores. Data moves between devices by JAX's collectives and lax.ppermute only.
A program may use at most 64 MiB of HBM per device.

v0:
```python
import jax
import jax.numpy as jnp
from jax import lax
from jax.sharding import PartitionSpec as P

SUBDIM = 16


softness_scale = 4.0


def quantize_rows(block, codebook):
    block = block.astype(jnp.float32)
    cross_product = jnp.dot(codebook, block, precision=lax.Precision.HIGHEST)
    squared_norms = jnp.sum(codebook * codebook, axis=1)
    affinity_scores = (2.0 * cross_product - squared_norms[:, None]) / softness_scale
    weights = jax.nn.softmax(affinity_scores, axis=0)
    recon = jnp.dot(codebook.T, weights, precision=lax.Precision.HIGHEST)
    sums = lax.dot_general(
        weights, block, (((1,), (1,)), ((), ())), precision=lax.Precision.HIGHEST
    )
    counts = jnp.sum(weights, axis=1)
    return (recon, sums, counts)


def on_device(vectors, rotation, codebooks):
    row_count = vectors.shape[0]
    width = vectors.shape[1]
    groups = lax.axis_size("sub")
    group_width = width // groups
    rotated_t = lax.dot_general(
        rotation, vectors, (((0,), (1,)), ((), ())), preferred_element_type=jnp.float32
    ).astype(jnp.bfloat16)
    grouped = rotated_t.reshape(groups, group_width, row_count)
    received = lax.all_to_all(grouped, "sub", split_axis=0, concat_axis=2, tiled=True)
    columns = received.shape[2]
    blocks = received.reshape(group_width // SUBDIM, SUBDIM, columns)
    recon, sums_local, counts_local = lax.map(
        lambda pair: quantize_rows(pair[0], pair[1]), (blocks, codebooks)
    )
    recon_sent = recon.astype(jnp.bfloat16).reshape(1, group_width, columns)
    returned = lax.all_to_all(recon_sent, "sub", split_axis=2, concat_axis=0, tiled=True)
    recon_t = returned.reshape(width, row_count)
    total = row_count * lax.axis_size("row") * groups * lax.axis_size("rep")
    code_sums, counts = lax.psum((sums_local, counts_local), ("row", "rep"))
    partial_term = lax.dot_general(
        vectors, recon_t, (((0,), (1,)), ((), ())), preferred_element_type=jnp.float32
    )
    whole_cross = lax.psum(partial_term, ("row", "sub", "rep"))
    cross_rows = lax.dynamic_slice_in_dim(
        whole_cross, lax.axis_index("sub") * group_width, group_width, 0
    )
    new_codebooks = (code_sums + codebooks) / (counts[:, :, None] + 1.0)
    reconstruction = recon_t.T
    return (reconstruction, new_codebooks, cross_rows / total)


def solution(mesh):
    placed = (P(("dom", "row", "sub", "rep"), None), P("dom", None), P(("dom", "sub"), None, None))
    return jax.shard_map(
        on_device,
        mesh=mesh,
        in_specs=placed,
        out_specs=(
            P(("dom", "row", "sub", "rep"), None),
            P(("dom", "sub"), None, None),
            P(("dom", "sub"), None),
        ),
        check_vma=False,
    )
```

profile of v0, /device:TPU:0, one launch (start us, length us, event | category | flops | bytes accessed | tf_op | source)
XLA Modules:
  0.0 368.6 jit_solution(16869227199885064852)
XLA Ops:
  8.5 3.8 %convolution_convert_fusion = bf16[768,896]{1,0:T(8,128)(2,1)} fusion(bf16[768,768]{1,0:T(8,128)(2,1)} %param.6, bf16[896,768]{1,0:T(8,128)(2,1)S(1)} %copy-done), kind=kOutput, calls=%fused_computation.25 | convolution fusion | flops 1057652736 | bytes 3932160 | tf_op jit(solution)/shard_map/dot_general | solution.py:31
  12.3 4.2 %all-to-all-start = ((bf16[2,384,896]{2,1,0:T(8,128)(2,1)}), bf16[2,384,896]{2,1,0:T(8,128)(2,1)S(1)}, u32[]{:S(2)}, u32[]{:S(2)}) async-start(bf16[2,384,896]{2,1,0:T(8,128)(2,1)} %bitcast.68), calls=%async_computation | async-start | bytes 2752512 | tf_op jit(solution)/shard_map/all_to_all | solution.py:35
  16.5 18.0 %all-to-all-done = bf16[2,384,896]{2,1,0:T(8,128)(2,1)S(1)} async-done(((bf16[2,384,896]{2,1,0:T(8,128)(2,1)}), bf16[2,384,896]{2,1,0:T(8,128)(2,1)S(1)}, u32[]{:S(2)}, u32[]{:S(2)}) %all-to-all-start) | async-done | bytes 1376288 | tf_op jit(solution)/shard_map/all_to_all | solution.py:35
  34.5 2.5 copy.16
  37.0 3.5 reshape.26
  40.5 130.4 %while.14 = (s32[]{:T(128)}, bf16[24,16,1792]{2,1,0:T(8,128)(2,1)}, f32[24,256,16]{1,2,0:T(8,128)}, f32[24,256]{1,0:T(8,128)S(1)}, f32[24,256,16]{1,2,0:T(8,128)...) while((s32[]{:T(128)}, bf16[24,16,1792]{2,1,0:T(8,128)(2,1)}, f32[24,256,16]{1,2,0:T(8,128)}, ...), condition=%wide.region_5.6_spmd, body=%wide.region_0.5_spmd.sunk | while | flops 270209024 | bytes 9546853 | solution.py:38
  41.9 1.8 fusion.43
  58.2 1.8 fusion.43
  74.5 1.8 fusion.43
  80.0 1.8 fusion.43
  90.8 1.8 fusion.43
  96.3 1.8 fusion.43
  101.7 1.8 fusion.43
  170.9 7.0 %copy.17 = bf16[1,384,1792]{1,0,2:T(2,128)(2,1)} copy(bf16[1,384,1792]{2,1,0:T(8,128)(2,1)} %bitcast.67) | data formatting | bytes 2752512 | tf_op jit(solution)/shard_map/reshape | solution.py:41
  178.4 12.4 %reduce = bf16[1792,384]{1,0:T(8,128)(2,1)S(1)} reduce(bf16[1792,1,384]{2,1,0:T(2,128)(2,1)} %bitcast.61, bf16[]{:T(256)} %broadcast.16), dimensions={1}, to_apply=%bitcast.35.reduce_sub_computation | reduce | bytes 2752514
  192.0 3.6 all-to-all-start.1
  196.7 15.8 %all-to-all-done.1 = bf16[2,2,172032]{2,1,0:T(2,128)(2,1)S(1)} async-done(((bf16[2,2,172032]{2,1,0:T(2,128)(2,1)}), bf16[2,2,172032]{2,1,0:T(2,128)(2,1)S(1)}, u32[]{:S(2)}, u32[]{:S(2)}) %all-to-all-start.1) | async-done | bytes 1376288 | tf_op jit(solution)/shard_map/all_to_all | solution.py:42
  212.5 2.3 reshape.30
  214.8 3.1 copy.21
  219.7 2.8 convolution_bitcast_fusion.2
  222.5 27.0 %psum.22 = f32[24,256]{1,0:T(8,128)S(1)} all-reduce(f32[24,256]{1,0:T(8,128)S(1)} %get-tuple-element.39), channel_id=1, replica_groups=mesh['dom'=2,'row'=4,'sub'=2,'rep'=2] {'row','rep'}, use_global_device_ids=true, to_apply=%region_7.8 | all-reduce | flops 6144 | bytes 49152 | tf_op jit(solution)/shard_map/psum | solution.py:45
  249.5 7.6 %all-reduce.3.cloned.1.call-done = f32[24,256,16]{1,2,0:T(8,128)} async-done(((f32[24,256,16]{1,2,0:T(8,128)}), f32[24,256,16]{1,2,0:T(8,128)}) %all-reduce.3.cloned.1.call-update) | async-done | bytes 393232 | tf_op jit(solution)/shard_map/psum | solution.py:45
  257.1 1.8 add_divide_fusion
  260.4 98.6 %all-reduce.5.cloned.1.call-done = f32[768,768]{0,1:T(8,128)} async-done(((f32[768,768]{0,1:T(8,128)}), f32[768,768]{0,1:T(8,128)}) %all-reduce.5.cloned.1.call-update) | async-done | bytes 2359312 | tf_op jit(solution)/shard_map/psum | solution.py:49
  (179 shorter events, 127.1 us)
Async XLA Ops:
  7.2 1.3 copy-start
  12.3 22.2 %all-to-all-start = ((bf16[2,384,896]{2,1,0:T(8,128)(2,1)}), bf16[2,384,896]{2,1,0:T(8,128)(2,1)S(1)}, u32[]{:S(2)}, u32[]{:S(2)}) async-start(bf16[2,384,896]{2,1,0:T(8,128)(2,1)} %bitcast.68), calls=%async_computation | async-start | bytes 2752512 | tf_op jit(solution)/shard_map/all_to_all | solution.py:35
  37.0 3.5 copy-start.1
  192.0 20.5 %all-to-all-start.1 = ((bf16[2,2,172032]{2,1,0:T(2,128)(2,1)}), bf16[2,2,172032]{2,1,0:T(2,128)(2,1)S(1)}, u32[]{:S(2)}, u32[]{:S(2)}) async-start(bf16[2,2,172032]{2,1,0:T(2,128)(2,1)} %reshape.29), calls=%async_computation.1 | async-start | bytes 2752512 | tf_op jit(solution)/shard_map/all_to_all | solution.py:42
  195.7 61.4 %all-reduce.3.cloned.1.call-start = ((), (), s32[]{:S(2)}) async-start(), calls=%async_computation.2 | async-start | bytes 786432 | tf_op jit(solution)/shard_map/psum | solution.py:45
  196.4 162.6 %all-reduce.5.cloned.1.call-start = ((), (), s32[]{:S(2)}) async-start(), calls=%async_computation.3 | async-start | bytes 4718592 | tf_op jit(solution)/shard_map/psum | solution.py:49
Sparse Core Ops, SparseCore 0:
  199.4 57.6 all-reduce.2
  261.1 97.9 all-reduce.4
where the time goes:
time: 369 us
  waiting for transfers between devices  141 us (38%)
  matrix products  119 us (32%)
  other arithmetic  31.9 us (9%)
  local copies, waits for them, and re-layouts  27.1 us (7%)
  blocking collectives  27 us (7%)
  between operations  14.1 us (4%)
  starting transfers between devices  8.1 us (2%)
    psum x1, waiting for transfers between devices, on_device(): whole_cross = lax.psum(partial_term, ('row', 'sub', 'rep'))  98.6 us
    dot_general x24, matrix products, quantize_rows(): recon = jnp.dot(codebook.T, weights, precision=lax.Precision.HIGHEST)  43.4 us
    dot_general x24, matrix products, quantize_rows(): lax.dot_general(weights, block, (((1,), (1,)), ((), ())), precision=lax.P...  43.1 us
    psum x1, blocking collectives, on_device(): code_sums, counts = lax.psum((sums_local, counts_local), ('row', 'rep'))  27 us
    dot_general x24, matrix products, quantize_rows(): cross_product = jnp.dot(codebook, block, precision=lax.Precision.HIGHEST)  25.8 us
    all_to_all x1, waiting for transfers between devices, on_device(): lax.all_to_all(grouped, 'sub', split_axis=0, concat_axis=2, tiled=True)  18 us
    all_to_all x1, waiting for transfers between devices, on_device(): lax.all_to_all(recon_sent, 'sub', split_axis=2, concat_axis=0, tiled=True)  15.8 us
    unnamed x1, other arithmetic  12.4 us
  transfers between devices with their start and end apart: 4, of which 4 were waited for; matrix products, arithmetic and copies ran while one was open for 4% of the time, Pallas kernels for 0%

commit v1 on v0

v1 whole, which is shorter than its diff:
```python
import functools
import math

import jax
import jax.numpy as jnp
from jax import lax
from jax.experimental import pallas as pl
from jax.experimental.pallas import tpu as pltpu
from jax.sharding import PartitionSpec as P

SUBDIM = 16
SOFTNESS = 4.0
LOG2E = math.log2(math.e)
F32, BF16 = jnp.float32, jnp.bfloat16
GROUP = 4
VMEM_BYTES = 56 * 2**20


def quantize_rows(block, codebook):
    block = block.astype(F32)
    cross_product = jnp.dot(codebook, block, precision=lax.Precision.HIGHEST)
    squared_norms = jnp.sum(codebook * codebook, axis=1)
    affinity_scores = (2.0 * cross_product - squared_norms[:, None]) / SOFTNESS
    weights = jax.nn.softmax(affinity_scores, axis=0)
    recon = jnp.dot(codebook.T, weights, precision=lax.Precision.HIGHEST)
    sums = lax.dot_general(weights, block, (((1,), (1,)), ((), ())), precision=lax.Precision.HIGHEST)
    return recon, sums, jnp.sum(weights, axis=1)


def any_mesh(vectors, rotation, codebooks):
    rows, width = vectors.shape
    groups = lax.axis_size("sub")
    part = width // groups
    rotated_t = lax.dot_general(
        rotation, vectors, (((0,), (1,)), ((), ())), preferred_element_type=F32
    ).astype(BF16)
    received = lax.all_to_all(rotated_t.reshape(groups, part, rows), "sub", split_axis=0, concat_axis=2, tiled=True)
    columns = received.shape[2]
    blocks = received.reshape(part // SUBDIM, SUBDIM, columns)
    recon, sums, counts = lax.map(lambda pair: quantize_rows(pair[0], pair[1]), (blocks, codebooks))
    sent = recon.astype(BF16).reshape(1, part, columns)
    recon_t = lax.all_to_all(sent, "sub", split_axis=2, concat_axis=0, tiled=True).reshape(width, rows)
    total = rows * lax.axis_size("row") * groups * lax.axis_size("rep")
    sums, counts = lax.psum((sums, counts), ("row", "rep"))
    term = lax.dot_general(vectors, recon_t, (((0,), (1,)), ((), ())), preferred_element_type=F32)
    whole = lax.psum(term, ("row", "sub", "rep"))
    mine = lax.dynamic_slice_in_dim(whole, lax.axis_index("sub") * part, part, 0)
    return recon_t.T, (sums + codebooks) / (counts[:, :, None] + 1.0), mine / total


def rotate_kernel(vec_ref, rot_ref, y_ref, rott_ref):
    s, r = lax.axis_index("sub"), lax.axis_index("rep")
    n, w = y_ref.shape[0], y_ref.shape[1]
    turned = rot_ref[...].T
    for h in range(n):
        for q in range(2):
            @pl.when(r == q)
            def _():
                rott_ref[(h + n - s) % n] = turned[(2 * h + q) * w : (2 * h + q + 1) * w]
    for k in range(n):
        y_ref[k] = lax.dot_general(
            rott_ref[k], vec_ref[...], (((1,), (1,)), ((), ())), preferred_element_type=F32
        ).astype(BF16)


def rotate_more_kernel(vec_ref, rott_ref, y_ref):
    for k in range(y_ref.shape[0]):
        y_ref[k] = lax.dot_general(
            rott_ref[k], vec_ref[...], (((1,), (1,)), ((), ())), preferred_element_type=F32
        ).astype(BF16)


def operands(c):
    codes = c.shape[1]
    scaled = c * (2.0 / SOFTNESS * LOG2E)
    hi = scaled.astype(BF16).astype(F32)
    mid = (scaled - hi).astype(BF16).astype(F32)
    lo = (scaled - hi) - mid
    n = jnp.sum(c * c, axis=0, keepdims=True) * (-LOG2E / SOFTNESS)
    n_hi = n.astype(BF16).astype(F32)
    n_mid = (n - n_hi).astype(BF16).astype(F32)
    n_lo = (n - n_hi) - n_mid
    row = lax.broadcasted_iota(jnp.int32, (SUBDIM, codes), 0)
    norms = jnp.where(row == 0, n_hi, jnp.where(row == 1, n_mid, jnp.where(row == 2, n_lo, 0.0)))
    a = jnp.concatenate([hi, mid, lo, norms], axis=0).T.astype(BF16)
    c_hi = c.astype(BF16)
    c_lo = (c - c_hi.astype(F32)).astype(BF16)
    b = jnp.concatenate([c_hi, c_lo, jnp.ones((SUBDIM, codes), BF16)], axis=0)
    return a, b


def quantize_kernel(cb_ref, y0_ref, y1_ref, v0_hbm, v1_hbm, rec0_ref, rec1_ref, keep_ref, send_ref,
                    v0, v1, cnt, sem0, sem1, *, k, per):
    step, steps = pl.program_id(0), pl.num_programs(0)
    s, r = lax.axis_index("sub"), lax.axis_index("rep")
    codes = cb_ref.shape[2]
    cols = y0_ref.shape[2]
    w = per * SUBDIM
    lanes = 128
    part = v0.shape[1] // 2
    base = r * per if k == 0 else 0
    p_rows = (part // lanes) * w
    sums_ref = keep_ref if k == 0 else send_ref

    @pl.when(step == 0)
    def _():
        pltpu.make_async_copy(v0_hbm, v0, sem0).start()
        pltpu.make_async_copy(v1_hbm, v1, sem1).start()
        cnt[...] = jnp.zeros_like(cnt)

    ab = [operands(cb_ref[base + step * GROUP + j]) for j in range(GROUP)]
    acc = [jnp.zeros((2 * SUBDIM, codes), F32) for _ in range(GROUP)]
    ys, recs = (y0_ref, y1_ref), (rec0_ref, rec1_ref)
    ones = jnp.ones((SUBDIM, cols), BF16)

    def score(j, i):
        y = ys[i][0, SUBDIM * j : SUBDIM * (j + 1), :]
        return y, jnp.dot(ab[j][0], jnp.concatenate([y, y, y, ones], axis=0), preferred_element_type=F32)

    def spread(sc):
        return jnp.exp2(sc - jnp.max(sc, axis=0, keepdims=True)).astype(BF16)

    def finish(j, i, y, e):
        out = jnp.dot(ab[j][1], e, preferred_element_type=F32)
        inv = 1.0 / out[2 * SUBDIM :]
        at = pl.multiple_of(step * (GROUP * SUBDIM), GROUP * SUBDIM) + SUBDIM * j
        recs[i][pl.ds(pl.multiple_of(at, SUBDIM), SUBDIM), :] = (
            (out[:SUBDIM] + out[SUBDIM : 2 * SUBDIM]) * inv
        ).astype(BF16)
        yz = jnp.concatenate([(y.astype(F32) * inv).astype(BF16), inv.astype(BF16)], axis=0)
        acc[j] = acc[j] + lax.dot_general(yz, e, (((1,), (1,)), ((), ())), preferred_element_type=F32)

    work = [(j, i) for j in range(GROUP) for i in range(2)]
    first = second = None
    for item in work + [None, None]:
        new_first = (item, *score(*item)) if item is not None else None
        new_second = (first[0], first[1], spread(first[2])) if first is not None else None
        if second is not None:
            finish(*second[0], second[1], second[2])
        first, second = new_first, new_second

    for j in range(GROUP):
        m = step * GROUP + j
        for half in range(codes // lanes):
            at = p_rows + half * w + m * SUBDIM
            sums_ref[pl.ds(pl.multiple_of(at, SUBDIM), SUBDIM), :] = acc[j][
                :SUBDIM, half * lanes : (half + 1) * lanes
            ].astype(sums_ref.dtype)
            cnt[pl.ds(half * SUBDIM + m, 1), :] = acc[j][SUBDIM : SUBDIM + 1, half * lanes : (half + 1) * lanes]

    @pl.when(step == steps - 1)
    def _():
        at = p_rows + (codes // lanes) * w
        sums_ref[at : at + cnt.shape[0], :] = cnt[...].astype(sums_ref.dtype)
        pltpu.make_async_copy(v0_hbm, v0, sem0).wait()
        pltpu.make_async_copy(v1_hbm, v1, sem1).wait()
        cross = jnp.dot(rec0_ref[...], v0[...], preferred_element_type=F32) + jnp.dot(
            rec1_ref[...], v1[...], preferred_element_type=F32
        )
        for h in range(2):
            @pl.when(s == h)
            def _():
                for g in range(part // lanes):
                    near = h * part + g * lanes
                    far = (1 - h) * part + g * lanes
                    keep_ref[g * w : (g + 1) * w, :] = cross[:, near : near + lanes]
                    send_ref[g * w : (g + 1) * w, :] = cross[:, far : far + lanes].astype(BF16)


def turn_kernel(m0_ref, m1_ref, t0_ref, t1_ref, out_ref, buf):
    s, r = lax.axis_index("sub"), lax.axis_index("rep")
    w = m0_ref.shape[0]
    for k, (mine, theirs) in enumerate(((m0_ref, t0_ref), (m1_ref, t1_ref))):
        h = (s + k) % 2
        buf[pl.ds(pl.multiple_of((2 * h + r) * w, SUBDIM), w), :] = mine[...]
        buf[pl.ds(pl.multiple_of((2 * h + 1 - r) * w, SUBDIM), w), :] = theirs[...]
    out_ref[...] = buf[...].T


def final_kernel(mine_ref, theirs_ref, cb_ref, cross_ref, new_ref, buf, *, per, total):
    s, r, z = lax.axis_index("sub"), lax.axis_index("rep"), lax.axis_index("row")
    n = mine_ref.shape[0]
    piece = mine_ref.shape[1]
    lanes = 128
    w = per * SUBDIM
    codes = cb_ref.shape[2]
    groups = cross_ref.shape[0] // lanes
    halves = codes // lanes
    for side, ref in enumerate((mine_ref, theirs_ref)):
        for d in range(n):
            at = ((z + n - d) % n) * piece
            buf[side, pl.ds(pl.multiple_of(at, SUBDIM), piece), :] = ref[d].astype(F32)
    a_rows = groups * w + halves * (w + SUBDIM)
    for g in range(groups):
        for h in range(2):
            for q in range(2):
                @pl.when((s == h) & (r == q))
                def _():
                    pieces = []
                    for col in range(2):
                        k = col ^ h
                        for rep in range(2):
                            start = k * a_rows + g * w
                            pieces.append(buf[rep ^ q, start : start + w, :])
                    cross_ref[g * lanes : (g + 1) * lanes, :] = jnp.concatenate(pieces, axis=0).T * (1.0 / total)
    first = groups * w
    for side in range(2):
        part = r if side == 0 else 1 - r
        for m in range(per):
            c = cb_ref[part * per + m]
            sums = jnp.concatenate(
                [buf[side, first + hf * w + m * SUBDIM : first + hf * w + (m + 1) * SUBDIM, :] for hf in range(halves)],
                axis=1,
            )
            at = first + halves * w + m
            count = jnp.concatenate([buf[side, at + hf * SUBDIM : at + hf * SUBDIM + 1, :] for hf in range(halves)], axis=1)
            new_ref[part * per + m] = (sums + c) / (count + 1.0)


def shifts(x, n, d):
    return lax.ppermute(x, "row", [(i, (i + d) % n) for i in range(n)])


def on_device(vectors, rotation, codebooks):
    rows, width = vectors.shape
    subs, rows_n = 2, lax.axis_size("row")
    part = width // subs
    per = part // SUBDIM // 2
    w = per * SUBDIM
    codes = codebooks.shape[1]
    lanes = 128
    steps = per // GROUP
    total = rows * rows_n * subs * 2
    swap = [(0, 1), (1, 0)]
    r, z = lax.axis_index("rep"), lax.axis_index("row")
    params = pltpu.CompilerParams(vmem_limit_bytes=VMEM_BYTES)
    vmem = pl.BlockSpec(memory_space=pltpu.VMEM)

    cb = codebooks.transpose(0, 2, 1)
    cb_far = lax.ppermute(lax.dynamic_slice_in_dim(cb, r * per, per, 0), "sub", swap)
    vec_far = lax.ppermute(vectors, "rep", swap)

    y_shape = jax.ShapeDtypeStruct((subs, w, rows), BF16)
    y0, rott = pl.pallas_call(
        rotate_kernel,
        out_shape=(y_shape, jax.ShapeDtypeStruct((subs, w, width), BF16)),
        in_specs=[vmem] * 2,
        out_specs=(vmem, vmem),
        compiler_params=params,
        name="rotate",
    )(vectors, rotation)
    y1 = pl.pallas_call(
        rotate_more_kernel, out_shape=y_shape, in_specs=[vmem] * 2, out_specs=vmem, compiler_params=params, name="rotate_far"
    )(vec_far, rott)

    p_rows = (part // lanes) * w
    s_rows = (codes // lanes) * (w + SUBDIM)
    rec_shape = jax.ShapeDtypeStruct((w, rows), BF16)

    def quantize(k, cb_k):
        n_keep, n_send = (p_rows + s_rows, p_rows) if k == 0 else (p_rows, p_rows + s_rows)
        whole = lambda shape: pl.BlockSpec(shape, lambda m: (0,) * len(shape))
        y_spec = pl.BlockSpec((1, GROUP * SUBDIM, rows), lambda m: (k, m, 0))
        any_spec = pl.BlockSpec(memory_space=pl.ANY)
        return pl.pallas_call(
            functools.partial(quantize_kernel, k=k, per=per),
            grid=(steps,),
            in_specs=[whole(cb_k.shape), y_spec, y_spec, any_spec, any_spec],
            out_specs=[whole((w, rows)), whole((w, rows)), whole((n_keep, lanes)), whole((n_send, lanes))],
            out_shape=[
                rec_shape,
                rec_shape,
                jax.ShapeDtypeStruct((n_keep, lanes), F32),
                jax.ShapeDtypeStruct((n_send, lanes), BF16),
            ],
            scratch_shapes=[
                pltpu.VMEM((rows, width), BF16),
                pltpu.VMEM((rows, width), BF16),
                pltpu.VMEM(((codes // lanes) * SUBDIM, lanes), F32),
                pltpu.SemaphoreType.DMA,
                pltpu.SemaphoreType.DMA,
            ],
            compiler_params=params,
            name="quantize_near" if k == 0 else "quantize_far",
        )(cb_k, y0, y1, vectors, vec_far)

    mine0, other0, keep0, send0 = quantize(0, cb)
    got0 = lax.ppermute(send0, "sub", swap)
    theirs0 = lax.ppermute(other0, "rep", swap)
    mine1, other1, keep1, send1 = quantize(1, cb_far)
    got1 = lax.ppermute(send1, "sub", swap)
    theirs1 = lax.ppermute(other1, "rep", swap)

    reconstruction = pl.pallas_call(
        turn_kernel,
        out_shape=jax.ShapeDtypeStruct((rows, width), BF16),
        in_specs=[vmem] * 4,
        out_specs=vmem,
        scratch_shapes=[pltpu.VMEM((width, rows), BF16)],
        compiler_params=params,
        name="turn",
    )(mine0, mine1, theirs0, theirs1)

    used = 2 * p_rows + s_rows
    piece = -(-used // (rows_n * SUBDIM)) * SUBDIM
    pad = jnp.zeros((piece * rows_n - used, lanes), BF16)
    half = jnp.concatenate(
        [(keep0 + got1.astype(F32)).astype(BF16), (keep1 + got0.astype(F32)).astype(BF16), pad], axis=0
    ).reshape(rows_n, piece, lanes)
    own = lax.dynamic_index_in_dim(half, z, 0, keepdims=False)
    gathered = [
        shifts(lax.dynamic_index_in_dim(half, (z + d) % rows_n, 0, keepdims=False), rows_n, d) for d in range(1, rows_n)
    ]
    summed = functools.reduce(lambda a, b: a + b.astype(F32), gathered, own.astype(F32)).astype(BF16)
    all_mine = jnp.stack([summed] + [shifts(summed, rows_n, d) for d in range(1, rows_n)])
    all_theirs = lax.ppermute(all_mine, "rep", swap)

    cross, new = pl.pallas_call(
        functools.partial(final_kernel, per=per, total=total),
        out_shape=(jax.ShapeDtypeStruct((part, width), F32), jax.ShapeDtypeStruct(cb.shape, F32)),
        in_specs=[vmem] * 3,
        out_specs=(vmem, vmem),
        scratch_shapes=[pltpu.VMEM((2, rows_n * piece, lanes), F32)],
        compiler_params=params,
        name="final",
    )(all_mine, all_theirs, cb)
    return reconstruction, new.transpose(0, 2, 1), cross


def solution(mesh):
    placed = (P(("dom", "row", "sub", "rep"), None), P("dom", None), P(("dom", "sub"), None, None))
    body = on_device if mesh.shape["sub"] == 2 and mesh.shape["row"] <= 8 else any_mesh
    return jax.shard_map(
        body,
        mesh=mesh,
        in_specs=placed,
        out_specs=(
            P(("dom", "row", "sub", "rep"), None),
            P(("dom", "sub"), None, None),
            P(("dom", "sub"), None),
        ),
        check_vma=False,
    )
```

time: 369 us -> 81 us (0.22)
  waiting for transfers between devices: 141 us -> 21.5 us
  matrix products: 119 us -> 0 us
  Pallas kernels: 0 us -> 36.9 us
  other arithmetic: 31.9 us -> 1.45 us
  blocking collectives: 27 us -> 0 us
  local copies, waits for them, and re-layouts: 27.1 us -> 4.3 us
  between operations: 14.1 us -> 0.75 us
  starting transfers between devices: 8.1 us -> 15.8 us
    dot_general x74 -> x0, matrix products: 119 us -> none  [the longest x24 43.4 us: quantize_rows(): recon = jnp.dot(codebook.T, weights, precision=lax.Precision.HIGHEST)]
    psum x2 -> x0, waiting for transfers between devices: 106 us -> none  [the longest x1 98.6 us: on_device(): whole_cross = lax.psum(partial_term, ('row', 'sub', 'rep'))]
    pallas_call x0 -> x6, Pallas kernels: none -> 36.9 us  [the longest x2 23.6 us: quantize(): pl.pallas_call(functools.partial(quantize_kernel, k=k, per=per), grid=(st...]
    all_to_all x2 -> x0, waiting for transfers between devices: 33.8 us -> none  [the longest x1 18 us: on_device(): lax.all_to_all(grouped, 'sub', split_axis=0, concat_axis=2, tiled=True)]
    psum x1 -> x0, blocking collectives: 27 us -> none  [on_device(): code_sums, counts = lax.psum((sums_local, counts_local), ('row', 'rep'))]
    ppermute x0 -> x13, waiting for transfers between devices: none -> 21.5 us  [the longest x6 14 us: shifts(): return lax.ppermute(x, 'row', [(i, (i + d) % n) for i in range(n)])]
    reduce_sum x72 -> x0, other arithmetic: 16.4 us -> none  [the longest x24 9.31 us: quantize_rows(): counts = jnp.sum(weights, axis=1)]
    ppermute x0 -> x13, starting transfers between devices: none -> 15.8 us  [the longest x6 9.94 us: shifts(): return lax.ppermute(x, 'row', [(i, (i + d) % n) for i in range(n)])]
  transfers between devices with their start and end apart: 4 -> 13, of which waited for: 4 -> 9; matrix products, arithmetic and copies ran while one was open for 4% -> 3% of each run, Pallas kernels for 0% -> 42%
where the time goes in v1:
time: 81 us; the launch traced here: 80.7 us
  Pallas kernels  36.9 us (46%)
  waiting for transfers between devices  21.5 us (27%)
  starting transfers between devices  15.8 us (20%)
  local copies, waits for them, and re-layouts  4.3 us (5%)
  other arithmetic  1.45 us (2%)
    pallas_call x2, Pallas kernels, quantize(): pl.pallas_call(functools.partial(quantize_kernel, k=k, per=per), grid=(st...  23.6 us
    ppermute x6, waiting for transfers between devices, shifts(): return lax.ppermute(x, 'row', [(i, (i + d) % n) for i in range(n)])  14 us
    ppermute x6, starting transfers between devices, shifts(): return lax.ppermute(x, 'row', [(i, (i + d) % n) for i in range(n)])  9.94 us
    ppermute x1, waiting for transfers between devices, on_device(): got1 = lax.ppermute(send1, 'sub', swap)  5.35 us
    pallas_call x1, Pallas kernels, on_device(): pl.pallas_call(rotate_kernel, out_shape=(y_shape, jax.ShapeDtypeStruct((s...  3.94 us
    pallas_call x1, Pallas kernels, on_device(): pl.pallas_call(rotate_more_kernel, out_shape=y_shape, in_specs=[vmem] * 2...  3.32 us
    unnamed x18, local copies, waits for them, and re-layouts  3.25 us
    pallas_call x1, Pallas kernels, on_device(): pl.pallas_call(functools.partial(final_kernel, per=per, total=total), out...  3.08 us
  transfers between devices with their start and end apart: 13, of which 9 were waited for; matrix products, arithmetic and copies ran while one was open for 3% of the time, Pallas kernels for 42%

profile of v1, /device:TPU:0, one launch (start us, length us, event | category | flops | bytes accessed | tf_op | source)
XLA Modules:
  0.0 80.7 jit_solution(3154108993885529293)
XLA Ops:
  1.1 0.9 %dynamic-slice_bitcast_fusion = f32[12,16,256]{2,1,0:T(8,128)S(1)} fusion(f32[24,256,16]{1,2,0:T(8,128)} %param.5, s32[]{:T(128)S(6)} %select_n.31), kind=kLoop, calls=%fused_computation.8 | loop fusion | bytes 393220 | tf_op jit(solution)/shard_map/dynamic_slice | solution.py:240
  2.1 2.6 %collective-permute-start.1 = (f32[12,16,256]{2,1,0:T(8,128)S(1)}, f32[12,16,256]{2,1,0:T(8,128)S(1)}, u32[]{:S(2)}, u32[]{:S(2)}) collective-permute-start(f32[12,16,256]{2,1,0:T(8,128)S(1)} %dynamic-slice_bitcast_fusion), channel_id=1, source_target_pairs={{0,2},{2,0},{1,3},{3,1},{4,6},{6,4},{5,7},{7,5},{8,10},{10,8},{9,1... | collective-permute-start | bytes 589832 | tf_op jit(solution)/shard_map/ppermute | solution.py:240
  4.7 3.9 %rotate.1 = (bf16[2,192,896]{2,1,0:T(8,128)(2,1)}, bf16[2,192,768]{2,1,0:T(8,128)(2,1)}) custom-call(bf16[896,768]{1,0:T(8,128)(2,1)} %v0_hbm.3, bf16[768,768]{1,0:T(8,128)(2,1)} %rot_ref.1), custom_call_target="tpu_custom_call" | custom-call | tf_op jit(solution)/shard_map/rotate/pallas_call | solution.py:244
  8.6 1.1 %copy-done = bf16[896,768]{1,0:T(8,128)(2,1)} copy-done((bf16[896,768]{1,0:T(8,128)(2,1)}, bf16[896,768]{1,0:T(8,128)(2,1)S(1)}, u32[]{:S(2)}) %copy-start) | copy-done | bytes 1376280
  9.7 3.3 %rotate_far.1.y1_ref = bf16[2,192,896]{2,1,0:T(8,128)(2,1)} custom-call(bf16[896,768]{1,0:T(8,128)(2,1)} %copy-done, bf16[2,192,768]{2,1,0:T(8,128)(2,1)} %get-tuple-element.16.rott_ref), custom_call_target="tpu_custom_call" | custom-call | tf_op jit(solution)/shard_map/rotate_far/pallas_call | solution.py:252
  13.0 11.9 %quantize_near.1 = (bf16[192,896]{1,0:T(8,128)(2,1)}, bf16[192,896]{1,0:T(8,128)(2,1)}, f32[992,128]{1,0:T(8,128)}, bf16[576,128]{1,0:T(8,128)(2,1)}) custom-call(f32[24,16,256]{2,1,0:T(8,128)} %bitcast.18, bf16[2,192,896]{2,1,0:T(8,128)(2,1)} %get-tuple-element.15.y0_ref, bf16[2,192,896]{2,1,0:T(8,128)(2,1)} %rotate_far.1.y1_ref, bf16[896,768]{1,0:T(8,128)(2,1)} %v0_hbm.3, ...), custom_call_target="tpu_custom_call" | custom-call | tf_op jit(solution)/shard_map/quantize_near/pallas_call | solution.py:265
  25.0 0.7 copy-done.6
  25.7 11.8 %quantize_far.1 = (bf16[192,896]{1,0:T(8,128)(2,1)}, bf16[192,896]{1,0:T(8,128)(2,1)}, f32[576,128]{1,0:T(8,128)}, bf16[992,128]{1,0:T(8,128)(2,1)}) custom-call(f32[12,16,256]{2,1,0:T(8,128)} %copy-done.6, bf16[2,192,896]{2,1,0:T(8,128)(2,1)} %get-tuple-element.15.y0_ref, bf16[2,192,896]{2,1,0:T(8,128)(2,1)} %rotate_far.1.y1_ref, bf16[896,768]{1,0:T(8,128)(2,1)} %v0_hbm.3, ...), custom_call_target="tpu_custom_call" | custom-call | tf_op jit(solution)/shard_map/quantize_far/pallas_call | solution.py:265
  37.4 2.1 %collective-permute-start.4 = (bf16[992,128]{1,0:T(8,128)(2,1)}, bf16[992,128]{1,0:T(8,128)(2,1)S(1)}, u32[]{:S(2)}, u32[]{:S(2)}) collective-permute-start(bf16[992,128]{1,0:T(8,128)(2,1)} %get-tuple-element.22), channel_id=1, source_target_pairs={{0,2},{2,0},{1,3},{3,1},{4,6},{6,4},{5,7},{7,5},{8,10},{10,8},{9,1... | collective-permute-start | bytes 761864 | tf_op jit(solution)/shard_map/ppermute | solution.py:291
  39.6 1.0 %add_convert_fusion.1 = bf16[576,128]{1,0:T(8,128)(2,1)S(1)} fusion(f32[576,128]{1,0:T(8,128)} %get-tuple-element.23, bf16[576,128]{1,0:T(8,128)(2,1)S(1)} %collective-permute-done.5), kind=kLoop, calls=%fused_computation.3 | loop fusion | flops 221184 | bytes 589824 | tf_op jit(solution)/shard_map/convert_element_type | solution.py:308
  40.6 5.4 %collective-permute-done.4 = bf16[992,128]{1,0:T(8,128)(2,1)S(1)} collective-permute-done((bf16[992,128]{1,0:T(8,128)(2,1)}, bf16[992,128]{1,0:T(8,128)(2,1)S(1)}, u32[]{:S(2)}, u32[]{:S(2)}) %collective-permute-start.4) | collective-permute-done | bytes 253984 | tf_op jit(solution)/shard_map/ppermute | solution.py:291
  46.3 1.9 %collective-permute-start.6 = (bf16[400,128]{1,0:T(8,128)(2,1)S(1)}, bf16[400,128]{1,0:T(8,128)(2,1)S(1)}, u32[]{:S(2)}, u32[]{:S(2)}) collective-permute-start(bf16[400,128]{1,0:T(8,128)(2,1)S(1)} %get-tuple-element.27), channel_id=1, source_target_pairs={{0,4},{4,8},{8,12},{12,0},{1,5},{5,9},{9,13},{13,1},{2,6},{6,10},{... | collective-permute-start | bytes 307208 | tf_op jit(solution)/shard_map/ppermute | solution.py:221
  48.2 2.6 %collective-permute-start.7 = (bf16[400,128]{1,0:T(8,128)(2,1)S(1)}, bf16[400,128]{1,0:T(8,128)(2,1)S(1)}, u32[]{:S(2)}, u32[]{:S(2)}) collective-permute-start(bf16[400,128]{1,0:T(8,128)(2,1)S(1)} %get-tuple-element.29), channel_id=1, source_target_pairs={{0,8},{4,12},{8,0},{12,4},{1,9},{5,13},{9,1},{13,5},{2,10},{6,14},... | collective-permute-start | bytes 307208 | tf_op jit(solution)/shard_map/ppermute | solution.py:221
  50.8 1.3 %collective-permute-start.8 = (bf16[400,128]{1,0:T(8,128)(2,1)S(1)}, bf16[400,128]{1,0:T(8,128)(2,1)S(1)}, u32[]{:S(2)}, u32[]{:S(2)}) collective-permute-start(bf16[400,128]{1,0:T(8,128)(2,1)S(1)} %get-tuple-element.28), channel_id=1, source_target_pairs={{0,12},{4,0},{8,4},{12,8},{1,13},{5,1},{9,5},{13,9},{2,14},{6,2},{... | collective-permute-start | bytes 307208 | tf_op jit(solution)/shard_map/ppermute | solution.py:221
  52.1 1.9 %collective-permute-done.6 = bf16[400,128]{1,0:T(8,128)(2,1)S(1)} collective-permute-done((bf16[400,128]{1,0:T(8,128)(2,1)S(1)}, bf16[400,128]{1,0:T(8,128)(2,1)S(1)}, u32[]{:S(2)}, u32[]{:S(2)}) %collective-permute-start.6) | collective-permute-done | bytes 102432 | tf_op jit(solution)/shard_map/ppermute | solution.py:221
  54.1 2.9 %collective-permute-done.7 = bf16[400,128]{1,0:T(8,128)(2,1)S(1)} collective-permute-done((bf16[400,128]{1,0:T(8,128)(2,1)S(1)}, bf16[400,128]{1,0:T(8,128)(2,1)S(1)}, u32[]{:S(2)}, u32[]{:S(2)}) %collective-permute-start.7) | collective-permute-done | bytes 102432 | tf_op jit(solution)/shard_map/ppermute | solution.py:221
  57.2 3.5 %collective-permute-start.11 = (bf16[400,128]{1,0:T(8,128)(2,1)S(1)}, bf16[400,128]{1,0:T(8,128)(2,1)S(1)}, u32[]{:S(2)}, u32[]{:S(2)}) collective-permute-start(bf16[400,128]{1,0:T(8,128)(2,1)S(1)} %fusion.2), channel_id=1, source_target_pairs={{0,12},{4,0},{8,4},{12,8},{1,13},{5,1},{9,5},{13,9},{2,14},{6,2},{... | collective-permute-start | bytes 307208 | tf_op jit(solution)/shard_map/ppermute | solution.py:221
  61.3 2.3 %collective-permute-done.11 = bf16[400,128]{1,0:T(8,128)(2,1)S(1)} collective-permute-done((bf16[400,128]{1,0:T(8,128)(2,1)S(1)}, bf16[400,128]{1,0:T(8,128)(2,1)S(1)}, u32[]{:S(2)}, u32[]{:S(2)}) %collective-permute-start.11) | collective-permute-done | bytes 102432 | tf_op jit(solution)/shard_map/ppermute | solution.py:221
  63.7 3.6 %collective-permute-done.9 = bf16[400,128]{1,0:T(8,128)(2,1)S(1)} collective-permute-done((bf16[400,128]{1,0:T(8,128)(2,1)S(1)}, bf16[400,128]{1,0:T(8,128)(2,1)S(1)}, u32[]{:S(2)}, u32[]{:S(2)}) %collective-permute-start.9) | collective-permute-done | bytes 102432 | tf_op jit(solution)/shard_map/ppermute | solution.py:221
  67.2 3.1 %collective-permute-done.10 = bf16[400,128]{1,0:T(8,128)(2,1)S(1)} collective-permute-done((bf16[400,128]{1,0:T(8,128)(2,1)S(1)}, bf16[400,128]{1,0:T(8,128)(2,1)S(1)}, u32[]{:S(2)}, u32[]{:S(2)}) %collective-permute-start.10) | collective-permute-done | bytes 102432 | tf_op jit(solution)/shard_map/ppermute | solution.py:221
  71.1 1.6 %collective-permute-done.3.t1_ref = bf16[192,896]{1,0:T(8,128)(2,1)S(1)} collective-permute-done((bf16[192,896]{1,0:T(8,128)(2,1)S(1)}, bf16[192,896]{1,0:T(8,128)(2,1)S(1)}, u32[]{:S(2)}, u32[]{:S(2)}) %collective-permute-start.3) | collective-permute-done | bytes 344096 | tf_op jit(solution)/shard_map/ppermute | solution.py:292
  73.9 2.9 %turn.1 = bf16[896,768]{1,0:T(8,128)(2,1)} custom-call(bf16[192,896]{1,0:T(8,128)(2,1)} %get-tuple-element.17.m0_ref, bf16[192,896]{1,0:T(8,128)(2,1)} %get-tuple-element.18.m1_ref, bf16[192,896]{1,0:T(8,128)(2,1)} %copy-done.5, bf16[192,896]{1,0:T(8,128)(2,1)} %copy-done.4), custom_call_target="tpu_custom_call" | custom-call | tf_op jit(solution)/shard_map/turn/pallas_call | solution.py:294
  76.8 0.8 copy-done.3
  77.6 3.1 %final.1 = (f32[384,768]{1,0:T(8,128)}, f32[24,16,256]{2,1,0:T(8,128)}) custom-call(bf16[4,400,128]{2,1,0:T(8,128)(2,1)} %copy-done.1, bf16[4,400,128]{2,1,0:T(8,128)(2,1)} %copy-done.3, f32[24,16,256]{2,1,0:T(8,128)} %bitcast.19), custom_call_target="tpu_custom_call" | custom-call | tf_op jit(solution)/shard_map/final/pallas_call | solution.py:318
  (35 shorter events, 3.8 us)
Async XLA Ops:
  0.6 8.0 %collective-permute-start = (bf16[896,768]{1,0:T(8,128)(2,1)}, bf16[896,768]{1,0:T(8,128)(2,1)S(1)}, u32[]{:S(2)}, u32[]{:S(2)}) collective-permute-start(bf16[896,768]{1,0:T(8,128)(2,1)} %v0_hbm.3), channel_id=1, source_target_pairs={{0,1},{1,0},{2,3},{3,2},{4,5},{5,4},{6,7},{7,6},{8,9},{9,8},{10,11... | collective-permute-start | bytes 4128776 | tf_op jit(solution)/shard_map/ppermute | solution.py:241
  2.1 22.9 %collective-permute-start.1 = (f32[12,16,256]{2,1,0:T(8,128)S(1)}, f32[12,16,256]{2,1,0:T(8,128)S(1)}, u32[]{:S(2)}, u32[]{:S(2)}) collective-permute-start(f32[12,16,256]{2,1,0:T(8,128)S(1)} %dynamic-slice_bitcast_fusion), channel_id=1, source_target_pairs={{0,2},{2,0},{1,3},{3,1},{4,6},{6,4},{5,7},{7,5},{8,10},{10,8},{9,1... | collective-permute-start | bytes 589832 | tf_op jit(solution)/shard_map/ppermute | solution.py:240
  8.6 1.1 %copy-start = (bf16[896,768]{1,0:T(8,128)(2,1)}, bf16[896,768]{1,0:T(8,128)(2,1)S(1)}, u32[]{:S(2)}) copy-start(bf16[896,768]{1,0:T(8,128)(2,1)S(1)} %collective-permute-done.vec_ref.v1_hbm) | copy-start | bytes 4128772
  24.9 21.1 %copy-start.2 = (f32[992,128]{1,0:T(8,128)S(1)}, f32[992,128]{1,0:T(8,128)}, u32[]{:S(2)}) copy-start(f32[992,128]{1,0:T(8,128)} %get-tuple-element.21) | copy-start | bytes 1523716
  24.9 14.7 %collective-permute-start.5 = (bf16[576,128]{1,0:T(8,128)(2,1)}, bf16[576,128]{1,0:T(8,128)(2,1)S(1)}, u32[]{:S(2)}, u32[]{:S(2)}) collective-permute-start(bf16[576,128]{1,0:T(8,128)(2,1)} %get-tuple-element.24), channel_id=1, source_target_pairs={{0,2},{2,0},{1,3},{3,1},{4,6},{6,4},{5,7},{7,5},{8,10},{10,8},{9,1... | collective-permute-start | bytes 442376 | tf_op jit(solution)/shard_map/ppermute | solution.py:288
  25.0 0.7 copy-start.6
  37.4 8.5 %collective-permute-start.4 = (bf16[992,128]{1,0:T(8,128)(2,1)}, bf16[992,128]{1,0:T(8,128)(2,1)S(1)}, u32[]{:S(2)}, u32[]{:S(2)}) collective-permute-start(bf16[992,128]{1,0:T(8,128)(2,1)} %get-tuple-element.22), channel_id=1, source_target_pairs={{0,2},{2,0},{1,3},{3,1},{4,6},{6,4},{5,7},{7,5},{8,10},{10,8},{9,1... | collective-permute-start | bytes 761864 | tf_op jit(solution)/shard_map/ppermute | solution.py:291
  46.0 24.5 %copy-start.8 = (bf16[192,896]{1,0:T(8,128)(2,1)S(1)}, bf16[192,896]{1,0:T(8,128)(2,1)}, u32[]{:S(2)}) copy-start(bf16[192,896]{1,0:T(8,128)(2,1)} %get-tuple-element.20) | copy-start | bytes 1032196
  46.0 25.0 %copy-start.7 = (bf16[192,896]{1,0:T(8,128)(2,1)S(1)}, bf16[192,896]{1,0:T(8,128)(2,1)}, u32[]{:S(2)}) copy-start(bf16[192,896]{1,0:T(8,128)(2,1)} %get-tuple-element.19) | copy-start | bytes 1032196
  46.3 7.7 %collective-permute-start.6 = (bf16[400,128]{1,0:T(8,128)(2,1)S(1)}, bf16[400,128]{1,0:T(8,128)(2,1)S(1)}, u32[]{:S(2)}, u32[]{:S(2)}) collective-permute-start(bf16[400,128]{1,0:T(8,128)(2,1)S(1)} %get-tuple-element.27), channel_id=1, source_target_pairs={{0,4},{4,8},{8,12},{12,0},{1,5},{5,9},{9,13},{13,1},{2,6},{6,10},{... | collective-permute-start | bytes 307208 | tf_op jit(solution)/shard_map/ppermute | solution.py:221
  48.2 8.8 %collective-permute-start.7 = (bf16[400,128]{1,0:T(8,128)(2,1)S(1)}, bf16[400,128]{1,0:T(8,128)(2,1)S(1)}, u32[]{:S(2)}, u32[]{:S(2)}) collective-permute-start(bf16[400,128]{1,0:T(8,128)(2,1)S(1)} %get-tuple-element.29), channel_id=1, source_target_pairs={{0,8},{4,12},{8,0},{12,4},{1,9},{5,13},{9,1},{13,5},{2,10},{6,14},... | collective-permute-start | bytes 307208 | tf_op jit(solution)/shard_map/ppermute | solution.py:221
  50.8 6.3 %collective-permute-start.8 = (bf16[400,128]{1,0:T(8,128)(2,1)S(1)}, bf16[400,128]{1,0:T(8,128)(2,1)S(1)}, u32[]{:S(2)}, u32[]{:S(2)}) collective-permute-start(bf16[400,128]{1,0:T(8,128)(2,1)S(1)} %get-tuple-element.28), channel_id=1, source_target_pairs={{0,12},{4,0},{8,4},{12,8},{1,13},{5,1},{9,5},{13,9},{2,14},{6,2},{... | collective-permute-start | bytes 307208 | tf_op jit(solution)/shard_map/ppermute | solution.py:221
  57.2 6.5 %collective-permute-start.11 = (bf16[400,128]{1,0:T(8,128)(2,1)S(1)}, bf16[400,128]{1,0:T(8,128)(2,1)S(1)}, u32[]{:S(2)}, u32[]{:S(2)}) collective-permute-start(bf16[400,128]{1,0:T(8,128)(2,1)S(1)} %fusion.2), channel_id=1, source_target_pairs={{0,12},{4,0},{8,4},{12,8},{1,13},{5,1},{9,5},{13,9},{2,14},{6,2},{... | collective-permute-start | bytes 307208 | tf_op jit(solution)/shard_map/ppermute | solution.py:221
  60.7 6.6 %collective-permute-start.9 = (bf16[400,128]{1,0:T(8,128)(2,1)S(1)}, bf16[400,128]{1,0:T(8,128)(2,1)S(1)}, u32[]{:S(2)}, u32[]{:S(2)}) collective-permute-start(bf16[400,128]{1,0:T(8,128)(2,1)S(1)} %fusion.2), channel_id=1, source_target_pairs={{0,4},{4,8},{8,12},{12,0},{1,5},{5,9},{9,13},{13,1},{2,6},{6,10},{... | collective-permute-start | bytes 307208 | tf_op jit(solution)/shard_map/ppermute | solution.py:221
  60.7 9.6 %collective-permute-start.10 = (bf16[400,128]{1,0:T(8,128)(2,1)S(1)}, bf16[400,128]{1,0:T(8,128)(2,1)S(1)}, u32[]{:S(2)}, u32[]{:S(2)}) collective-permute-start(bf16[400,128]{1,0:T(8,128)(2,1)S(1)} %fusion.2), channel_id=1, source_target_pairs={{0,8},{4,12},{8,0},{12,4},{1,9},{5,13},{9,1},{13,5},{2,10},{6,14},... | collective-permute-start | bytes 307208 | tf_op jit(solution)/shard_map/ppermute | solution.py:221
  70.4 6.4 %copy-start.1 = (bf16[4,400,128]{2,1,0:T(8,128)(2,1)}, bf16[4,400,128]{2,1,0:T(8,128)(2,1)S(1)}, u32[]{:S(2)}) copy-start(bf16[4,400,128]{2,1,0:T(8,128)(2,1)S(1)} %pad_maximum_fusion.mine_ref) | copy-start | bytes 1228804
  70.4 6.4 %collective-permute-start.12 = (bf16[4,400,128]{2,1,0:T(8,128)(2,1)S(1)}, bf16[4,400,128]{2,1,0:T(8,128)(2,1)S(1)}, u32[]{:S(2)}, u32[]{:S(2)}) collective-permute-start(bf16[4,400,128]{2,1,0:T(8,128)(2,1)S(1)} %pad_maximum_fusion.mine_ref), channel_id=1, source_target_pairs={{0,1},{1,0},{2,3},{3,2},{4,5},{5,4},{6,7},{7,6},{8,9},{9,8},{10,11... | collective-permute-start | bytes 1228808 | tf_op jit(solution)/shard_map/ppermute | solution.py:316
  70.5 2.2 %collective-permute-start.3 = (bf16[192,896]{1,0:T(8,128)(2,1)S(1)}, bf16[192,896]{1,0:T(8,128)(2,1)S(1)}, u32[]{:S(2)}, u32[]{:S(2)}) collective-permute-start(bf16[192,896]{1,0:T(8,128)(2,1)S(1)} %copy-done.8), channel_id=1, source_target_pairs={{0,1},{1,0},{2,3},{3,2},{4,5},{5,4},{6,7},{7,6},{8,9},{9,8},{10,11... | collective-permute-start | bytes 1032200 | tf_op jit(solution)/shard_map/ppermute | solution.py:292
  71.0 2.2 %collective-permute-start.2 = (bf16[192,896]{1,0:T(8,128)(2,1)S(1)}, bf16[192,896]{1,0:T(8,128)(2,1)S(1)}, u32[]{:S(2)}, u32[]{:S(2)}) collective-permute-start(bf16[192,896]{1,0:T(8,128)(2,1)S(1)} %copy-done.7), channel_id=1, source_target_pairs={{0,1},{1,0},{2,3},{3,2},{4,5},{5,4},{6,7},{7,6},{8,9},{9,8},{10,11... | collective-permute-start | bytes 1032200 | tf_op jit(solution)/shard_map/ppermute | solution.py:289
  72.7 0.7 copy-start.4
  73.2 0.7 copy-start.5
  76.8 0.8 copy-start.3

commit v2 on v1

--- a/solution.py
+++ b/solution.py
@@ -13,7 +13,7 @@
 LOG2E = math.log2(math.e)
 F32, BF16 = jnp.float32, jnp.bfloat16
 GROUP = 4
-VMEM_BYTES = 56 * 2**20
+VMEM_BYTES = 28 * 2**20
 
 
 def quantize_rows(block, codebook):
@@ -63,13 +63,6 @@
         ).astype(BF16)
 
 
-def rotate_more_kernel(vec_ref, rott_ref, y_ref):
-    for k in range(y_ref.shape[0]):
-        y_ref[k] = lax.dot_general(
-            rott_ref[k], vec_ref[...], (((1,), (1,)), ((), ())), preferred_element_type=F32
-        ).astype(BF16)
-
-
 def operands(c):
     codes = c.shape[1]
     scaled = c * (2.0 / SOFTNESS * LOG2E)
@@ -89,8 +82,13 @@
     return a, b
 
 
-def quantize_kernel(cb_ref, y0_ref, y1_ref, v0_hbm, v1_hbm, rec0_ref, rec1_ref, keep_ref, send_ref,
-                    v0, v1, cnt, sem0, sem1, *, k, per):
+def quantize_kernel(*refs, k, per):
+    if k == 1:
+        (cb_ref, y0_ref, rott_ref, v0_hbm, v1_hbm,
+         rec0_ref, rec1_ref, keep_ref, send_ref, y1_ref, v0, v1, cnt, sem0, sem1) = refs
+    else:
+        (cb_ref, y0_ref, y1_ref, v0_hbm, v1_hbm,
+         rec0_ref, rec1_ref, keep_ref, send_ref, v0, v1, cnt, sem0, sem1) = refs
     step, steps = pl.program_id(0), pl.num_programs(0)
     s, r = lax.axis_index("sub"), lax.axis_index("rep")
     codes = cb_ref.shape[2]
@@ -104,17 +102,29 @@
 
     @pl.when(step == 0)
     def _():
+        pltpu.make_async_copy(v1_hbm, v1, sem1).start()
         pltpu.make_async_copy(v0_hbm, v0, sem0).start()
-        pltpu.make_async_copy(v1_hbm, v1, sem1).start()
         cnt[...] = jnp.zeros_like(cnt)
+        pltpu.make_async_copy(v1_hbm, v1, sem1).wait()
+        if k == 1:
+            for q in range(2):
+                y1_ref[q] = lax.dot_general(
+                    rott_ref[q], v1[...], (((1,), (1,)), ((), ())), preferred_element_type=F32
+                ).astype(BF16)
 
     ab = [operands(cb_ref[base + step * GROUP + j]) for j in range(GROUP)]
     acc = [jnp.zeros((2 * SUBDIM, codes), F32) for _ in range(GROUP)]
-    ys, recs = (y0_ref, y1_ref), (rec0_ref, rec1_ref)
+    recs = (rec0_ref, rec1_ref)
     ones = jnp.ones((SUBDIM, cols), BF16)
 
+    def rows_at(j):
+        return pl.multiple_of(step * (GROUP * SUBDIM), GROUP * SUBDIM) + SUBDIM * j
+
     def score(j, i):
-        y = ys[i][0, SUBDIM * j : SUBDIM * (j + 1), :]
+        if i == 1 and k == 1:
+            y = y1_ref[1, pl.ds(pl.multiple_of(rows_at(j), SUBDIM), SUBDIM), :]
+        else:
+            y = (y0_ref, y1_ref)[i][0, SUBDIM * j : SUBDIM * (j + 1), :]
         return y, jnp.dot(ab[j][0], jnp.concatenate([y, y, y, ones], axis=0), preferred_element_type=F32)
 
     def spread(sc):
@@ -123,8 +133,7 @@
     def finish(j, i, y, e):
         out = jnp.dot(ab[j][1], e, preferred_element_type=F32)
         inv = 1.0 / out[2 * SUBDIM :]
-        at = pl.multiple_of(step * (GROUP * SUBDIM), GROUP * SUBDIM) + SUBDIM * j
-        recs[i][pl.ds(pl.multiple_of(at, SUBDIM), SUBDIM), :] = (
+        recs[i][pl.ds(pl.multiple_of(rows_at(j), SUBDIM), SUBDIM), :] = (
             (out[:SUBDIM] + out[SUBDIM : 2 * SUBDIM]) * inv
         ).astype(BF16)
         yz = jnp.concatenate([(y.astype(F32) * inv).astype(BF16), inv.astype(BF16)], axis=0)
@@ -153,7 +162,6 @@
         at = p_rows + (codes // lanes) * w
         sums_ref[at : at + cnt.shape[0], :] = cnt[...].astype(sums_ref.dtype)
         pltpu.make_async_copy(v0_hbm, v0, sem0).wait()
-        pltpu.make_async_copy(v1_hbm, v1, sem1).wait()
         cross = jnp.dot(rec0_ref[...], v0[...], preferred_element_type=F32) + jnp.dot(
             rec1_ref[...], v1[...], preferred_element_type=F32
         )
@@ -234,6 +242,7 @@
     swap = [(0, 1), (1, 0)]
     r, z = lax.axis_index("rep"), lax.axis_index("row")
     params = pltpu.CompilerParams(vmem_limit_bytes=VMEM_BYTES)
+    small = pltpu.CompilerParams(vmem_limit_bytes=VMEM_BYTES // 2)
     vmem = pl.BlockSpec(memory_space=pltpu.VMEM)
 
     cb = codebooks.transpose(0, 2, 1)
@@ -246,33 +255,33 @@
         out_shape=(y_shape, jax.ShapeDtypeStruct((subs, w, width), BF16)),
         in_specs=[vmem] * 2,
         out_specs=(vmem, vmem),
-        compiler_params=params,
+        compiler_params=small,
         name="rotate",
     )(vectors, rotation)
-    y1 = pl.pallas_call(
-        rotate_more_kernel, out_shape=y_shape, in_specs=[vmem] * 2, out_specs=vmem, compiler_params=params, name="rotate_far"
-    )(vec_far, rott)
 
     p_rows = (part // lanes) * w
     s_rows = (codes // lanes) * (w + SUBDIM)
     rec_shape = jax.ShapeDtypeStruct((w, rows), BF16)
 
-    def quantize(k, cb_k):
+    def quantize(k, cb_k, extra):
         n_keep, n_send = (p_rows + s_rows, p_rows) if k == 0 else (p_rows, p_rows + s_rows)
         whole = lambda shape: pl.BlockSpec(shape, lambda m: (0,) * len(shape))
         y_spec = pl.BlockSpec((1, GROUP * SUBDIM, rows), lambda m: (k, m, 0))
         any_spec = pl.BlockSpec(memory_space=pl.ANY)
+        more = k == 1
         return pl.pallas_call(
             functools.partial(quantize_kernel, k=k, per=per),
             grid=(steps,),
-            in_specs=[whole(cb_k.shape), y_spec, y_spec, any_spec, any_spec],
-            out_specs=[whole((w, rows)), whole((w, rows)), whole((n_keep, lanes)), whole((n_send, lanes))],
+            in_specs=[whole(cb_k.shape), y_spec, whole(extra.shape) if more else y_spec, any_spec, any_spec],
+            out_specs=[whole((w, rows)), whole((w, rows)), whole((n_keep, lanes)), whole((n_send, lanes))]
+            + [whole(y_shape.shape)] * more,
             out_shape=[
                 rec_shape,
                 rec_shape,
                 jax.ShapeDtypeStruct((n_keep, lanes), F32),
                 jax.ShapeDtypeStruct((n_send, lanes), BF16),
-            ],
+            ]
+            + [y_shape] * more,
             scratch_shapes=[
                 pltpu.VMEM((rows, width), BF16),
                 pltpu.VMEM((rows, width), BF16),
@@ -282,14 +291,15 @@
             ],
             compiler_params=params,
             name="quantize_near" if k == 0 else "quantize_far",
-        )(cb_k, y0, y1, vectors, vec_far)
-
-    mine0, other0, keep0, send0 = quantize(0, cb)
+        )(cb_k, y0, extra, vectors, vec_far)
+
+    mine1, other1, keep1, send1, y1 = quantize(1, cb_far, rott)
+    got1 = lax.ppermute(send1, "sub", swap)
+    theirs1 = lax.ppermute(other1, "rep", swap)
+    mine0, other0, keep0, send0 = quantize(0, cb, y1)
     got0 = lax.ppermute(send0, "sub", swap)
     theirs0 = lax.ppermute(other0, "rep", swap)
-    mine1, other1, keep1, send1 = quantize(1, cb_far)
-    got1 = lax.ppermute(send1, "sub", swap)
-    theirs1 = lax.ppermute(other1, "rep", swap)
+    got0, theirs0, theirs1 = lax.optimization_barrier((got0, theirs0, theirs1))
 
     reconstruction = pl.pallas_call(
         turn_kernel,
@@ -297,7 +307,7 @@
         in_specs=[vmem] * 4,
         out_specs=vmem,
         scratch_shapes=[pltpu.VMEM((width, rows), BF16)],
-        compiler_params=params,
+        compiler_params=small,
         name="turn",
     )(mine0, mine1, theirs0, theirs1)
 
@@ -312,6 +322,7 @@
         shifts(lax.dynamic_index_in_dim(half, (z + d) % rows_n, 0, keepdims=False), rows_n, d) for d in range(1, rows_n)
     ]
     summed = functools.reduce(lambda a, b: a + b.astype(F32), gathered, own.astype(F32)).astype(BF16)
+    summed, reconstruction = lax.optimization_barrier((summed, reconstruction))
     all_mine = jnp.stack([summed] + [shifts(summed, rows_n, d) for d in range(1, rows_n)])
     all_theirs = lax.ppermute(all_mine, "rep", swap)
 
@@ -321,7 +332,7 @@
         in_specs=[vmem] * 3,
         out_specs=(vmem, vmem),
         scratch_shapes=[pltpu.VMEM((2, rows_n * piece, lanes), F32)],
-        compiler_params=params,
+        compiler_params=small,
         name="final",
     )(all_mine, all_theirs, cb)
     return reconstruction, new.transpose(0, 2, 1), cross

time: 81 us -> 69.9 us (0.86)
  Pallas kernels: 36.9 us -> 27.3 us
  waiting for transfers between devices: 21.5 us -> 20.4 us
    ppermute x1, waiting for transfers between devices: 5.35 us -> 0.01 us  [on_device(): got1 = lax.ppermute(send1, 'sub', swap)]
    ppermute x1, waiting for transfers between devices: 0.01 us -> 4.68 us  [on_device(): got0 = lax.ppermute(send0, 'sub', swap)]
    pallas_call x1 -> x0, Pallas kernels: 3.32 us -> none  [on_device(): pl.pallas_call(rotate_more_kernel, out_shape=y_shape, in_specs=[vmem] * 2...]
    pallas_call x1, Pallas kernels: 3.94 us -> 1.4 us  [on_device(): pl.pallas_call(rotate_kernel, out_shape=(y_shape, jax.ShapeDtypeStruct((s...]
    ppermute x1, waiting for transfers between devices: 0.01 us -> 1.73 us  [on_device(): all_theirs = lax.ppermute(all_mine, 'rep', swap)]
    ppermute x1, waiting for transfers between devices: 1.64 us -> 0.01 us  [on_device(): theirs1 = lax.ppermute(other1, 'rep', swap)]
    ppermute x6, waiting for transfers between devices: 14 us -> 12.4 us  [shifts(): return lax.ppermute(x, 'row', [(i, (i + d) % n) for i in range(n)])]
    ppermute x1, waiting for transfers between devices: 0.01 us -> 1.53 us  [on_device(): lax.ppermute(lax.dynamic_slice_in_dim(cb, r * per, per, 0), 'sub', swap)]
  transfers between devices with their start and end apart: 13 -> 13, of which waited for: 9 -> 9; matrix products, arithmetic and copies ran while one was open for 3% -> 3% of each run, Pallas kernels for 42% -> 20%
where the time goes in v2:
time: 69.9 us; the launch traced here: 69.6 us
  Pallas kernels  27.3 us (39%)
  waiting for transfers between devices  20.4 us (29%)
  starting transfers between devices  15.5 us (22%)
  local copies, waits for them, and re-layouts  4.33 us (6%)
  other arithmetic  1.43 us (2%)
  between operations  0.72 us (1%)
    pallas_call x2, Pallas kernels, quantize(): pl.pallas_call(functools.partial(quantize_kernel, k=k, per=per), grid=(st...  22.5 us
    ppermute x6, waiting for transfers between devices, shifts(): return lax.ppermute(x, 'row', [(i, (i + d) % n) for i in range(n)])  12.4 us
    ppermute x6, starting transfers between devices, shifts(): return lax.ppermute(x, 'row', [(i, (i + d) % n) for i in range(n)])  9.68 us
    ppermute x1, waiting for transfers between devices, on_device(): got0 = lax.ppermute(send0, 'sub', swap)  4.68 us
    unnamed x10, local copies, waits for them, and re-layouts  3.27 us
    ppermute x1, starting transfers between devices, on_device(): lax.ppermute(lax.dynamic_slice_in_dim(cb, r * per, per, 0), 'sub', swap)  2.58 us
    ppermute x1, starting transfers between devices, on_device(): got1 = lax.ppermute(send1, 'sub', swap)  1.81 us
    pallas_call x1, Pallas kernels, on_device(): pl.pallas_call(functools.partial(final_kernel, per=per, total=total), out...  1.8 us
  transfers between devices with their start and end apart: 13, of which 9 were waited for; matrix products, arithmetic and copies ran while one was open for 3% of the time, Pallas kernels for 20%

profile of v2, /device:TPU:0, one launch (start us, length us, event | category | flops | bytes accessed | tf_op | source)
XLA Modules:
  0.0 69.6 jit_solution(3212075879988620869)
XLA Ops:
  1.1 0.9 %dynamic-slice_bitcast_fusion = f32[12,16,256]{2,1,0:T(8,128)S(1)} fusion(f32[24,256,16]{1,2,0:T(8,128)} %param.5, s32[]{:T(128)S(6)} %select_n.31), kind=kLoop, calls=%fused_computation.8 | loop fusion | bytes 393220 | tf_op jit(solution)/shard_map/dynamic_slice | solution.py:249
  2.1 2.6 %collective-permute-start = (f32[12,16,256]{2,1,0:T(8,128)S(1)}, f32[12,16,256]{2,1,0:T(8,128)S(1)}, u32[]{:S(2)}, u32[]{:S(2)}) collective-permute-start(f32[12,16,256]{2,1,0:T(8,128)S(1)} %dynamic-slice_bitcast_fusion), channel_id=1, source_target_pairs={{0,2},{2,0},{1,3},{3,1},{4,6},{6,4},{5,7},{7,5},{8,10},{10,8},{9,1... | collective-permute-start | bytes 589832 | tf_op jit(solution)/shard_map/ppermute | solution.py:249
  4.7 1.3 %copy-done = bf16[896,768]{1,0:T(8,128)(2,1)S(1)} copy-done((bf16[896,768]{1,0:T(8,128)(2,1)S(1)}, bf16[896,768]{1,0:T(8,128)(2,1)}, u32[]{:S(2)}) %copy-start) | copy-done | bytes 1376280
  6.0 1.3 %copy-done.3 = bf16[768,768]{1,0:T(8,128)(2,1)S(1)} copy-done((bf16[768,768]{1,0:T(8,128)(2,1)S(1)}, bf16[768,768]{1,0:T(8,128)(2,1)}, u32[]{:S(2)}) %copy-start.3) | copy-done | bytes 1179672
  7.3 1.4 %rotate.1 = (bf16[2,192,896]{2,1,0:T(8,128)(2,1)S(1)}, bf16[2,192,768]{2,1,0:T(8,128)(2,1)S(1)}) custom-call(bf16[896,768]{1,0:T(8,128)(2,1)S(1)} %copy-done, bf16[768,768]{1,0:T(8,128)(2,1)S(1)} %copy-done.3), custom_call_target="tpu_custom_call" | custom-call | tf_op jit(solution)/shard_map/rotate/pallas_call | solution.py:253
  8.7 1.5 %collective-permute-done.refs_0_ = f32[12,16,256]{2,1,0:T(8,128)S(1)} collective-permute-done((f32[12,16,256]{2,1,0:T(8,128)S(1)}, f32[12,16,256]{2,1,0:T(8,128)S(1)}, u32[]{:S(2)}, u32[]{:S(2)}) %collective-permute-start) | collective-permute-done | bytes 196640 | tf_op jit(solution)/shard_map/ppermute | solution.py:249
  10.2 11.8 %quantize_far.1 = (bf16[192,896]{1,0:T(8,128)(2,1)S(1)}, bf16[192,896]{1,0:T(8,128)(2,1)}, f32[576,128]{1,0:T(8,128)S(1)}, bf16[992,128]{1,0:T(8,128)(2,1)S(1)}, bf16[2,192,896]{2,1,0:T(8,128)(2,1)S(1)}) custom-call(f32[12,16,256]{2,1,0:T(8,128)S(1)} %collective-permute-done.refs_0_, bf16[2,192,896]{2,1,0:T(8,128)(2,1)S(1)} %get-tuple-element.21.refs_1_, ...), custom_call_target="tpu_custom_call" | custom-call | tf_op jit(solution)/shard_map/quantize_far/pallas_call | solution.py:272
  22.0 1.8 %collective-permute-start.2 = (bf16[992,128]{1,0:T(8,128)(2,1)S(1)}, bf16[992,128]{1,0:T(8,128)(2,1)}, u32[]{:S(2)}, u32[]{:S(2)}) collective-permute-start(bf16[992,128]{1,0:T(8,128)(2,1)S(1)} %get-tuple-element.25), channel_id=1, source_target_pairs={{0,2},{2,0},{1,3},{3,1},{4,6},{6,4},{5,7},{7,5},{8,10},{10,8},{9,1... | collective-permute-start | bytes 761864 | tf_op jit(solution)/shard_map/ppermute | solution.py:297
  23.8 10.7 %quantize_near.1 = (bf16[192,896]{1,0:T(8,128)(2,1)S(1)}, bf16[192,896]{1,0:T(8,128)(2,1)}, f32[992,128]{1,0:T(8,128)S(1)}, bf16[576,128]{1,0:T(8,128)(2,1)S(1)}) custom-call(f32[24,16,256]{2,1,0:T(8,128)S(1)} %bitcast.18, bf16[2,192,896]{2,1,0:T(8,128)(2,1)S(1)} %get-tuple-element.21.refs_1_, bf16[2,192,896]{2,1,0:T(8,128)(2,1)S(1)} %get-tuple-element.23.refs_2_, ...), custom_call_target="tpu_custom_call" | custom-call | tf_op jit(solution)/shard_map/quantize_near/pallas_call | solution.py:272
  34.6 0.7 copy-done.4
  36.1 1.0 %add_convert_fusion = bf16[992,128]{1,0:T(8,128)(2,1)S(1)} fusion(f32[992,128]{1,0:T(8,128)S(1)} %get-tuple-element.24, bf16[992,128]{1,0:T(8,128)(2,1)} %collective-permute-done.2), kind=kLoop, calls=%fused_computation | loop fusion | flops 380928 | bytes 1015808 | tf_op jit(solution)/shard_map/convert_element_type | solution.py:318
  37.1 4.7 %collective-permute-done.3 = bf16[576,128]{1,0:T(8,128)(2,1)S(1)} collective-permute-done((bf16[576,128]{1,0:T(8,128)(2,1)}, bf16[576,128]{1,0:T(8,128)(2,1)S(1)}, u32[]{:S(2)}, u32[]{:S(2)}) %collective-permute-start.3) | collective-permute-done | bytes 147488 | tf_op jit(solution)/shard_map/ppermute | solution.py:300
  42.2 1.6 %collective-permute-start.6 = (bf16[400,128]{1,0:T(8,128)(2,1)S(1)}, bf16[400,128]{1,0:T(8,128)(2,1)S(1)}, u32[]{:S(2)}, u32[]{:S(2)}) collective-permute-start(bf16[400,128]{1,0:T(8,128)(2,1)S(1)} %get-tuple-element.39), channel_id=1, source_target_pairs={{0,4},{4,8},{8,12},{12,0},{1,5},{5,9},{9,13},{13,1},{2,6},{6,10},{... | collective-permute-start | bytes 307208 | tf_op jit(solution)/shard_map/ppermute | solution.py:229
  43.8 2.6 %collective-permute-start.7 = (bf16[400,128]{1,0:T(8,128)(2,1)S(1)}, bf16[400,128]{1,0:T(8,128)(2,1)S(1)}, u32[]{:S(2)}, u32[]{:S(2)}) collective-permute-start(bf16[400,128]{1,0:T(8,128)(2,1)S(1)} %get-tuple-element.41), channel_id=1, source_target_pairs={{0,8},{4,12},{8,0},{12,4},{1,9},{5,13},{9,1},{13,5},{2,10},{6,14},... | collective-permute-start | bytes 307208 | tf_op jit(solution)/shard_map/ppermute | solution.py:229
  46.4 1.3 %collective-permute-start.8 = (bf16[400,128]{1,0:T(8,128)(2,1)S(1)}, bf16[400,128]{1,0:T(8,128)(2,1)S(1)}, u32[]{:S(2)}, u32[]{:S(2)}) collective-permute-start(bf16[400,128]{1,0:T(8,128)(2,1)S(1)} %get-tuple-element.40), channel_id=1, source_target_pairs={{0,12},{4,0},{8,4},{12,8},{1,13},{5,1},{9,5},{13,9},{2,14},{6,2},{... | collective-permute-start | bytes 307208 | tf_op jit(solution)/shard_map/ppermute | solution.py:229
  47.7 1.6 %turn.1 = bf16[896,768]{1,0:T(8,128)(2,1)} custom-call(bf16[192,896]{1,0:T(8,128)(2,1)S(1)} %get-tuple-element.31.m0_ref, bf16[192,896]{1,0:T(8,128)(2,1)S(1)} %get-tuple-element.32.m1_ref, bf16[192,896]{1,0:T(8,128)(2,1)S(1)} %collective-permute-done.4.t0_ref, bf16[192,896]{1,0:T(8,128)(2,1)S(1)} %collective-permute-done.5.t1_ref), custom_call_target="tpu_custom_call" | custom-call | tf_op jit(solution)/shard_map/turn/pallas_call | solution.py:304
  49.8 2.9 %collective-permute-done.7 = bf16[400,128]{1,0:T(8,128)(2,1)S(1)} collective-permute-done((bf16[400,128]{1,0:T(8,128)(2,1)S(1)}, bf16[400,128]{1,0:T(8,128)(2,1)S(1)}, u32[]{:S(2)}, u32[]{:S(2)}) %collective-permute-start.7) | collective-permute-done | bytes 102432 | tf_op jit(solution)/shard_map/ppermute | solution.py:229
  52.9 3.5 %collective-permute-start.11 = (bf16[400,128]{1,0:T(8,128)(2,1)S(1)}, bf16[400,128]{1,0:T(8,128)(2,1)S(1)}, u32[]{:S(2)}, u32[]{:S(2)}) collective-permute-start(bf16[400,128]{1,0:T(8,128)(2,1)S(1)} %fusion.2), channel_id=1, source_target_pairs={{0,12},{4,0},{8,4},{12,8},{1,13},{5,1},{9,5},{13,9},{2,14},{6,2},{... | collective-permute-start | bytes 307208 | tf_op jit(solution)/shard_map/ppermute | solution.py:229
  56.4 0.6 collective-permute-start.10
  57.0 2.3 %collective-permute-done.11 = bf16[400,128]{1,0:T(8,128)(2,1)S(1)} collective-permute-done((bf16[400,128]{1,0:T(8,128)(2,1)S(1)}, bf16[400,128]{1,0:T(8,128)(2,1)S(1)}, u32[]{:S(2)}, u32[]{:S(2)}) %collective-permute-start.11) | collective-permute-done | bytes 102432 | tf_op jit(solution)/shard_map/ppermute | solution.py:229
  59.3 3.6 %collective-permute-done.9 = bf16[400,128]{1,0:T(8,128)(2,1)S(1)} collective-permute-done((bf16[400,128]{1,0:T(8,128)(2,1)S(1)}, bf16[400,128]{1,0:T(8,128)(2,1)S(1)}, u32[]{:S(2)}, u32[]{:S(2)}) %collective-permute-start.9) | collective-permute-done | bytes 102432 | tf_op jit(solution)/shard_map/ppermute | solution.py:229
  62.9 3.0 %collective-permute-done.10 = bf16[400,128]{1,0:T(8,128)(2,1)S(1)} collective-permute-done((bf16[400,128]{1,0:T(8,128)(2,1)S(1)}, bf16[400,128]{1,0:T(8,128)(2,1)S(1)}, u32[]{:S(2)}, u32[]{:S(2)}) %collective-permute-start.10) | collective-permute-done | bytes 102432 | tf_op jit(solution)/shard_map/ppermute | solution.py:229
  66.1 1.7 %collective-permute-done.12.theirs_ref = bf16[4,400,128]{2,1,0:T(8,128)(2,1)S(1)} collective-permute-done((bf16[4,400,128]{2,1,0:T(8,128)(2,1)S(1)}, bf16[4,400,128]{2,1,0:T(8,128)(2,1)S(1)}, u32[]{:S(2)}, u32[]{:S(2)}) %collective-permute-start.12) | collective-permute-done | bytes 409632 | tf_op jit(solution)/shard_map/ppermute | solution.py:327
  67.8 1.8 %final.1 = (f32[384,768]{1,0:T(8,128)}, f32[24,16,256]{2,1,0:T(8,128)}) custom-call(bf16[4,400,128]{2,1,0:T(8,128)(2,1)S(1)} %pad_maximum_fusion.mine_ref, bf16[4,400,128]{2,1,0:T(8,128)(2,1)S(1)} %collective-permute-done.12.theirs_ref, f32[24,16,256]{2,1,0:T(8,128)S(1)} %bitcast.19), custom_call_target="tpu_custom_call" | custom-call | tf_op jit(solution)/shard_map/final/pallas_call | solution.py:329
  (26 shorter events, 2.5 us)
Async XLA Ops:
  0.6 9.6 %collective-permute-start.1 = (bf16[896,768]{1,0:T(8,128)(2,1)}, bf16[896,768]{1,0:T(8,128)(2,1)S(1)}, u32[]{:S(2)}, u32[]{:S(2)}) collective-permute-start(bf16[896,768]{1,0:T(8,128)(2,1)} %refs_3_.3), channel_id=1, source_target_pairs={{0,1},{1,0},{2,3},{3,2},{4,5},{5,4},{6,7},{7,6},{8,9},{9,8},{10,11... | collective-permute-start | bytes 4128776 | tf_op jit(solution)/shard_map/ppermute | solution.py:250
  2.1 8.1 %collective-permute-start = (f32[12,16,256]{2,1,0:T(8,128)S(1)}, f32[12,16,256]{2,1,0:T(8,128)S(1)}, u32[]{:S(2)}, u32[]{:S(2)}) collective-permute-start(f32[12,16,256]{2,1,0:T(8,128)S(1)} %dynamic-slice_bitcast_fusion), channel_id=1, source_target_pairs={{0,2},{2,0},{1,3},{3,1},{4,6},{6,4},{5,7},{7,5},{8,10},{10,8},{9,1... | collective-permute-start | bytes 589832 | tf_op jit(solution)/shard_map/ppermute | solution.py:249
  4.7 1.3 %copy-start = (bf16[896,768]{1,0:T(8,128)(2,1)S(1)}, bf16[896,768]{1,0:T(8,128)(2,1)}, u32[]{:S(2)}) copy-start(bf16[896,768]{1,0:T(8,128)(2,1)} %refs_3_.3) | copy-start | bytes 4128772
  6.0 1.3 %copy-start.3 = (bf16[768,768]{1,0:T(8,128)(2,1)S(1)}, bf16[768,768]{1,0:T(8,128)(2,1)}, u32[]{:S(2)}) copy-start(bf16[768,768]{1,0:T(8,128)(2,1)} %rot_ref.1) | copy-start | bytes 3538948
  7.3 2.9 %copy-start.1 = (bf16[896,768]{1,0:T(8,128)(2,1)S(1)}, bf16[896,768]{1,0:T(8,128)(2,1)}, u32[]{:S(2)}) copy-start(bf16[896,768]{1,0:T(8,128)(2,1)} %refs_3_.3) | copy-start | bytes 4128772
  10.2 13.6 %copy-start.2 = (f32[24,256,16]{1,2,0:T(8,128)S(1)}, f32[24,256,16]{1,2,0:T(8,128)}, u32[]{:S(2)}) copy-start(f32[24,256,16]{1,2,0:T(8,128)} %param.5) | copy-start | bytes 1179652
  22.0 14.1 %collective-permute-start.2 = (bf16[992,128]{1,0:T(8,128)(2,1)S(1)}, bf16[992,128]{1,0:T(8,128)(2,1)}, u32[]{:S(2)}, u32[]{:S(2)}) collective-permute-start(bf16[992,128]{1,0:T(8,128)(2,1)S(1)} %get-tuple-element.25), channel_id=1, source_target_pairs={{0,2},{2,0},{1,3},{3,1},{4,6},{6,4},{5,7},{7,5},{8,10},{10,8},{9,1... | collective-permute-start | bytes 761864 | tf_op jit(solution)/shard_map/ppermute | solution.py:297
  34.6 0.7 copy-start.4
  35.2 6.6 %collective-permute-start.4 = (bf16[192,896]{1,0:T(8,128)(2,1)}, bf16[192,896]{1,0:T(8,128)(2,1)S(1)}, u32[]{:S(2)}, u32[]{:S(2)}) collective-permute-start(bf16[192,896]{1,0:T(8,128)(2,1)} %get-tuple-element.28), channel_id=1, source_target_pairs={{0,1},{1,0},{2,3},{3,2},{4,5},{5,4},{6,7},{7,6},{8,9},{9,8},{10,11... | collective-permute-start | bytes 1032200 | tf_op jit(solution)/shard_map/ppermute | solution.py:301
  35.3 6.6 %collective-permute-start.5 = (bf16[192,896]{1,0:T(8,128)(2,1)}, bf16[192,896]{1,0:T(8,128)(2,1)S(1)}, u32[]{:S(2)}, u32[]{:S(2)}) collective-permute-start(bf16[192,896]{1,0:T(8,128)(2,1)} %get-tuple-element.29), channel_id=1, source_target_pairs={{0,1},{1,0},{2,3},{3,2},{4,5},{5,4},{6,7},{7,6},{8,9},{9,8},{10,11... | collective-permute-start | bytes 1032200 | tf_op jit(solution)/shard_map/ppermute | solution.py:298
  35.8 6.0 %collective-permute-start.3 = (bf16[576,128]{1,0:T(8,128)(2,1)}, bf16[576,128]{1,0:T(8,128)(2,1)S(1)}, u32[]{:S(2)}, u32[]{:S(2)}) collective-permute-start(bf16[576,128]{1,0:T(8,128)(2,1)} %copy-done.4), channel_id=1, source_target_pairs={{0,2},{2,0},{1,3},{3,1},{4,6},{6,4},{5,7},{7,5},{8,10},{10,8},{9,1... | collective-permute-start | bytes 442376 | tf_op jit(solution)/shard_map/ppermute | solution.py:300
  42.2 7.6 %collective-permute-start.6 = (bf16[400,128]{1,0:T(8,128)(2,1)S(1)}, bf16[400,128]{1,0:T(8,128)(2,1)S(1)}, u32[]{:S(2)}, u32[]{:S(2)}) collective-permute-start(bf16[400,128]{1,0:T(8,128)(2,1)S(1)} %get-tuple-element.39), channel_id=1, source_target_pairs={{0,4},{4,8},{8,12},{12,0},{1,5},{5,9},{9,13},{13,1},{2,6},{6,10},{... | collective-permute-start | bytes 307208 | tf_op jit(solution)/shard_map/ppermute | solution.py:229
  43.8 8.9 %collective-permute-start.7 = (bf16[400,128]{1,0:T(8,128)(2,1)S(1)}, bf16[400,128]{1,0:T(8,128)(2,1)S(1)}, u32[]{:S(2)}, u32[]{:S(2)}) collective-permute-start(bf16[400,128]{1,0:T(8,128)(2,1)S(1)} %get-tuple-element.41), channel_id=1, source_target_pairs={{0,8},{4,12},{8,0},{12,4},{1,9},{5,13},{9,1},{13,5},{2,10},{6,14},... | collective-permute-start | bytes 307208 | tf_op jit(solution)/shard_map/ppermute | solution.py:229
  46.4 6.4 %collective-permute-start.8 = (bf16[400,128]{1,0:T(8,128)(2,1)S(1)}, bf16[400,128]{1,0:T(8,128)(2,1)S(1)}, u32[]{:S(2)}, u32[]{:S(2)}) collective-permute-start(bf16[400,128]{1,0:T(8,128)(2,1)S(1)} %get-tuple-element.40), channel_id=1, source_target_pairs={{0,12},{4,0},{8,4},{12,8},{1,13},{5,1},{9,5},{13,9},{2,14},{6,2},{... | collective-permute-start | bytes 307208 | tf_op jit(solution)/shard_map/ppermute | solution.py:229
  52.9 6.4 %collective-permute-start.11 = (bf16[400,128]{1,0:T(8,128)(2,1)S(1)}, bf16[400,128]{1,0:T(8,128)(2,1)S(1)}, u32[]{:S(2)}, u32[]{:S(2)}) collective-permute-start(bf16[400,128]{1,0:T(8,128)(2,1)S(1)} %fusion.2), channel_id=1, source_target_pairs={{0,12},{4,0},{8,4},{12,8},{1,13},{5,1},{9,5},{13,9},{2,14},{6,2},{... | collective-permute-start | bytes 307208 | tf_op jit(solution)/shard_map/ppermute | solution.py:229
  56.4 6.6 %collective-permute-start.9 = (bf16[400,128]{1,0:T(8,128)(2,1)S(1)}, bf16[400,128]{1,0:T(8,128)(2,1)S(1)}, u32[]{:S(2)}, u32[]{:S(2)}) collective-permute-start(bf16[400,128]{1,0:T(8,128)(2,1)S(1)} %fusion.2), channel_id=1, source_target_pairs={{0,4},{4,8},{8,12},{12,0},{1,5},{5,9},{9,13},{13,1},{2,6},{6,10},{... | collective-permute-start | bytes 307208 | tf_op jit(solution)/shard_map/ppermute | solution.py:229
  56.4 9.6 %collective-permute-start.10 = (bf16[400,128]{1,0:T(8,128)(2,1)S(1)}, bf16[400,128]{1,0:T(8,128)(2,1)S(1)}, u32[]{:S(2)}, u32[]{:S(2)}) collective-permute-start(bf16[400,128]{1,0:T(8,128)(2,1)S(1)} %fusion.2), channel_id=1, source_target_pairs={{0,8},{4,12},{8,0},{12,4},{1,9},{5,13},{9,1},{13,5},{2,10},{6,14},... | collective-permute-start | bytes 307208 | tf_op jit(solution)/shard_map/ppermute | solution.py:229
  66.0 1.8 %collective-permute-start.12 = (bf16[4,400,128]{2,1,0:T(8,128)(2,1)S(1)}, bf16[4,400,128]{2,1,0:T(8,128)(2,1)S(1)}, u32[]{:S(2)}, u32[]{:S(2)}) collective-permute-start(bf16[4,400,128]{2,1,0:T(8,128)(2,1)S(1)} %pad_maximum_fusion.mine_ref), channel_id=1, source_target_pairs={{0,1},{1,0},{2,3},{3,2},{4,5},{5,4},{6,7},{7,6},{8,9},{9,8},{10,11... | collective-permute-start | bytes 1228808 | tf_op jit(solution)/shard_map/ppermute | solution.py:327

commit v3 on v1

--- a/solution.py
+++ b/solution.py
@@ -12,8 +12,7 @@
 SOFTNESS = 4.0
 LOG2E = math.log2(math.e)
 F32, BF16 = jnp.float32, jnp.bfloat16
-GROUP = 4
-VMEM_BYTES = 56 * 2**20
+VMEM_BYTES = 28 * 2**20
 
 
 def quantize_rows(block, codebook):
@@ -89,82 +88,70 @@
     return a, b
 
 
-def quantize_kernel(cb_ref, y0_ref, y1_ref, v0_hbm, v1_hbm, rec0_ref, rec1_ref, keep_ref, send_ref,
-                    v0, v1, cnt, sem0, sem1, *, k, per):
-    step, steps = pl.program_id(0), pl.num_programs(0)
+def quantize_kernel(cb_ref, y0_ref, y1_ref, v0_ref, v1_ref, rec0_ref, rec1_ref, keep_ref, send_ref, cnt, *, k, per):
     s, r = lax.axis_index("sub"), lax.axis_index("rep")
     codes = cb_ref.shape[2]
     cols = y0_ref.shape[2]
     w = per * SUBDIM
     lanes = 128
-    part = v0.shape[1] // 2
+    part = v0_ref.shape[1] // 2
     base = r * per if k == 0 else 0
     p_rows = (part // lanes) * w
     sums_ref = keep_ref if k == 0 else send_ref
-
-    @pl.when(step == 0)
-    def _():
-        pltpu.make_async_copy(v0_hbm, v0, sem0).start()
-        pltpu.make_async_copy(v1_hbm, v1, sem1).start()
-        cnt[...] = jnp.zeros_like(cnt)
-
-    ab = [operands(cb_ref[base + step * GROUP + j]) for j in range(GROUP)]
-    acc = [jnp.zeros((2 * SUBDIM, codes), F32) for _ in range(GROUP)]
+    ones = jnp.ones((SUBDIM, cols), BF16)
     ys, recs = (y0_ref, y1_ref), (rec0_ref, rec1_ref)
-    ones = jnp.ones((SUBDIM, cols), BF16)
+    cnt[...] = jnp.zeros_like(cnt)
+    ab, acc = {}, {}
 
     def score(j, i):
-        y = ys[i][0, SUBDIM * j : SUBDIM * (j + 1), :]
+        if j not in ab:
+            ab[j] = operands(cb_ref[base + j])
+        y = ys[i][k, SUBDIM * j : SUBDIM * (j + 1), :]
         return y, jnp.dot(ab[j][0], jnp.concatenate([y, y, y, ones], axis=0), preferred_element_type=F32)
 
     def spread(sc):
         return jnp.exp2(sc - jnp.max(sc, axis=0, keepdims=True)).astype(BF16)
 
-    def finish(j, i, y, e):
+    def rebuild(j, i, y, e):
         out = jnp.dot(ab[j][1], e, preferred_element_type=F32)
         inv = 1.0 / out[2 * SUBDIM :]
-        at = pl.multiple_of(step * (GROUP * SUBDIM), GROUP * SUBDIM) + SUBDIM * j
-        recs[i][pl.ds(pl.multiple_of(at, SUBDIM), SUBDIM), :] = (
-            (out[:SUBDIM] + out[SUBDIM : 2 * SUBDIM]) * inv
-        ).astype(BF16)
-        yz = jnp.concatenate([(y.astype(F32) * inv).astype(BF16), inv.astype(BF16)], axis=0)
-        acc[j] = acc[j] + lax.dot_general(yz, e, (((1,), (1,)), ((), ())), preferred_element_type=F32)
-
-    work = [(j, i) for j in range(GROUP) for i in range(2)]
-    first = second = None
-    for item in work + [None, None]:
+        recs[i][SUBDIM * j : SUBDIM * (j + 1), :] = ((out[:SUBDIM] + out[SUBDIM : 2 * SUBDIM]) * inv).astype(BF16)
+        return jnp.concatenate([(y.astype(F32) * inv).astype(BF16), inv.astype(BF16)], axis=0)
+
+    def gather(j, i, yz, e):
+        sums = lax.dot_general(yz, e, (((1,), (1,)), ((), ())), preferred_element_type=F32)
+        if i == 0:
+            acc[j] = sums
+            return
+        sums = acc.pop(j) + sums
+        for half in range(codes // lanes):
+            at = p_rows + half * w + j * SUBDIM
+            sums_ref[at : at + SUBDIM, :] = sums[:SUBDIM, half * lanes : (half + 1) * lanes].astype(sums_ref.dtype)
+            at = half * SUBDIM + j
+            cnt[at : at + 1, :] = sums[SUBDIM : SUBDIM + 1, half * lanes : (half + 1) * lanes]
+
+    first = second = third = None
+    for item in [(j, i) for j in range(per) for i in range(2)] + [None] * 3:
         new_first = (item, *score(*item)) if item is not None else None
         new_second = (first[0], first[1], spread(first[2])) if first is not None else None
-        if second is not None:
-            finish(*second[0], second[1], second[2])
-        first, second = new_first, new_second
-
-    for j in range(GROUP):
-        m = step * GROUP + j
-        for half in range(codes // lanes):
-            at = p_rows + half * w + m * SUBDIM
-            sums_ref[pl.ds(pl.multiple_of(at, SUBDIM), SUBDIM), :] = acc[j][
-                :SUBDIM, half * lanes : (half + 1) * lanes
-            ].astype(sums_ref.dtype)
-            cnt[pl.ds(half * SUBDIM + m, 1), :] = acc[j][SUBDIM : SUBDIM + 1, half * lanes : (half + 1) * lanes]
-
-    @pl.when(step == steps - 1)
-    def _():
-        at = p_rows + (codes // lanes) * w
-        sums_ref[at : at + cnt.shape[0], :] = cnt[...].astype(sums_ref.dtype)
-        pltpu.make_async_copy(v0_hbm, v0, sem0).wait()
-        pltpu.make_async_copy(v1_hbm, v1, sem1).wait()
-        cross = jnp.dot(rec0_ref[...], v0[...], preferred_element_type=F32) + jnp.dot(
-            rec1_ref[...], v1[...], preferred_element_type=F32
-        )
-        for h in range(2):
-            @pl.when(s == h)
-            def _():
-                for g in range(part // lanes):
-                    near = h * part + g * lanes
-                    far = (1 - h) * part + g * lanes
-                    keep_ref[g * w : (g + 1) * w, :] = cross[:, near : near + lanes]
-                    send_ref[g * w : (g + 1) * w, :] = cross[:, far : far + lanes].astype(BF16)
+        new_third = (second[0], rebuild(*second[0], second[1], second[2]), second[2]) if second is not None else None
+        if third is not None:
+            gather(*third[0], third[1], third[2])
+        first, second, third = new_first, new_second, new_third
+
+    at = p_rows + (codes // lanes) * w
+    sums_ref[at : at + cnt.shape[0], :] = cnt[...].astype(sums_ref.dtype)
+    cross = jnp.dot(rec0_ref[...], v0_ref[...], preferred_element_type=F32) + jnp.dot(
+        rec1_ref[...], v1_ref[...], preferred_element_type=F32
+    )
+    for h in range(2):
+        @pl.when(s == h)
+        def _():
+            for g in range(part // lanes):
+                near = h * part + g * lanes
+                far = (1 - h) * part + g * lanes
+                keep_ref[g * w : (g + 1) * w, :] = cross[:, near : near + lanes]
+                send_ref[g * w : (g + 1) * w, :] = cross[:, far : far + lanes].astype(BF16)
 
 
 def turn_kernel(m0_ref, m1_ref, t0_ref, t1_ref, out_ref, buf):
@@ -187,9 +174,9 @@
     groups = cross_ref.shape[0] // lanes
     halves = codes // lanes
     for side, ref in enumerate((mine_ref, theirs_ref)):
-        for d in range(n):
-            at = ((z + n - d) % n) * piece
-            buf[side, pl.ds(pl.multiple_of(at, SUBDIM), piece), :] = ref[d].astype(F32)
+        for i in range(n):
+            at = (z ^ ((n - i) % n)) * piece
+            buf[side, pl.ds(pl.multiple_of(at, SUBDIM), piece), :] = ref[i].astype(F32)
     a_rows = groups * w + halves * (w + SUBDIM)
     for g in range(groups):
         for h in range(2):
@@ -217,8 +204,8 @@
             new_ref[part * per + m] = (sums + c) / (count + 1.0)
 
 
-def shifts(x, n, d):
-    return lax.ppermute(x, "row", [(i, (i + d) % n) for i in range(n)])
+def exchange(x, n, d):
+    return lax.ppermute(x, "row", [(i, i ^ d) for i in range(n)])
 
 
 def on_device(vectors, rotation, codebooks):
@@ -229,16 +216,17 @@
     w = per * SUBDIM
     codes = codebooks.shape[1]
     lanes = 128
-    steps = per // GROUP
     total = rows * rows_n * subs * 2
     swap = [(0, 1), (1, 0)]
     r, z = lax.axis_index("rep"), lax.axis_index("row")
     params = pltpu.CompilerParams(vmem_limit_bytes=VMEM_BYTES)
+    small = pltpu.CompilerParams(vmem_limit_bytes=VMEM_BYTES // 2)
     vmem = pl.BlockSpec(memory_space=pltpu.VMEM)
 
     cb = codebooks.transpose(0, 2, 1)
-    cb_far = lax.ppermute(lax.dynamic_slice_in_dim(cb, r * per, per, 0), "sub", swap)
-    vec_far = lax.ppermute(vectors, "rep", swap)
+    cb_sent, vec_sent = lax.optimization_barrier((lax.dynamic_slice_in_dim(cb, r * per, per, 0), vectors))
+    cb_far = lax.ppermute(cb_sent, "sub", swap)
+    vec_far = lax.ppermute(vec_sent, "rep", swap)
 
     y_shape = jax.ShapeDtypeStruct((subs, w, rows), BF16)
     y0, rott = pl.pallas_call(
@@ -246,11 +234,12 @@
         out_shape=(y_shape, jax.ShapeDtypeStruct((subs, w, width), BF16)),
         in_specs=[vmem] * 2,
         out_specs=(vmem, vmem),
-        compiler_params=params,
+        compiler_params=small,
         name="rotate",
     )(vectors, rotation)
+
     y1 = pl.pallas_call(
-        rotate_more_kernel, out_shape=y_shape, in_specs=[vmem] * 2, out_specs=vmem, compiler_params=params, name="rotate_far"
+        rotate_more_kernel, out_shape=y_shape, in_specs=[vmem] * 2, out_specs=vmem, compiler_params=small, name="rotate_far"
     )(vec_far, rott)
 
     p_rows = (part // lanes) * w
@@ -259,37 +248,28 @@
 
     def quantize(k, cb_k):
         n_keep, n_send = (p_rows + s_rows, p_rows) if k == 0 else (p_rows, p_rows + s_rows)
-        whole = lambda shape: pl.BlockSpec(shape, lambda m: (0,) * len(shape))
-        y_spec = pl.BlockSpec((1, GROUP * SUBDIM, rows), lambda m: (k, m, 0))
-        any_spec = pl.BlockSpec(memory_space=pl.ANY)
         return pl.pallas_call(
             functools.partial(quantize_kernel, k=k, per=per),
-            grid=(steps,),
-            in_specs=[whole(cb_k.shape), y_spec, y_spec, any_spec, any_spec],
-            out_specs=[whole((w, rows)), whole((w, rows)), whole((n_keep, lanes)), whole((n_send, lanes))],
+            in_specs=[vmem] * 5,
+            out_specs=[vmem] * 4,
             out_shape=[
                 rec_shape,
                 rec_shape,
                 jax.ShapeDtypeStruct((n_keep, lanes), F32),
                 jax.ShapeDtypeStruct((n_send, lanes), BF16),
             ],
-            scratch_shapes=[
-                pltpu.VMEM((rows, width), BF16),
-                pltpu.VMEM((rows, width), BF16),
-                pltpu.VMEM(((codes // lanes) * SUBDIM, lanes), F32),
-                pltpu.SemaphoreType.DMA,
-                pltpu.SemaphoreType.DMA,
-            ],
+            scratch_shapes=[pltpu.VMEM(((codes // lanes) * SUBDIM, lanes), F32)],
             compiler_params=params,
             name="quantize_near" if k == 0 else "quantize_far",
         )(cb_k, y0, y1, vectors, vec_far)
 
+    mine1, other1, keep1, send1 = quantize(1, cb_far)
+    got1 = lax.ppermute(send1, "sub", swap)
+    theirs1 = lax.ppermute(other1, "rep", swap)
     mine0, other0, keep0, send0 = quantize(0, cb)
     got0 = lax.ppermute(send0, "sub", swap)
     theirs0 = lax.ppermute(other0, "rep", swap)
-    mine1, other1, keep1, send1 = quantize(1, cb_far)
-    got1 = lax.ppermute(send1, "sub", swap)
-    theirs1 = lax.ppermute(other1, "rep", swap)
+    got0, theirs0, theirs1 = lax.optimization_barrier((got0, theirs0, theirs1))
 
     reconstruction = pl.pallas_call(
         turn_kernel,
@@ -297,7 +277,7 @@
         in_specs=[vmem] * 4,
         out_specs=vmem,
         scratch_shapes=[pltpu.VMEM((width, rows), BF16)],
-        compiler_params=params,
+        compiler_params=small,
         name="turn",
     )(mine0, mine1, theirs0, theirs1)
 
@@ -308,11 +288,11 @@
         [(keep0 + got1.astype(F32)).astype(BF16), (keep1 + got0.astype(F32)).astype(BF16), pad], axis=0
     ).reshape(rows_n, piece, lanes)
     own = lax.dynamic_index_in_dim(half, z, 0, keepdims=False)
-    gathered = [
-        shifts(lax.dynamic_index_in_dim(half, (z + d) % rows_n, 0, keepdims=False), rows_n, d) for d in range(1, rows_n)
-    ]
+    apart = range(rows_n - 1, 0, -1)
+    gathered = [exchange(lax.dynamic_index_in_dim(half, z ^ d, 0, keepdims=False), rows_n, d) for d in apart]
     summed = functools.reduce(lambda a, b: a + b.astype(F32), gathered, own.astype(F32)).astype(BF16)
-    all_mine = jnp.stack([summed] + [shifts(summed, rows_n, d) for d in range(1, rows_n)])
+    summed, reconstruction = lax.optimization_barrier((summed, reconstruction))
+    all_mine = jnp.stack([summed] + [exchange(summed, rows_n, d) for d in apart])
     all_theirs = lax.ppermute(all_mine, "rep", swap)
 
     cross, new = pl.pallas_call(
@@ -321,7 +301,7 @@
         in_specs=[vmem] * 3,
         out_specs=(vmem, vmem),
         scratch_shapes=[pltpu.VMEM((2, rows_n * piece, lanes), F32)],
-        compiler_params=params,
+        compiler_params=small,
         name="final",
     )(all_mine, all_theirs, cb)
     return reconstruction, new.transpose(0, 2, 1), cross
@@ -329,7 +309,7 @@
 
 def solution(mesh):
     placed = (P(("dom", "row", "sub", "rep"), None), P("dom", None), P(("dom", "sub"), None, None))
-    body = on_device if mesh.shape["sub"] == 2 and mesh.shape["row"] <= 8 else any_mesh
+    body = on_device if mesh.shape["sub"] == 2 and mesh.shape["row"] in (2, 4, 8) else any_mesh
     return jax.shard_map(
         body,
         mesh=mesh,

time: 81 us -> 64 us (0.79)
  Pallas kernels: 36.9 us -> 22.9 us
  starting transfers between devices: 15.8 us -> 13.8 us
  waiting for transfers between devices: 21.5 us -> 20.6 us
    pallas_call x2, Pallas kernels: 23.6 us -> 17.1 us  [quantize(): pl.pallas_call(functools.partial(quantize_kernel, k=k, per=per), in_specs...]
    ppermute x1, waiting for transfers between devices: 5.35 us -> 0.01 us  [on_device(): got1 = lax.ppermute(send1, 'sub', swap)]
    ppermute x1, waiting for transfers between devices: 0.01 us -> 4.68 us  [on_device(): got0 = lax.ppermute(send0, 'sub', swap)]
    pallas_call x1, Pallas kernels: 3.94 us -> 1.4 us  [on_device(): pl.pallas_call(rotate_kernel, out_shape=(y_shape, jax.ShapeDtypeStruct((s...]
    pallas_call x1, Pallas kernels: 3.32 us -> 0.99 us  [on_device(): pl.pallas_call(rotate_more_kernel, out_shape=y_shape, in_specs=[vmem] * 2...]
    ppermute x8, starting transfers between devices: 13 us -> 11.1 us  [the longest x6 8.01 us: exchange(): return lax.ppermute(x, 'row', [(i, i ^ d) for i in range(n)])]
    ppermute x1, waiting for transfers between devices: 0.01 us -> 1.73 us  [on_device(): all_theirs = lax.ppermute(all_mine, 'rep', swap)]
    ppermute x1, waiting for transfers between devices: 1.64 us -> 0.01 us  [on_device(): theirs1 = lax.ppermute(other1, 'rep', swap)]
  transfers between devices with their start and end apart: 13 -> 13, of which waited for: 9 -> 8; matrix products, arithmetic and copies ran while one was open for 3% -> 2% of each run, Pallas kernels for 42% -> 20%
where the time goes in v3:
time: 64 us; the launch traced here: 63.7 us
  Pallas kernels  22.9 us (36%)
  waiting for transfers between devices  20.6 us (32%)
  starting transfers between devices  13.8 us (22%)
  local copies, waits for them, and re-layouts  4.34 us (7%)
  other arithmetic  1.44 us (2%)
  between operations  0.74 us (1%)
    pallas_call x2, Pallas kernels, quantize(): pl.pallas_call(functools.partial(quantize_kernel, k=k, per=per), in_specs...  17.1 us
    ppermute x6, waiting for transfers between devices, exchange(): return lax.ppermute(x, 'row', [(i, i ^ d) for i in range(n)])  13.7 us
    ppermute x6, starting transfers between devices, exchange(): return lax.ppermute(x, 'row', [(i, i ^ d) for i in range(n)])  8.01 us
    ppermute x1, waiting for transfers between devices, on_device(): got0 = lax.ppermute(send0, 'sub', swap)  4.68 us
    unnamed x10, local copies, waits for them, and re-layouts  3.27 us
    ppermute x1, starting transfers between devices, on_device(): cb_far = lax.ppermute(cb_sent, 'sub', swap)  2.57 us
    ppermute x1, starting transfers between devices, on_device(): got1 = lax.ppermute(send1, 'sub', swap)  1.82 us
    pallas_call x1, Pallas kernels, on_device(): pl.pallas_call(functools.partial(final_kernel, per=per, total=total), out...  1.79 us
  transfers between devices with their start and end apart: 13, of which 8 were waited for; matrix products, arithmetic and copies ran while one was open for 2% of the time, Pallas kernels for 20%

profile of v3, /device:TPU:0, one launch (start us, length us, event | category | flops | bytes accessed | tf_op | source)
XLA Modules:
  0.0 63.7 jit_solution(8668027151847705815)
XLA Ops:
  0.6 0.9 %dynamic-slice_bitcast_fusion = f32[12,16,256]{2,1,0:T(8,128)S(1)} fusion(f32[24,256,16]{1,2,0:T(8,128)} %param.5, s32[]{:T(128)S(6)} %select_n.16), kind=kLoop, calls=%fused_computation.8 | loop fusion | bytes 393220 | tf_op jit(solution)/shard_map/dynamic_slice | solution.py:227
  2.1 2.6 %collective-permute-start.1 = (f32[12,16,256]{2,1,0:T(8,128)S(1)}, f32[12,16,256]{2,1,0:T(8,128)S(1)}, u32[]{:S(2)}, u32[]{:S(2)}) collective-permute-start(f32[12,16,256]{2,1,0:T(8,128)S(1)} %dynamic-slice_bitcast_fusion), channel_id=1, source_target_pairs={{0,2},{2,0},{1,3},{3,1},{4,6},{6,4},{5,7},{7,5},{8,10},{10,8},{9,1... | collective-permute-start | bytes 589832 | tf_op jit(solution)/shard_map/ppermute | solution.py:228
  4.7 1.3 %copy-done = bf16[896,768]{1,0:T(8,128)(2,1)S(1)} copy-done((bf16[896,768]{1,0:T(8,128)(2,1)S(1)}, bf16[896,768]{1,0:T(8,128)(2,1)}, u32[]{:S(2)}) %copy-start) | copy-done | bytes 1376280
  6.0 1.3 %copy-done.3 = bf16[768,768]{1,0:T(8,128)(2,1)S(1)} copy-done((bf16[768,768]{1,0:T(8,128)(2,1)S(1)}, bf16[768,768]{1,0:T(8,128)(2,1)}, u32[]{:S(2)}) %copy-start.3) | copy-done | bytes 1179672
  7.3 1.4 %rotate.1 = (bf16[2,192,896]{2,1,0:T(8,128)(2,1)S(1)}, bf16[2,192,768]{2,1,0:T(8,128)(2,1)S(1)}) custom-call(bf16[896,768]{1,0:T(8,128)(2,1)S(1)} %copy-done, bf16[768,768]{1,0:T(8,128)(2,1)S(1)} %copy-done.3), custom_call_target="tpu_custom_call" | custom-call | tf_op jit(solution)/shard_map/rotate/pallas_call | solution.py:232
  8.7 1.0 %rotate_far.1.y1_ref = bf16[2,192,896]{2,1,0:T(8,128)(2,1)S(1)} custom-call(bf16[896,768]{1,0:T(8,128)(2,1)S(1)} %collective-permute-done.vec_ref.v1_ref, bf16[2,192,768]{2,1,0:T(8,128)(2,1)S(1)} %get-tuple-element.24.rott_ref), custom_call_target="tpu_custom_call" | custom-call | tf_op jit(solution)/shard_map/rotate_far/pallas_call | solution.py:241
  10.2 8.6 %quantize_far.1 = (bf16[192,896]{1,0:T(8,128)(2,1)S(1)}, bf16[192,896]{1,0:T(8,128)(2,1)S(1)}, f32[576,128]{1,0:T(8,128)S(1)}, bf16[992,128]{1,0:T(8,128)(2,1)S(1)}) custom-call(f32[12,16,256]{2,1,0:T(8,128)S(1)} %collective-permute-done.1.cb_ref, bf16[2,192,896]{2,1,0:T(8,128)(2,1)S(1)} %get-tuple-element.22.y0_ref, ...), custom_call_target="tpu_custom_call" | custom-call | tf_op jit(solution)/shard_map/quantize_far/pallas_call | solution.py:251
  18.8 1.8 %collective-permute-start.2 = (bf16[992,128]{1,0:T(8,128)(2,1)S(1)}, bf16[992,128]{1,0:T(8,128)(2,1)}, u32[]{:S(2)}, u32[]{:S(2)}) collective-permute-start(bf16[992,128]{1,0:T(8,128)(2,1)S(1)} %get-tuple-element.27), channel_id=1, source_target_pairs={{0,2},{2,0},{1,3},{3,1},{4,6},{6,4},{5,7},{7,5},{8,10},{10,8},{9,1... | collective-permute-start | bytes 761864 | tf_op jit(solution)/shard_map/ppermute | solution.py:267
  20.6 8.5 %quantize_near.1 = (bf16[192,896]{1,0:T(8,128)(2,1)S(1)}, bf16[192,896]{1,0:T(8,128)(2,1)S(1)}, f32[992,128]{1,0:T(8,128)S(1)}, bf16[576,128]{1,0:T(8,128)(2,1)S(1)}) custom-call(f32[24,16,256]{2,1,0:T(8,128)S(1)} %bitcast.18, bf16[2,192,896]{2,1,0:T(8,128)(2,1)S(1)} %get-tuple-element.22.y0_ref, bf16[2,192,896]{2,1,0:T(8,128)(2,1)S(1)} %rotate_far.1.y1_ref, ...), custom_call_target="tpu_custom_call" | custom-call | tf_op jit(solution)/shard_map/quantize_near/pallas_call | solution.py:251
  29.1 0.7 %copy-done.4 = bf16[576,128]{1,0:T(8,128)(2,1)} copy-done((bf16[576,128]{1,0:T(8,128)(2,1)}, bf16[576,128]{1,0:T(8,128)(2,1)S(1)}, u32[]{:S(2)}) %copy-start.4) | copy-done | bytes 147480
  30.6 1.0 %add_convert_fusion = bf16[992,128]{1,0:T(8,128)(2,1)S(1)} fusion(f32[992,128]{1,0:T(8,128)S(1)} %get-tuple-element.25, bf16[992,128]{1,0:T(8,128)(2,1)} %collective-permute-done.2), kind=kLoop, calls=%fused_computation | loop fusion | flops 380928 | bytes 1015808 | tf_op jit(solution)/shard_map/convert_element_type | solution.py:288
  31.6 4.7 %collective-permute-done.3 = bf16[576,128]{1,0:T(8,128)(2,1)S(1)} collective-permute-done((bf16[576,128]{1,0:T(8,128)(2,1)}, bf16[576,128]{1,0:T(8,128)(2,1)S(1)}, u32[]{:S(2)}, u32[]{:S(2)}) %collective-permute-start.3) | collective-permute-done | bytes 147488 | tf_op jit(solution)/shard_map/ppermute | solution.py:270
  36.7 3.7 %collective-permute-start.6 = (bf16[400,128]{1,0:T(8,128)(2,1)S(1)}, bf16[400,128]{1,0:T(8,128)(2,1)S(1)}, u32[]{:S(2)}, u32[]{:S(2)}) collective-permute-start(bf16[400,128]{1,0:T(8,128)(2,1)S(1)} %get-tuple-element.41), channel_id=1, source_target_pairs={{0,12},{4,8},{8,4},{12,0},{1,13},{5,9},{9,5},{13,1},{2,14},{6,10},... | collective-permute-start | bytes 307208 | tf_op jit(solution)/shard_map/ppermute | solution.py:208
  40.3 0.8 %collective-permute-start.8 = (bf16[400,128]{1,0:T(8,128)(2,1)S(1)}, bf16[400,128]{1,0:T(8,128)(2,1)S(1)}, u32[]{:S(2)}, u32[]{:S(2)}) collective-permute-start(bf16[400,128]{1,0:T(8,128)(2,1)S(1)} %get-tuple-element.42), channel_id=1, source_target_pairs={{0,4},{4,0},{8,12},{12,8},{1,5},{5,1},{9,13},{13,9},{2,6},{6,2},{1... | collective-permute-start | bytes 307208 | tf_op jit(solution)/shard_map/ppermute | solution.py:208
  41.1 1.6 %turn.1 = bf16[896,768]{1,0:T(8,128)(2,1)} custom-call(bf16[192,896]{1,0:T(8,128)(2,1)S(1)} %get-tuple-element.33.m0_ref, bf16[192,896]{1,0:T(8,128)(2,1)S(1)} %get-tuple-element.34.m1_ref, bf16[192,896]{1,0:T(8,128)(2,1)S(1)} %collective-permute-done.4.t0_ref, bf16[192,896]{1,0:T(8,128)(2,1)S(1)} %collective-permute-done.5.t1_ref), custom_call_target="tpu_custom_call" | custom-call | tf_op jit(solution)/shard_map/turn/pallas_call | solution.py:274
  42.7 1.3 %collective-permute-done.6 = bf16[400,128]{1,0:T(8,128)(2,1)S(1)} collective-permute-done((bf16[400,128]{1,0:T(8,128)(2,1)S(1)}, bf16[400,128]{1,0:T(8,128)(2,1)S(1)}, u32[]{:S(2)}, u32[]{:S(2)}) %collective-permute-start.6) | collective-permute-done | bytes 102432 | tf_op jit(solution)/shard_map/ppermute | solution.py:208
  44.0 4.3 %collective-permute-done.7 = bf16[400,128]{1,0:T(8,128)(2,1)S(1)} collective-permute-done((bf16[400,128]{1,0:T(8,128)(2,1)S(1)}, bf16[400,128]{1,0:T(8,128)(2,1)S(1)}, u32[]{:S(2)}, u32[]{:S(2)}) %collective-permute-start.7) | collective-permute-done | bytes 102432 | tf_op jit(solution)/shard_map/ppermute | solution.py:208
  48.8 2.2 %collective-permute-start.9 = (bf16[400,128]{1,0:T(8,128)(2,1)S(1)}, bf16[400,128]{1,0:T(8,128)(2,1)S(1)}, u32[]{:S(2)}, u32[]{:S(2)}) collective-permute-start(bf16[400,128]{1,0:T(8,128)(2,1)S(1)} %fusion.2), channel_id=1, source_target_pairs={{0,12},{4,8},{8,4},{12,0},{1,13},{5,9},{9,5},{13,1},{2,14},{6,10},... | collective-permute-start | bytes 307208 | tf_op jit(solution)/shard_map/ppermute | solution.py:208
  51.0 0.9 %collective-permute-start.10 = (bf16[400,128]{1,0:T(8,128)(2,1)S(1)}, bf16[400,128]{1,0:T(8,128)(2,1)S(1)}, u32[]{:S(2)}, u32[]{:S(2)}) collective-permute-start(bf16[400,128]{1,0:T(8,128)(2,1)S(1)} %fusion.2), channel_id=1, source_target_pairs={{0,8},{4,12},{8,0},{12,4},{1,9},{5,13},{9,1},{13,5},{2,10},{6,14},... | collective-permute-start | bytes 307208 | tf_op jit(solution)/shard_map/ppermute | solution.py:208
  51.9 2.7 %collective-permute-done.11 = bf16[400,128]{1,0:T(8,128)(2,1)S(1)} collective-permute-done((bf16[400,128]{1,0:T(8,128)(2,1)S(1)}, bf16[400,128]{1,0:T(8,128)(2,1)S(1)}, u32[]{:S(2)}, u32[]{:S(2)}) %collective-permute-start.11) | collective-permute-done | bytes 102432 | tf_op jit(solution)/shard_map/ppermute | solution.py:208
  54.6 1.8 %collective-permute-done.9 = bf16[400,128]{1,0:T(8,128)(2,1)S(1)} collective-permute-done((bf16[400,128]{1,0:T(8,128)(2,1)S(1)}, bf16[400,128]{1,0:T(8,128)(2,1)S(1)}, u32[]{:S(2)}, u32[]{:S(2)}) %collective-permute-start.9) | collective-permute-done | bytes 102432 | tf_op jit(solution)/shard_map/ppermute | solution.py:208
  56.4 3.7 %collective-permute-done.10 = bf16[400,128]{1,0:T(8,128)(2,1)S(1)} collective-permute-done((bf16[400,128]{1,0:T(8,128)(2,1)S(1)}, bf16[400,128]{1,0:T(8,128)(2,1)S(1)}, u32[]{:S(2)}, u32[]{:S(2)}) %collective-permute-start.10) | collective-permute-done | bytes 102432 | tf_op jit(solution)/shard_map/ppermute | solution.py:208
  60.2 1.7 %collective-permute-done.12.theirs_ref = bf16[4,400,128]{2,1,0:T(8,128)(2,1)S(1)} collective-permute-done((bf16[4,400,128]{2,1,0:T(8,128)(2,1)S(1)}, bf16[4,400,128]{2,1,0:T(8,128)(2,1)S(1)}, u32[]{:S(2)}, u32[]{:S(2)}) %collective-permute-start.12) | collective-permute-done | bytes 409632 | tf_op jit(solution)/shard_map/ppermute | solution.py:296
  61.9 1.8 %final.1 = (f32[384,768]{1,0:T(8,128)}, f32[24,16,256]{2,1,0:T(8,128)}) custom-call(bf16[4,400,128]{2,1,0:T(8,128)(2,1)S(1)} %pad_maximum_fusion.mine_ref, bf16[4,400,128]{2,1,0:T(8,128)(2,1)S(1)} %collective-permute-done.12.theirs_ref, f32[24,16,256]{2,1,0:T(8,128)S(1)} %bitcast.19), custom_call_target="tpu_custom_call" | custom-call | tf_op jit(solution)/shard_map/final/pallas_call | solution.py:298
  (27 shorter events, 2.9 us)
Async XLA Ops:
  1.6 7.1 %collective-permute-start = (bf16[896,768]{1,0:T(8,128)(2,1)}, bf16[896,768]{1,0:T(8,128)(2,1)S(1)}, u32[]{:S(2)}, u32[]{:S(2)}) collective-permute-start(bf16[896,768]{1,0:T(8,128)(2,1)} %v0_ref.3), channel_id=1, source_target_pairs={{0,1},{1,0},{2,3},{3,2},{4,5},{5,4},{6,7},{7,6},{8,9},{9,8},{10,11... | collective-permute-start | bytes 4128776 | tf_op jit(solution)/shard_map/ppermute | solution.py:229
  2.1 8.1 %collective-permute-start.1 = (f32[12,16,256]{2,1,0:T(8,128)S(1)}, f32[12,16,256]{2,1,0:T(8,128)S(1)}, u32[]{:S(2)}, u32[]{:S(2)}) collective-permute-start(f32[12,16,256]{2,1,0:T(8,128)S(1)} %dynamic-slice_bitcast_fusion), channel_id=1, source_target_pairs={{0,2},{2,0},{1,3},{3,1},{4,6},{6,4},{5,7},{7,5},{8,10},{10,8},{9,1... | collective-permute-start | bytes 589832 | tf_op jit(solution)/shard_map/ppermute | solution.py:228
  4.7 1.3 %copy-start = (bf16[896,768]{1,0:T(8,128)(2,1)S(1)}, bf16[896,768]{1,0:T(8,128)(2,1)}, u32[]{:S(2)}) copy-start(bf16[896,768]{1,0:T(8,128)(2,1)} %v0_ref.3) | copy-start | bytes 4128772
  6.0 1.3 %copy-start.3 = (bf16[768,768]{1,0:T(8,128)(2,1)S(1)}, bf16[768,768]{1,0:T(8,128)(2,1)}, u32[]{:S(2)}) copy-start(bf16[768,768]{1,0:T(8,128)(2,1)} %rot_ref.1) | copy-start | bytes 3538948
  8.7 1.5 %copy-start.1 = (bf16[896,768]{1,0:T(8,128)(2,1)S(1)}, bf16[896,768]{1,0:T(8,128)(2,1)}, u32[]{:S(2)}) copy-start(bf16[896,768]{1,0:T(8,128)(2,1)} %v0_ref.3) | copy-start | bytes 4128772
  10.2 10.4 %copy-start.2 = (f32[24,256,16]{1,2,0:T(8,128)S(1)}, f32[24,256,16]{1,2,0:T(8,128)}, u32[]{:S(2)}) copy-start(f32[24,256,16]{1,2,0:T(8,128)} %param.5) | copy-start | bytes 1179652
  18.8 11.8 %collective-permute-start.2 = (bf16[992,128]{1,0:T(8,128)(2,1)S(1)}, bf16[992,128]{1,0:T(8,128)(2,1)}, u32[]{:S(2)}, u32[]{:S(2)}) collective-permute-start(bf16[992,128]{1,0:T(8,128)(2,1)S(1)} %get-tuple-element.27), channel_id=1, source_target_pairs={{0,2},{2,0},{1,3},{3,1},{4,6},{6,4},{5,7},{7,5},{8,10},{10,8},{9,1... | collective-permute-start | bytes 761864 | tf_op jit(solution)/shard_map/ppermute | solution.py:267
  20.6 15.7 %collective-permute-start.5 = (bf16[192,896]{1,0:T(8,128)(2,1)S(1)}, bf16[192,896]{1,0:T(8,128)(2,1)S(1)}, u32[]{:S(2)}, u32[]{:S(2)}) collective-permute-start(bf16[192,896]{1,0:T(8,128)(2,1)S(1)} %get-tuple-element.31), channel_id=1, source_target_pairs={{0,1},{1,0},{2,3},{3,2},{4,5},{5,4},{6,7},{7,6},{8,9},{9,8},{10,11... | collective-permute-start | bytes 1032200 | tf_op jit(solution)/shard_map/ppermute | solution.py:268
  29.1 0.7 %copy-start.4 = (bf16[576,128]{1,0:T(8,128)(2,1)}, bf16[576,128]{1,0:T(8,128)(2,1)S(1)}, u32[]{:S(2)}) copy-start(bf16[576,128]{1,0:T(8,128)(2,1)S(1)} %get-tuple-element.29) | copy-start | bytes 442372
  29.7 6.6 %collective-permute-start.4 = (bf16[192,896]{1,0:T(8,128)(2,1)S(1)}, bf16[192,896]{1,0:T(8,128)(2,1)S(1)}, u32[]{:S(2)}, u32[]{:S(2)}) collective-permute-start(bf16[192,896]{1,0:T(8,128)(2,1)S(1)} %get-tuple-element.30), channel_id=1, source_target_pairs={{0,1},{1,0},{2,3},{3,2},{4,5},{5,4},{6,7},{7,6},{8,9},{9,8},{10,11... | collective-permute-start | bytes 1032200 | tf_op jit(solution)/shard_map/ppermute | solution.py:271
  30.3 6.0 %collective-permute-start.3 = (bf16[576,128]{1,0:T(8,128)(2,1)}, bf16[576,128]{1,0:T(8,128)(2,1)S(1)}, u32[]{:S(2)}, u32[]{:S(2)}) collective-permute-start(bf16[576,128]{1,0:T(8,128)(2,1)} %copy-done.4), channel_id=1, source_target_pairs={{0,2},{2,0},{1,3},{3,1},{4,6},{6,4},{5,7},{7,5},{8,10},{10,8},{9,1... | collective-permute-start | bytes 442376 | tf_op jit(solution)/shard_map/ppermute | solution.py:270
  36.7 7.3 %collective-permute-start.6 = (bf16[400,128]{1,0:T(8,128)(2,1)S(1)}, bf16[400,128]{1,0:T(8,128)(2,1)S(1)}, u32[]{:S(2)}, u32[]{:S(2)}) collective-permute-start(bf16[400,128]{1,0:T(8,128)(2,1)S(1)} %get-tuple-element.41), channel_id=1, source_target_pairs={{0,12},{4,8},{8,4},{12,0},{1,13},{5,9},{9,5},{13,1},{2,14},{6,10},... | collective-permute-start | bytes 307208 | tf_op jit(solution)/shard_map/ppermute | solution.py:208
  40.3 7.9 %collective-permute-start.7 = (bf16[400,128]{1,0:T(8,128)(2,1)S(1)}, bf16[400,128]{1,0:T(8,128)(2,1)S(1)}, u32[]{:S(2)}, u32[]{:S(2)}) collective-permute-start(bf16[400,128]{1,0:T(8,128)(2,1)S(1)} %get-tuple-element.43), channel_id=1, source_target_pairs={{0,8},{4,12},{8,0},{12,4},{1,9},{5,13},{9,1},{13,5},{2,10},{6,14},... | collective-permute-start | bytes 307208 | tf_op jit(solution)/shard_map/ppermute | solution.py:208
  40.3 7.9 %collective-permute-start.8 = (bf16[400,128]{1,0:T(8,128)(2,1)S(1)}, bf16[400,128]{1,0:T(8,128)(2,1)S(1)}, u32[]{:S(2)}, u32[]{:S(2)}) collective-permute-start(bf16[400,128]{1,0:T(8,128)(2,1)S(1)} %get-tuple-element.42), channel_id=1, source_target_pairs={{0,4},{4,0},{8,12},{12,8},{1,5},{5,1},{9,13},{13,9},{2,6},{6,2},{1... | collective-permute-start | bytes 307208 | tf_op jit(solution)/shard_map/ppermute | solution.py:208
  48.3 6.3 %collective-permute-start.11 = (bf16[400,128]{1,0:T(8,128)(2,1)S(1)}, bf16[400,128]{1,0:T(8,128)(2,1)S(1)}, u32[]{:S(2)}, u32[]{:S(2)}) collective-permute-start(bf16[400,128]{1,0:T(8,128)(2,1)S(1)} %fusion.2), channel_id=1, source_target_pairs={{0,4},{4,0},{8,12},{12,8},{1,5},{5,1},{9,13},{13,9},{2,6},{6,2},{1... | collective-permute-start | bytes 307208 | tf_op jit(solution)/shard_map/ppermute | solution.py:208
  48.8 7.5 %collective-permute-start.9 = (bf16[400,128]{1,0:T(8,128)(2,1)S(1)}, bf16[400,128]{1,0:T(8,128)(2,1)S(1)}, u32[]{:S(2)}, u32[]{:S(2)}) collective-permute-start(bf16[400,128]{1,0:T(8,128)(2,1)S(1)} %fusion.2), channel_id=1, source_target_pairs={{0,12},{4,8},{8,4},{12,0},{1,13},{5,9},{9,5},{13,1},{2,14},{6,10},... | collective-permute-start | bytes 307208 | tf_op jit(solution)/shard_map/ppermute | solution.py:208
  51.0 9.0 %collective-permute-start.10 = (bf16[400,128]{1,0:T(8,128)(2,1)S(1)}, bf16[400,128]{1,0:T(8,128)(2,1)S(1)}, u32[]{:S(2)}, u32[]{:S(2)}) collective-permute-start(bf16[400,128]{1,0:T(8,128)(2,1)S(1)} %fusion.2), channel_id=1, source_target_pairs={{0,8},{4,12},{8,0},{12,4},{1,9},{5,13},{9,1},{13,5},{2,10},{6,14},... | collective-permute-start | bytes 307208 | tf_op jit(solution)/shard_map/ppermute | solution.py:208
  60.1 1.8 %collective-permute-start.12 = (bf16[4,400,128]{2,1,0:T(8,128)(2,1)S(1)}, bf16[4,400,128]{2,1,0:T(8,128)(2,1)S(1)}, u32[]{:S(2)}, u32[]{:S(2)}) collective-permute-start(bf16[4,400,128]{2,1,0:T(8,128)(2,1)S(1)} %pad_maximum_fusion.mine_ref), channel_id=1, source_target_pairs={{0,1},{1,0},{2,3},{3,2},{4,5},{5,4},{6,7},{7,6},{8,9},{9,8},{10,11... | collective-permute-start | bytes 1228808 | tf_op jit(solution)/shard_map/ppermute | solution.py:296

commit v4 on v3

--- a/solution.py
+++ b/solution.py
@@ -12,7 +12,7 @@
 SOFTNESS = 4.0
 LOG2E = math.log2(math.e)
 F32, BF16 = jnp.float32, jnp.bfloat16
-VMEM_BYTES = 28 * 2**20
+VMEM_BYTES = 24 * 2**20
 
 
 def quantize_rows(block, codebook):
@@ -164,44 +164,60 @@
     out_ref[...] = buf[...].T
 
 
-def final_kernel(mine_ref, theirs_ref, cb_ref, cross_ref, new_ref, buf, *, per, total):
+def final_kernel(*refs, n, per, total):
+    pieces, (cb_ref, cross_hbm, new_hbm, buf, cross, new, sems) = refs[: 2 * n], refs[2 * n :]
     s, r, z = lax.axis_index("sub"), lax.axis_index("rep"), lax.axis_index("row")
-    n = mine_ref.shape[0]
-    piece = mine_ref.shape[1]
     lanes = 128
     w = per * SUBDIM
-    codes = cb_ref.shape[2]
-    groups = cross_ref.shape[0] // lanes
-    halves = codes // lanes
-    for side, ref in enumerate((mine_ref, theirs_ref)):
+    groups = cross.shape[0] // lanes
+    halves = cb_ref.shape[2] // lanes
+    near_rows = groups * w + halves * (w + SUBDIM)
+    near, far = near_rows // n, groups * w // n
+    for side in range(2):
         for i in range(n):
-            at = (z ^ ((n - i) % n)) * piece
-            buf[side, pl.ds(pl.multiple_of(at, SUBDIM), piece), :] = ref[i].astype(F32)
-    a_rows = groups * w + halves * (w + SUBDIM)
+            ref = pieces[side * n + i]
+            source = z ^ ((n - i) % n)
+            buf[side, pl.ds(pl.multiple_of(source * near, 8), near), :] = ref[:near].astype(F32)
+            buf[side, pl.ds(pl.multiple_of(near_rows + source * far, 8), far), :] = ref[near:].astype(F32)
+
+    copies = []
     for g in range(groups):
         for h in range(2):
             for q in range(2):
                 @pl.when((s == h) & (r == q))
                 def _():
-                    pieces = []
+                    parts = []
                     for col in range(2):
-                        k = col ^ h
-                        for rep in range(2):
-                            start = k * a_rows + g * w
-                            pieces.append(buf[rep ^ q, start : start + w, :])
-                    cross_ref[g * lanes : (g + 1) * lanes, :] = jnp.concatenate(pieces, axis=0).T * (1.0 / total)
+                        start = (col ^ h) * near_rows + g * w
+                        parts += [buf[rep ^ q, start : start + w, :] for rep in range(2)]
+                    cross[g * lanes : (g + 1) * lanes, :] = jnp.concatenate(parts, axis=0).T * (1.0 / total)
+        block = pl.ds(g * lanes, lanes)
+        copies.append(pltpu.make_async_copy(cross.at[block], cross_hbm.at[block], sems.at[g]))
+        copies[-1].start()
     first = groups * w
     for side in range(2):
         part = r if side == 0 else 1 - r
         for m in range(per):
             c = cb_ref[part * per + m]
-            sums = jnp.concatenate(
-                [buf[side, first + hf * w + m * SUBDIM : first + hf * w + (m + 1) * SUBDIM, :] for hf in range(halves)],
-                axis=1,
-            )
-            at = first + halves * w + m
-            count = jnp.concatenate([buf[side, at + hf * SUBDIM : at + hf * SUBDIM + 1, :] for hf in range(halves)], axis=1)
-            new_ref[part * per + m] = (sums + c) / (count + 1.0)
+            rows = [first + hf * w + m * SUBDIM for hf in range(halves)]
+            sums = jnp.concatenate([buf[side, a : a + SUBDIM, :] for a in rows], axis=1)
+            rows = [first + halves * w + hf * SUBDIM + m for hf in range(halves)]
+            count = jnp.concatenate([buf[side, a : a + 1, :] for a in rows], axis=1)
+            new[part * per + m] = (sums + c) / (count + 1.0)
+    copies.append(pltpu.make_async_copy(new, new_hbm, sems.at[groups]))
+    copies[-1].start()
+    for copy in copies:
+        copy.wait()
+
+
+def pieces_kernel(kept_ref, got_ref, *refs, n):
+    outs, total = refs[:n], refs[n]
+    z = lax.axis_index("row")
+    total[...] = kept_ref[...] + got_ref[...].astype(F32)
+    size = outs[0].shape[0]
+    for i, out in enumerate(outs):
+        at = (z ^ ((n - i) % n)) * size
+        out[...] = total[pl.ds(pl.multiple_of(at, 8), size), :].astype(out.dtype)
 
 
 def exchange(x, n, d):
@@ -218,15 +234,15 @@
     lanes = 128
     total = rows * rows_n * subs * 2
     swap = [(0, 1), (1, 0)]
-    r, z = lax.axis_index("rep"), lax.axis_index("row")
+    r = lax.axis_index("rep")
     params = pltpu.CompilerParams(vmem_limit_bytes=VMEM_BYTES)
     small = pltpu.CompilerParams(vmem_limit_bytes=VMEM_BYTES // 2)
     vmem = pl.BlockSpec(memory_space=pltpu.VMEM)
 
     cb = codebooks.transpose(0, 2, 1)
-    cb_sent, vec_sent = lax.optimization_barrier((lax.dynamic_slice_in_dim(cb, r * per, per, 0), vectors))
+    cb_sent = lax.dynamic_slice_in_dim(cb, r * per, per, 0)
     cb_far = lax.ppermute(cb_sent, "sub", swap)
-    vec_far = lax.ppermute(vec_sent, "rep", swap)
+    vec_far = lax.ppermute(vectors, "rep", swap)
 
     y_shape = jax.ShapeDtypeStruct((subs, w, rows), BF16)
     y0, rott = pl.pallas_call(
@@ -269,7 +285,7 @@
     mine0, other0, keep0, send0 = quantize(0, cb)
     got0 = lax.ppermute(send0, "sub", swap)
     theirs0 = lax.ppermute(other0, "rep", swap)
-    got0, theirs0, theirs1 = lax.optimization_barrier((got0, theirs0, theirs1))
+    theirs0, theirs1, got0 = lax.optimization_barrier((theirs0, theirs1, got0))
 
     reconstruction = pl.pallas_call(
         turn_kernel,
@@ -281,29 +297,43 @@
         name="turn",
     )(mine0, mine1, theirs0, theirs1)
 
-    used = 2 * p_rows + s_rows
-    piece = -(-used // (rows_n * SUBDIM)) * SUBDIM
-    pad = jnp.zeros((piece * rows_n - used, lanes), BF16)
-    half = jnp.concatenate(
-        [(keep0 + got1.astype(F32)).astype(BF16), (keep1 + got0.astype(F32)).astype(BF16), pad], axis=0
-    ).reshape(rows_n, piece, lanes)
-    own = lax.dynamic_index_in_dim(half, z, 0, keepdims=False)
+    def scatter(kept, got):
+        size = (kept.shape[0] // rows_n, lanes)
+        own, *sent = pl.pallas_call(
+            functools.partial(pieces_kernel, n=rows_n),
+            out_shape=[jax.ShapeDtypeStruct(size, F32)] + [jax.ShapeDtypeStruct(size, BF16)] * (rows_n - 1),
+            in_specs=[vmem] * 2,
+            out_specs=[vmem] * rows_n,
+            scratch_shapes=[pltpu.VMEM(kept.shape, F32)],
+            compiler_params=small,
+            name="pieces",
+        )(kept, got)
+        return [own] + [exchange(x, rows_n, d) for x, d in zip(sent, apart)]
+
+    def add_up(parts):
+        return functools.reduce(lambda a, b: a + b.astype(F32), parts[1:], parts[0]).astype(BF16)
+
     apart = range(rows_n - 1, 0, -1)
-    gathered = [exchange(lax.dynamic_index_in_dim(half, z ^ d, 0, keepdims=False), rows_n, d) for d in apart]
-    summed = functools.reduce(lambda a, b: a + b.astype(F32), gathered, own.astype(F32)).astype(BF16)
+    summed = jnp.concatenate([add_up(scatter(keep0, got1)), add_up(scatter(keep1, got0))], axis=0)
     summed, reconstruction = lax.optimization_barrier((summed, reconstruction))
-    all_mine = jnp.stack([summed] + [exchange(summed, rows_n, d) for d in apart])
-    all_theirs = lax.ppermute(all_mine, "rep", swap)
-
+    mine = [summed] + [exchange(summed, rows_n, d) for d in apart]
+    theirs = [lax.ppermute(x, "rep", swap) for x in mine]
+
+    any_spec = pl.BlockSpec(memory_space=pl.ANY)
     cross, new = pl.pallas_call(
-        functools.partial(final_kernel, per=per, total=total),
+        functools.partial(final_kernel, n=rows_n, per=per, total=total),
         out_shape=(jax.ShapeDtypeStruct((part, width), F32), jax.ShapeDtypeStruct(cb.shape, F32)),
-        in_specs=[vmem] * 3,
-        out_specs=(vmem, vmem),
-        scratch_shapes=[pltpu.VMEM((2, rows_n * piece, lanes), F32)],
+        in_specs=[vmem] * (2 * rows_n + 1),
+        out_specs=(any_spec, any_spec),
+        scratch_shapes=[
+            pltpu.VMEM((2, rows_n * summed.shape[0], lanes), F32),
+            pltpu.VMEM((part, width), F32),
+            pltpu.VMEM(cb.shape, F32),
+            pltpu.SemaphoreType.DMA((part // lanes + 1,)),
+        ],
         compiler_params=small,
         name="final",
-    )(all_mine, all_theirs, cb)
+    )(*mine, *theirs, cb)
     return reconstruction, new.transpose(0, 2, 1), cross
 
 

time: 64 us -> 62.6 us (0.978)
  starting transfers between devices: 13.8 us -> 19.7 us
  waiting for transfers between devices: 20.6 us -> 15.3 us
  other arithmetic: 1.44 us -> 0.07 us
  local copies, waits for them, and re-layouts: 4.34 us -> 3.56 us
    ppermute x6 -> x9, waiting for transfers between devices: 13.7 us -> 6.58 us  [exchange(): return lax.ppermute(x, 'row', [(i, i ^ d) for i in range(n)])]
    ppermute x1, waiting for transfers between devices: 0.01 us -> 6.96 us  [on_device(): got1 = lax.ppermute(send1, 'sub', swap)]
    ppermute x6 -> x9, starting transfers between devices: 8.01 us -> 13.4 us  [exchange(): return lax.ppermute(x, 'row', [(i, i ^ d) for i in range(n)])]
    ppermute x1, waiting for transfers between devices: 4.68 us -> 0.01 us  [on_device(): got0 = lax.ppermute(send0, 'sub', swap)]
    convert_element_type x3 -> x2, other arithmetic: 1.11 us -> 0.07 us  [add_up(): functools.reduce(lambda a, b: a + b.astype(F32), parts[1:], parts[0])]
    unnamed x10 -> x8, local copies, waits for them, and re-layouts: 3.27 us -> 2.62 us
    ppermute x2 -> x5, waiting for transfers between devices: 1.74 us -> 1.29 us  [the longest x4 1.29 us: on_device(): theirs = [lax.ppermute(x, 'rep', swap) for x in mine]]
    pallas_call x1 -> x3, Pallas kernels: 1.79 us -> 1.7 us  [the longest x1 1.57 us: on_device(): pl.pallas_call(functools.partial(final_kernel, n=rows_n, per=per, total=t...]
  transfers between devices with their start and end apart: 13 -> 19, of which waited for: 8 -> 7; matrix products, arithmetic and copies ran while one was open for 2% -> 2% of each run, Pallas kernels for 20% -> 20%
where the time goes in v4:
time: 62.6 us; the launch traced here: 62.4 us
  Pallas kernels  22.8 us (36%)
  starting transfers between devices  19.7 us (31%)
  waiting for transfers between devices  15.3 us (24%)
  local copies, waits for them, and re-layouts  3.56 us (6%)
  between operations  0.92 us (1%)
    pallas_call x2, Pallas kernels, quantize(): pl.pallas_call(functools.partial(quantize_kernel, k=k, per=per), in_specs...  17.1 us
    ppermute x9, starting transfers between devices, exchange(): return lax.ppermute(x, 'row', [(i, i ^ d) for i in range(n)])  13.4 us
    ppermute x1, waiting for transfers between devices, on_device(): got1 = lax.ppermute(send1, 'sub', swap)  6.96 us
    ppermute x9, waiting for transfers between devices, exchange(): return lax.ppermute(x, 'row', [(i, i ^ d) for i in range(n)])  6.58 us
    unnamed x8, local copies, waits for them, and re-layouts  2.62 us
    ppermute x1, starting transfers between devices, on_device(): cb_far = lax.ppermute(cb_sent, 'sub', swap)  2.58 us
    ppermute x1, starting transfers between devices, on_device(): got1 = lax.ppermute(send1, 'sub', swap)  1.74 us
    pallas_call x1, Pallas kernels, on_device(): pl.pallas_call(turn_kernel, out_shape=jax.ShapeDtypeStruct((rows, width),...  1.61 us
  transfers between devices with their start and end apart: 19, of which 7 were waited for; matrix products, arithmetic and copies ran while one was open for 2% of the time, Pallas kernels for 20%

profile of v4, /device:TPU:0, one launch (start us, length us, event | category | flops | bytes accessed | tf_op | source)
XLA Modules:
  0.0 62.4 jit_solution(12108113794278061995)
XLA Ops:
  1.1 0.9 %dynamic-slice_bitcast_fusion = f32[12,16,256]{2,1,0:T(8,128)S(1)} fusion(f32[24,256,16]{1,2,0:T(8,128)} %param.5, s32[]{:T(128)S(6)} %select_n.3), kind=kLoop, calls=%fused_computation | loop fusion | bytes 393220 | tf_op jit(solution)/shard_map/dynamic_slice | solution.py:243
  2.1 2.6 %collective-permute-start.1 = (f32[12,16,256]{2,1,0:T(8,128)S(1)}, f32[12,16,256]{2,1,0:T(8,128)S(1)}, u32[]{:S(2)}, u32[]{:S(2)}) collective-permute-start(f32[12,16,256]{2,1,0:T(8,128)S(1)} %dynamic-slice_bitcast_fusion), channel_id=1, source_target_pairs={{0,2},{2,0},{1,3},{3,1},{4,6},{6,4},{5,7},{7,5},{8,10},{10,8},{9,1... | collective-permute-start | bytes 589832 | tf_op jit(solution)/shard_map/ppermute | solution.py:244
  4.7 1.3 %copy-done = bf16[896,768]{1,0:T(8,128)(2,1)S(1)} copy-done((bf16[896,768]{1,0:T(8,128)(2,1)S(1)}, bf16[896,768]{1,0:T(8,128)(2,1)}, u32[]{:S(2)}) %copy-start) | copy-done | bytes 1376280
  6.0 1.3 %copy-done.3 = bf16[768,768]{1,0:T(8,128)(2,1)S(1)} copy-done((bf16[768,768]{1,0:T(8,128)(2,1)S(1)}, bf16[768,768]{1,0:T(8,128)(2,1)}, u32[]{:S(2)}) %copy-start.3) | copy-done | bytes 1179672
  7.3 1.4 %rotate.1 = (bf16[2,192,896]{2,1,0:T(8,128)(2,1)S(1)}, bf16[2,192,768]{2,1,0:T(8,128)(2,1)S(1)}) custom-call(bf16[896,768]{1,0:T(8,128)(2,1)S(1)} %copy-done, bf16[768,768]{1,0:T(8,128)(2,1)S(1)} %copy-done.3), custom_call_target="tpu_custom_call" | custom-call | tf_op jit(solution)/shard_map/rotate/pallas_call | solution.py:248
  8.7 1.0 %rotate_far.1.y1_ref = bf16[2,192,896]{2,1,0:T(8,128)(2,1)S(1)} custom-call(bf16[896,768]{1,0:T(8,128)(2,1)S(1)} %collective-permute-done.vec_ref.v1_ref, bf16[2,192,768]{2,1,0:T(8,128)(2,1)S(1)} %get-tuple-element.29.rott_ref), custom_call_target="tpu_custom_call" | custom-call | tf_op jit(solution)/shard_map/rotate_far/pallas_call | solution.py:257
  10.2 8.6 %quantize_far.1 = (bf16[192,896]{1,0:T(8,128)(2,1)S(1)}, bf16[192,896]{1,0:T(8,128)(2,1)S(1)}, f32[576,128]{1,0:T(8,128)S(1)}, bf16[992,128]{1,0:T(8,128)(2,1)S(1)}) custom-call(f32[12,16,256]{2,1,0:T(8,128)S(1)} %collective-permute-done.1.cb_ref, bf16[2,192,896]{2,1,0:T(8,128)(2,1)S(1)} %get-tuple-element.28.y0_ref, ...), custom_call_target="tpu_custom_call" | custom-call | tf_op jit(solution)/shard_map/quantize_far/pallas_call | solution.py:267
  18.9 8.4 %quantize_near.1 = (bf16[192,896]{1,0:T(8,128)(2,1)S(1)}, bf16[192,896]{1,0:T(8,128)(2,1)S(1)}, f32[992,128]{1,0:T(8,128)S(1)}, bf16[576,128]{1,0:T(8,128)(2,1)S(1)}) custom-call(f32[24,16,256]{2,1,0:T(8,128)S(1)} %bitcast.4, bf16[2,192,896]{2,1,0:T(8,128)(2,1)S(1)} %get-tuple-element.28.y0_ref, bf16[2,192,896]{2,1,0:T(8,128)(2,1)S(1)} %rotate_far.1.y1_ref, ...), custom_call_target="tpu_custom_call" | custom-call | tf_op jit(solution)/shard_map/quantize_near/pallas_call | solution.py:267
  27.4 0.5 collective-permute-start.6
  27.9 1.7 %collective-permute-start.2 = (bf16[992,128]{1,0:T(8,128)(2,1)S(1)}, bf16[992,128]{1,0:T(8,128)(2,1)S(1)}, u32[]{:S(2)}, u32[]{:S(2)}) collective-permute-start(bf16[992,128]{1,0:T(8,128)(2,1)S(1)} %get-tuple-element.31), channel_id=1, source_target_pairs={{0,2},{2,0},{1,3},{3,1},{4,6},{6,4},{5,7},{7,5},{8,10},{10,8},{9,1... | collective-permute-start | bytes 761864 | tf_op jit(solution)/shard_map/ppermute | solution.py:283
  30.0 7.0 %collective-permute-done.2.got_ref = bf16[992,128]{1,0:T(8,128)(2,1)S(1)} collective-permute-done((bf16[992,128]{1,0:T(8,128)(2,1)S(1)}, bf16[992,128]{1,0:T(8,128)(2,1)S(1)}, u32[]{:S(2)}, u32[]{:S(2)}) %collective-permute-start.2) | collective-permute-done | bytes 253984 | tf_op jit(solution)/shard_map/ppermute | solution.py:283
  37.0 3.9 %collective-permute-start.3 = (bf16[248,128]{1,0:T(8,128)(2,1)S(1)}, bf16[248,128]{1,0:T(8,128)(2,1)S(1)}, u32[]{:S(2)}, u32[]{:S(2)}) collective-permute-start(bf16[248,128]{1,0:T(8,128)(2,1)S(1)} %get-tuple-element.33), channel_id=1, source_target_pairs={{0,12},{4,8},{8,4},{12,0},{1,13},{5,9},{9,5},{13,1},{2,14},{6,10},... | collective-permute-start | bytes 190472 | tf_op jit(solution)/shard_map/ppermute | solution.py:224
  40.9 0.6 %collective-permute-start.5 = (bf16[248,128]{1,0:T(8,128)(2,1)S(1)}, bf16[248,128]{1,0:T(8,128)(2,1)S(1)}, u32[]{:S(2)}, u32[]{:S(2)}) collective-permute-start(bf16[248,128]{1,0:T(8,128)(2,1)S(1)} %get-tuple-element.35), channel_id=1, source_target_pairs={{0,4},{4,0},{8,12},{12,8},{1,5},{5,1},{9,13},{13,9},{2,6},{6,2},{1... | collective-permute-start | bytes 190472 | tf_op jit(solution)/shard_map/ppermute | solution.py:224
  41.6 3.8 %collective-permute-start.9 = (bf16[144,128]{1,0:T(8,128)(2,1)S(1)}, bf16[144,128]{1,0:T(8,128)(2,1)S(1)}, u32[]{:S(2)}, u32[]{:S(2)}) collective-permute-start(bf16[144,128]{1,0:T(8,128)(2,1)S(1)} %get-tuple-element.42), channel_id=1, source_target_pairs={{0,12},{4,8},{8,4},{12,0},{1,13},{5,9},{9,5},{13,1},{2,14},{6,10},... | collective-permute-start | bytes 110600 | tf_op jit(solution)/shard_map/ppermute | solution.py:224
  45.4 0.6 %collective-permute-start.11 = (bf16[144,128]{1,0:T(8,128)(2,1)S(1)}, bf16[144,128]{1,0:T(8,128)(2,1)S(1)}, u32[]{:S(2)}, u32[]{:S(2)}) collective-permute-start(bf16[144,128]{1,0:T(8,128)(2,1)S(1)} %get-tuple-element.44), channel_id=1, source_target_pairs={{0,4},{4,0},{8,12},{12,8},{1,5},{5,1},{9,13},{13,9},{2,6},{6,2},{1... | collective-permute-start | bytes 110600 | tf_op jit(solution)/shard_map/ppermute | solution.py:224
  46.1 1.1 %collective-permute-done.4 = bf16[248,128]{1,0:T(8,128)(2,1)S(1)} collective-permute-done((bf16[248,128]{1,0:T(8,128)(2,1)S(1)}, bf16[248,128]{1,0:T(8,128)(2,1)S(1)}, u32[]{:S(2)}, u32[]{:S(2)}) %collective-permute-start.4) | collective-permute-done | bytes 63520 | tf_op jit(solution)/shard_map/ppermute | solution.py:224
  47.2 1.6 %turn.1 = bf16[896,768]{1,0:T(8,128)(2,1)} custom-call(bf16[192,896]{1,0:T(8,128)(2,1)S(1)} %get-tuple-element.45.m0_ref, bf16[192,896]{1,0:T(8,128)(2,1)S(1)} %get-tuple-element.46.m1_ref, bf16[192,896]{1,0:T(8,128)(2,1)S(1)} %collective-permute-done.6.t0_ref, bf16[192,896]{1,0:T(8,128)(2,1)S(1)} %collective-permute-done.7.t1_ref), custom_call_target="tpu_custom_call" | custom-call | tf_op jit(solution)/shard_map/turn/pallas_call | solution.py:290
  48.8 1.5 %collective-permute-done.10 = bf16[144,128]{1,0:T(8,128)(2,1)S(1)} collective-permute-done((bf16[144,128]{1,0:T(8,128)(2,1)S(1)}, bf16[144,128]{1,0:T(8,128)(2,1)S(1)}, u32[]{:S(2)}, u32[]{:S(2)}) %collective-permute-start.10) | collective-permute-done | bytes 36896 | tf_op jit(solution)/shard_map/ppermute | solution.py:224
  50.5 2.4 %collective-permute-start.13 = (bf16[392,128]{1,0:T(8,128)(2,1)S(1)}, bf16[392,128]{1,0:T(8,128)(2,1)S(1)}, u32[]{:S(2)}, u32[]{:S(2)}) collective-permute-start(bf16[392,128]{1,0:T(8,128)(2,1)S(1)} %pad_maximum_fusion.refs_0_), channel_id=1, source_target_pairs={{0,8},{4,12},{8,0},{12,4},{1,9},{5,13},{9,1},{13,5},{2,10},{6,14},... | collective-permute-start | bytes 301064 | tf_op jit(solution)/shard_map/ppermute | solution.py:224
  52.8 2.0 %collective-permute-start.12 = (bf16[392,128]{1,0:T(8,128)(2,1)S(1)}, bf16[392,128]{1,0:T(8,128)(2,1)S(1)}, u32[]{:S(2)}, u32[]{:S(2)}) collective-permute-start(bf16[392,128]{1,0:T(8,128)(2,1)S(1)} %pad_maximum_fusion.refs_0_), channel_id=1, source_target_pairs={{0,12},{4,8},{8,4},{12,0},{1,13},{5,9},{9,5},{13,1},{2,14},{6,10},... | collective-permute-start | bytes 301064 | tf_op jit(solution)/shard_map/ppermute | solution.py:224
  54.8 2.4 %collective-permute-done.14.refs_3_ = bf16[392,128]{1,0:T(8,128)(2,1)S(1)} collective-permute-done((bf16[392,128]{1,0:T(8,128)(2,1)S(1)}, bf16[392,128]{1,0:T(8,128)(2,1)S(1)}, u32[]{:S(2)}, u32[]{:S(2)}) %collective-permute-start.14) | collective-permute-done | bytes 100384 | tf_op jit(solution)/shard_map/ppermute | solution.py:224
  57.7 1.6 %collective-permute-done.12.refs_1_ = bf16[392,128]{1,0:T(8,128)(2,1)S(1)} collective-permute-done((bf16[392,128]{1,0:T(8,128)(2,1)S(1)}, bf16[392,128]{1,0:T(8,128)(2,1)S(1)}, u32[]{:S(2)}, u32[]{:S(2)}) %collective-permute-start.12) | collective-permute-done | bytes 100384 | tf_op jit(solution)/shard_map/ppermute | solution.py:224
  59.3 1.3 %collective-permute-done.16.refs_5_ = bf16[392,128]{1,0:T(8,128)(2,1)S(1)} collective-permute-done((bf16[392,128]{1,0:T(8,128)(2,1)S(1)}, bf16[392,128]{1,0:T(8,128)(2,1)S(1)}, u32[]{:S(2)}, u32[]{:S(2)}) %collective-permute-start.16) | collective-permute-done | bytes 100384 | tf_op jit(solution)/shard_map/ppermute | solution.py:320
  60.6 1.6 %final.1 = (f32[384,768]{1,0:T(8,128)}, f32[24,16,256]{2,1,0:T(8,128)}) custom-call(bf16[392,128]{1,0:T(8,128)(2,1)S(1)} %pad_maximum_fusion.refs_0_, bf16[392,128]{1,0:T(8,128)(2,1)S(1)} %collective-permute-done.12.refs_1_, bf16[392,128]{1,0:T(8,128)(2,1)S(1)} %collective-permute-done.13.refs_2_, bf16[392,128]{1,0:T(8,128)(2,1)S(1)} %collective-permute-done.14.refs_3_, ...), custom_call_target="tpu_custom_call" | custom-call | tf_op jit(solution)/shard_map/final/pallas_call | solution.py:323
  (34 shorter events, 2.2 us)
Async XLA Ops:
  0.6 8.1 %collective-permute-start = (bf16[896,768]{1,0:T(8,128)(2,1)}, bf16[896,768]{1,0:T(8,128)(2,1)S(1)}, u32[]{:S(2)}, u32[]{:S(2)}) collective-permute-start(bf16[896,768]{1,0:T(8,128)(2,1)} %v0_ref.3), channel_id=1, source_target_pairs={{0,1},{1,0},{2,3},{3,2},{4,5},{5,4},{6,7},{7,6},{8,9},{9,8},{10,11... | collective-permute-start | bytes 4128776 | tf_op jit(solution)/shard_map/ppermute | solution.py:245
  2.1 8.1 %collective-permute-start.1 = (f32[12,16,256]{2,1,0:T(8,128)S(1)}, f32[12,16,256]{2,1,0:T(8,128)S(1)}, u32[]{:S(2)}, u32[]{:S(2)}) collective-permute-start(f32[12,16,256]{2,1,0:T(8,128)S(1)} %dynamic-slice_bitcast_fusion), channel_id=1, source_target_pairs={{0,2},{2,0},{1,3},{3,1},{4,6},{6,4},{5,7},{7,5},{8,10},{10,8},{9,1... | collective-permute-start | bytes 589832 | tf_op jit(solution)/shard_map/ppermute | solution.py:244
  4.7 1.3 %copy-start = (bf16[896,768]{1,0:T(8,128)(2,1)S(1)}, bf16[896,768]{1,0:T(8,128)(2,1)}, u32[]{:S(2)}) copy-start(bf16[896,768]{1,0:T(8,128)(2,1)} %v0_ref.3) | copy-start | bytes 4128772
  6.0 1.3 %copy-start.3 = (bf16[768,768]{1,0:T(8,128)(2,1)S(1)}, bf16[768,768]{1,0:T(8,128)(2,1)}, u32[]{:S(2)}) copy-start(bf16[768,768]{1,0:T(8,128)(2,1)} %rot_ref.1) | copy-start | bytes 3538948
  8.7 1.5 %copy-start.1 = (bf16[896,768]{1,0:T(8,128)(2,1)S(1)}, bf16[896,768]{1,0:T(8,128)(2,1)}, u32[]{:S(2)}) copy-start(bf16[896,768]{1,0:T(8,128)(2,1)} %v0_ref.3) | copy-start | bytes 4128772
  10.2 8.7 %copy-start.2 = (f32[24,256,16]{1,2,0:T(8,128)S(1)}, f32[24,256,16]{1,2,0:T(8,128)}, u32[]{:S(2)}) copy-start(f32[24,256,16]{1,2,0:T(8,128)} %param.5) | copy-start | bytes 1179652
  18.8 22.7 %collective-permute-start.7 = (bf16[192,896]{1,0:T(8,128)(2,1)S(1)}, bf16[192,896]{1,0:T(8,128)(2,1)S(1)}, u32[]{:S(2)}, u32[]{:S(2)}) collective-permute-start(bf16[192,896]{1,0:T(8,128)(2,1)S(1)} %get-tuple-element.38), channel_id=1, source_target_pairs={{0,1},{1,0},{2,3},{3,2},{4,5},{5,4},{6,7},{7,6},{8,9},{9,8},{10,11... | collective-permute-start | bytes 1032200 | tf_op jit(solution)/shard_map/ppermute | solution.py:284
  27.4 14.2 %collective-permute-start.6 = (bf16[192,896]{1,0:T(8,128)(2,1)S(1)}, bf16[192,896]{1,0:T(8,128)(2,1)S(1)}, u32[]{:S(2)}, u32[]{:S(2)}) collective-permute-start(bf16[192,896]{1,0:T(8,128)(2,1)S(1)} %get-tuple-element.37), channel_id=1, source_target_pairs={{0,1},{1,0},{2,3},{3,2},{4,5},{5,4},{6,7},{7,6},{8,9},{9,8},{10,11... | collective-permute-start | bytes 1032200 | tf_op jit(solution)/shard_map/ppermute | solution.py:287
  27.9 9.0 %collective-permute-start.2 = (bf16[992,128]{1,0:T(8,128)(2,1)S(1)}, bf16[992,128]{1,0:T(8,128)(2,1)S(1)}, u32[]{:S(2)}, u32[]{:S(2)}) collective-permute-start(bf16[992,128]{1,0:T(8,128)(2,1)S(1)} %get-tuple-element.31), channel_id=1, source_target_pairs={{0,2},{2,0},{1,3},{3,1},{4,6},{6,4},{5,7},{7,5},{8,10},{10,8},{9,1... | collective-permute-start | bytes 761864 | tf_op jit(solution)/shard_map/ppermute | solution.py:283
  29.7 11.2 %collective-permute-start.8 = (bf16[576,128]{1,0:T(8,128)(2,1)S(1)}, bf16[576,128]{1,0:T(8,128)(2,1)S(1)}, u32[]{:S(2)}, u32[]{:S(2)}) collective-permute-start(bf16[576,128]{1,0:T(8,128)(2,1)S(1)} %get-tuple-element.39), channel_id=1, source_target_pairs={{0,2},{2,0},{1,3},{3,1},{4,6},{6,4},{5,7},{7,5},{8,10},{10,8},{9,1... | collective-permute-start | bytes 442376 | tf_op jit(solution)/shard_map/ppermute | solution.py:286
  37.0 8.4 %collective-permute-start.3 = (bf16[248,128]{1,0:T(8,128)(2,1)S(1)}, bf16[248,128]{1,0:T(8,128)(2,1)S(1)}, u32[]{:S(2)}, u32[]{:S(2)}) collective-permute-start(bf16[248,128]{1,0:T(8,128)(2,1)S(1)} %get-tuple-element.33), channel_id=1, source_target_pairs={{0,12},{4,8},{8,4},{12,0},{1,13},{5,9},{9,5},{13,1},{2,14},{6,10},... | collective-permute-start | bytes 190472 | tf_op jit(solution)/shard_map/ppermute | solution.py:224
  40.9 6.2 %collective-permute-start.4 = (bf16[248,128]{1,0:T(8,128)(2,1)S(1)}, bf16[248,128]{1,0:T(8,128)(2,1)S(1)}, u32[]{:S(2)}, u32[]{:S(2)}) collective-permute-start(bf16[248,128]{1,0:T(8,128)(2,1)S(1)} %get-tuple-element.34), channel_id=1, source_target_pairs={{0,8},{4,12},{8,0},{12,4},{1,9},{5,13},{9,1},{13,5},{2,10},{6,14},... | collective-permute-start | bytes 190472 | tf_op jit(solution)/shard_map/ppermute | solution.py:224
  40.9 6.2 %collective-permute-start.5 = (bf16[248,128]{1,0:T(8,128)(2,1)S(1)}, bf16[248,128]{1,0:T(8,128)(2,1)S(1)}, u32[]{:S(2)}, u32[]{:S(2)}) collective-permute-start(bf16[248,128]{1,0:T(8,128)(2,1)S(1)} %get-tuple-element.35), channel_id=1, source_target_pairs={{0,4},{4,0},{8,12},{12,8},{1,5},{5,1},{9,13},{13,9},{2,6},{6,2},{1... | collective-permute-start | bytes 190472 | tf_op jit(solution)/shard_map/ppermute | solution.py:224
  41.6 7.2 %collective-permute-start.9 = (bf16[144,128]{1,0:T(8,128)(2,1)S(1)}, bf16[144,128]{1,0:T(8,128)(2,1)S(1)}, u32[]{:S(2)}, u32[]{:S(2)}) collective-permute-start(bf16[144,128]{1,0:T(8,128)(2,1)S(1)} %get-tuple-element.42), channel_id=1, source_target_pairs={{0,12},{4,8},{8,4},{12,0},{1,13},{5,9},{9,5},{13,1},{2,14},{6,10},... | collective-permute-start | bytes 110600 | tf_op jit(solution)/shard_map/ppermute | solution.py:224
  45.4 4.9 %collective-permute-start.10 = (bf16[144,128]{1,0:T(8,128)(2,1)S(1)}, bf16[144,128]{1,0:T(8,128)(2,1)S(1)}, u32[]{:S(2)}, u32[]{:S(2)}) collective-permute-start(bf16[144,128]{1,0:T(8,128)(2,1)S(1)} %get-tuple-element.43), channel_id=1, source_target_pairs={{0,8},{4,12},{8,0},{12,4},{1,9},{5,13},{9,1},{13,5},{2,10},{6,14},... | collective-permute-start | bytes 110600 | tf_op jit(solution)/shard_map/ppermute | solution.py:224
  45.4 4.9 %collective-permute-start.11 = (bf16[144,128]{1,0:T(8,128)(2,1)S(1)}, bf16[144,128]{1,0:T(8,128)(2,1)S(1)}, u32[]{:S(2)}, u32[]{:S(2)}) collective-permute-start(bf16[144,128]{1,0:T(8,128)(2,1)S(1)} %get-tuple-element.44), channel_id=1, source_target_pairs={{0,4},{4,0},{8,12},{12,8},{1,5},{5,1},{9,13},{13,9},{2,6},{6,2},{1... | collective-permute-start | bytes 110600 | tf_op jit(solution)/shard_map/ppermute | solution.py:224
  50.4 6.9 %collective-permute-start.14 = (bf16[392,128]{1,0:T(8,128)(2,1)S(1)}, bf16[392,128]{1,0:T(8,128)(2,1)S(1)}, u32[]{:S(2)}, u32[]{:S(2)}) collective-permute-start(bf16[392,128]{1,0:T(8,128)(2,1)S(1)} %pad_maximum_fusion.refs_0_), channel_id=1, source_target_pairs={{0,4},{4,0},{8,12},{12,8},{1,5},{5,1},{9,13},{13,9},{2,6},{6,2},{1... | collective-permute-start | bytes 301064 | tf_op jit(solution)/shard_map/ppermute | solution.py:224
  50.5 6.8 %collective-permute-start.13 = (bf16[392,128]{1,0:T(8,128)(2,1)S(1)}, bf16[392,128]{1,0:T(8,128)(2,1)S(1)}, u32[]{:S(2)}, u32[]{:S(2)}) collective-permute-start(bf16[392,128]{1,0:T(8,128)(2,1)S(1)} %pad_maximum_fusion.refs_0_), channel_id=1, source_target_pairs={{0,8},{4,12},{8,0},{12,4},{1,9},{5,13},{9,1},{13,5},{2,10},{6,14},... | collective-permute-start | bytes 301064 | tf_op jit(solution)/shard_map/ppermute | solution.py:224
  52.8 6.5 %collective-permute-start.12 = (bf16[392,128]{1,0:T(8,128)(2,1)S(1)}, bf16[392,128]{1,0:T(8,128)(2,1)S(1)}, u32[]{:S(2)}, u32[]{:S(2)}) collective-permute-start(bf16[392,128]{1,0:T(8,128)(2,1)S(1)} %pad_maximum_fusion.refs_0_), channel_id=1, source_target_pairs={{0,12},{4,8},{8,4},{12,0},{1,13},{5,9},{9,5},{13,1},{2,14},{6,10},... | collective-permute-start | bytes 301064 | tf_op jit(solution)/shard_map/ppermute | solution.py:224
  54.8 4.5 %collective-permute-start.15 = (bf16[392,128]{1,0:T(8,128)(2,1)S(1)}, bf16[392,128]{1,0:T(8,128)(2,1)S(1)}, u32[]{:S(2)}, u32[]{:S(2)}) collective-permute-start(bf16[392,128]{1,0:T(8,128)(2,1)S(1)} %pad_maximum_fusion.refs_0_), channel_id=1, source_target_pairs={{0,1},{1,0},{2,3},{3,2},{4,5},{5,4},{6,7},{7,6},{8,9},{9,8},{10,11... | collective-permute-start | bytes 301064 | tf_op jit(solution)/shard_map/ppermute | solution.py:320
  57.2 2.1 %collective-permute-start.18 = (bf16[392,128]{1,0:T(8,128)(2,1)S(1)}, bf16[392,128]{1,0:T(8,128)(2,1)S(1)}, u32[]{:S(2)}, u32[]{:S(2)}) collective-permute-start(bf16[392,128]{1,0:T(8,128)(2,1)S(1)} %collective-permute-done.14.refs_3_), channel_id=1, source_target_pairs={{0,1},{1,0},{2,3},{3,2},{4,5},{5,4},{6,7},{7,6},{8,9},{9,8},{10,11... | collective-permute-start | bytes 301064 | tf_op jit(solution)/shard_map/ppermute | solution.py:320
  57.2 2.1 %collective-permute-start.17 = (bf16[392,128]{1,0:T(8,128)(2,1)S(1)}, bf16[392,128]{1,0:T(8,128)(2,1)S(1)}, u32[]{:S(2)}, u32[]{:S(2)}) collective-permute-start(bf16[392,128]{1,0:T(8,128)(2,1)S(1)} %collective-permute-done.13.refs_2_), channel_id=1, source_target_pairs={{0,1},{1,0},{2,3},{3,2},{4,5},{5,4},{6,7},{7,6},{8,9},{9,8},{10,11... | collective-permute-start | bytes 301064 | tf_op jit(solution)/shard_map/ppermute | solution.py:320
  59.3 1.3 %collective-permute-start.16 = (bf16[392,128]{1,0:T(8,128)(2,1)S(1)}, bf16[392,128]{1,0:T(8,128)(2,1)S(1)}, u32[]{:S(2)}, u32[]{:S(2)}) collective-permute-start(bf16[392,128]{1,0:T(8,128)(2,1)S(1)} %collective-permute-done.12.refs_1_), channel_id=1, source_target_pairs={{0,1},{1,0},{2,3},{3,2},{4,5},{5,4},{6,7},{7,6},{8,9},{9,8},{10,11... | collective-permute-start | bytes 301064 | tf_op jit(solution)/shard_map/ppermute | solution.py:320

commit v5 on v4

--- a/solution.py
+++ b/solution.py
@@ -13,6 +13,7 @@
 LOG2E = math.log2(math.e)
 F32, BF16 = jnp.float32, jnp.bfloat16
 VMEM_BYTES = 24 * 2**20
+COST_BYTES = 2**23
 
 
 def quantize_rows(block, codebook):
@@ -276,6 +277,11 @@
             ],
             scratch_shapes=[pltpu.VMEM(((codes // lanes) * SUBDIM, lanes), F32)],
             compiler_params=params,
+            cost_estimate=pl.CostEstimate(
+                flops=per * codes * rows * 2 * 2 * (9 * SUBDIM) + 2 * w * 2 * rows * width,
+                transcendentals=per * codes * rows * 2,
+                bytes_accessed=COST_BYTES,
+            ),
             name="quantize_near" if k == 0 else "quantize_far",
         )(cb_k, y0, y1, vectors, vec_far)
 
@@ -285,7 +291,6 @@
     mine0, other0, keep0, send0 = quantize(0, cb)
     got0 = lax.ppermute(send0, "sub", swap)
     theirs0 = lax.ppermute(other0, "rep", swap)
-    theirs0, theirs1, got0 = lax.optimization_barrier((theirs0, theirs1, got0))
 
     reconstruction = pl.pallas_call(
         turn_kernel,
@@ -314,7 +319,9 @@
         return functools.reduce(lambda a, b: a + b.astype(F32), parts[1:], parts[0]).astype(BF16)
 
     apart = range(rows_n - 1, 0, -1)
-    summed = jnp.concatenate([add_up(scatter(keep0, got1)), add_up(scatter(keep1, got0))], axis=0)
+    near = scatter(keep0, got1)
+    near[0], got0, theirs1 = lax.optimization_barrier((near[0], got0, theirs1))
+    summed = jnp.concatenate([add_up(near), add_up(scatter(keep1, got0))], axis=0)
     summed, reconstruction = lax.optimization_barrier((summed, reconstruction))
     mine = [summed] + [exchange(summed, rows_n, d) for d in apart]
     theirs = [lax.ppermute(x, "rep", swap) for x in mine]

time: 62.6 us -> 58 us (0.927)
  waiting for transfers between devices: 15.3 us -> 9.8 us
  starting transfers between devices: 19.7 us -> 20.7 us
    ppermute x1, waiting for transfers between devices: 6.96 us -> 0.01 us  [on_device(): got1 = lax.ppermute(send1, 'sub', swap)]
    ppermute x1, waiting for transfers between devices: 0.01 us -> 1.73 us  [on_device(): got0 = lax.ppermute(send0, 'sub', swap)]
    ppermute x9, starting transfers between devices: 13.4 us -> 14.3 us  [exchange(): return lax.ppermute(x, 'row', [(i, i ^ d) for i in range(n)])]
  transfers between devices with their start and end apart: 19 -> 19, of which waited for: 7 -> 8; matrix products, arithmetic and copies ran while one was open for 2% -> 2% of each run, Pallas kernels for 20% -> 22%
where the time goes in v5:
time: 58 us; the launch traced here: 57.8 us
  Pallas kernels  22.8 us (39%)
  starting transfers between devices  20.7 us (36%)
  waiting for transfers between devices  9.8 us (17%)
  local copies, waits for them, and re-layouts  3.56 us (6%)
  between operations  0.89 us (2%)
    pallas_call x2, Pallas kernels, quantize(): pl.pallas_call(functools.partial(quantize_kernel, k=k, per=per), in_specs...  17.1 us
    ppermute x9, starting transfers between devices, exchange(): return lax.ppermute(x, 'row', [(i, i ^ d) for i in range(n)])  14.3 us
    ppermute x9, waiting for transfers between devices, exchange(): return lax.ppermute(x, 'row', [(i, i ^ d) for i in range(n)])  6.6 us
    unnamed x8, local copies, waits for them, and re-layouts  2.62 us
    ppermute x1, starting transfers between devices, on_device(): cb_far = lax.ppermute(cb_sent, 'sub', swap)  2.58 us
    ppermute x1, starting transfers between devices, on_device(): got1 = lax.ppermute(send1, 'sub', swap)  1.81 us
    ppermute x1, waiting for transfers between devices, on_device(): got0 = lax.ppermute(send0, 'sub', swap)  1.73 us
    pallas_call x1, Pallas kernels, on_device(): pl.pallas_call(turn_kernel, out_shape=jax.ShapeDtypeStruct((rows, width),...  1.61 us
  transfers between devices with their start and end apart: 19, of which 8 were waited for; matrix products, arithmetic and copies ran while one was open for 2% of the time, Pallas kernels for 22%

profile of v5, /device:TPU:0, one launch (start us, length us, event | category | flops | bytes accessed | tf_op | source)
XLA Modules:
  0.0 57.8 jit_solution(2779734287245527090)
XLA Ops:
  0.6 0.5 collective-permute-start
  1.1 0.9 %dynamic-slice_bitcast_fusion = f32[12,16,256]{2,1,0:T(8,128)S(1)} fusion(f32[24,256,16]{1,2,0:T(8,128)} %param.5, s32[]{:T(128)S(6)} %select_n.3), kind=kLoop, calls=%fused_computation | loop fusion | bytes 393220 | tf_op jit(solution)/shard_map/dynamic_slice | solution.py:244
  2.1 2.6 %collective-permute-start.1 = (f32[12,16,256]{2,1,0:T(8,128)S(1)}, f32[12,16,256]{2,1,0:T(8,128)S(1)}, u32[]{:S(2)}, u32[]{:S(2)}) collective-permute-start(f32[12,16,256]{2,1,0:T(8,128)S(1)} %dynamic-slice_bitcast_fusion), channel_id=1, source_target_pairs={{0,2},{2,0},{1,3},{3,1},{4,6},{6,4},{5,7},{7,5},{8,10},{10,8},{9,1... | collective-permute-start | bytes 589832 | tf_op jit(solution)/shard_map/ppermute | solution.py:245
  4.7 1.3 %copy-done = bf16[896,768]{1,0:T(8,128)(2,1)S(1)} copy-done((bf16[896,768]{1,0:T(8,128)(2,1)S(1)}, bf16[896,768]{1,0:T(8,128)(2,1)}, u32[]{:S(2)}) %copy-start) | copy-done | bytes 1376280
  6.0 1.3 %copy-done.2 = bf16[768,768]{1,0:T(8,128)(2,1)S(1)} copy-done((bf16[768,768]{1,0:T(8,128)(2,1)S(1)}, bf16[768,768]{1,0:T(8,128)(2,1)}, u32[]{:S(2)}) %copy-start.2) | copy-done | bytes 1179672
  7.3 1.4 %rotate.1 = (bf16[2,192,896]{2,1,0:T(8,128)(2,1)S(1)}, bf16[2,192,768]{2,1,0:T(8,128)(2,1)S(1)}) custom-call(bf16[896,768]{1,0:T(8,128)(2,1)S(1)} %copy-done, bf16[768,768]{1,0:T(8,128)(2,1)S(1)} %copy-done.2), custom_call_target="tpu_custom_call" | custom-call | tf_op jit(solution)/shard_map/rotate/pallas_call | solution.py:249
  8.7 1.0 %rotate_far.1.y1_ref = bf16[2,192,896]{2,1,0:T(8,128)(2,1)S(1)} custom-call(bf16[896,768]{1,0:T(8,128)(2,1)S(1)} %collective-permute-done.vec_ref.v1_ref, bf16[2,192,768]{2,1,0:T(8,128)(2,1)S(1)} %get-tuple-element.28.rott_ref), custom_call_target="tpu_custom_call" | custom-call | tf_op jit(solution)/shard_map/rotate_far/pallas_call | solution.py:258
  9.7 0.5 collective-permute-done.1.cb_ref
  10.2 8.6 %quantize_far.1 = (bf16[192,896]{1,0:T(8,128)(2,1)S(1)}, bf16[192,896]{1,0:T(8,128)(2,1)S(1)}, f32[576,128]{1,0:T(8,128)S(1)}, bf16[992,128]{1,0:T(8,128)(2,1)S(1)}) custom-call(f32[12,16,256]{2,1,0:T(8,128)S(1)} %collective-permute-done.1.cb_ref, bf16[2,192,896]{2,1,0:T(8,128)(2,1)S(1)} %get-tuple-element.27.y0_ref, ...), custom_call_target="tpu_custom_call" | custom-call | flops 2113929216 | bytes 8388608 | tf_op jit(solution)/shard_map/quantize_far/pallas_call | solution.py:268
  18.9 1.8 %collective-permute-start.2 = (bf16[992,128]{1,0:T(8,128)(2,1)S(1)}, bf16[992,128]{1,0:T(8,128)(2,1)S(1)}, u32[]{:S(2)}, u32[]{:S(2)}) collective-permute-start(bf16[992,128]{1,0:T(8,128)(2,1)S(1)} %get-tuple-element.30), channel_id=1, source_target_pairs={{0,2},{2,0},{1,3},{3,1},{4,6},{6,4},{5,7},{7,5},{8,10},{10,8},{9,1... | collective-permute-start | bytes 761864 | tf_op jit(solution)/shard_map/ppermute | solution.py:289
  20.7 8.5 %quantize_near.1 = (bf16[192,896]{1,0:T(8,128)(2,1)S(1)}, bf16[192,896]{1,0:T(8,128)(2,1)S(1)}, f32[992,128]{1,0:T(8,128)S(1)}, bf16[576,128]{1,0:T(8,128)(2,1)S(1)}) custom-call(f32[24,16,256]{2,1,0:T(8,128)S(1)} %bitcast.4, bf16[2,192,896]{2,1,0:T(8,128)(2,1)S(1)} %get-tuple-element.27.y0_ref, bf16[2,192,896]{2,1,0:T(8,128)(2,1)S(1)} %rotate_far.1.y1_ref, ...), custom_call_target="tpu_custom_call" | custom-call | flops 2113929216 | bytes 8388608 | tf_op jit(solution)/shard_map/quantize_near/pallas_call | solution.py:268
  29.9 3.9 %collective-permute-start.5 = (bf16[248,128]{1,0:T(8,128)(2,1)S(1)}, bf16[248,128]{1,0:T(8,128)(2,1)S(1)}, u32[]{:S(2)}, u32[]{:S(2)}) collective-permute-start(bf16[248,128]{1,0:T(8,128)(2,1)S(1)} %get-tuple-element.35), channel_id=1, source_target_pairs={{0,12},{4,8},{8,4},{12,0},{1,13},{5,9},{9,5},{13,1},{2,14},{6,10},... | collective-permute-start | bytes 190472 | tf_op jit(solution)/shard_map/ppermute | solution.py:225
  33.7 1.7 %collective-permute-done.3.got_ref = bf16[576,128]{1,0:T(8,128)(2,1)S(1)} collective-permute-done((bf16[576,128]{1,0:T(8,128)(2,1)S(1)}, bf16[576,128]{1,0:T(8,128)(2,1)S(1)}, u32[]{:S(2)}, u32[]{:S(2)}) %collective-permute-start.3) | collective-permute-done | bytes 147488 | tf_op jit(solution)/shard_map/ppermute | solution.py:292
  35.5 1.6 %collective-permute-start.7 = (bf16[248,128]{1,0:T(8,128)(2,1)S(1)}, bf16[248,128]{1,0:T(8,128)(2,1)S(1)}, u32[]{:S(2)}, u32[]{:S(2)}) collective-permute-start(bf16[248,128]{1,0:T(8,128)(2,1)S(1)} %get-tuple-element.37), channel_id=1, source_target_pairs={{0,4},{4,0},{8,12},{12,8},{1,5},{5,1},{9,13},{13,9},{2,6},{6,2},{1... | collective-permute-start | bytes 190472 | tf_op jit(solution)/shard_map/ppermute | solution.py:225
  37.1 2.5 %collective-permute-start.8 = (bf16[144,128]{1,0:T(8,128)(2,1)S(1)}, bf16[144,128]{1,0:T(8,128)(2,1)S(1)}, u32[]{:S(2)}, u32[]{:S(2)}) collective-permute-start(bf16[144,128]{1,0:T(8,128)(2,1)S(1)} %get-tuple-element.41), channel_id=1, source_target_pairs={{0,12},{4,8},{8,4},{12,0},{1,13},{5,9},{9,5},{13,1},{2,14},{6,10},... | collective-permute-start | bytes 110600 | tf_op jit(solution)/shard_map/ppermute | solution.py:225
  39.9 1.7 %collective-permute-start.10 = (bf16[144,128]{1,0:T(8,128)(2,1)S(1)}, bf16[144,128]{1,0:T(8,128)(2,1)S(1)}, u32[]{:S(2)}, u32[]{:S(2)}) collective-permute-start(bf16[144,128]{1,0:T(8,128)(2,1)S(1)} %get-tuple-element.43), channel_id=1, source_target_pairs={{0,4},{4,0},{8,12},{12,8},{1,5},{5,1},{9,13},{13,9},{2,6},{6,2},{1... | collective-permute-start | bytes 110600 | tf_op jit(solution)/shard_map/ppermute | solution.py:225
  41.6 1.6 %turn.1 = bf16[896,768]{1,0:T(8,128)(2,1)} custom-call(bf16[192,896]{1,0:T(8,128)(2,1)S(1)} %get-tuple-element.44.m0_ref, bf16[192,896]{1,0:T(8,128)(2,1)S(1)} %get-tuple-element.45.m1_ref, bf16[192,896]{1,0:T(8,128)(2,1)S(1)} %collective-permute-done.11.t0_ref, bf16[192,896]{1,0:T(8,128)(2,1)S(1)} %collective-permute-done.4.t1_ref), custom_call_target="tpu_custom_call" | custom-call | tf_op jit(solution)/shard_map/turn/pallas_call | solution.py:295
  43.3 1.6 %collective-permute-done.9 = bf16[144,128]{1,0:T(8,128)(2,1)S(1)} collective-permute-done((bf16[144,128]{1,0:T(8,128)(2,1)S(1)}, bf16[144,128]{1,0:T(8,128)(2,1)S(1)}, u32[]{:S(2)}, u32[]{:S(2)}) %collective-permute-start.9) | collective-permute-done | bytes 36896 | tf_op jit(solution)/shard_map/ppermute | solution.py:225
  45.0 0.7 %collective-permute-start.14 = (bf16[392,128]{1,0:T(8,128)(2,1)S(1)}, bf16[392,128]{1,0:T(8,128)(2,1)S(1)}, u32[]{:S(2)}, u32[]{:S(2)}) collective-permute-start(bf16[392,128]{1,0:T(8,128)(2,1)S(1)} %pad_maximum_fusion.refs_0_), channel_id=1, source_target_pairs={{0,4},{4,0},{8,12},{12,8},{1,5},{5,1},{9,13},{13,9},{2,6},{6,2},{1... | collective-permute-start | bytes 301064 | tf_op jit(solution)/shard_map/ppermute | solution.py:225
  45.6 1.9 %collective-permute-start.13 = (bf16[392,128]{1,0:T(8,128)(2,1)S(1)}, bf16[392,128]{1,0:T(8,128)(2,1)S(1)}, u32[]{:S(2)}, u32[]{:S(2)}) collective-permute-start(bf16[392,128]{1,0:T(8,128)(2,1)S(1)} %pad_maximum_fusion.refs_0_), channel_id=1, source_target_pairs={{0,8},{4,12},{8,0},{12,4},{1,9},{5,13},{9,1},{13,5},{2,10},{6,14},... | collective-permute-start | bytes 301064 | tf_op jit(solution)/shard_map/ppermute | solution.py:225
  47.5 1.9 %collective-permute-start.12 = (bf16[392,128]{1,0:T(8,128)(2,1)S(1)}, bf16[392,128]{1,0:T(8,128)(2,1)S(1)}, u32[]{:S(2)}, u32[]{:S(2)}) collective-permute-start(bf16[392,128]{1,0:T(8,128)(2,1)S(1)} %pad_maximum_fusion.refs_0_), channel_id=1, source_target_pairs={{0,12},{4,8},{8,4},{12,0},{1,13},{5,9},{9,5},{13,1},{2,14},{6,10},... | collective-permute-start | bytes 301064 | tf_op jit(solution)/shard_map/ppermute | solution.py:225
  49.9 4.7 %collective-permute-done.13.refs_2_ = bf16[392,128]{1,0:T(8,128)(2,1)S(1)} collective-permute-done((bf16[392,128]{1,0:T(8,128)(2,1)S(1)}, bf16[392,128]{1,0:T(8,128)(2,1)S(1)}, u32[]{:S(2)}, u32[]{:S(2)}) %collective-permute-start.13) | collective-permute-done | bytes 100384 | tf_op jit(solution)/shard_map/ppermute | solution.py:225
  55.1 0.8 %collective-permute-done.17.refs_6_ = bf16[392,128]{1,0:T(8,128)(2,1)S(1)} collective-permute-done((bf16[392,128]{1,0:T(8,128)(2,1)S(1)}, bf16[392,128]{1,0:T(8,128)(2,1)S(1)}, u32[]{:S(2)}, u32[]{:S(2)}) %collective-permute-start.17) | collective-permute-done | bytes 100384 | tf_op jit(solution)/shard_map/ppermute | solution.py:327
  56.1 1.6 %final.1 = (f32[384,768]{1,0:T(8,128)}, f32[24,16,256]{2,1,0:T(8,128)}) custom-call(bf16[392,128]{1,0:T(8,128)(2,1)S(1)} %pad_maximum_fusion.refs_0_, bf16[392,128]{1,0:T(8,128)(2,1)S(1)} %collective-permute-done.12.refs_1_, bf16[392,128]{1,0:T(8,128)(2,1)S(1)} %collective-permute-done.13.refs_2_, bf16[392,128]{1,0:T(8,128)(2,1)S(1)} %collective-permute-done.14.refs_3_, ...), custom_call_target="tpu_custom_call" | custom-call | tf_op jit(solution)/shard_map/final/pallas_call | solution.py:330
  (34 shorter events, 2.4 us)
Async XLA Ops:
  0.6 8.1 %collective-permute-start = (bf16[896,768]{1,0:T(8,128)(2,1)}, bf16[896,768]{1,0:T(8,128)(2,1)S(1)}, u32[]{:S(2)}, u32[]{:S(2)}) collective-permute-start(bf16[896,768]{1,0:T(8,128)(2,1)} %v0_ref.3), channel_id=1, source_target_pairs={{0,1},{1,0},{2,3},{3,2},{4,5},{5,4},{6,7},{7,6},{8,9},{9,8},{10,11... | collective-permute-start | bytes 4128776 | tf_op jit(solution)/shard_map/ppermute | solution.py:246
  2.1 8.1 %collective-permute-start.1 = (f32[12,16,256]{2,1,0:T(8,128)S(1)}, f32[12,16,256]{2,1,0:T(8,128)S(1)}, u32[]{:S(2)}, u32[]{:S(2)}) collective-permute-start(f32[12,16,256]{2,1,0:T(8,128)S(1)} %dynamic-slice_bitcast_fusion), channel_id=1, source_target_pairs={{0,2},{2,0},{1,3},{3,1},{4,6},{6,4},{5,7},{7,5},{8,10},{10,8},{9,1... | collective-permute-start | bytes 589832 | tf_op jit(solution)/shard_map/ppermute | solution.py:245
  4.7 1.3 %copy-start = (bf16[896,768]{1,0:T(8,128)(2,1)S(1)}, bf16[896,768]{1,0:T(8,128)(2,1)}, u32[]{:S(2)}) copy-start(bf16[896,768]{1,0:T(8,128)(2,1)} %v0_ref.3) | copy-start | bytes 4128772
  6.0 1.3 %copy-start.2 = (bf16[768,768]{1,0:T(8,128)(2,1)S(1)}, bf16[768,768]{1,0:T(8,128)(2,1)}, u32[]{:S(2)}) copy-start(bf16[768,768]{1,0:T(8,128)(2,1)} %rot_ref.1) | copy-start | bytes 3538948
  8.7 1.5 %copy-start.1 = (bf16[896,768]{1,0:T(8,128)(2,1)S(1)}, bf16[896,768]{1,0:T(8,128)(2,1)}, u32[]{:S(2)}) copy-start(bf16[896,768]{1,0:T(8,128)(2,1)} %v0_ref.3) | copy-start | bytes 4128772
  10.2 10.5 %copy-start.3 = (f32[24,256,16]{1,2,0:T(8,128)S(1)}, f32[24,256,16]{1,2,0:T(8,128)}, u32[]{:S(2)}) copy-start(f32[24,256,16]{1,2,0:T(8,128)} %param.5) | copy-start | bytes 1179652
  18.9 10.9 %collective-permute-start.2 = (bf16[992,128]{1,0:T(8,128)(2,1)S(1)}, bf16[992,128]{1,0:T(8,128)(2,1)S(1)}, u32[]{:S(2)}, u32[]{:S(2)}) collective-permute-start(bf16[992,128]{1,0:T(8,128)(2,1)S(1)} %get-tuple-element.30), channel_id=1, source_target_pairs={{0,2},{2,0},{1,3},{3,1},{4,6},{6,4},{5,7},{7,5},{8,10},{10,8},{9,1... | collective-permute-start | bytes 761864 | tf_op jit(solution)/shard_map/ppermute | solution.py:289
  20.7 16.4 %collective-permute-start.4 = (bf16[192,896]{1,0:T(8,128)(2,1)S(1)}, bf16[192,896]{1,0:T(8,128)(2,1)S(1)}, u32[]{:S(2)}, u32[]{:S(2)}) collective-permute-start(bf16[192,896]{1,0:T(8,128)(2,1)S(1)} %get-tuple-element.33), channel_id=1, source_target_pairs={{0,1},{1,0},{2,3},{3,2},{4,5},{5,4},{6,7},{7,6},{8,9},{9,8},{10,11... | collective-permute-start | bytes 1032200 | tf_op jit(solution)/shard_map/ppermute | solution.py:290
  29.1 6.3 %collective-permute-start.3 = (bf16[576,128]{1,0:T(8,128)(2,1)S(1)}, bf16[576,128]{1,0:T(8,128)(2,1)S(1)}, u32[]{:S(2)}, u32[]{:S(2)}) collective-permute-start(bf16[576,128]{1,0:T(8,128)(2,1)S(1)} %get-tuple-element.32), channel_id=1, source_target_pairs={{0,2},{2,0},{1,3},{3,1},{4,6},{6,4},{5,7},{7,5},{8,10},{10,8},{9,1... | collective-permute-start | bytes 442376 | tf_op jit(solution)/shard_map/ppermute | solution.py:292
  29.5 12.1 %collective-permute-start.11 = (bf16[192,896]{1,0:T(8,128)(2,1)S(1)}, bf16[192,896]{1,0:T(8,128)(2,1)S(1)}, u32[]{:S(2)}, u32[]{:S(2)}) collective-permute-start(bf16[192,896]{1,0:T(8,128)(2,1)S(1)} %get-tuple-element.46), channel_id=1, source_target_pairs={{0,1},{1,0},{2,3},{3,2},{4,5},{5,4},{6,7},{7,6},{8,9},{9,8},{10,11... | collective-permute-start | bytes 1032200 | tf_op jit(solution)/shard_map/ppermute | solution.py:293
  29.9 9.8 %collective-permute-start.5 = (bf16[248,128]{1,0:T(8,128)(2,1)S(1)}, bf16[248,128]{1,0:T(8,128)(2,1)S(1)}, u32[]{:S(2)}, u32[]{:S(2)}) collective-permute-start(bf16[248,128]{1,0:T(8,128)(2,1)S(1)} %get-tuple-element.35), channel_id=1, source_target_pairs={{0,12},{4,8},{8,4},{12,0},{1,13},{5,9},{9,5},{13,1},{2,14},{6,10},... | collective-permute-start | bytes 190472 | tf_op jit(solution)/shard_map/ppermute | solution.py:225
  33.7 6.1 %collective-permute-start.6 = (bf16[248,128]{1,0:T(8,128)(2,1)S(1)}, bf16[248,128]{1,0:T(8,128)(2,1)S(1)}, u32[]{:S(2)}, u32[]{:S(2)}) collective-permute-start(bf16[248,128]{1,0:T(8,128)(2,1)S(1)} %get-tuple-element.36), channel_id=1, source_target_pairs={{0,8},{4,12},{8,0},{12,4},{1,9},{5,13},{9,1},{13,5},{2,10},{6,14},... | collective-permute-start | bytes 190472 | tf_op jit(solution)/shard_map/ppermute | solution.py:225
  35.5 6.1 %collective-permute-start.7 = (bf16[248,128]{1,0:T(8,128)(2,1)S(1)}, bf16[248,128]{1,0:T(8,128)(2,1)S(1)}, u32[]{:S(2)}, u32[]{:S(2)}) collective-permute-start(bf16[248,128]{1,0:T(8,128)(2,1)S(1)} %get-tuple-element.37), channel_id=1, source_target_pairs={{0,4},{4,0},{8,12},{12,8},{1,5},{5,1},{9,13},{13,9},{2,6},{6,2},{1... | collective-permute-start | bytes 190472 | tf_op jit(solution)/shard_map/ppermute | solution.py:225
  37.1 6.2 %collective-permute-start.8 = (bf16[144,128]{1,0:T(8,128)(2,1)S(1)}, bf16[144,128]{1,0:T(8,128)(2,1)S(1)}, u32[]{:S(2)}, u32[]{:S(2)}) collective-permute-start(bf16[144,128]{1,0:T(8,128)(2,1)S(1)} %get-tuple-element.41), channel_id=1, source_target_pairs={{0,12},{4,8},{8,4},{12,0},{1,13},{5,9},{9,5},{13,1},{2,14},{6,10},... | collective-permute-start | bytes 110600 | tf_op jit(solution)/shard_map/ppermute | solution.py:225
  39.6 5.3 %collective-permute-start.9 = (bf16[144,128]{1,0:T(8,128)(2,1)S(1)}, bf16[144,128]{1,0:T(8,128)(2,1)S(1)}, u32[]{:S(2)}, u32[]{:S(2)}) collective-permute-start(bf16[144,128]{1,0:T(8,128)(2,1)S(1)} %get-tuple-element.42), channel_id=1, source_target_pairs={{0,8},{4,12},{8,0},{12,4},{1,9},{5,13},{9,1},{13,5},{2,10},{6,14},... | collective-permute-start | bytes 110600 | tf_op jit(solution)/shard_map/ppermute | solution.py:225
  39.9 5.1 %collective-permute-start.10 = (bf16[144,128]{1,0:T(8,128)(2,1)S(1)}, bf16[144,128]{1,0:T(8,128)(2,1)S(1)}, u32[]{:S(2)}, u32[]{:S(2)}) collective-permute-start(bf16[144,128]{1,0:T(8,128)(2,1)S(1)} %get-tuple-element.43), channel_id=1, source_target_pairs={{0,4},{4,0},{8,12},{12,8},{1,5},{5,1},{9,13},{13,9},{2,6},{6,2},{1... | collective-permute-start | bytes 110600 | tf_op jit(solution)/shard_map/ppermute | solution.py:225
  45.0 4.7 %collective-permute-start.14 = (bf16[392,128]{1,0:T(8,128)(2,1)S(1)}, bf16[392,128]{1,0:T(8,128)(2,1)S(1)}, u32[]{:S(2)}, u32[]{:S(2)}) collective-permute-start(bf16[392,128]{1,0:T(8,128)(2,1)S(1)} %pad_maximum_fusion.refs_0_), channel_id=1, source_target_pairs={{0,4},{4,0},{8,12},{12,8},{1,5},{5,1},{9,13},{13,9},{2,6},{6,2},{1... | collective-permute-start | bytes 301064 | tf_op jit(solution)/shard_map/ppermute | solution.py:225
  45.6 9.0 %collective-permute-start.13 = (bf16[392,128]{1,0:T(8,128)(2,1)S(1)}, bf16[392,128]{1,0:T(8,128)(2,1)S(1)}, u32[]{:S(2)}, u32[]{:S(2)}) collective-permute-start(bf16[392,128]{1,0:T(8,128)(2,1)S(1)} %pad_maximum_fusion.refs_0_), channel_id=1, source_target_pairs={{0,8},{4,12},{8,0},{12,4},{1,9},{5,13},{9,1},{13,5},{2,10},{6,14},... | collective-permute-start | bytes 301064 | tf_op jit(solution)/shard_map/ppermute | solution.py:225
  47.5 7.1 %collective-permute-start.12 = (bf16[392,128]{1,0:T(8,128)(2,1)S(1)}, bf16[392,128]{1,0:T(8,128)(2,1)S(1)}, u32[]{:S(2)}, u32[]{:S(2)}) collective-permute-start(bf16[392,128]{1,0:T(8,128)(2,1)S(1)} %pad_maximum_fusion.refs_0_), channel_id=1, source_target_pairs={{0,12},{4,8},{8,4},{12,0},{1,13},{5,9},{9,5},{13,1},{2,14},{6,10},... | collective-permute-start | bytes 301064 | tf_op jit(solution)/shard_map/ppermute | solution.py:225
  49.4 5.7 %collective-permute-start.15 = (bf16[392,128]{1,0:T(8,128)(2,1)S(1)}, bf16[392,128]{1,0:T(8,128)(2,1)S(1)}, u32[]{:S(2)}, u32[]{:S(2)}) collective-permute-start(bf16[392,128]{1,0:T(8,128)(2,1)S(1)} %pad_maximum_fusion.refs_0_), channel_id=1, source_target_pairs={{0,1},{1,0},{2,3},{3,2},{4,5},{5,4},{6,7},{7,6},{8,9},{9,8},{10,11... | collective-permute-start | bytes 301064 | tf_op jit(solution)/shard_map/ppermute | solution.py:327
  49.7 5.5 %collective-permute-start.18 = (bf16[392,128]{1,0:T(8,128)(2,1)S(1)}, bf16[392,128]{1,0:T(8,128)(2,1)S(1)}, u32[]{:S(2)}, u32[]{:S(2)}) collective-permute-start(bf16[392,128]{1,0:T(8,128)(2,1)S(1)} %collective-permute-done.14.refs_3_), channel_id=1, source_target_pairs={{0,1},{1,0},{2,3},{3,2},{4,5},{5,4},{6,7},{7,6},{8,9},{9,8},{10,11... | collective-permute-start | bytes 301064 | tf_op jit(solution)/shard_map/ppermute | solution.py:327
  54.6 1.3 %collective-permute-start.17 = (bf16[392,128]{1,0:T(8,128)(2,1)S(1)}, bf16[392,128]{1,0:T(8,128)(2,1)S(1)}, u32[]{:S(2)}, u32[]{:S(2)}) collective-permute-start(bf16[392,128]{1,0:T(8,128)(2,1)S(1)} %collective-permute-done.13.refs_2_), channel_id=1, source_target_pairs={{0,1},{1,0},{2,3},{3,2},{4,5},{5,4},{6,7},{7,6},{8,9},{9,8},{10,11... | collective-permute-start | bytes 301064 | tf_op jit(solution)/shard_map/ppermute | solution.py:327
  54.6 1.5 %collective-permute-start.16 = (bf16[392,128]{1,0:T(8,128)(2,1)S(1)}, bf16[392,128]{1,0:T(8,128)(2,1)S(1)}, u32[]{:S(2)}, u32[]{:S(2)}) collective-permute-start(bf16[392,128]{1,0:T(8,128)(2,1)S(1)} %collective-permute-done.12.refs_1_), channel_id=1, source_target_pairs={{0,1},{1,0},{2,3},{3,2},{4,5},{5,4},{6,7},{7,6},{8,9},{9,8},{10,11... | collective-permute-start | bytes 301064 | tf_op jit(solution)/shard_map/ppermute | solution.py:327

commit v6 on v4

--- a/solution.py
+++ b/solution.py
@@ -13,6 +13,7 @@
 LOG2E = math.log2(math.e)
 F32, BF16 = jnp.float32, jnp.bfloat16
 VMEM_BYTES = 24 * 2**20
+HEAD = 3
 
 
 def quantize_rows(block, codebook):
@@ -88,19 +89,42 @@
     return a, b
 
 
-def quantize_kernel(cb_ref, y0_ref, y1_ref, v0_ref, v1_ref, rec0_ref, rec1_ref, keep_ref, send_ref, cnt, *, k, per):
+def quantize_kernel(*refs, k, per, first, last):
+    cb_ref, y0_ref, y1_ref = refs[:3]
+    refs = refs[3:]
     s, r = lax.axis_index("sub"), lax.axis_index("rep")
     codes = cb_ref.shape[2]
     cols = y0_ref.shape[2]
     w = per * SUBDIM
     lanes = 128
-    part = v0_ref.shape[1] // 2
+    halves = codes // lanes
+    whole = last == per
     base = r * per if k == 0 else 0
-    p_rows = (part // lanes) * w
-    sums_ref = keep_ref if k == 0 else send_ref
+    if whole:
+        v0_ref, v1_ref, *refs = refs
+        part = v0_ref.shape[1] // 2
+        p_rows = (part // lanes) * w
+        if first:
+            *head, rec0_ref, rec1_ref, keep_ref, send_ref, cnt = refs
+        else:
+            rec0_ref, rec1_ref, keep_ref, send_ref, cnt = refs
+        sums_ref = keep_ref if k == 0 else send_ref
+    else:
+        rec0_ref, rec1_ref, sums_ref, cnt = refs
+        p_rows = 0
+    stride = w if whole else last * SUBDIM
     ones = jnp.ones((SUBDIM, cols), BF16)
     ys, recs = (y0_ref, y1_ref), (rec0_ref, rec1_ref)
-    cnt[...] = jnp.zeros_like(cnt)
+    if first:
+        done = first * SUBDIM
+        rec0_ref[:done, :] = head[0][...]
+        rec1_ref[:done, :] = head[1][...]
+        for half in range(halves):
+            at = p_rows + half * stride
+            sums_ref[at : at + done, :] = head[2][half * done : (half + 1) * done, :].astype(sums_ref.dtype)
+        cnt[...] = head[3][...]
+    else:
+        cnt[...] = jnp.zeros_like(cnt)
     ab, acc = {}, {}
 
     def score(j, i):
@@ -124,22 +148,24 @@
             acc[j] = sums
             return
         sums = acc.pop(j) + sums
-        for half in range(codes // lanes):
-            at = p_rows + half * w + j * SUBDIM
+        for half in range(halves):
+            at = p_rows + half * stride + j * SUBDIM
             sums_ref[at : at + SUBDIM, :] = sums[:SUBDIM, half * lanes : (half + 1) * lanes].astype(sums_ref.dtype)
             at = half * SUBDIM + j
             cnt[at : at + 1, :] = sums[SUBDIM : SUBDIM + 1, half * lanes : (half + 1) * lanes]
 
-    first = second = third = None
-    for item in [(j, i) for j in range(per) for i in range(2)] + [None] * 3:
-        new_first = (item, *score(*item)) if item is not None else None
-        new_second = (first[0], first[1], spread(first[2])) if first is not None else None
-        new_third = (second[0], rebuild(*second[0], second[1], second[2]), second[2]) if second is not None else None
-        if third is not None:
-            gather(*third[0], third[1], third[2])
-        first, second, third = new_first, new_second, new_third
-
-    at = p_rows + (codes // lanes) * w
+    one = two = three = None
+    for item in [(j, i) for j in range(first, last) for i in range(2)] + [None] * 3:
+        new_one = (item, *score(*item)) if item is not None else None
+        new_two = (one[0], one[1], spread(one[2])) if one is not None else None
+        new_three = (two[0], rebuild(*two[0], two[1], two[2]), two[2]) if two is not None else None
+        if three is not None:
+            gather(*three[0], three[1], three[2])
+        one, two, three = new_one, new_two, new_three
+    if not whole:
+        return
+
+    at = p_rows + halves * w
     sums_ref[at : at + cnt.shape[0], :] = cnt[...].astype(sums_ref.dtype)
     cross = jnp.dot(rec0_ref[...], v0_ref[...], preferred_element_type=F32) + jnp.dot(
         rec1_ref[...], v1_ref[...], preferred_element_type=F32
@@ -165,7 +191,7 @@
 
 
 def final_kernel(*refs, n, per, total):
-    pieces, (cb_ref, cross_hbm, new_hbm, buf, cross, new, sems) = refs[: 2 * n], refs[2 * n :]
+    held, (cb_ref, cross_hbm, new_hbm, buf, cross, new, sems) = refs[:4], refs[4:]
     s, r, z = lax.axis_index("sub"), lax.axis_index("rep"), lax.axis_index("row")
     lanes = 128
     w = per * SUBDIM
@@ -174,11 +200,11 @@
     near_rows = groups * w + halves * (w + SUBDIM)
     near, far = near_rows // n, groups * w // n
     for side in range(2):
+        near_ref, far_ref = held[2 * side : 2 * side + 2]
         for i in range(n):
-            ref = pieces[side * n + i]
             source = z ^ ((n - i) % n)
-            buf[side, pl.ds(pl.multiple_of(source * near, 8), near), :] = ref[:near].astype(F32)
-            buf[side, pl.ds(pl.multiple_of(near_rows + source * far, 8), far), :] = ref[near:].astype(F32)
+            buf[side, pl.ds(pl.multiple_of(source * near, 8), near), :] = near_ref[i].astype(F32)
+            buf[side, pl.ds(pl.multiple_of(near_rows + source * far, 8), far), :] = far_ref[i].astype(F32)
 
     copies = []
     for g in range(groups):
@@ -234,13 +260,12 @@
     lanes = 128
     total = rows * rows_n * subs * 2
     swap = [(0, 1), (1, 0)]
-    r = lax.axis_index("rep")
     params = pltpu.CompilerParams(vmem_limit_bytes=VMEM_BYTES)
     small = pltpu.CompilerParams(vmem_limit_bytes=VMEM_BYTES // 2)
     vmem = pl.BlockSpec(memory_space=pltpu.VMEM)
 
     cb = codebooks.transpose(0, 2, 1)
-    cb_sent = lax.dynamic_slice_in_dim(cb, r * per, per, 0)
+    cb_sent = lax.dynamic_slice_in_dim(cb, lax.axis_index("rep") * per, per, 0)
     cb_far = lax.ppermute(cb_sent, "sub", swap)
     vec_far = lax.ppermute(vectors, "rep", swap)
 
@@ -262,11 +287,20 @@
     s_rows = (codes // lanes) * (w + SUBDIM)
     rec_shape = jax.ShapeDtypeStruct((w, rows), BF16)
 
-    def quantize(k, cb_k):
+    cnt_shape = ((codes // lanes) * SUBDIM, lanes)
+
+    def cost(count, cross):
+        return pl.CostEstimate(
+            flops=count * codes * rows * 2 * 2 * (9 * SUBDIM) + cross * 2 * w * 2 * rows * width,
+            transcendentals=count * codes * rows * 2,
+            bytes_accessed=2**23,
+        )
+
+    def quantize(k, cb_k, first=0, head=()):
         n_keep, n_send = (p_rows + s_rows, p_rows) if k == 0 else (p_rows, p_rows + s_rows)
         return pl.pallas_call(
-            functools.partial(quantize_kernel, k=k, per=per),
-            in_specs=[vmem] * 5,
+            functools.partial(quantize_kernel, k=k, per=per, first=first, last=per),
+            in_specs=[vmem] * (5 + len(head)),
             out_specs=[vmem] * 4,
             out_shape=[
                 rec_shape,
@@ -274,28 +308,36 @@
                 jax.ShapeDtypeStruct((n_keep, lanes), F32),
                 jax.ShapeDtypeStruct((n_send, lanes), BF16),
             ],
-            scratch_shapes=[pltpu.VMEM(((codes // lanes) * SUBDIM, lanes), F32)],
+            scratch_shapes=[pltpu.VMEM(cnt_shape, F32)],
             compiler_params=params,
+            cost_estimate=cost(per - first, 1),
             name="quantize_near" if k == 0 else "quantize_far",
-        )(cb_k, y0, y1, vectors, vec_far)
-
+        )(cb_k, y0, y1, vectors, vec_far, *head)
+
+    head = ()
+    if HEAD:
+        early = jax.ShapeDtypeStruct((HEAD * SUBDIM, rows), BF16)
+        head = pl.pallas_call(
+            functools.partial(quantize_kernel, k=0, per=per, first=0, last=HEAD),
+            in_specs=[vmem] * 3,
+            out_specs=[vmem] * 4,
+            out_shape=[
+                early,
+                early,
+                jax.ShapeDtypeStruct(((codes // lanes) * HEAD * SUBDIM, lanes), F32),
+                jax.ShapeDtypeStruct(cnt_shape, F32),
+            ],
+            compiler_params=params,
+            cost_estimate=cost(HEAD, 0),
+            name="quantize_head",
+        )(cb, y0, y1)
+        cb_far, *head = lax.optimization_barrier((cb_far, *head))
     mine1, other1, keep1, send1 = quantize(1, cb_far)
     got1 = lax.ppermute(send1, "sub", swap)
     theirs1 = lax.ppermute(other1, "rep", swap)
-    mine0, other0, keep0, send0 = quantize(0, cb)
+    mine0, other0, keep0, send0 = quantize(0, cb, HEAD, head)
     got0 = lax.ppermute(send0, "sub", swap)
     theirs0 = lax.ppermute(other0, "rep", swap)
-    theirs0, theirs1, got0 = lax.optimization_barrier((theirs0, theirs1, got0))
-
-    reconstruction = pl.pallas_call(
-        turn_kernel,
-        out_shape=jax.ShapeDtypeStruct((rows, width), BF16),
-        in_specs=[vmem] * 4,
-        out_specs=vmem,
-        scratch_shapes=[pltpu.VMEM((width, rows), BF16)],
-        compiler_params=small,
-        name="turn",
-    )(mine0, mine1, theirs0, theirs1)
 
     def scatter(kept, got):
         size = (kept.shape[0] // rows_n, lanes)
@@ -314,26 +356,47 @@
         return functools.reduce(lambda a, b: a + b.astype(F32), parts[1:], parts[0]).astype(BF16)
 
     apart = range(rows_n - 1, 0, -1)
-    summed = jnp.concatenate([add_up(scatter(keep0, got1)), add_up(scatter(keep1, got0))], axis=0)
-    summed, reconstruction = lax.optimization_barrier((summed, reconstruction))
-    mine = [summed] + [exchange(summed, rows_n, d) for d in apart]
-    theirs = [lax.ppermute(x, "rep", swap) for x in mine]
+    near = scatter(keep0, got1)
+    near[0], got0, theirs1 = lax.optimization_barrier((near[0], got0, theirs1))
+    far = scatter(keep1, got0)
+
+    def spread_out(x):
+        return [x] + [exchange(x, rows_n, d) for d in apart]
+
+    near_held = jnp.stack(spread_out(add_up(near)))
+    near_theirs = lax.ppermute(near_held, "rep", swap)
+    near_held, theirs0 = lax.optimization_barrier((near_held, theirs0))
+
+    reconstruction = pl.pallas_call(
+        turn_kernel,
+        out_shape=jax.ShapeDtypeStruct((rows, width), BF16),
+        in_specs=[vmem] * 4,
+        out_specs=vmem,
+        scratch_shapes=[pltpu.VMEM((width, rows), BF16)],
+        compiler_params=small,
+        name="turn",
+    )(mine0, mine1, theirs0, theirs1)
+
+    far_held = spread_out(add_up(far))
+    *far_held, reconstruction = lax.optimization_barrier((*far_held, reconstruction))
+    far_held = jnp.stack(far_held)
+    far_theirs = lax.ppermute(far_held, "rep", swap)
 
     any_spec = pl.BlockSpec(memory_space=pl.ANY)
     cross, new = pl.pallas_call(
         functools.partial(final_kernel, n=rows_n, per=per, total=total),
         out_shape=(jax.ShapeDtypeStruct((part, width), F32), jax.ShapeDtypeStruct(cb.shape, F32)),
-        in_specs=[vmem] * (2 * rows_n + 1),
+        in_specs=[vmem] * 5,
         out_specs=(any_spec, any_spec),
         scratch_shapes=[
-            pltpu.VMEM((2, rows_n * summed.shape[0], lanes), F32),
+            pltpu.VMEM((2, 2 * p_rows + s_rows, lanes), F32),
             pltpu.VMEM((part, width), F32),
             pltpu.VMEM(cb.shape, F32),
             pltpu.SemaphoreType.DMA((part // lanes + 1,)),
         ],
         compiler_params=small,
         name="final",
-    )(*mine, *theirs, cb)
+    )(near_held, far_held, near_theirs, far_theirs, cb)
     return reconstruction, new.transpose(0, 2, 1), cross
 
 

time: 62.6 us -> 57.3 us (0.915)
  waiting for transfers between devices: 15.3 us -> 6.23 us
  starting transfers between devices: 19.7 us -> 23.1 us
    ppermute x1, waiting for transfers between devices: 6.96 us -> 0.01 us  [on_device(): got1 = lax.ppermute(send1, 'sub', swap)]
    ppermute x9 -> x12, starting transfers between devices: 13.4 us -> 17.6 us  [exchange(): return lax.ppermute(x, 'row', [(i, i ^ d) for i in range(n)])]
    ppermute x9 -> x12, waiting for transfers between devices: 6.58 us -> 4.85 us  [exchange(): return lax.ppermute(x, 'row', [(i, i ^ d) for i in range(n)])]
    ppermute x1, starting transfers between devices: 0.28 us -> 1.76 us  [on_device(): got0 = lax.ppermute(send0, 'sub', swap)]
    ppermute x1, starting transfers between devices: 1.74 us -> 0.32 us  [on_device(): got1 = lax.ppermute(send1, 'sub', swap)]
    pallas_call x2 -> x3, Pallas kernels: 17.1 us -> 17.3 us  [the longest x2 15.1 us: quantize(): pl.pallas_call(functools.partial(quantize_kernel, k=k, per=per, first=fir...]
    ppermute x4 -> x2, waiting for transfers between devices: 1.29 us -> 1.36 us  [the longest x1 1.36 us: on_device(): far_theirs = lax.ppermute(far_held, 'rep', swap)]
  transfers between devices with their start and end apart: 19 -> 20, of which waited for: 7 -> 5; matrix products, arithmetic and copies ran while one was open for 2% -> 2% of each run, Pallas kernels for 20% -> 22%
where the time goes in v6:
time: 57.3 us; the launch traced here: 57.1 us
  starting transfers between devices  23.1 us (40%)
  Pallas kernels  23 us (40%)
  waiting for transfers between devices  6.23 us (11%)
  local copies, waits for them, and re-layouts  3.59 us (6%)
  between operations  0.94 us (2%)
    ppermute x12, starting transfers between devices, exchange(): return lax.ppermute(x, 'row', [(i, i ^ d) for i in range(n)])  17.6 us
    pallas_call x2, Pallas kernels, quantize(): pl.pallas_call(functools.partial(quantize_kernel, k=k, per=per, first=fir...  15.1 us
    ppermute x12, waiting for transfers between devices, exchange(): return lax.ppermute(x, 'row', [(i, i ^ d) for i in range(n)])  4.85 us
    unnamed x8, local copies, waits for them, and re-layouts  2.65 us
    ppermute x1, starting transfers between devices, on_device(): cb_far = lax.ppermute(cb_sent, 'sub', swap)  2.58 us
    pallas_call x1, Pallas kernels, on_device(): pl.pallas_call(functools.partial(quantize_kernel, k=0, per=per, first=0,...  2.2 us
    ppermute x1, starting transfers between devices, on_device(): got0 = lax.ppermute(send0, 'sub', swap)  1.76 us
    pallas_call x1, Pallas kernels, on_device(): pl.pallas_call(turn_kernel, out_shape=jax.ShapeDtypeStruct((rows, width),...  1.61 us
  transfers between devices with their start and end apart: 20, of which 5 were waited for; matrix products, arithmetic and copies ran while one was open for 2% of the time, Pallas kernels for 22%

profile of v6, /device:TPU:0, one launch (start us, length us, event | category | flops | bytes accessed | tf_op | source)
XLA Modules:
  0.0 57.1 jit_solution(3291827447350025121)
XLA Ops:
  1.1 0.9 %dynamic-slice_bitcast_fusion = f32[12,16,256]{2,1,0:T(8,128)S(1)} fusion(f32[24,256,16]{1,2,0:T(8,128)} %param.5, s32[]{:T(128)S(6)} %select_n.3), kind=kLoop, calls=%fused_computation.1 | loop fusion | bytes 393220 | tf_op jit(solution)/shard_map/dynamic_slice | solution.py:268
  2.1 2.6 %collective-permute-start = (f32[12,16,256]{2,1,0:T(8,128)S(1)}, f32[12,16,256]{2,1,0:T(8,128)S(1)}, u32[]{:S(2)}, u32[]{:S(2)}) collective-permute-start(f32[12,16,256]{2,1,0:T(8,128)S(1)} %dynamic-slice_bitcast_fusion), channel_id=1, source_target_pairs={{0,2},{2,0},{1,3},{3,1},{4,6},{6,4},{5,7},{7,5},{8,10},{10,8},{9,1... | collective-permute-start | bytes 589832 | tf_op jit(solution)/shard_map/ppermute | solution.py:269
  4.7 1.3 %copy-done = bf16[896,768]{1,0:T(8,128)(2,1)S(1)} copy-done((bf16[896,768]{1,0:T(8,128)(2,1)S(1)}, bf16[896,768]{1,0:T(8,128)(2,1)}, u32[]{:S(2)}) %copy-start) | copy-done | bytes 1376280
  6.0 1.3 %copy-done.2 = bf16[768,768]{1,0:T(8,128)(2,1)S(1)} copy-done((bf16[768,768]{1,0:T(8,128)(2,1)S(1)}, bf16[768,768]{1,0:T(8,128)(2,1)}, u32[]{:S(2)}) %copy-start.2) | copy-done | bytes 1179672
  7.3 1.4 %rotate.1 = (bf16[2,192,896]{2,1,0:T(8,128)(2,1)S(1)}, bf16[2,192,768]{2,1,0:T(8,128)(2,1)S(1)}) custom-call(bf16[896,768]{1,0:T(8,128)(2,1)S(1)} %copy-done, bf16[768,768]{1,0:T(8,128)(2,1)S(1)} %copy-done.2), custom_call_target="tpu_custom_call" | custom-call | tf_op jit(solution)/shard_map/rotate/pallas_call | solution.py:273
  8.7 1.0 %rotate_far.1.refs_2_ = bf16[2,192,896]{2,1,0:T(8,128)(2,1)S(1)} custom-call(bf16[896,768]{1,0:T(8,128)(2,1)S(1)} %collective-permute-done.1.vec_ref.refs_4_, bf16[2,192,768]{2,1,0:T(8,128)(2,1)S(1)} %get-tuple-element.43.rott_ref), custom_call_target="tpu_custom_call" | custom-call | tf_op jit(solution)/shard_map/rotate_far/pallas_call | solution.py:282
  9.7 2.2 %quantize_head.1 = (bf16[48,896]{1,0:T(8,128)(2,1)S(1)}, bf16[48,896]{1,0:T(8,128)(2,1)S(1)}, f32[96,128]{1,0:T(8,128)S(1)}, f32[32,128]{1,0:T(8,128)S(1)}) custom-call(f32[24,16,256]{2,1,0:T(8,128)S(1)} %bitcast.12, bf16[2,192,896]{2,1,0:T(8,128)(2,1)S(1)} %get-tuple-element.42.refs_1_, bf16[2,192,896]{2,1,0:T(8,128)(2,1)S(1)} %rotate_far.1.refs_2_), custom_call_target="tpu_custom_call" | custom-call | flops 396361728 | bytes 8388608 | tf_op jit(solution)/shard_map/quantize_head/pallas_call | solution.py:320
  12.0 8.7 %quantize_far.1 = (bf16[192,896]{1,0:T(8,128)(2,1)S(1)}, bf16[192,896]{1,0:T(8,128)(2,1)S(1)}, f32[576,128]{1,0:T(8,128)S(1)}, bf16[992,128]{1,0:T(8,128)(2,1)S(1)}) custom-call(f32[12,16,256]{2,1,0:T(8,128)S(1)} %collective-permute-done.refs_0_, bf16[2,192,896]{2,1,0:T(8,128)(2,1)S(1)} %get-tuple-element.42.refs_1_, ...), custom_call_target="tpu_custom_call" | custom-call | flops 2113929216 | bytes 8388608 | tf_op jit(solution)/shard_map/quantize_far/pallas_call | solution.py:301
  21.2 6.5 %quantize_near.1 = (bf16[192,896]{1,0:T(8,128)(2,1)S(1)}, bf16[192,896]{1,0:T(8,128)(2,1)S(1)}, f32[992,128]{1,0:T(8,128)S(1)}, bf16[576,128]{1,0:T(8,128)(2,1)S(1)}) custom-call(f32[24,16,256]{2,1,0:T(8,128)S(1)} %bitcast.13, bf16[2,192,896]{2,1,0:T(8,128)(2,1)S(1)} %get-tuple-element.42.refs_1_, bf16[2,192,896]{2,1,0:T(8,128)(2,1)S(1)} %rotate_far.1.refs_2_, ...), custom_call_target="tpu_custom_call" | custom-call | flops 1717567488 | bytes 8388608 | tf_op jit(solution)/shard_map/quantize_near/pallas_call | solution.py:301
  27.7 1.8 %collective-permute-start.3 = (bf16[576,128]{1,0:T(8,128)(2,1)S(1)}, bf16[576,128]{1,0:T(8,128)(2,1)S(1)}, u32[]{:S(2)}, u32[]{:S(2)}) collective-permute-start(bf16[576,128]{1,0:T(8,128)(2,1)S(1)} %get-tuple-element.57), channel_id=1, source_target_pairs={{0,2},{2,0},{1,3},{3,1},{4,6},{6,4},{5,7},{7,5},{8,10},{10,8},{9,1... | collective-permute-start | bytes 442376 | tf_op jit(solution)/shard_map/ppermute | solution.py:339
  29.6 3.7 %collective-permute-start.11 = (bf16[248,128]{1,0:T(8,128)(2,1)S(1)}, bf16[248,128]{1,0:T(8,128)(2,1)S(1)}, u32[]{:S(2)}, u32[]{:S(2)}) collective-permute-start(bf16[248,128]{1,0:T(8,128)(2,1)S(1)} %get-tuple-element.67), channel_id=1, source_target_pairs={{0,12},{4,8},{8,4},{12,0},{1,13},{5,9},{9,5},{13,1},{2,14},{6,10},... | collective-permute-start | bytes 190472 | tf_op jit(solution)/shard_map/ppermute | solution.py:250
  33.2 0.8 %collective-permute-start.13 = (bf16[248,128]{1,0:T(8,128)(2,1)S(1)}, bf16[248,128]{1,0:T(8,128)(2,1)S(1)}, u32[]{:S(2)}, u32[]{:S(2)}) collective-permute-start(bf16[248,128]{1,0:T(8,128)(2,1)S(1)} %get-tuple-element.69), channel_id=1, source_target_pairs={{0,4},{4,0},{8,12},{12,8},{1,5},{5,1},{9,13},{13,9},{2,6},{6,2},{1... | collective-permute-start | bytes 190472 | tf_op jit(solution)/shard_map/ppermute | solution.py:250
  34.1 3.7 %collective-permute-start.5 = (bf16[144,128]{1,0:T(8,128)(2,1)S(1)}, bf16[144,128]{1,0:T(8,128)(2,1)S(1)}, u32[]{:S(2)}, u32[]{:S(2)}) collective-permute-start(bf16[144,128]{1,0:T(8,128)(2,1)S(1)} %get-tuple-element.61), channel_id=1, source_target_pairs={{0,12},{4,8},{8,4},{12,0},{1,13},{5,9},{9,5},{13,1},{2,14},{6,10},... | collective-permute-start | bytes 110600 | tf_op jit(solution)/shard_map/ppermute | solution.py:250
  37.7 1.3 %collective-permute-start.6 = (bf16[144,128]{1,0:T(8,128)(2,1)S(1)}, bf16[144,128]{1,0:T(8,128)(2,1)S(1)}, u32[]{:S(2)}, u32[]{:S(2)}) collective-permute-start(bf16[144,128]{1,0:T(8,128)(2,1)S(1)} %get-tuple-element.62), channel_id=1, source_target_pairs={{0,8},{4,12},{8,0},{12,4},{1,9},{5,13},{9,1},{13,5},{2,10},{6,14},... | collective-permute-start | bytes 110600 | tf_op jit(solution)/shard_map/ppermute | solution.py:250
  39.0 1.5 %collective-permute-start.7 = (bf16[144,128]{1,0:T(8,128)(2,1)S(1)}, bf16[144,128]{1,0:T(8,128)(2,1)S(1)}, u32[]{:S(2)}, u32[]{:S(2)}) collective-permute-start(bf16[144,128]{1,0:T(8,128)(2,1)S(1)} %get-tuple-element.63), channel_id=1, source_target_pairs={{0,4},{4,0},{8,12},{12,8},{1,5},{5,1},{9,13},{13,9},{2,6},{6,2},{1... | collective-permute-start | bytes 110600 | tf_op jit(solution)/shard_map/ppermute | solution.py:250
  40.6 1.7 %collective-permute-start.14 = (bf16[248,128]{1,0:T(8,128)(2,1)S(1)}, bf16[248,128]{1,0:T(8,128)(2,1)S(1)}, u32[]{:S(2)}, u32[]{:S(2)}) collective-permute-start(bf16[248,128]{1,0:T(8,128)(2,1)S(1)} %add_convert_fusion), channel_id=1, source_target_pairs={{0,12},{4,8},{8,4},{12,0},{1,13},{5,9},{9,5},{13,1},{2,14},{6,10},... | collective-permute-start | bytes 190472 | tf_op jit(solution)/shard_map/ppermute | solution.py:250
  43.0 2.1 %collective-permute-start.16 = (bf16[248,128]{1,0:T(8,128)(2,1)S(1)}, bf16[248,128]{1,0:T(8,128)(2,1)S(1)}, u32[]{:S(2)}, u32[]{:S(2)}) collective-permute-start(bf16[248,128]{1,0:T(8,128)(2,1)S(1)} %add_convert_fusion), channel_id=1, source_target_pairs={{0,4},{4,0},{8,12},{12,8},{1,5},{5,1},{9,13},{13,9},{2,6},{6,2},{1... | collective-permute-start | bytes 190472 | tf_op jit(solution)/shard_map/ppermute | solution.py:250
  45.1 1.9 %collective-permute-done.14 = bf16[248,128]{1,0:T(8,128)(2,1)S(1)} collective-permute-done((bf16[248,128]{1,0:T(8,128)(2,1)S(1)}, bf16[248,128]{1,0:T(8,128)(2,1)S(1)}, u32[]{:S(2)}, u32[]{:S(2)}) %collective-permute-start.14) | collective-permute-done | bytes 63520 | tf_op jit(solution)/shard_map/ppermute | solution.py:250
  47.1 1.9 %collective-permute-start.8 = (bf16[144,128]{1,0:T(8,128)(2,1)S(1)}, bf16[144,128]{1,0:T(8,128)(2,1)S(1)}, u32[]{:S(2)}, u32[]{:S(2)}) collective-permute-start(bf16[144,128]{1,0:T(8,128)(2,1)S(1)} %add_convert_fusion.1), channel_id=1, source_target_pairs={{0,12},{4,8},{8,4},{12,0},{1,13},{5,9},{9,5},{13,1},{2,14},{6,10},... | collective-permute-start | bytes 110600 | tf_op jit(solution)/shard_map/ppermute | solution.py:250
  49.7 1.6 %turn.1 = bf16[896,768]{1,0:T(8,128)(2,1)} custom-call(bf16[192,896]{1,0:T(8,128)(2,1)S(1)} %get-tuple-element.64.m0_ref, bf16[192,896]{1,0:T(8,128)(2,1)S(1)} %get-tuple-element.65.m1_ref, bf16[192,896]{1,0:T(8,128)(2,1)S(1)} %collective-permute-done.17.t0_ref, bf16[192,896]{1,0:T(8,128)(2,1)S(1)} %collective-permute-done.4.t1_ref), custom_call_target="tpu_custom_call" | custom-call | tf_op jit(solution)/shard_map/turn/pallas_call | solution.py:370
  51.3 1.5 %collective-permute-done.8 = bf16[144,128]{1,0:T(8,128)(2,1)S(1)} collective-permute-done((bf16[144,128]{1,0:T(8,128)(2,1)S(1)}, bf16[144,128]{1,0:T(8,128)(2,1)S(1)}, u32[]{:S(2)}, u32[]{:S(2)}) %collective-permute-start.8) | collective-permute-done | bytes 36896 | tf_op jit(solution)/shard_map/ppermute | solution.py:250
  52.8 1.0 %collective-permute-done.9 = bf16[144,128]{1,0:T(8,128)(2,1)S(1)} collective-permute-done((bf16[144,128]{1,0:T(8,128)(2,1)S(1)}, bf16[144,128]{1,0:T(8,128)(2,1)S(1)}, u32[]{:S(2)}, u32[]{:S(2)}) %collective-permute-start.9) | collective-permute-done | bytes 36896 | tf_op jit(solution)/shard_map/ppermute | solution.py:250
  54.0 1.4 %collective-permute-done.19.refs_3_ = bf16[4,144,128]{2,1,0:T(8,128)(2,1)S(1)} collective-permute-done((bf16[4,144,128]{2,1,0:T(8,128)(2,1)S(1)}, bf16[4,144,128]{2,1,0:T(8,128)(2,1)S(1)}, u32[]{:S(2)}, u32[]{:S(2)}) %collective-permute-start.19) | collective-permute-done | bytes 147488 | tf_op jit(solution)/shard_map/ppermute | solution.py:383
  55.3 1.6 %final.1 = (f32[384,768]{1,0:T(8,128)}, f32[24,16,256]{2,1,0:T(8,128)}) custom-call(bf16[4,248,128]{2,1,0:T(8,128)(2,1)S(1)} %pad_maximum_fusion.refs_0_, bf16[4,144,128]{2,1,0:T(8,128)(2,1)S(1)} %pad_maximum_fusion.1.refs_1_, bf16[4,248,128]{2,1,0:T(8,128)(2,1)S(1)} %collective-permute-done.18.refs_2_, ...), custom_call_target="tpu_custom_call" | custom-call | tf_op jit(solution)/shard_map/final/pallas_call | solution.py:386
  (38 shorter events, 2.9 us)
Async XLA Ops:
  0.6 8.1 %collective-permute-start.1 = (bf16[896,768]{1,0:T(8,128)(2,1)}, bf16[896,768]{1,0:T(8,128)(2,1)S(1)}, u32[]{:S(2)}, u32[]{:S(2)}) collective-permute-start(bf16[896,768]{1,0:T(8,128)(2,1)} %refs_3_.3), channel_id=1, source_target_pairs={{0,1},{1,0},{2,3},{3,2},{4,5},{5,4},{6,7},{7,6},{8,9},{9,8},{10,11... | collective-permute-start | bytes 4128776 | tf_op jit(solution)/shard_map/ppermute | solution.py:270
  2.1 9.8 %collective-permute-start = (f32[12,16,256]{2,1,0:T(8,128)S(1)}, f32[12,16,256]{2,1,0:T(8,128)S(1)}, u32[]{:S(2)}, u32[]{:S(2)}) collective-permute-start(f32[12,16,256]{2,1,0:T(8,128)S(1)} %dynamic-slice_bitcast_fusion), channel_id=1, source_target_pairs={{0,2},{2,0},{1,3},{3,1},{4,6},{6,4},{5,7},{7,5},{8,10},{10,8},{9,1... | collective-permute-start | bytes 589832 | tf_op jit(solution)/shard_map/ppermute | solution.py:269
  4.7 1.3 %copy-start = (bf16[896,768]{1,0:T(8,128)(2,1)S(1)}, bf16[896,768]{1,0:T(8,128)(2,1)}, u32[]{:S(2)}) copy-start(bf16[896,768]{1,0:T(8,128)(2,1)} %refs_3_.3) | copy-start | bytes 4128772
  6.0 1.3 %copy-start.2 = (bf16[768,768]{1,0:T(8,128)(2,1)S(1)}, bf16[768,768]{1,0:T(8,128)(2,1)}, u32[]{:S(2)}) copy-start(bf16[768,768]{1,0:T(8,128)(2,1)} %rot_ref.1) | copy-start | bytes 3538948
  8.7 1.0 %copy-start.3 = (f32[24,256,16]{1,2,0:T(8,128)S(1)}, f32[24,256,16]{1,2,0:T(8,128)}, u32[]{:S(2)}) copy-start(f32[24,256,16]{1,2,0:T(8,128)} %param.5) | copy-start | bytes 1179652
  9.7 2.3 %copy-start.1 = (bf16[896,768]{1,0:T(8,128)(2,1)S(1)}, bf16[896,768]{1,0:T(8,128)(2,1)}, u32[]{:S(2)}) copy-start(bf16[896,768]{1,0:T(8,128)(2,1)} %refs_3_.3) | copy-start | bytes 4128772
  20.6 13.4 %collective-permute-start.4 = (bf16[192,896]{1,0:T(8,128)(2,1)S(1)}, bf16[192,896]{1,0:T(8,128)(2,1)S(1)}, u32[]{:S(2)}, u32[]{:S(2)}) collective-permute-start(bf16[192,896]{1,0:T(8,128)(2,1)S(1)} %get-tuple-element.58), channel_id=1, source_target_pairs={{0,1},{1,0},{2,3},{3,2},{4,5},{5,4},{6,7},{7,6},{8,9},{9,8},{10,11... | collective-permute-start | bytes 1032200 | tf_op jit(solution)/shard_map/ppermute | solution.py:337
  20.9 8.6 %collective-permute-start.2 = (bf16[992,128]{1,0:T(8,128)(2,1)S(1)}, bf16[992,128]{1,0:T(8,128)(2,1)S(1)}, u32[]{:S(2)}, u32[]{:S(2)}) collective-permute-start(bf16[992,128]{1,0:T(8,128)(2,1)S(1)} %get-tuple-element.55), channel_id=1, source_target_pairs={{0,2},{2,0},{1,3},{3,1},{4,6},{6,4},{5,7},{7,5},{8,10},{10,8},{9,1... | collective-permute-start | bytes 761864 | tf_op jit(solution)/shard_map/ppermute | solution.py:336
  27.7 6.3 %collective-permute-start.3 = (bf16[576,128]{1,0:T(8,128)(2,1)S(1)}, bf16[576,128]{1,0:T(8,128)(2,1)S(1)}, u32[]{:S(2)}, u32[]{:S(2)}) collective-permute-start(bf16[576,128]{1,0:T(8,128)(2,1)S(1)} %get-tuple-element.57), channel_id=1, source_target_pairs={{0,2},{2,0},{1,3},{3,1},{4,6},{6,4},{5,7},{7,5},{8,10},{10,8},{9,1... | collective-permute-start | bytes 442376 | tf_op jit(solution)/shard_map/ppermute | solution.py:339
  29.6 8.2 %collective-permute-start.11 = (bf16[248,128]{1,0:T(8,128)(2,1)S(1)}, bf16[248,128]{1,0:T(8,128)(2,1)S(1)}, u32[]{:S(2)}, u32[]{:S(2)}) collective-permute-start(bf16[248,128]{1,0:T(8,128)(2,1)S(1)} %get-tuple-element.67), channel_id=1, source_target_pairs={{0,12},{4,8},{8,4},{12,0},{1,13},{5,9},{9,5},{13,1},{2,14},{6,10},... | collective-permute-start | bytes 190472 | tf_op jit(solution)/shard_map/ppermute | solution.py:250
  33.2 5.8 %collective-permute-start.12 = (bf16[248,128]{1,0:T(8,128)(2,1)S(1)}, bf16[248,128]{1,0:T(8,128)(2,1)S(1)}, u32[]{:S(2)}, u32[]{:S(2)}) collective-permute-start(bf16[248,128]{1,0:T(8,128)(2,1)S(1)} %get-tuple-element.68), channel_id=1, source_target_pairs={{0,8},{4,12},{8,0},{12,4},{1,9},{5,13},{9,1},{13,5},{2,10},{6,14},... | collective-permute-start | bytes 190472 | tf_op jit(solution)/shard_map/ppermute | solution.py:250
  33.2 7.3 %collective-permute-start.13 = (bf16[248,128]{1,0:T(8,128)(2,1)S(1)}, bf16[248,128]{1,0:T(8,128)(2,1)S(1)}, u32[]{:S(2)}, u32[]{:S(2)}) collective-permute-start(bf16[248,128]{1,0:T(8,128)(2,1)S(1)} %get-tuple-element.69), channel_id=1, source_target_pairs={{0,4},{4,0},{8,12},{12,8},{1,5},{5,1},{9,13},{13,9},{2,6},{6,2},{1... | collective-permute-start | bytes 190472 | tf_op jit(solution)/shard_map/ppermute | solution.py:250
  34.0 15.6 %collective-permute-start.17 = (bf16[192,896]{1,0:T(8,128)(2,1)S(1)}, bf16[192,896]{1,0:T(8,128)(2,1)S(1)}, u32[]{:S(2)}, u32[]{:S(2)}) collective-permute-start(bf16[192,896]{1,0:T(8,128)(2,1)S(1)} %get-tuple-element.70), channel_id=1, source_target_pairs={{0,1},{1,0},{2,3},{3,2},{4,5},{5,4},{6,7},{7,6},{8,9},{9,8},{10,11... | collective-permute-start | bytes 1032200 | tf_op jit(solution)/shard_map/ppermute | solution.py:340
  34.1 8.2 %collective-permute-start.5 = (bf16[144,128]{1,0:T(8,128)(2,1)S(1)}, bf16[144,128]{1,0:T(8,128)(2,1)S(1)}, u32[]{:S(2)}, u32[]{:S(2)}) collective-permute-start(bf16[144,128]{1,0:T(8,128)(2,1)S(1)} %get-tuple-element.61), channel_id=1, source_target_pairs={{0,12},{4,8},{8,4},{12,0},{1,13},{5,9},{9,5},{13,1},{2,14},{6,10},... | collective-permute-start | bytes 110600 | tf_op jit(solution)/shard_map/ppermute | solution.py:250
  37.7 5.2 %collective-permute-start.6 = (bf16[144,128]{1,0:T(8,128)(2,1)S(1)}, bf16[144,128]{1,0:T(8,128)(2,1)S(1)}, u32[]{:S(2)}, u32[]{:S(2)}) collective-permute-start(bf16[144,128]{1,0:T(8,128)(2,1)S(1)} %get-tuple-element.62), channel_id=1, source_target_pairs={{0,8},{4,12},{8,0},{12,4},{1,9},{5,13},{9,1},{13,5},{2,10},{6,14},... | collective-permute-start | bytes 110600 | tf_op jit(solution)/shard_map/ppermute | solution.py:250
  39.0 6.0 %collective-permute-start.7 = (bf16[144,128]{1,0:T(8,128)(2,1)S(1)}, bf16[144,128]{1,0:T(8,128)(2,1)S(1)}, u32[]{:S(2)}, u32[]{:S(2)}) collective-permute-start(bf16[144,128]{1,0:T(8,128)(2,1)S(1)} %get-tuple-element.63), channel_id=1, source_target_pairs={{0,4},{4,0},{8,12},{12,8},{1,5},{5,1},{9,13},{13,9},{2,6},{6,2},{1... | collective-permute-start | bytes 110600 | tf_op jit(solution)/shard_map/ppermute | solution.py:250
  40.6 6.5 %collective-permute-start.14 = (bf16[248,128]{1,0:T(8,128)(2,1)S(1)}, bf16[248,128]{1,0:T(8,128)(2,1)S(1)}, u32[]{:S(2)}, u32[]{:S(2)}) collective-permute-start(bf16[248,128]{1,0:T(8,128)(2,1)S(1)} %add_convert_fusion), channel_id=1, source_target_pairs={{0,12},{4,8},{8,4},{12,0},{1,13},{5,9},{9,5},{13,1},{2,14},{6,10},... | collective-permute-start | bytes 190472 | tf_op jit(solution)/shard_map/ppermute | solution.py:250
  42.2 6.8 %collective-permute-start.15 = (bf16[248,128]{1,0:T(8,128)(2,1)S(1)}, bf16[248,128]{1,0:T(8,128)(2,1)S(1)}, u32[]{:S(2)}, u32[]{:S(2)}) collective-permute-start(bf16[248,128]{1,0:T(8,128)(2,1)S(1)} %add_convert_fusion), channel_id=1, source_target_pairs={{0,8},{4,12},{8,0},{12,4},{1,9},{5,13},{9,1},{13,5},{2,10},{6,14},... | collective-permute-start | bytes 190472 | tf_op jit(solution)/shard_map/ppermute | solution.py:250
  43.0 6.6 %collective-permute-start.16 = (bf16[248,128]{1,0:T(8,128)(2,1)S(1)}, bf16[248,128]{1,0:T(8,128)(2,1)S(1)}, u32[]{:S(2)}, u32[]{:S(2)}) collective-permute-start(bf16[248,128]{1,0:T(8,128)(2,1)S(1)} %add_convert_fusion), channel_id=1, source_target_pairs={{0,4},{4,0},{8,12},{12,8},{1,5},{5,1},{9,13},{13,9},{2,6},{6,2},{1... | collective-permute-start | bytes 190472 | tf_op jit(solution)/shard_map/ppermute | solution.py:250
  45.1 6.2 %collective-permute-start.10 = (bf16[144,128]{1,0:T(8,128)(2,1)S(1)}, bf16[144,128]{1,0:T(8,128)(2,1)S(1)}, u32[]{:S(2)}, u32[]{:S(2)}) collective-permute-start(bf16[144,128]{1,0:T(8,128)(2,1)S(1)} %add_convert_fusion.1), channel_id=1, source_target_pairs={{0,4},{4,0},{8,12},{12,8},{1,5},{5,1},{9,13},{13,9},{2,6},{6,2},{1... | collective-permute-start | bytes 110600 | tf_op jit(solution)/shard_map/ppermute | solution.py:250
  47.1 5.8 %collective-permute-start.8 = (bf16[144,128]{1,0:T(8,128)(2,1)S(1)}, bf16[144,128]{1,0:T(8,128)(2,1)S(1)}, u32[]{:S(2)}, u32[]{:S(2)}) collective-permute-start(bf16[144,128]{1,0:T(8,128)(2,1)S(1)} %add_convert_fusion.1), channel_id=1, source_target_pairs={{0,12},{4,8},{8,4},{12,0},{1,13},{5,9},{9,5},{13,1},{2,14},{6,10},... | collective-permute-start | bytes 110600 | tf_op jit(solution)/shard_map/ppermute | solution.py:250
  49.0 4.9 %collective-permute-start.9 = (bf16[144,128]{1,0:T(8,128)(2,1)S(1)}, bf16[144,128]{1,0:T(8,128)(2,1)S(1)}, u32[]{:S(2)}, u32[]{:S(2)}) collective-permute-start(bf16[144,128]{1,0:T(8,128)(2,1)S(1)} %add_convert_fusion.1), channel_id=1, source_target_pairs={{0,8},{4,12},{8,0},{12,4},{1,9},{5,13},{9,1},{13,5},{2,10},{6,14},... | collective-permute-start | bytes 110600 | tf_op jit(solution)/shard_map/ppermute | solution.py:250
  49.6 5.8 %collective-permute-start.18 = (bf16[4,248,128]{2,1,0:T(8,128)(2,1)S(1)}, bf16[4,248,128]{2,1,0:T(8,128)(2,1)S(1)}, u32[]{:S(2)}, u32[]{:S(2)}) collective-permute-start(bf16[4,248,128]{2,1,0:T(8,128)(2,1)S(1)} %pad_maximum_fusion.refs_0_), channel_id=1, source_target_pairs={{0,1},{1,0},{2,3},{3,2},{4,5},{5,4},{6,7},{7,6},{8,9},{9,8},{10,11... | collective-permute-start | bytes 761864 | tf_op jit(solution)/shard_map/ppermute | solution.py:367
  53.9 1.4 %collective-permute-start.19 = (bf16[4,144,128]{2,1,0:T(8,128)(2,1)S(1)}, bf16[4,144,128]{2,1,0:T(8,128)(2,1)S(1)}, u32[]{:S(2)}, u32[]{:S(2)}) collective-permute-start(bf16[4,144,128]{2,1,0:T(8,128)(2,1)S(1)} %pad_maximum_fusion.1.refs_1_), channel_id=1, source_target_pairs={{0,1},{1,0},{2,3},{3,2},{4,5},{5,4},{6,7},{7,6},{8,9},{9,8},{10,11... | collective-permute-start | bytes 442376 | tf_op jit(solution)/shard_map/ppermute | solution.py:383

commit v7 on v6

--- a/solution.py
+++ b/solution.py
@@ -191,7 +191,7 @@
 
 
 def final_kernel(*refs, n, per, total):
-    held, (cb_ref, cross_hbm, new_hbm, buf, cross, new, sems) = refs[:4], refs[4:]
+    pieces, (cb_ref, cross_hbm, new_hbm, buf, cross, new, sems) = refs[: 2 * n], refs[2 * n :]
     s, r, z = lax.axis_index("sub"), lax.axis_index("rep"), lax.axis_index("row")
     lanes = 128
     w = per * SUBDIM
@@ -200,11 +200,11 @@
     near_rows = groups * w + halves * (w + SUBDIM)
     near, far = near_rows // n, groups * w // n
     for side in range(2):
-        near_ref, far_ref = held[2 * side : 2 * side + 2]
         for i in range(n):
+            ref = pieces[side * n + i]
             source = z ^ ((n - i) % n)
-            buf[side, pl.ds(pl.multiple_of(source * near, 8), near), :] = near_ref[i].astype(F32)
-            buf[side, pl.ds(pl.multiple_of(near_rows + source * far, 8), far), :] = far_ref[i].astype(F32)
+            buf[side, pl.ds(pl.multiple_of(source * near, 8), near), :] = ref[:near].astype(F32)
+            buf[side, pl.ds(pl.multiple_of(near_rows + source * far, 8), far), :] = ref[near:].astype(F32)
 
     copies = []
     for g in range(groups):
@@ -236,14 +236,13 @@
         copy.wait()
 
 
-def pieces_kernel(kept_ref, got_ref, *refs, n):
-    outs, total = refs[:n], refs[n]
+def pieces_kernel(kept_ref, got_ref, own_ref, sent_ref, total):
     z = lax.axis_index("row")
     total[...] = kept_ref[...] + got_ref[...].astype(F32)
-    size = outs[0].shape[0]
-    for i, out in enumerate(outs):
-        at = (z ^ ((n - i) % n)) * size
-        out[...] = total[pl.ds(pl.multiple_of(at, 8), size), :].astype(out.dtype)
+    size = own_ref.shape[1]
+    for i in range(2):
+        own_ref[i] = total[pl.ds(pl.multiple_of((z ^ (2 * i)) * size, 8), size), :]
+        sent_ref[i] = total[pl.ds(pl.multiple_of((z ^ (2 * i + 1)) * size, 8), size), :].astype(BF16)
 
 
 def exchange(x, n, d):
@@ -337,36 +336,32 @@
     theirs1 = lax.ppermute(other1, "rep", swap)
     mine0, other0, keep0, send0 = quantize(0, cb, HEAD, head)
     got0 = lax.ppermute(send0, "sub", swap)
-    theirs0 = lax.ppermute(other0, "rep", swap)
 
     def scatter(kept, got):
-        size = (kept.shape[0] // rows_n, lanes)
-        own, *sent = pl.pallas_call(
-            functools.partial(pieces_kernel, n=rows_n),
-            out_shape=[jax.ShapeDtypeStruct(size, F32)] + [jax.ShapeDtypeStruct(size, BF16)] * (rows_n - 1),
+        size = (2, kept.shape[0] // rows_n, lanes)
+        return pl.pallas_call(
+            pieces_kernel,
+            out_shape=[jax.ShapeDtypeStruct(size, F32), jax.ShapeDtypeStruct(size, BF16)],
             in_specs=[vmem] * 2,
-            out_specs=[vmem] * rows_n,
+            out_specs=[vmem] * 2,
             scratch_shapes=[pltpu.VMEM(kept.shape, F32)],
             compiler_params=small,
             name="pieces",
         )(kept, got)
-        return [own] + [exchange(x, rows_n, d) for x, d in zip(sent, apart)]
-
-    def add_up(parts):
-        return functools.reduce(lambda a, b: a + b.astype(F32), parts[1:], parts[0]).astype(BF16)
-
-    apart = range(rows_n - 1, 0, -1)
-    near = scatter(keep0, got1)
-    near[0], got0, theirs1 = lax.optimization_barrier((near[0], got0, theirs1))
-    far = scatter(keep1, got0)
-
-    def spread_out(x):
-        return [x] + [exchange(x, rows_n, d) for d in apart]
-
-    near_held = jnp.stack(spread_out(add_up(near)))
-    near_theirs = lax.ppermute(near_held, "rep", swap)
-    near_held, theirs0 = lax.optimization_barrier((near_held, theirs0))
-
+
+    def pair(own, sent):
+        both = own + exchange(sent, rows_n, 1).astype(F32)
+        return both[0], both[1].astype(BF16)
+
+    def finish(own, sent):
+        return (own + exchange(sent, rows_n, 2).astype(F32)).astype(BF16)
+
+    near_own, near_sent = scatter(keep0, got1)
+    near_own, other0, got0, theirs1 = lax.optimization_barrier((near_own, other0, got0, theirs1))
+    theirs0 = lax.ppermute(other0, "rep", swap)
+    near = pair(near_own, near_sent)
+    far_own, far_sent = pair(*scatter(keep1, got0))
+    far_sent, theirs0 = lax.optimization_barrier((far_sent, theirs0))
     reconstruction = pl.pallas_call(
         turn_kernel,
         out_shape=jax.ShapeDtypeStruct((rows, width), BF16),
@@ -376,17 +371,17 @@
         compiler_params=small,
         name="turn",
     )(mine0, mine1, theirs0, theirs1)
-
-    far_held = spread_out(add_up(far))
-    *far_held, reconstruction = lax.optimization_barrier((*far_held, reconstruction))
-    far_held = jnp.stack(far_held)
-    far_theirs = lax.ppermute(far_held, "rep", swap)
+    summed = jnp.concatenate([finish(*near), finish(far_own, far_sent)], axis=0)
+    summed, reconstruction = lax.optimization_barrier((summed, reconstruction))
+    apart = range(rows_n - 1, 0, -1)
+    mine = [summed] + [exchange(summed, rows_n, d) for d in apart]
+    theirs = [lax.ppermute(x, "rep", swap) for x in mine]
 
     any_spec = pl.BlockSpec(memory_space=pl.ANY)
     cross, new = pl.pallas_call(
         functools.partial(final_kernel, n=rows_n, per=per, total=total),
         out_shape=(jax.ShapeDtypeStruct((part, width), F32), jax.ShapeDtypeStruct(cb.shape, F32)),
-        in_specs=[vmem] * 5,
+        in_specs=[vmem] * (2 * rows_n + 1),
         out_specs=(any_spec, any_spec),
         scratch_shapes=[
             pltpu.VMEM((2, 2 * p_rows + s_rows, lanes), F32),
@@ -396,13 +391,13 @@
         ],
         compiler_params=small,
         name="final",
-    )(near_held, far_held, near_theirs, far_theirs, cb)
+    )(*mine, *theirs, cb)
     return reconstruction, new.transpose(0, 2, 1), cross
 
 
 def solution(mesh):
     placed = (P(("dom", "row", "sub", "rep"), None), P("dom", None), P(("dom", "sub"), None, None))
-    body = on_device if mesh.shape["sub"] == 2 and mesh.shape["row"] in (2, 4, 8) else any_mesh
+    body = on_device if mesh.shape["sub"] == 2 and mesh.shape["row"] == 4 else any_mesh
     return jax.shard_map(
         body,
         mesh=mesh,

time: 57.3 us -> 59.1 us (1.031)
  waiting for transfers between devices: 6.23 us -> 11.4 us
  starting transfers between devices: 23.1 us -> 19.7 us
    ppermute x12 -> x7, starting transfers between devices: 17.6 us -> 14 us  [exchange(): return lax.ppermute(x, 'row', [(i, i ^ d) for i in range(n)])]
    ppermute x12 -> x7, waiting for transfers between devices: 4.85 us -> 7.67 us  [exchange(): return lax.ppermute(x, 'row', [(i, i ^ d) for i in range(n)])]
    ppermute x1, waiting for transfers between devices: 0.01 us -> 2.79 us  [on_device(): got0 = lax.ppermute(send0, 'sub', swap)]
    ppermute x2 -> x4, waiting for transfers between devices: 1.36 us -> 0.95 us  [on_device(): theirs = [lax.ppermute(x, 'rep', swap) for x in mine]]
  transfers between devices with their start and end apart: 20 -> 17, of which waited for: 5 -> 6; matrix products, arithmetic and copies ran while one was open for 2% -> 2% of each run, Pallas kernels for 22% -> 22%
where the time goes in v7:
time: 59.1 us; the launch traced here: 58.8 us
  Pallas kernels  23 us (39%)
  starting transfers between devices  19.7 us (33%)
  waiting for transfers between devices  11.4 us (19%)
  local copies, waits for them, and re-layouts  3.6 us (6%)
  between operations  0.95 us (2%)
    pallas_call x2, Pallas kernels, quantize(): pl.pallas_call(functools.partial(quantize_kernel, k=k, per=per, first=fir...  15.1 us
    ppermute x7, starting transfers between devices, exchange(): return lax.ppermute(x, 'row', [(i, i ^ d) for i in range(n)])  14 us
    ppermute x7, waiting for transfers between devices, exchange(): return lax.ppermute(x, 'row', [(i, i ^ d) for i in range(n)])  7.67 us
    ppermute x1, waiting for transfers between devices, on_device(): got0 = lax.ppermute(send0, 'sub', swap)  2.79 us
    unnamed x8, local copies, waits for them, and re-layouts  2.65 us
    ppermute x1, starting transfers between devices, on_device(): cb_far = lax.ppermute(cb_sent, 'sub', swap)  2.58 us
    pallas_call x1, Pallas kernels, on_device(): pl.pallas_call(functools.partial(quantize_kernel, k=0, per=per, first=0,...  2.2 us
    ppermute x1, starting transfers between devices, on_device(): got0 = lax.ppermute(send0, 'sub', swap)  1.8 us
  transfers between devices with their start and end apart: 17, of which 6 were waited for; matrix products, arithmetic and copies ran while one was open for 2% of the time, Pallas kernels for 22%

profile of v7, /device:TPU:0, one launch (start us, length us, event | category | flops | bytes accessed | tf_op | source)
XLA Modules:
  0.0 58.8 jit_solution(16517372817491757609)
XLA Ops:
  0.6 0.5 collective-permute-start
  1.1 0.9 %dynamic-slice_bitcast_fusion = f32[12,16,256]{2,1,0:T(8,128)S(1)} fusion(f32[24,256,16]{1,2,0:T(8,128)} %param.5, s32[]{:T(128)S(6)} %select_n.3), kind=kLoop, calls=%fused_computation.1 | loop fusion | bytes 393220 | tf_op jit(solution)/shard_map/dynamic_slice | solution.py:267
  2.1 2.6 %collective-permute-start.1 = (f32[12,16,256]{2,1,0:T(8,128)S(1)}, f32[12,16,256]{2,1,0:T(8,128)S(1)}, u32[]{:S(2)}, u32[]{:S(2)}) collective-permute-start(f32[12,16,256]{2,1,0:T(8,128)S(1)} %dynamic-slice_bitcast_fusion), channel_id=1, source_target_pairs={{0,2},{2,0},{1,3},{3,1},{4,6},{6,4},{5,7},{7,5},{8,10},{10,8},{9,1... | collective-permute-start | bytes 589832 | tf_op jit(solution)/shard_map/ppermute | solution.py:268
  4.7 1.3 %copy-done = bf16[896,768]{1,0:T(8,128)(2,1)S(1)} copy-done((bf16[896,768]{1,0:T(8,128)(2,1)S(1)}, bf16[896,768]{1,0:T(8,128)(2,1)}, u32[]{:S(2)}) %copy-start) | copy-done | bytes 1376280
  6.0 1.3 %copy-done.2 = bf16[768,768]{1,0:T(8,128)(2,1)S(1)} copy-done((bf16[768,768]{1,0:T(8,128)(2,1)S(1)}, bf16[768,768]{1,0:T(8,128)(2,1)}, u32[]{:S(2)}) %copy-start.2) | copy-done | bytes 1179672
  7.3 1.4 %rotate.1 = (bf16[2,192,896]{2,1,0:T(8,128)(2,1)S(1)}, bf16[2,192,768]{2,1,0:T(8,128)(2,1)S(1)}) custom-call(bf16[896,768]{1,0:T(8,128)(2,1)S(1)} %copy-done, bf16[768,768]{1,0:T(8,128)(2,1)S(1)} %copy-done.2), custom_call_target="tpu_custom_call" | custom-call | tf_op jit(solution)/shard_map/rotate/pallas_call | solution.py:272
  8.7 1.0 %rotate_far.1.refs_2_ = bf16[2,192,896]{2,1,0:T(8,128)(2,1)S(1)} custom-call(bf16[896,768]{1,0:T(8,128)(2,1)S(1)} %collective-permute-done.vec_ref.refs_4_, bf16[2,192,768]{2,1,0:T(8,128)(2,1)S(1)} %get-tuple-element.37.rott_ref), custom_call_target="tpu_custom_call" | custom-call | tf_op jit(solution)/shard_map/rotate_far/pallas_call | solution.py:281
  9.7 2.2 %quantize_head.1 = (bf16[48,896]{1,0:T(8,128)(2,1)S(1)}, bf16[48,896]{1,0:T(8,128)(2,1)S(1)}, f32[96,128]{1,0:T(8,128)S(1)}, f32[32,128]{1,0:T(8,128)S(1)}) custom-call(f32[24,16,256]{2,1,0:T(8,128)S(1)} %bitcast.20, bf16[2,192,896]{2,1,0:T(8,128)(2,1)S(1)} %get-tuple-element.36.refs_1_, bf16[2,192,896]{2,1,0:T(8,128)(2,1)S(1)} %rotate_far.1.refs_2_), custom_call_target="tpu_custom_call" | custom-call | flops 396361728 | bytes 8388608 | tf_op jit(solution)/shard_map/quantize_head/pallas_call | solution.py:319
  12.0 8.7 %quantize_far.1 = (bf16[192,896]{1,0:T(8,128)(2,1)S(1)}, bf16[192,896]{1,0:T(8,128)(2,1)S(1)}, f32[576,128]{1,0:T(8,128)S(1)}, bf16[992,128]{1,0:T(8,128)(2,1)S(1)}) custom-call(f32[12,16,256]{2,1,0:T(8,128)S(1)} %collective-permute-done.1.refs_0_, bf16[2,192,896]{2,1,0:T(8,128)(2,1)S(1)} %get-tuple-element.36.refs_1_, ...), custom_call_target="tpu_custom_call" | custom-call | flops 2113929216 | bytes 8388608 | tf_op jit(solution)/shard_map/quantize_far/pallas_call | solution.py:300
  21.0 6.5 %quantize_near.1 = (bf16[192,896]{1,0:T(8,128)(2,1)S(1)}, bf16[192,896]{1,0:T(8,128)(2,1)S(1)}, f32[992,128]{1,0:T(8,128)S(1)}, bf16[576,128]{1,0:T(8,128)(2,1)S(1)}) custom-call(f32[24,16,256]{2,1,0:T(8,128)S(1)} %bitcast.21, bf16[2,192,896]{2,1,0:T(8,128)(2,1)S(1)} %get-tuple-element.36.refs_1_, bf16[2,192,896]{2,1,0:T(8,128)(2,1)S(1)} %rotate_far.1.refs_2_, ...), custom_call_target="tpu_custom_call" | custom-call | flops 1717567488 | bytes 8388608 | tf_op jit(solution)/shard_map/quantize_near/pallas_call | solution.py:300
  27.5 1.8 %collective-permute-start.3 = (bf16[576,128]{1,0:T(8,128)(2,1)S(1)}, bf16[576,128]{1,0:T(8,128)(2,1)S(1)}, u32[]{:S(2)}, u32[]{:S(2)}) collective-permute-start(bf16[576,128]{1,0:T(8,128)(2,1)S(1)} %get-tuple-element.51), channel_id=1, source_target_pairs={{0,2},{2,0},{1,3},{3,1},{4,6},{6,4},{5,7},{7,5},{8,10},{10,8},{9,1... | collective-permute-start | bytes 442376 | tf_op jit(solution)/shard_map/ppermute | solution.py:338
  29.4 1.6 %collective-permute-start.5 = (bf16[2,248,128]{2,1,0:T(8,128)(2,1)S(1)}, bf16[2,248,128]{2,1,0:T(8,128)(2,1)S(1)}, u32[]{:S(2)}, u32[]{:S(2)}) collective-permute-start(bf16[2,248,128]{2,1,0:T(8,128)(2,1)S(1)} %get-tuple-element.54), channel_id=1, source_target_pairs={{0,4},{4,0},{8,12},{12,8},{1,5},{5,1},{9,13},{13,9},{2,6},{6,2},{1... | collective-permute-start | bytes 380936 | tf_op jit(solution)/shard_map/ppermute | solution.py:249
  31.0 2.8 %collective-permute-done.3.got_ref = bf16[576,128]{1,0:T(8,128)(2,1)S(1)} collective-permute-done((bf16[576,128]{1,0:T(8,128)(2,1)S(1)}, bf16[576,128]{1,0:T(8,128)(2,1)S(1)}, u32[]{:S(2)}, u32[]{:S(2)}) %collective-permute-start.3) | collective-permute-done | bytes 147488 | tf_op jit(solution)/shard_map/ppermute | solution.py:338
  33.8 1.9 %collective-permute-start.7 = (bf16[2,144,128]{2,1,0:T(8,128)(2,1)S(1)}, bf16[2,144,128]{2,1,0:T(8,128)(2,1)S(1)}, u32[]{:S(2)}, u32[]{:S(2)}) collective-permute-start(bf16[2,144,128]{2,1,0:T(8,128)(2,1)S(1)} %get-tuple-element.58), channel_id=1, source_target_pairs={{0,4},{4,0},{8,12},{12,8},{1,5},{5,1},{9,13},{13,9},{2,6},{6,2},{1... | collective-permute-start | bytes 221192 | tf_op jit(solution)/shard_map/ppermute | solution.py:249
  35.8 2.7 %collective-permute-start.6 = (bf16[248,128]{1,0:T(8,128)(2,1)S(1)}, bf16[248,128]{1,0:T(8,128)(2,1)S(1)}, u32[]{:S(2)}, u32[]{:S(2)}) collective-permute-start(bf16[248,128]{1,0:T(8,128)(2,1)S(1)} %fusion.4), channel_id=1, source_target_pairs={{0,8},{4,12},{8,0},{12,4},{1,9},{5,13},{9,1},{13,5},{2,10},{6,14},... | collective-permute-start | bytes 190472 | tf_op jit(solution)/shard_map/ppermute | solution.py:249
  38.5 3.3 %collective-permute-start.9 = (bf16[144,128]{1,0:T(8,128)(2,1)S(1)}, bf16[144,128]{1,0:T(8,128)(2,1)S(1)}, u32[]{:S(2)}, u32[]{:S(2)}) collective-permute-start(bf16[144,128]{1,0:T(8,128)(2,1)S(1)} %fusion.5), channel_id=1, source_target_pairs={{0,8},{4,12},{8,0},{12,4},{1,9},{5,13},{9,1},{13,5},{2,10},{6,14},... | collective-permute-start | bytes 110600 | tf_op jit(solution)/shard_map/ppermute | solution.py:249
  41.8 1.3 %collective-permute-done.6 = bf16[248,128]{1,0:T(8,128)(2,1)S(1)} collective-permute-done((bf16[248,128]{1,0:T(8,128)(2,1)S(1)}, bf16[248,128]{1,0:T(8,128)(2,1)S(1)}, u32[]{:S(2)}, u32[]{:S(2)}) %collective-permute-start.6) | collective-permute-done | bytes 63520 | tf_op jit(solution)/shard_map/ppermute | solution.py:249
  43.1 1.6 %turn.1 = bf16[896,768]{1,0:T(8,128)(2,1)} custom-call(bf16[192,896]{1,0:T(8,128)(2,1)S(1)} %get-tuple-element.61.m0_ref, bf16[192,896]{1,0:T(8,128)(2,1)S(1)} %get-tuple-element.62.m1_ref, bf16[192,896]{1,0:T(8,128)(2,1)S(1)} %collective-permute-done.8.t0_ref, bf16[192,896]{1,0:T(8,128)(2,1)S(1)} %collective-permute-done.4.t1_ref), custom_call_target="tpu_custom_call" | custom-call | tf_op jit(solution)/shard_map/turn/pallas_call | solution.py:365
  45.2 3.1 %collective-permute-start.11 = (bf16[392,128]{1,0:T(8,128)(2,1)S(1)}, bf16[392,128]{1,0:T(8,128)(2,1)S(1)}, u32[]{:S(2)}, u32[]{:S(2)}) collective-permute-start(bf16[392,128]{1,0:T(8,128)(2,1)S(1)} %pad_maximum_fusion.refs_0_), channel_id=1, source_target_pairs={{0,8},{4,12},{8,0},{12,4},{1,9},{5,13},{9,1},{13,5},{2,10},{6,14},... | collective-permute-start | bytes 301064 | tf_op jit(solution)/shard_map/ppermute | solution.py:249
  48.2 1.0 %collective-permute-start.10 = (bf16[392,128]{1,0:T(8,128)(2,1)S(1)}, bf16[392,128]{1,0:T(8,128)(2,1)S(1)}, u32[]{:S(2)}, u32[]{:S(2)}) collective-permute-start(bf16[392,128]{1,0:T(8,128)(2,1)S(1)} %pad_maximum_fusion.refs_0_), channel_id=1, source_target_pairs={{0,12},{4,8},{8,4},{12,0},{1,13},{5,9},{9,5},{13,1},{2,14},{6,10},... | collective-permute-start | bytes 301064 | tf_op jit(solution)/shard_map/ppermute | solution.py:249
  49.2 1.2 %collective-permute-done.12.refs_3_ = bf16[392,128]{1,0:T(8,128)(2,1)S(1)} collective-permute-done((bf16[392,128]{1,0:T(8,128)(2,1)S(1)}, bf16[392,128]{1,0:T(8,128)(2,1)S(1)}, u32[]{:S(2)}, u32[]{:S(2)}) %collective-permute-start.12) | collective-permute-done | bytes 100384 | tf_op jit(solution)/shard_map/ppermute | solution.py:249
  50.4 5.2 %collective-permute-done.11.refs_2_ = bf16[392,128]{1,0:T(8,128)(2,1)S(1)} collective-permute-done((bf16[392,128]{1,0:T(8,128)(2,1)S(1)}, bf16[392,128]{1,0:T(8,128)(2,1)S(1)}, u32[]{:S(2)}, u32[]{:S(2)}) %collective-permute-start.11) | collective-permute-done | bytes 100384 | tf_op jit(solution)/shard_map/ppermute | solution.py:249
  56.1 0.8 %collective-permute-done.15.refs_6_ = bf16[392,128]{1,0:T(8,128)(2,1)S(1)} collective-permute-done((bf16[392,128]{1,0:T(8,128)(2,1)S(1)}, bf16[392,128]{1,0:T(8,128)(2,1)S(1)}, u32[]{:S(2)}, u32[]{:S(2)}) %collective-permute-start.15) | collective-permute-done | bytes 100384 | tf_op jit(solution)/shard_map/ppermute | solution.py:378
  57.1 1.6 %final.1 = (f32[384,768]{1,0:T(8,128)}, f32[24,16,256]{2,1,0:T(8,128)}) custom-call(bf16[392,128]{1,0:T(8,128)(2,1)S(1)} %pad_maximum_fusion.refs_0_, bf16[392,128]{1,0:T(8,128)(2,1)S(1)} %collective-permute-done.10.refs_1_, bf16[392,128]{1,0:T(8,128)(2,1)S(1)} %collective-permute-done.11.refs_2_, bf16[392,128]{1,0:T(8,128)(2,1)S(1)} %collective-permute-done.12.refs_3_, ...), custom_call_target="tpu_custom_call" | custom-call | tf_op jit(solution)/shard_map/final/pallas_call | solution.py:381
  (35 shorter events, 1.7 us)
Async XLA Ops:
  0.6 8.1 %collective-permute-start = (bf16[896,768]{1,0:T(8,128)(2,1)}, bf16[896,768]{1,0:T(8,128)(2,1)S(1)}, u32[]{:S(2)}, u32[]{:S(2)}) collective-permute-start(bf16[896,768]{1,0:T(8,128)(2,1)} %refs_3_.3), channel_id=1, source_target_pairs={{0,1},{1,0},{2,3},{3,2},{4,5},{5,4},{6,7},{7,6},{8,9},{9,8},{10,11... | collective-permute-start | bytes 4128776 | tf_op jit(solution)/shard_map/ppermute | solution.py:269
  2.1 9.8 %collective-permute-start.1 = (f32[12,16,256]{2,1,0:T(8,128)S(1)}, f32[12,16,256]{2,1,0:T(8,128)S(1)}, u32[]{:S(2)}, u32[]{:S(2)}) collective-permute-start(f32[12,16,256]{2,1,0:T(8,128)S(1)} %dynamic-slice_bitcast_fusion), channel_id=1, source_target_pairs={{0,2},{2,0},{1,3},{3,1},{4,6},{6,4},{5,7},{7,5},{8,10},{10,8},{9,1... | collective-permute-start | bytes 589832 | tf_op jit(solution)/shard_map/ppermute | solution.py:268
  4.7 1.3 %copy-start = (bf16[896,768]{1,0:T(8,128)(2,1)S(1)}, bf16[896,768]{1,0:T(8,128)(2,1)}, u32[]{:S(2)}) copy-start(bf16[896,768]{1,0:T(8,128)(2,1)} %refs_3_.3) | copy-start | bytes 4128772
  6.0 1.3 %copy-start.2 = (bf16[768,768]{1,0:T(8,128)(2,1)S(1)}, bf16[768,768]{1,0:T(8,128)(2,1)}, u32[]{:S(2)}) copy-start(bf16[768,768]{1,0:T(8,128)(2,1)} %rot_ref.1) | copy-start | bytes 3538948
  8.7 1.0 %copy-start.3 = (f32[24,256,16]{1,2,0:T(8,128)S(1)}, f32[24,256,16]{1,2,0:T(8,128)}, u32[]{:S(2)}) copy-start(f32[24,256,16]{1,2,0:T(8,128)} %param.5) | copy-start | bytes 1179652
  9.7 2.3 %copy-start.1 = (bf16[896,768]{1,0:T(8,128)(2,1)S(1)}, bf16[896,768]{1,0:T(8,128)(2,1)}, u32[]{:S(2)}) copy-start(bf16[896,768]{1,0:T(8,128)(2,1)} %refs_3_.3) | copy-start | bytes 4128772
  20.6 8.6 %collective-permute-start.2 = (bf16[992,128]{1,0:T(8,128)(2,1)S(1)}, bf16[992,128]{1,0:T(8,128)(2,1)S(1)}, u32[]{:S(2)}, u32[]{:S(2)}) collective-permute-start(bf16[992,128]{1,0:T(8,128)(2,1)S(1)} %get-tuple-element.48), channel_id=1, source_target_pairs={{0,2},{2,0},{1,3},{3,1},{4,6},{6,4},{5,7},{7,5},{8,10},{10,8},{9,1... | collective-permute-start | bytes 761864 | tf_op jit(solution)/shard_map/ppermute | solution.py:335
  20.7 13.1 %collective-permute-start.4 = (bf16[192,896]{1,0:T(8,128)(2,1)S(1)}, bf16[192,896]{1,0:T(8,128)(2,1)S(1)}, u32[]{:S(2)}, u32[]{:S(2)}) collective-permute-start(bf16[192,896]{1,0:T(8,128)(2,1)S(1)} %get-tuple-element.52), channel_id=1, source_target_pairs={{0,1},{1,0},{2,3},{3,2},{4,5},{5,4},{6,7},{7,6},{8,9},{9,8},{10,11... | collective-permute-start | bytes 1032200 | tf_op jit(solution)/shard_map/ppermute | solution.py:336
  27.5 6.3 %collective-permute-start.3 = (bf16[576,128]{1,0:T(8,128)(2,1)S(1)}, bf16[576,128]{1,0:T(8,128)(2,1)S(1)}, u32[]{:S(2)}, u32[]{:S(2)}) collective-permute-start(bf16[576,128]{1,0:T(8,128)(2,1)S(1)} %get-tuple-element.51), channel_id=1, source_target_pairs={{0,2},{2,0},{1,3},{3,1},{4,6},{6,4},{5,7},{7,5},{8,10},{10,8},{9,1... | collective-permute-start | bytes 442376 | tf_op jit(solution)/shard_map/ppermute | solution.py:338
  29.4 6.4 %collective-permute-start.5 = (bf16[2,248,128]{2,1,0:T(8,128)(2,1)S(1)}, bf16[2,248,128]{2,1,0:T(8,128)(2,1)S(1)}, u32[]{:S(2)}, u32[]{:S(2)}) collective-permute-start(bf16[2,248,128]{2,1,0:T(8,128)(2,1)S(1)} %get-tuple-element.54), channel_id=1, source_target_pairs={{0,4},{4,0},{8,12},{12,8},{1,5},{5,1},{9,13},{13,9},{2,6},{6,2},{1... | collective-permute-start | bytes 380936 | tf_op jit(solution)/shard_map/ppermute | solution.py:249
  33.8 4.6 %collective-permute-start.7 = (bf16[2,144,128]{2,1,0:T(8,128)(2,1)S(1)}, bf16[2,144,128]{2,1,0:T(8,128)(2,1)S(1)}, u32[]{:S(2)}, u32[]{:S(2)}) collective-permute-start(bf16[2,144,128]{2,1,0:T(8,128)(2,1)S(1)} %get-tuple-element.58), channel_id=1, source_target_pairs={{0,4},{4,0},{8,12},{12,8},{1,5},{5,1},{9,13},{13,9},{2,6},{6,2},{1... | collective-permute-start | bytes 221192 | tf_op jit(solution)/shard_map/ppermute | solution.py:249
  35.7 2.8 %collective-permute-start.8 = (bf16[192,896]{1,0:T(8,128)(2,1)S(1)}, bf16[192,896]{1,0:T(8,128)(2,1)S(1)}, u32[]{:S(2)}, u32[]{:S(2)}) collective-permute-start(bf16[192,896]{1,0:T(8,128)(2,1)S(1)} %get-tuple-element.59), channel_id=1, source_target_pairs={{0,1},{1,0},{2,3},{3,2},{4,5},{5,4},{6,7},{7,6},{8,9},{9,8},{10,11... | collective-permute-start | bytes 1032200 | tf_op jit(solution)/shard_map/ppermute | solution.py:361
  35.8 7.3 %collective-permute-start.6 = (bf16[248,128]{1,0:T(8,128)(2,1)S(1)}, bf16[248,128]{1,0:T(8,128)(2,1)S(1)}, u32[]{:S(2)}, u32[]{:S(2)}) collective-permute-start(bf16[248,128]{1,0:T(8,128)(2,1)S(1)} %fusion.4), channel_id=1, source_target_pairs={{0,8},{4,12},{8,0},{12,4},{1,9},{5,13},{9,1},{13,5},{2,10},{6,14},... | collective-permute-start | bytes 190472 | tf_op jit(solution)/shard_map/ppermute | solution.py:249
  38.5 6.2 %collective-permute-start.9 = (bf16[144,128]{1,0:T(8,128)(2,1)S(1)}, bf16[144,128]{1,0:T(8,128)(2,1)S(1)}, u32[]{:S(2)}, u32[]{:S(2)}) collective-permute-start(bf16[144,128]{1,0:T(8,128)(2,1)S(1)} %fusion.5), channel_id=1, source_target_pairs={{0,8},{4,12},{8,0},{12,4},{1,9},{5,13},{9,1},{13,5},{2,10},{6,14},... | collective-permute-start | bytes 110600 | tf_op jit(solution)/shard_map/ppermute | solution.py:249
  44.8 5.6 %collective-permute-start.12 = (bf16[392,128]{1,0:T(8,128)(2,1)S(1)}, bf16[392,128]{1,0:T(8,128)(2,1)S(1)}, u32[]{:S(2)}, u32[]{:S(2)}) collective-permute-start(bf16[392,128]{1,0:T(8,128)(2,1)S(1)} %pad_maximum_fusion.refs_0_), channel_id=1, source_target_pairs={{0,4},{4,0},{8,12},{12,8},{1,5},{5,1},{9,13},{13,9},{2,6},{6,2},{1... | collective-permute-start | bytes 301064 | tf_op jit(solution)/shard_map/ppermute | solution.py:249
  45.2 10.5 %collective-permute-start.11 = (bf16[392,128]{1,0:T(8,128)(2,1)S(1)}, bf16[392,128]{1,0:T(8,128)(2,1)S(1)}, u32[]{:S(2)}, u32[]{:S(2)}) collective-permute-start(bf16[392,128]{1,0:T(8,128)(2,1)S(1)} %pad_maximum_fusion.refs_0_), channel_id=1, source_target_pairs={{0,8},{4,12},{8,0},{12,4},{1,9},{5,13},{9,1},{13,5},{2,10},{6,14},... | collective-permute-start | bytes 301064 | tf_op jit(solution)/shard_map/ppermute | solution.py:249
  48.2 7.4 %collective-permute-start.10 = (bf16[392,128]{1,0:T(8,128)(2,1)S(1)}, bf16[392,128]{1,0:T(8,128)(2,1)S(1)}, u32[]{:S(2)}, u32[]{:S(2)}) collective-permute-start(bf16[392,128]{1,0:T(8,128)(2,1)S(1)} %pad_maximum_fusion.refs_0_), channel_id=1, source_target_pairs={{0,12},{4,8},{8,4},{12,0},{1,13},{5,9},{9,5},{13,1},{2,14},{6,10},... | collective-permute-start | bytes 301064 | tf_op jit(solution)/shard_map/ppermute | solution.py:249
  49.2 6.9 %collective-permute-start.13 = (bf16[392,128]{1,0:T(8,128)(2,1)S(1)}, bf16[392,128]{1,0:T(8,128)(2,1)S(1)}, u32[]{:S(2)}, u32[]{:S(2)}) collective-permute-start(bf16[392,128]{1,0:T(8,128)(2,1)S(1)} %pad_maximum_fusion.refs_0_), channel_id=1, source_target_pairs={{0,1},{1,0},{2,3},{3,2},{4,5},{5,4},{6,7},{7,6},{8,9},{9,8},{10,11... | collective-permute-start | bytes 301064 | tf_op jit(solution)/shard_map/ppermute | solution.py:378
  50.4 5.8 %collective-permute-start.16 = (bf16[392,128]{1,0:T(8,128)(2,1)S(1)}, bf16[392,128]{1,0:T(8,128)(2,1)S(1)}, u32[]{:S(2)}, u32[]{:S(2)}) collective-permute-start(bf16[392,128]{1,0:T(8,128)(2,1)S(1)} %collective-permute-done.12.refs_3_), channel_id=1, source_target_pairs={{0,1},{1,0},{2,3},{3,2},{4,5},{5,4},{6,7},{7,6},{8,9},{9,8},{10,11... | collective-permute-start | bytes 301064 | tf_op jit(solution)/shard_map/ppermute | solution.py:378
  55.6 1.3 %collective-permute-start.15 = (bf16[392,128]{1,0:T(8,128)(2,1)S(1)}, bf16[392,128]{1,0:T(8,128)(2,1)S(1)}, u32[]{:S(2)}, u32[]{:S(2)}) collective-permute-start(bf16[392,128]{1,0:T(8,128)(2,1)S(1)} %collective-permute-done.11.refs_2_), channel_id=1, source_target_pairs={{0,1},{1,0},{2,3},{3,2},{4,5},{5,4},{6,7},{7,6},{8,9},{9,8},{10,11... | collective-permute-start | bytes 301064 | tf_op jit(solution)/shard_map/ppermute | solution.py:378
  55.6 1.5 %collective-permute-start.14 = (bf16[392,128]{1,0:T(8,128)(2,1)S(1)}, bf16[392,128]{1,0:T(8,128)(2,1)S(1)}, u32[]{:S(2)}, u32[]{:S(2)}) collective-permute-start(bf16[392,128]{1,0:T(8,128)(2,1)S(1)} %collective-permute-done.10.refs_1_), channel_id=1, source_target_pairs={{0,1},{1,0},{2,3},{3,2},{4,5},{5,4},{6,7},{7,6},{8,9},{9,8},{10,11... | collective-permute-start | bytes 301064 | tf_op jit(solution)/shard_map/ppermute | solution.py:378

commit v8 on v7

--- a/solution.py
+++ b/solution.py
@@ -14,6 +14,8 @@
 F32, BF16 = jnp.float32, jnp.bfloat16
 VMEM_BYTES = 24 * 2**20
 HEAD = 3
+SCATTER = (3, 2, 1)
+GATHER = (1, 3, 2)
 
 
 def quantize_rows(block, codebook):
@@ -83,9 +85,7 @@
     row = lax.broadcasted_iota(jnp.int32, (SUBDIM, codes), 0)
     norms = jnp.where(row == 0, n_hi, jnp.where(row == 1, n_mid, jnp.where(row == 2, n_lo, 0.0)))
     a = jnp.concatenate([hi, mid, lo, norms], axis=0).T.astype(BF16)
-    c_hi = c.astype(BF16)
-    c_lo = (c - c_hi.astype(F32)).astype(BF16)
-    b = jnp.concatenate([c_hi, c_lo, jnp.ones((SUBDIM, codes), BF16)], axis=0)
+    b = jnp.concatenate([c.astype(BF16), jnp.ones((SUBDIM, codes), BF16)], axis=0)
     return a, b
 
 
@@ -100,18 +100,18 @@
     halves = codes // lanes
     whole = last == per
     base = r * per if k == 0 else 0
-    if whole:
+    if not whole:
+        rec0_ref, rec1_ref, sums_ref, cnt = refs
+        p_rows = 0
+    else:
         v0_ref, v1_ref, *refs = refs
         part = v0_ref.shape[1] // 2
         p_rows = (part // lanes) * w
-        if first:
+        if k == 1:
+            head0_ref, head1_ref, rec0_ref, rec1_ref, keep_ref, send_ref, also_ref, cnt = refs
+        else:
             *head, rec0_ref, rec1_ref, keep_ref, send_ref, cnt = refs
-        else:
-            rec0_ref, rec1_ref, keep_ref, send_ref, cnt = refs
         sums_ref = keep_ref if k == 0 else send_ref
-    else:
-        rec0_ref, rec1_ref, sums_ref, cnt = refs
-        p_rows = 0
     stride = w if whole else last * SUBDIM
     ones = jnp.ones((SUBDIM, cols), BF16)
     ys, recs = (y0_ref, y1_ref), (rec0_ref, rec1_ref)
@@ -138,8 +138,8 @@
 
     def rebuild(j, i, y, e):
         out = jnp.dot(ab[j][1], e, preferred_element_type=F32)
-        inv = 1.0 / out[2 * SUBDIM :]
-        recs[i][SUBDIM * j : SUBDIM * (j + 1), :] = ((out[:SUBDIM] + out[SUBDIM : 2 * SUBDIM]) * inv).astype(BF16)
+        inv = 1.0 / out[SUBDIM:]
+        recs[i][SUBDIM * j : SUBDIM * (j + 1), :] = (out[:SUBDIM] * inv).astype(BF16)
         return jnp.concatenate([(y.astype(F32) * inv).astype(BF16), inv.astype(BF16)], axis=0)
 
     def gather(j, i, yz, e):
@@ -167,17 +167,31 @@
 
     at = p_rows + halves * w
     sums_ref[at : at + cnt.shape[0], :] = cnt[...].astype(sums_ref.dtype)
-    cross = jnp.dot(rec0_ref[...], v0_ref[...], preferred_element_type=F32) + jnp.dot(
-        rec1_ref[...], v1_ref[...], preferred_element_type=F32
+    at_head = at + cnt.shape[0]
+    done = first * SUBDIM
+    early = HEAD * SUBDIM
+    cross = jnp.dot(rec0_ref[done:, :], v0_ref[...], preferred_element_type=F32) + jnp.dot(
+        rec1_ref[done:, :], v1_ref[...], preferred_element_type=F32
     )
+    if k == 1:
+        ahead = jnp.dot(head0_ref[...], v0_ref[...], preferred_element_type=F32) + jnp.dot(
+            head1_ref[...], v1_ref[...], preferred_element_type=F32
+        )
+    size = w - done
     for h in range(2):
         @pl.when(s == h)
         def _():
             for g in range(part // lanes):
-                near = h * part + g * lanes
-                far = (1 - h) * part + g * lanes
-                keep_ref[g * w : (g + 1) * w, :] = cross[:, near : near + lanes]
-                send_ref[g * w : (g + 1) * w, :] = cross[:, far : far + lanes].astype(BF16)
+                near = slice(h * part + g * lanes, h * part + (g + 1) * lanes)
+                away = slice((1 - h) * part + g * lanes, (1 - h) * part + (g + 1) * lanes)
+                keep_ref[g * w + done : (g + 1) * w, :] = cross[:, near]
+                send_ref[g * size : (g + 1) * size, :] = cross[:, away].astype(BF16)
+                if k == 1:
+                    at = at_head + g * early
+                    also_ref[g * early : (g + 1) * early, :] = ahead[:, near]
+                    send_ref[at : at + early, :] = ahead[:, away].astype(BF16)
+                elif done:
+                    keep_ref[g * w : g * w + done, :] = head[4][g * early : (g + 1) * early, :]
 
 
 def turn_kernel(m0_ref, m1_ref, t0_ref, t1_ref, out_ref, buf):
@@ -202,7 +216,7 @@
     for side in range(2):
         for i in range(n):
             ref = pieces[side * n + i]
-            source = z ^ ((n - i) % n)
+            source = z ^ ((0,) + GATHER)[i]
             buf[side, pl.ds(pl.multiple_of(source * near, 8), near), :] = ref[:near].astype(F32)
             buf[side, pl.ds(pl.multiple_of(near_rows + source * far, 8), far), :] = ref[near:].astype(F32)
 
@@ -236,13 +250,27 @@
         copy.wait()
 
 
-def pieces_kernel(kept_ref, got_ref, own_ref, sent_ref, total):
+def pieces_kernel(kept_ref, got_ref, *refs, n, late):
+    if late:
+        first_ref, *refs = refs
+    outs, total = refs[:n], refs[n]
     z = lax.axis_index("row")
-    total[...] = kept_ref[...] + got_ref[...].astype(F32)
-    size = own_ref.shape[1]
-    for i in range(2):
-        own_ref[i] = total[pl.ds(pl.multiple_of((z ^ (2 * i)) * size, 8), size), :]
-        sent_ref[i] = total[pl.ds(pl.multiple_of((z ^ (2 * i + 1)) * size, 8), size), :].astype(BF16)
+    rows = kept_ref.shape[0]
+    if late:
+        early = HEAD * SUBDIM
+        groups = (first_ref.shape[0] - late) // early
+        w = rows // groups
+        for g in range(groups):
+            a, b = g * w, g * w + early
+            c = late + g * early
+            total[a:b, :] = kept_ref[a:b, :] + first_ref[c : c + early, :].astype(F32)
+            c = g * (w - early)
+            total[b : a + w, :] = kept_ref[b : a + w, :] + got_ref[c : c + w - early, :].astype(F32)
+    else:
+        total[...] = kept_ref[...] + got_ref[:rows, :].astype(F32)
+    size = outs[0].shape[0]
+    for out, d in zip(outs, (0,) + SCATTER):
+        out[...] = total[pl.ds(pl.multiple_of((z ^ d) * size, 8), size), :].astype(out.dtype)
 
 
 def exchange(x, n, d):
@@ -295,73 +323,52 @@
             bytes_accessed=2**23,
         )
 
-    def quantize(k, cb_k, first=0, head=()):
-        n_keep, n_send = (p_rows + s_rows, p_rows) if k == 0 else (p_rows, p_rows + s_rows)
+    groups = part // lanes
+    early = HEAD * SUBDIM
+
+    def quantize(k, cb_k, *head):
+        n_keep, n_send = (p_rows + s_rows, p_rows - groups * early) if k == 0 else (p_rows, p_rows + s_rows + groups * early)
+        out_shape = [
+            rec_shape,
+            rec_shape,
+            jax.ShapeDtypeStruct((n_keep, lanes), F32),
+            jax.ShapeDtypeStruct((n_send, lanes), BF16),
+        ] + [jax.ShapeDtypeStruct((groups * early, lanes), F32)] * k
+        first = 0 if k else HEAD
         return pl.pallas_call(
             functools.partial(quantize_kernel, k=k, per=per, first=first, last=per),
             in_specs=[vmem] * (5 + len(head)),
-            out_specs=[vmem] * 4,
-            out_shape=[
-                rec_shape,
-                rec_shape,
-                jax.ShapeDtypeStruct((n_keep, lanes), F32),
-                jax.ShapeDtypeStruct((n_send, lanes), BF16),
-            ],
+            out_specs=[vmem] * len(out_shape),
+            out_shape=out_shape,
             scratch_shapes=[pltpu.VMEM(cnt_shape, F32)],
             compiler_params=params,
             cost_estimate=cost(per - first, 1),
-            name="quantize_near" if k == 0 else "quantize_far",
+            name="quantize_far" if k else "quantize_near",
         )(cb_k, y0, y1, vectors, vec_far, *head)
 
-    head = ()
-    if HEAD:
-        early = jax.ShapeDtypeStruct((HEAD * SUBDIM, rows), BF16)
-        head = pl.pallas_call(
-            functools.partial(quantize_kernel, k=0, per=per, first=0, last=HEAD),
-            in_specs=[vmem] * 3,
-            out_specs=[vmem] * 4,
-            out_shape=[
-                early,
-                early,
-                jax.ShapeDtypeStruct(((codes // lanes) * HEAD * SUBDIM, lanes), F32),
-                jax.ShapeDtypeStruct(cnt_shape, F32),
-            ],
-            compiler_params=params,
-            cost_estimate=cost(HEAD, 0),
-            name="quantize_head",
-        )(cb, y0, y1)
-        cb_far, *head = lax.optimization_barrier((cb_far, *head))
-    mine1, other1, keep1, send1 = quantize(1, cb_far)
+    early_shape = jax.ShapeDtypeStruct((early, rows), BF16)
+    head = pl.pallas_call(
+        functools.partial(quantize_kernel, k=0, per=per, first=0, last=HEAD),
+        in_specs=[vmem] * 3,
+        out_specs=[vmem] * 4,
+        out_shape=[
+            early_shape,
+            early_shape,
+            jax.ShapeDtypeStruct(((codes // lanes) * early, lanes), F32),
+            jax.ShapeDtypeStruct(cnt_shape, F32),
+        ],
+        compiler_params=params,
+        cost_estimate=cost(HEAD, 0),
+        name="quantize_head",
+    )(cb, y0, y1)
+
+    mine1, other1, keep1, send1, ahead = quantize(1, cb_far, *head[:2])
     got1 = lax.ppermute(send1, "sub", swap)
     theirs1 = lax.ppermute(other1, "rep", swap)
-    mine0, other0, keep0, send0 = quantize(0, cb, HEAD, head)
+    mine0, other0, keep0, send0 = quantize(0, cb, *head, ahead)
     got0 = lax.ppermute(send0, "sub", swap)
-
-    def scatter(kept, got):
-        size = (2, kept.shape[0] // rows_n, lanes)
-        return pl.pallas_call(
-            pieces_kernel,
-            out_shape=[jax.ShapeDtypeStruct(size, F32), jax.ShapeDtypeStruct(size, BF16)],
-            in_specs=[vmem] * 2,
-            out_specs=[vmem] * 2,
-            scratch_shapes=[pltpu.VMEM(kept.shape, F32)],
-            compiler_params=small,
-            name="pieces",
-        )(kept, got)
-
-    def pair(own, sent):
-        both = own + exchange(sent, rows_n, 1).astype(F32)
-        return both[0], both[1].astype(BF16)
-
-    def finish(own, sent):
-        return (own + exchange(sent, rows_n, 2).astype(F32)).astype(BF16)
-
-    near_own, near_sent = scatter(keep0, got1)
-    near_own, other0, got0, theirs1 = lax.optimization_barrier((near_own, other0, got0, theirs1))
     theirs0 = lax.ppermute(other0, "rep", swap)
-    near = pair(near_own, near_sent)
-    far_own, far_sent = pair(*scatter(keep1, got0))
-    far_sent, theirs0 = lax.optimization_barrier((far_sent, theirs0))
+
     reconstruction = pl.pallas_call(
         turn_kernel,
         out_shape=jax.ShapeDtypeStruct((rows, width), BF16),
@@ -371,10 +378,28 @@
         compiler_params=small,
         name="turn",
     )(mine0, mine1, theirs0, theirs1)
-    summed = jnp.concatenate([finish(*near), finish(far_own, far_sent)], axis=0)
+
+    def scatter(kept, got, *more):
+        size = (kept.shape[0] // rows_n, lanes)
+        own, *sent = pl.pallas_call(
+            functools.partial(pieces_kernel, n=rows_n, late=p_rows + s_rows if more else 0),
+            out_shape=[jax.ShapeDtypeStruct(size, F32)] + [jax.ShapeDtypeStruct(size, BF16)] * (rows_n - 1),
+            in_specs=[vmem] * (2 + len(more)),
+            out_specs=[vmem] * rows_n,
+            scratch_shapes=[pltpu.VMEM(kept.shape, F32)],
+            compiler_params=small,
+            name="pieces",
+        )(kept, got, *more)
+        return [own] + [exchange(x, rows_n, d) for x, d in zip(sent, SCATTER)]
+
+    def add_up(parts):
+        return functools.reduce(lambda a, b: a + b.astype(F32), parts[1:], parts[0]).astype(BF16)
+
+    near = scatter(keep0, got1)
+    near[0], got0, theirs1 = lax.optimization_barrier((near[0], got0, theirs1))
+    summed = jnp.concatenate([add_up(near), add_up(scatter(keep1, got0, got1))], axis=0)
     summed, reconstruction = lax.optimization_barrier((summed, reconstruction))
-    apart = range(rows_n - 1, 0, -1)
-    mine = [summed] + [exchange(summed, rows_n, d) for d in apart]
+    mine = [summed] + [exchange(summed, rows_n, d) for d in GATHER]
     theirs = [lax.ppermute(x, "rep", swap) for x in mine]
 
     any_spec = pl.BlockSpec(memory_space=pl.ANY)

time: 59.1 us -> 57.3 us (0.970)
  waiting for transfers between devices: 11.4 us -> 9.86 us
    ppermute x1, waiting for transfers between devices: 2.79 us -> 0.01 us  [on_device(): got0 = lax.ppermute(send0, 'sub', swap)]
    ppermute x7 -> x9, waiting for transfers between devices: 7.67 us -> 8.74 us  [exchange(): return lax.ppermute(x, 'row', [(i, i ^ d) for i in range(n)])]
    ppermute x7 -> x9, starting transfers between devices: 14 us -> 13.3 us  [exchange(): return lax.ppermute(x, 'row', [(i, i ^ d) for i in range(n)])]
  transfers between devices with their start and end apart: 17 -> 19, of which waited for: 6 -> 7; matrix products, arithmetic and copies ran while one was open for 2% -> 2% of each run, Pallas kernels for 22% -> 22%
where the time goes in v8:
time: 57.3 us; the launch traced here: 57 us
  Pallas kernels  23.3 us (41%)
  starting transfers between devices  19.3 us (34%)
  waiting for transfers between devices  9.86 us (17%)
  local copies, waits for them, and re-layouts  3.59 us (6%)
  between operations  0.92 us (2%)
    pallas_call x2, Pallas kernels, quantize(): pl.pallas_call(functools.partial(quantize_kernel, k=k, per=per, first=fir...  15.5 us
    ppermute x9, starting transfers between devices, exchange(): return lax.ppermute(x, 'row', [(i, i ^ d) for i in range(n)])  13.3 us
    ppermute x9, waiting for transfers between devices, exchange(): return lax.ppermute(x, 'row', [(i, i ^ d) for i in range(n)])  8.74 us
    unnamed x8, local copies, waits for them, and re-layouts  2.65 us
    ppermute x1, starting transfers between devices, on_device(): cb_far = lax.ppermute(cb_sent, 'sub', swap)  2.58 us
    pallas_call x1, Pallas kernels, on_device(): pl.pallas_call(functools.partial(quantize_kernel, k=0, per=per, first=0,...  2.13 us
    ppermute x1, starting transfers between devices, on_device(): got0 = lax.ppermute(send0, 'sub', swap)  1.95 us
    pallas_call x1, Pallas kernels, on_device(): pl.pallas_call(turn_kernel, out_shape=jax.ShapeDtypeStruct((rows, width),...  1.61 us
  transfers between devices with their start and end apart: 19, of which 7 were waited for; matrix products, arithmetic and copies ran while one was open for 2% of the time, Pallas kernels for 22%

profile of v8, /device:TPU:0, one launch (start us, length us, event | category | flops | bytes accessed | tf_op | source)
XLA Modules:
  0.0 57.0 jit_solution(13485200922900609453)
XLA Ops:
  0.6 0.5 collective-permute-start
  1.1 0.9 %dynamic-slice_bitcast_fusion = f32[12,16,256]{2,1,0:T(8,128)S(1)} fusion(f32[24,256,16]{1,2,0:T(8,128)} %param.5, s32[]{:T(128)S(6)} %select_n.3), kind=kLoop, calls=%fused_computation | loop fusion | bytes 393220 | tf_op jit(solution)/shard_map/dynamic_slice | solution.py:295
  2.1 2.6 %collective-permute-start.1 = (f32[12,16,256]{2,1,0:T(8,128)S(1)}, f32[12,16,256]{2,1,0:T(8,128)S(1)}, u32[]{:S(2)}, u32[]{:S(2)}) collective-permute-start(f32[12,16,256]{2,1,0:T(8,128)S(1)} %dynamic-slice_bitcast_fusion), channel_id=1, source_target_pairs={{0,2},{2,0},{1,3},{3,1},{4,6},{6,4},{5,7},{7,5},{8,10},{10,8},{9,1... | collective-permute-start | bytes 589832 | tf_op jit(solution)/shard_map/ppermute | solution.py:296
  4.7 1.3 %copy-done = bf16[896,768]{1,0:T(8,128)(2,1)S(1)} copy-done((bf16[896,768]{1,0:T(8,128)(2,1)S(1)}, bf16[896,768]{1,0:T(8,128)(2,1)}, u32[]{:S(2)}) %copy-start) | copy-done | bytes 1376280
  6.0 1.3 %copy-done.2 = bf16[768,768]{1,0:T(8,128)(2,1)S(1)} copy-done((bf16[768,768]{1,0:T(8,128)(2,1)S(1)}, bf16[768,768]{1,0:T(8,128)(2,1)}, u32[]{:S(2)}) %copy-start.2) | copy-done | bytes 1179672
  7.3 1.4 %rotate.1 = (bf16[2,192,896]{2,1,0:T(8,128)(2,1)S(1)}, bf16[2,192,768]{2,1,0:T(8,128)(2,1)S(1)}) custom-call(bf16[896,768]{1,0:T(8,128)(2,1)S(1)} %copy-done, bf16[768,768]{1,0:T(8,128)(2,1)S(1)} %copy-done.2), custom_call_target="tpu_custom_call" | custom-call | tf_op jit(solution)/shard_map/rotate/pallas_call | solution.py:300
  8.7 1.0 %rotate_far.1.refs_2_ = bf16[2,192,896]{2,1,0:T(8,128)(2,1)S(1)} custom-call(bf16[896,768]{1,0:T(8,128)(2,1)S(1)} %collective-permute-done.vec_ref.refs_4_, bf16[2,192,768]{2,1,0:T(8,128)(2,1)S(1)} %get-tuple-element.33.rott_ref), custom_call_target="tpu_custom_call" | custom-call | tf_op jit(solution)/shard_map/rotate_far/pallas_call | solution.py:309
  9.7 2.1 %quantize_head.1 = (bf16[48,896]{1,0:T(8,128)(2,1)S(1)}, bf16[48,896]{1,0:T(8,128)(2,1)S(1)}, f32[96,128]{1,0:T(8,128)S(1)}, f32[32,128]{1,0:T(8,128)S(1)}) custom-call(f32[24,16,256]{2,1,0:T(8,128)S(1)} %bitcast.4, bf16[2,192,896]{2,1,0:T(8,128)(2,1)S(1)} %get-tuple-element.32.refs_1_, bf16[2,192,896]{2,1,0:T(8,128)(2,1)S(1)} %rotate_far.1.refs_2_), custom_call_target="tpu_custom_call" | custom-call | flops 396361728 | bytes 8388608 | tf_op jit(solution)/shard_map/quantize_head/pallas_call | solution.py:350
  11.9 9.0 %quantize_far.1 = (bf16[192,896]{1,0:T(8,128)(2,1)S(1)}, bf16[192,896]{1,0:T(8,128)(2,1)S(1)}, f32[576,128]{1,0:T(8,128)S(1)}, bf16[1136,128]{1,0:T(8,128)(2,1)S(1)}, f32[144,128]{1,0:T(8,128)S(1)}) custom-call(f32[12,16,256]{2,1,0:T(8,128)S(1)} %collective-permute-done.1.refs_0_, bf16[2,192,896]{2,1,0:T(8,128)(2,1)S(1)} %get-tuple-element.32.refs_1_, ...), custom_call_target="tpu_custom_call" | custom-call | flops 2113929216 | bytes 8388608 | tf_op jit(solution)/shard_map/quantize_far/pallas_call | solution.py:338
  21.3 6.5 %quantize_near.1 = (bf16[192,896]{1,0:T(8,128)(2,1)S(1)}, bf16[192,896]{1,0:T(8,128)(2,1)S(1)}, f32[992,128]{1,0:T(8,128)S(1)}, bf16[432,128]{1,0:T(8,128)(2,1)S(1)}) custom-call(f32[24,16,256]{2,1,0:T(8,128)S(1)} %bitcast.5, bf16[2,192,896]{2,1,0:T(8,128)(2,1)S(1)} %get-tuple-element.32.refs_1_, bf16[2,192,896]{2,1,0:T(8,128)(2,1)S(1)} %rotate_far.1.refs_2_, ...), custom_call_target="tpu_custom_call" | custom-call | flops 1717567488 | bytes 8388608 | tf_op jit(solution)/shard_map/quantize_near/pallas_call | solution.py:338
  28.1 2.0 %collective-permute-start.3 = (bf16[432,128]{1,0:T(8,128)(2,1)S(1)}, bf16[432,128]{1,0:T(8,128)(2,1)S(1)}, u32[]{:S(2)}, u32[]{:S(2)}) collective-permute-start(bf16[432,128]{1,0:T(8,128)(2,1)S(1)} %get-tuple-element.42), channel_id=1, source_target_pairs={{0,2},{2,0},{1,3},{3,1},{4,6},{6,4},{5,7},{7,5},{8,10},{10,8},{9,1... | collective-permute-start | bytes 331784 | tf_op jit(solution)/shard_map/ppermute | solution.py:369
  30.2 3.7 %collective-permute-start.5 = (bf16[248,128]{1,0:T(8,128)(2,1)S(1)}, bf16[248,128]{1,0:T(8,128)(2,1)S(1)}, u32[]{:S(2)}, u32[]{:S(2)}) collective-permute-start(bf16[248,128]{1,0:T(8,128)(2,1)S(1)} %get-tuple-element.45), channel_id=1, source_target_pairs={{0,12},{4,8},{8,4},{12,0},{1,13},{5,9},{9,5},{13,1},{2,14},{6,10},... | collective-permute-start | bytes 190472 | tf_op jit(solution)/shard_map/ppermute | solution.py:277
  33.9 1.4 %collective-permute-start.7 = (bf16[248,128]{1,0:T(8,128)(2,1)S(1)}, bf16[248,128]{1,0:T(8,128)(2,1)S(1)}, u32[]{:S(2)}, u32[]{:S(2)}) collective-permute-start(bf16[248,128]{1,0:T(8,128)(2,1)S(1)} %get-tuple-element.47), channel_id=1, source_target_pairs={{0,4},{4,0},{8,12},{12,8},{1,5},{5,1},{9,13},{13,9},{2,6},{6,2},{1... | collective-permute-start | bytes 190472 | tf_op jit(solution)/shard_map/ppermute | solution.py:277
  35.3 3.1 %collective-permute-start.8 = (bf16[144,128]{1,0:T(8,128)(2,1)S(1)}, bf16[144,128]{1,0:T(8,128)(2,1)S(1)}, u32[]{:S(2)}, u32[]{:S(2)}) collective-permute-start(bf16[144,128]{1,0:T(8,128)(2,1)S(1)} %get-tuple-element.51), channel_id=1, source_target_pairs={{0,12},{4,8},{8,4},{12,0},{1,13},{5,9},{9,5},{13,1},{2,14},{6,10},... | collective-permute-start | bytes 110600 | tf_op jit(solution)/shard_map/ppermute | solution.py:277
  38.4 1.6 %turn.1 = bf16[896,768]{1,0:T(8,128)(2,1)} custom-call(bf16[192,896]{1,0:T(8,128)(2,1)S(1)} %get-tuple-element.54.m0_ref, bf16[192,896]{1,0:T(8,128)(2,1)S(1)} %get-tuple-element.55.m1_ref, bf16[192,896]{1,0:T(8,128)(2,1)S(1)} %collective-permute-done.11.t0_ref, bf16[192,896]{1,0:T(8,128)(2,1)S(1)} %collective-permute-done.4.t1_ref), custom_call_target="tpu_custom_call" | custom-call | tf_op jit(solution)/shard_map/turn/pallas_call | solution.py:372
  40.0 1.4 %collective-permute-start.10 = (bf16[144,128]{1,0:T(8,128)(2,1)S(1)}, bf16[144,128]{1,0:T(8,128)(2,1)S(1)}, u32[]{:S(2)}, u32[]{:S(2)}) collective-permute-start(bf16[144,128]{1,0:T(8,128)(2,1)S(1)} %get-tuple-element.53), channel_id=1, source_target_pairs={{0,4},{4,0},{8,12},{12,8},{1,5},{5,1},{9,13},{13,9},{2,6},{6,2},{1... | collective-permute-start | bytes 110600 | tf_op jit(solution)/shard_map/ppermute | solution.py:277
  41.4 1.8 %collective-permute-done.9 = bf16[144,128]{1,0:T(8,128)(2,1)S(1)} collective-permute-done((bf16[144,128]{1,0:T(8,128)(2,1)S(1)}, bf16[144,128]{1,0:T(8,128)(2,1)S(1)}, u32[]{:S(2)}, u32[]{:S(2)}) %collective-permute-start.9) | collective-permute-done | bytes 36896 | tf_op jit(solution)/shard_map/ppermute | solution.py:277
  43.2 0.7 %collective-permute-done.10 = bf16[144,128]{1,0:T(8,128)(2,1)S(1)} collective-permute-done((bf16[144,128]{1,0:T(8,128)(2,1)S(1)}, bf16[144,128]{1,0:T(8,128)(2,1)S(1)}, u32[]{:S(2)}, u32[]{:S(2)}) %collective-permute-start.10) | collective-permute-done | bytes 36896 | tf_op jit(solution)/shard_map/ppermute | solution.py:277
  44.0 3.1 %collective-permute-start.14 = (bf16[392,128]{1,0:T(8,128)(2,1)S(1)}, bf16[392,128]{1,0:T(8,128)(2,1)S(1)}, u32[]{:S(2)}, u32[]{:S(2)}) collective-permute-start(bf16[392,128]{1,0:T(8,128)(2,1)S(1)} %pad_maximum_fusion.refs_0_), channel_id=1, source_target_pairs={{0,8},{4,12},{8,0},{12,4},{1,9},{5,13},{9,1},{13,5},{2,10},{6,14},... | collective-permute-start | bytes 301064 | tf_op jit(solution)/shard_map/ppermute | solution.py:277
  47.1 0.7 %collective-permute-start.13 = (bf16[392,128]{1,0:T(8,128)(2,1)S(1)}, bf16[392,128]{1,0:T(8,128)(2,1)S(1)}, u32[]{:S(2)}, u32[]{:S(2)}) collective-permute-start(bf16[392,128]{1,0:T(8,128)(2,1)S(1)} %pad_maximum_fusion.refs_0_), channel_id=1, source_target_pairs={{0,12},{4,8},{8,4},{12,0},{1,13},{5,9},{9,5},{13,1},{2,14},{6,10},... | collective-permute-start | bytes 301064 | tf_op jit(solution)/shard_map/ppermute | solution.py:277
  47.8 4.2 %collective-permute-done.14.refs_3_ = bf16[392,128]{1,0:T(8,128)(2,1)S(1)} collective-permute-done((bf16[392,128]{1,0:T(8,128)(2,1)S(1)}, bf16[392,128]{1,0:T(8,128)(2,1)S(1)}, u32[]{:S(2)}, u32[]{:S(2)}) %collective-permute-start.14) | collective-permute-done | bytes 100384 | tf_op jit(solution)/shard_map/ppermute | solution.py:277
  52.0 1.7 %collective-permute-done.13.refs_2_ = bf16[392,128]{1,0:T(8,128)(2,1)S(1)} collective-permute-done((bf16[392,128]{1,0:T(8,128)(2,1)S(1)}, bf16[392,128]{1,0:T(8,128)(2,1)S(1)}, u32[]{:S(2)}, u32[]{:S(2)}) %collective-permute-start.13) | collective-permute-done | bytes 100384 | tf_op jit(solution)/shard_map/ppermute | solution.py:277
  54.2 0.8 %collective-permute-done.17.refs_6_ = bf16[392,128]{1,0:T(8,128)(2,1)S(1)} collective-permute-done((bf16[392,128]{1,0:T(8,128)(2,1)S(1)}, bf16[392,128]{1,0:T(8,128)(2,1)S(1)}, u32[]{:S(2)}, u32[]{:S(2)}) %collective-permute-start.17) | collective-permute-done | bytes 100384 | tf_op jit(solution)/shard_map/ppermute | solution.py:403
  55.3 1.6 %final.1 = (f32[384,768]{1,0:T(8,128)}, f32[24,16,256]{2,1,0:T(8,128)}) custom-call(bf16[392,128]{1,0:T(8,128)(2,1)S(1)} %pad_maximum_fusion.refs_0_, bf16[392,128]{1,0:T(8,128)(2,1)S(1)} %collective-permute-done.12.refs_1_, bf16[392,128]{1,0:T(8,128)(2,1)S(1)} %collective-permute-done.13.refs_2_, bf16[392,128]{1,0:T(8,128)(2,1)S(1)} %collective-permute-done.14.refs_3_, ...), custom_call_target="tpu_custom_call" | custom-call | tf_op jit(solution)/shard_map/final/pallas_call | solution.py:406
  (35 shorter events, 1.8 us)
Async XLA Ops:
  0.6 8.1 %collective-permute-start = (bf16[896,768]{1,0:T(8,128)(2,1)}, bf16[896,768]{1,0:T(8,128)(2,1)S(1)}, u32[]{:S(2)}, u32[]{:S(2)}) collective-permute-start(bf16[896,768]{1,0:T(8,128)(2,1)} %refs_3_.3), channel_id=1, source_target_pairs={{0,1},{1,0},{2,3},{3,2},{4,5},{5,4},{6,7},{7,6},{8,9},{9,8},{10,11... | collective-permute-start | bytes 4128776 | tf_op jit(solution)/shard_map/ppermute | solution.py:297
  2.1 9.8 %collective-permute-start.1 = (f32[12,16,256]{2,1,0:T(8,128)S(1)}, f32[12,16,256]{2,1,0:T(8,128)S(1)}, u32[]{:S(2)}, u32[]{:S(2)}) collective-permute-start(f32[12,16,256]{2,1,0:T(8,128)S(1)} %dynamic-slice_bitcast_fusion), channel_id=1, source_target_pairs={{0,2},{2,0},{1,3},{3,1},{4,6},{6,4},{5,7},{7,5},{8,10},{10,8},{9,1... | collective-permute-start | bytes 589832 | tf_op jit(solution)/shard_map/ppermute | solution.py:296
  4.7 1.3 %copy-start = (bf16[896,768]{1,0:T(8,128)(2,1)S(1)}, bf16[896,768]{1,0:T(8,128)(2,1)}, u32[]{:S(2)}) copy-start(bf16[896,768]{1,0:T(8,128)(2,1)} %refs_3_.3) | copy-start | bytes 4128772
  6.0 1.3 %copy-start.2 = (bf16[768,768]{1,0:T(8,128)(2,1)S(1)}, bf16[768,768]{1,0:T(8,128)(2,1)}, u32[]{:S(2)}) copy-start(bf16[768,768]{1,0:T(8,128)(2,1)} %rot_ref.1) | copy-start | bytes 3538948
  8.7 1.0 %copy-start.3 = (f32[24,256,16]{1,2,0:T(8,128)S(1)}, f32[24,256,16]{1,2,0:T(8,128)}, u32[]{:S(2)}) copy-start(f32[24,256,16]{1,2,0:T(8,128)} %param.5) | copy-start | bytes 1179652
  9.7 2.2 %copy-start.1 = (bf16[896,768]{1,0:T(8,128)(2,1)S(1)}, bf16[896,768]{1,0:T(8,128)(2,1)}, u32[]{:S(2)}) copy-start(bf16[896,768]{1,0:T(8,128)(2,1)} %refs_3_.3) | copy-start | bytes 4128772
  20.9 9.2 %collective-permute-start.2 = (bf16[1136,128]{1,0:T(8,128)(2,1)S(1)}, bf16[1136,128]{1,0:T(8,128)(2,1)S(1)}, u32[]{:S(2)}, u32[]{:S(2)}) collective-permute-start(bf16[1136,128]{1,0:T(8,128)(2,1)S(1)} %get-tuple-element.40), channel_id=1, source_target_pairs={{0,2},{2,0},{1,3},{3,1},{4,6},{6,4},{5,7},{7,5},{8,10},{10,8},{9,1... | collective-permute-start | bytes 872456 | tf_op jit(solution)/shard_map/ppermute | solution.py:366
  21.0 14.2 %collective-permute-start.4 = (bf16[192,896]{1,0:T(8,128)(2,1)S(1)}, bf16[192,896]{1,0:T(8,128)(2,1)S(1)}, u32[]{:S(2)}, u32[]{:S(2)}) collective-permute-start(bf16[192,896]{1,0:T(8,128)(2,1)S(1)} %get-tuple-element.43), channel_id=1, source_target_pairs={{0,1},{1,0},{2,3},{3,2},{4,5},{5,4},{6,7},{7,6},{8,9},{9,8},{10,11... | collective-permute-start | bytes 1032200 | tf_op jit(solution)/shard_map/ppermute | solution.py:367
  27.8 10.6 %collective-permute-start.11 = (bf16[192,896]{1,0:T(8,128)(2,1)S(1)}, bf16[192,896]{1,0:T(8,128)(2,1)S(1)}, u32[]{:S(2)}, u32[]{:S(2)}) collective-permute-start(bf16[192,896]{1,0:T(8,128)(2,1)S(1)} %get-tuple-element.56), channel_id=1, source_target_pairs={{0,1},{1,0},{2,3},{3,2},{4,5},{5,4},{6,7},{7,6},{8,9},{9,8},{10,11... | collective-permute-start | bytes 1032200 | tf_op jit(solution)/shard_map/ppermute | solution.py:370
  28.1 5.7 %collective-permute-start.3 = (bf16[432,128]{1,0:T(8,128)(2,1)S(1)}, bf16[432,128]{1,0:T(8,128)(2,1)S(1)}, u32[]{:S(2)}, u32[]{:S(2)}) collective-permute-start(bf16[432,128]{1,0:T(8,128)(2,1)S(1)} %get-tuple-element.42), channel_id=1, source_target_pairs={{0,2},{2,0},{1,3},{3,1},{4,6},{6,4},{5,7},{7,5},{8,10},{10,8},{9,1... | collective-permute-start | bytes 331784 | tf_op jit(solution)/shard_map/ppermute | solution.py:369
  30.2 9.8 %collective-permute-start.5 = (bf16[248,128]{1,0:T(8,128)(2,1)S(1)}, bf16[248,128]{1,0:T(8,128)(2,1)S(1)}, u32[]{:S(2)}, u32[]{:S(2)}) collective-permute-start(bf16[248,128]{1,0:T(8,128)(2,1)S(1)} %get-tuple-element.45), channel_id=1, source_target_pairs={{0,12},{4,8},{8,4},{12,0},{1,13},{5,9},{9,5},{13,1},{2,14},{6,10},... | collective-permute-start | bytes 190472 | tf_op jit(solution)/shard_map/ppermute | solution.py:277
  33.9 7.5 %collective-permute-start.6 = (bf16[248,128]{1,0:T(8,128)(2,1)S(1)}, bf16[248,128]{1,0:T(8,128)(2,1)S(1)}, u32[]{:S(2)}, u32[]{:S(2)}) collective-permute-start(bf16[248,128]{1,0:T(8,128)(2,1)S(1)} %get-tuple-element.46), channel_id=1, source_target_pairs={{0,8},{4,12},{8,0},{12,4},{1,9},{5,13},{9,1},{13,5},{2,10},{6,14},... | collective-permute-start | bytes 190472 | tf_op jit(solution)/shard_map/ppermute | solution.py:277
  33.9 7.5 %collective-permute-start.7 = (bf16[248,128]{1,0:T(8,128)(2,1)S(1)}, bf16[248,128]{1,0:T(8,128)(2,1)S(1)}, u32[]{:S(2)}, u32[]{:S(2)}) collective-permute-start(bf16[248,128]{1,0:T(8,128)(2,1)S(1)} %get-tuple-element.47), channel_id=1, source_target_pairs={{0,4},{4,0},{8,12},{12,8},{1,5},{5,1},{9,13},{13,9},{2,6},{6,2},{1... | collective-permute-start | bytes 190472 | tf_op jit(solution)/shard_map/ppermute | solution.py:277
  35.3 6.1 %collective-permute-start.8 = (bf16[144,128]{1,0:T(8,128)(2,1)S(1)}, bf16[144,128]{1,0:T(8,128)(2,1)S(1)}, u32[]{:S(2)}, u32[]{:S(2)}) collective-permute-start(bf16[144,128]{1,0:T(8,128)(2,1)S(1)} %get-tuple-element.51), channel_id=1, source_target_pairs={{0,12},{4,8},{8,4},{12,0},{1,13},{5,9},{9,5},{13,1},{2,14},{6,10},... | collective-permute-start | bytes 110600 | tf_op jit(solution)/shard_map/ppermute | solution.py:277
  38.4 4.9 %collective-permute-start.9 = (bf16[144,128]{1,0:T(8,128)(2,1)S(1)}, bf16[144,128]{1,0:T(8,128)(2,1)S(1)}, u32[]{:S(2)}, u32[]{:S(2)}) collective-permute-start(bf16[144,128]{1,0:T(8,128)(2,1)S(1)} %get-tuple-element.52), channel_id=1, source_target_pairs={{0,8},{4,12},{8,0},{12,4},{1,9},{5,13},{9,1},{13,5},{2,10},{6,14},... | collective-permute-start | bytes 110600 | tf_op jit(solution)/shard_map/ppermute | solution.py:277
  40.0 4.0 %collective-permute-start.10 = (bf16[144,128]{1,0:T(8,128)(2,1)S(1)}, bf16[144,128]{1,0:T(8,128)(2,1)S(1)}, u32[]{:S(2)}, u32[]{:S(2)}) collective-permute-start(bf16[144,128]{1,0:T(8,128)(2,1)S(1)} %get-tuple-element.53), channel_id=1, source_target_pairs={{0,4},{4,0},{8,12},{12,8},{1,5},{5,1},{9,13},{13,9},{2,6},{6,2},{1... | collective-permute-start | bytes 110600 | tf_op jit(solution)/shard_map/ppermute | solution.py:277
  44.0 8.0 %collective-permute-start.14 = (bf16[392,128]{1,0:T(8,128)(2,1)S(1)}, bf16[392,128]{1,0:T(8,128)(2,1)S(1)}, u32[]{:S(2)}, u32[]{:S(2)}) collective-permute-start(bf16[392,128]{1,0:T(8,128)(2,1)S(1)} %pad_maximum_fusion.refs_0_), channel_id=1, source_target_pairs={{0,8},{4,12},{8,0},{12,4},{1,9},{5,13},{9,1},{13,5},{2,10},{6,14},... | collective-permute-start | bytes 301064 | tf_op jit(solution)/shard_map/ppermute | solution.py:277
  47.1 6.6 %collective-permute-start.13 = (bf16[392,128]{1,0:T(8,128)(2,1)S(1)}, bf16[392,128]{1,0:T(8,128)(2,1)S(1)}, u32[]{:S(2)}, u32[]{:S(2)}) collective-permute-start(bf16[392,128]{1,0:T(8,128)(2,1)S(1)} %pad_maximum_fusion.refs_0_), channel_id=1, source_target_pairs={{0,12},{4,8},{8,4},{12,0},{1,13},{5,9},{9,5},{13,1},{2,14},{6,10},... | collective-permute-start | bytes 301064 | tf_op jit(solution)/shard_map/ppermute | solution.py:277
  47.8 6.2 %collective-permute-start.12 = (bf16[392,128]{1,0:T(8,128)(2,1)S(1)}, bf16[392,128]{1,0:T(8,128)(2,1)S(1)}, u32[]{:S(2)}, u32[]{:S(2)}) collective-permute-start(bf16[392,128]{1,0:T(8,128)(2,1)S(1)} %pad_maximum_fusion.refs_0_), channel_id=1, source_target_pairs={{0,4},{4,0},{8,12},{12,8},{1,5},{5,1},{9,13},{13,9},{2,6},{6,2},{1... | collective-permute-start | bytes 301064 | tf_op jit(solution)/shard_map/ppermute | solution.py:277
  47.8 6.4 %collective-permute-start.15 = (bf16[392,128]{1,0:T(8,128)(2,1)S(1)}, bf16[392,128]{1,0:T(8,128)(2,1)S(1)}, u32[]{:S(2)}, u32[]{:S(2)}) collective-permute-start(bf16[392,128]{1,0:T(8,128)(2,1)S(1)} %pad_maximum_fusion.refs_0_), channel_id=1, source_target_pairs={{0,1},{1,0},{2,3},{3,2},{4,5},{5,4},{6,7},{7,6},{8,9},{9,8},{10,11... | collective-permute-start | bytes 301064 | tf_op jit(solution)/shard_map/ppermute | solution.py:403
  52.0 2.2 %collective-permute-start.18 = (bf16[392,128]{1,0:T(8,128)(2,1)S(1)}, bf16[392,128]{1,0:T(8,128)(2,1)S(1)}, u32[]{:S(2)}, u32[]{:S(2)}) collective-permute-start(bf16[392,128]{1,0:T(8,128)(2,1)S(1)} %collective-permute-done.14.refs_3_), channel_id=1, source_target_pairs={{0,1},{1,0},{2,3},{3,2},{4,5},{5,4},{6,7},{7,6},{8,9},{9,8},{10,11... | collective-permute-start | bytes 301064 | tf_op jit(solution)/shard_map/ppermute | solution.py:403
  53.7 1.3 %collective-permute-start.17 = (bf16[392,128]{1,0:T(8,128)(2,1)S(1)}, bf16[392,128]{1,0:T(8,128)(2,1)S(1)}, u32[]{:S(2)}, u32[]{:S(2)}) collective-permute-start(bf16[392,128]{1,0:T(8,128)(2,1)S(1)} %collective-permute-done.13.refs_2_), channel_id=1, source_target_pairs={{0,1},{1,0},{2,3},{3,2},{4,5},{5,4},{6,7},{7,6},{8,9},{9,8},{10,11... | collective-permute-start | bytes 301064 | tf_op jit(solution)/shard_map/ppermute | solution.py:403
  54.0 1.3 %collective-permute-start.16 = (bf16[392,128]{1,0:T(8,128)(2,1)S(1)}, bf16[392,128]{1,0:T(8,128)(2,1)S(1)}, u32[]{:S(2)}, u32[]{:S(2)}) collective-permute-start(bf16[392,128]{1,0:T(8,128)(2,1)S(1)} %collective-permute-done.12.refs_1_), channel_id=1, source_target_pairs={{0,1},{1,0},{2,3},{3,2},{4,5},{5,4},{6,7},{7,6},{8,9},{9,8},{10,11... | collective-permute-start | bytes 301064 | tf_op jit(solution)/shard_map/ppermute | solution.py:403

commit v9 on v8

--- a/solution.py
+++ b/solution.py
@@ -14,6 +14,7 @@
 F32, BF16 = jnp.float32, jnp.bfloat16
 VMEM_BYTES = 24 * 2**20
 HEAD = 3
+FETCHES = 4
 SCATTER = (3, 2, 1)
 GATHER = (1, 3, 2)
 
@@ -50,18 +51,29 @@
     return recon_t.T, (sums + codebooks) / (counts[:, :, None] + 1.0), mine / total
 
 
-def rotate_kernel(vec_ref, rot_ref, y_ref, rott_ref):
+def rotate_kernel(vec_hbm, rot_hbm, y_ref, rott_ref, v_ref, rot, sems):
     s, r = lax.axis_index("sub"), lax.axis_index("rep")
     n, w = y_ref.shape[0], y_ref.shape[1]
-    turned = rot_ref[...].T
+    copies = []
+    for source, target in ((rot_hbm, rot), (vec_hbm, v_ref)):
+        size = source.shape[0] // FETCHES
+        for q in range(FETCHES):
+            block = pl.ds(q * size, size)
+            copies.append(pltpu.make_async_copy(source.at[block], target.at[block], sems.at[len(copies)]))
+            copies[-1].start()
+    for copy in copies[:FETCHES]:
+        copy.wait()
+    turned = rot[...].T
     for h in range(n):
         for q in range(2):
             @pl.when(r == q)
             def _():
                 rott_ref[(h + n - s) % n] = turned[(2 * h + q) * w : (2 * h + q + 1) * w]
+    for copy in copies[FETCHES:]:
+        copy.wait()
     for k in range(n):
         y_ref[k] = lax.dot_general(
-            rott_ref[k], vec_ref[...], (((1,), (1,)), ((), ())), preferred_element_type=F32
+            rott_ref[k], v_ref[...], (((1,), (1,)), ((), ())), preferred_element_type=F32
         ).astype(BF16)
 
 
@@ -194,6 +206,17 @@
                     keep_ref[g * w : g * w + done, :] = head[4][g * early : (g + 1) * early, :]
 
 
+def slice_kernel(cb_hbm, out_ref, sems, *, per):
+    size = per // FETCHES
+    copies = []
+    for q in range(FETCHES):
+        at = lax.axis_index("rep") * per + q * size
+        copies.append(pltpu.make_async_copy(cb_hbm.at[pl.ds(at, size)], out_ref.at[pl.ds(q * size, size)], sems.at[q]))
+        copies[-1].start()
+    for copy in copies:
+        copy.wait()
+
+
 def turn_kernel(m0_ref, m1_ref, t0_ref, t1_ref, out_ref, buf):
     s, r = lax.axis_index("sub"), lax.axis_index("rep")
     w = m0_ref.shape[0]
@@ -292,20 +315,33 @@
     vmem = pl.BlockSpec(memory_space=pltpu.VMEM)
 
     cb = codebooks.transpose(0, 2, 1)
-    cb_sent = lax.dynamic_slice_in_dim(cb, lax.axis_index("rep") * per, per, 0)
+    hbm = pl.BlockSpec(memory_space=pltpu.HBM)
+    cb_sent = pl.pallas_call(
+        functools.partial(slice_kernel, per=per),
+        out_shape=jax.ShapeDtypeStruct((per,) + cb.shape[1:], F32),
+        in_specs=[hbm],
+        out_specs=vmem,
+        scratch_shapes=[pltpu.SemaphoreType.DMA((FETCHES,))],
+        compiler_params=small,
+        name="slice",
+    )(pltpu.with_memory_space_constraint(cb, pltpu.HBM))
     cb_far = lax.ppermute(cb_sent, "sub", swap)
     vec_far = lax.ppermute(vectors, "rep", swap)
 
     y_shape = jax.ShapeDtypeStruct((subs, w, rows), BF16)
-    y0, rott = pl.pallas_call(
+    y0, rott, v0 = pl.pallas_call(
         rotate_kernel,
-        out_shape=(y_shape, jax.ShapeDtypeStruct((subs, w, width), BF16)),
-        in_specs=[vmem] * 2,
-        out_specs=(vmem, vmem),
+        out_shape=(
+            y_shape,
+            jax.ShapeDtypeStruct((subs, w, width), BF16),
+            jax.ShapeDtypeStruct(vectors.shape, BF16),
+        ),
+        in_specs=[hbm] * 2,
+        out_specs=(vmem,) * 3,
+        scratch_shapes=[pltpu.VMEM(rotation.shape, BF16), pltpu.SemaphoreType.DMA((2 * FETCHES,))],
         compiler_params=small,
         name="rotate",
-    )(vectors, rotation)
-
+    )(*(pltpu.with_memory_space_constraint(x, pltpu.HBM) for x in (vectors, rotation)))
     y1 = pl.pallas_call(
         rotate_more_kernel, out_shape=y_shape, in_specs=[vmem] * 2, out_specs=vmem, compiler_params=small, name="rotate_far"
     )(vec_far, rott)
@@ -344,7 +380,7 @@
             compiler_params=params,
             cost_estimate=cost(per - first, 1),
             name="quantize_far" if k else "quantize_near",
-        )(cb_k, y0, y1, vectors, vec_far, *head)
+        )(cb_k, y0, y1, v0, vec_far, *head)
 
     early_shape = jax.ShapeDtypeStruct((early, rows), BF16)
     head = pl.pallas_call(
@@ -367,6 +403,7 @@
     theirs1 = lax.ppermute(other1, "rep", swap)
     mine0, other0, keep0, send0 = quantize(0, cb, *head, ahead)
     got0 = lax.ppermute(send0, "sub", swap)
+    other0, got1 = lax.optimization_barrier((other0, got1))
     theirs0 = lax.ppermute(other0, "rep", swap)
 
     reconstruction = pl.pallas_call(
@@ -398,8 +435,8 @@
     near = scatter(keep0, got1)
     near[0], got0, theirs1 = lax.optimization_barrier((near[0], got0, theirs1))
     summed = jnp.concatenate([add_up(near), add_up(scatter(keep1, got0, got1))], axis=0)
-    summed, reconstruction = lax.optimization_barrier((summed, reconstruction))
     mine = [summed] + [exchange(summed, rows_n, d) for d in GATHER]
+    mine[2], mine[3], reconstruction = lax.optimization_barrier((mine[2], mine[3], reconstruction))
     theirs = [lax.ppermute(x, "rep", swap) for x in mine]
 
     any_spec = pl.BlockSpec(memory_space=pl.ANY)

time: 57.3 us -> 56 us (0.977)
  local copies, waits for them, and re-layouts: 3.59 us -> 0.01 us
  Pallas kernels: 23.3 us -> 25.6 us
  starting transfers between devices: 19.3 us -> 21.4 us
  waiting for transfers between devices: 9.86 us -> 7.78 us
    unnamed x8 -> x2, local copies, waits for them, and re-layouts: 2.65 us -> 0.01 us
    ppermute x9, waiting for transfers between devices: 8.74 us -> 6.44 us  [exchange(): return lax.ppermute(x, 'row', [(i, i ^ d) for i in range(n)])]
    ppermute x9, starting transfers between devices: 13.3 us -> 15.3 us  [exchange(): return lax.ppermute(x, 'row', [(i, i ^ d) for i in range(n)])]
    pallas_call x1, Pallas kernels: 1.4 us -> 2.71 us  [on_device(): pl.pallas_call(rotate_kernel, out_shape=(y_shape, jax.ShapeDtypeStruct((s...]
    ppermute x1, starting transfers between devices: 0.14 us -> 1.44 us  [on_device(): got1 = lax.ppermute(send1, 'sub', swap)]
    ppermute x1, starting transfers between devices: 1.95 us -> 0.72 us  [on_device(): got0 = lax.ppermute(send0, 'sub', swap)]
    dynamic_slice x1 -> x0, local copies, waits for them, and re-layouts: 0.94 us -> none  [on_device(): cb_sent = lax.dynamic_slice_in_dim(cb, lax.axis_index('rep') * per, per, 0)]
    pallas_call x0 -> x1, Pallas kernels: none -> 0.9 us  [on_device(): pl.pallas_call(functools.partial(slice_kernel, per=per), out_shape=jax.Sh...]
  transfers between devices with their start and end apart: 19 -> 19, of which waited for: 7 -> 8; matrix products, arithmetic and copies ran while one was open for 2% -> 0% of each run, Pallas kernels for 22% -> 27%
where the time goes in v9:
time: 56 us; the launch traced here: 55.8 us
  Pallas kernels  25.6 us (46%)
  starting transfers between devices  21.4 us (38%)
  waiting for transfers between devices  7.78 us (14%)
  between operations  0.9 us (2%)
    pallas_call x2, Pallas kernels, quantize(): pl.pallas_call(functools.partial(quantize_kernel, k=k, per=per, first=fir...  15.6 us
    ppermute x9, starting transfers between devices, exchange(): return lax.ppermute(x, 'row', [(i, i ^ d) for i in range(n)])  15.3 us
    ppermute x9, waiting for transfers between devices, exchange(): return lax.ppermute(x, 'row', [(i, i ^ d) for i in range(n)])  6.44 us
    pallas_call x1, Pallas kernels, on_device(): pl.pallas_call(rotate_kernel, out_shape=(y_shape, jax.ShapeDtypeStruct((s...  2.71 us
    ppermute x1, starting transfers between devices, on_device(): cb_far = lax.ppermute(cb_sent, 'sub', swap)  2.58 us
    pallas_call x1, Pallas kernels, on_device(): pl.pallas_call(functools.partial(quantize_kernel, k=0, per=per, first=0,...  2.13 us
    pallas_call x1, Pallas kernels, on_device(): pl.pallas_call(turn_kernel, out_shape=jax.ShapeDtypeStruct((rows, width),...  1.61 us
    pallas_call x1, Pallas kernels, on_device(): pl.pallas_call(functools.partial(final_kernel, n=rows_n, per=per, total=t...  1.57 us
  transfers between devices with their start and end apart: 19, of which 8 were waited for; matrix products, arithmetic and copies ran while one was open for 0% of the time, Pallas kernels for 27%

profile of v9, /device:TPU:0, one launch (start us, length us, event | category | flops | bytes accessed | tf_op | source)
XLA Modules:
  0.0 55.8 jit_solution(11957019256820316635)
XLA Ops:
  0.6 0.5 collective-permute-start
  1.1 0.9 %slice.1 = f32[12,16,256]{2,1,0:T(8,128)S(1)} custom-call(f32[24,16,256]{2,1,0:T(8,128)} %bitcast.2), custom_call_target="tpu_custom_call" | custom-call | tf_op jit(solution)/shard_map/slice/pallas_call | solution.py:319
  2.1 2.6 %collective-permute-start.1 = (f32[12,16,256]{2,1,0:T(8,128)S(1)}, f32[12,16,256]{2,1,0:T(8,128)S(1)}, u32[]{:S(2)}, u32[]{:S(2)}) collective-permute-start(f32[12,16,256]{2,1,0:T(8,128)S(1)} %slice.1), channel_id=1, source_target_pairs={{0,2},{2,0},{1,3},{3,1},{4,6},{6,4},{5,7},{7,5},{8,10},{10,8},{9,1... | collective-permute-start | bytes 589832 | tf_op jit(solution)/shard_map/ppermute | solution.py:328
  4.6 2.7 %rotate.1 = (bf16[2,192,896]{2,1,0:T(8,128)(2,1)S(1)}, bf16[2,192,768]{2,1,0:T(8,128)(2,1)S(1)}, bf16[896,768]{1,0:T(8,128)(2,1)S(1)}) custom-call(bf16[896,768]{1,0:T(8,128)(2,1)} %vec_hbm.1, bf16[768,768]{1,0:T(8,128)(2,1)} %rot_hbm.1), custom_call_target="tpu_custom_call" | custom-call | tf_op jit(solution)/shard_map/rotate/pallas_call | solution.py:332
  7.4 1.0 %rotate_far.1.refs_2_ = bf16[2,192,896]{2,1,0:T(8,128)(2,1)S(1)} custom-call(bf16[896,768]{1,0:T(8,128)(2,1)S(1)} %collective-permute-done.vec_ref.refs_4_, bf16[2,192,768]{2,1,0:T(8,128)(2,1)S(1)} %get-tuple-element.37.rott_ref), custom_call_target="tpu_custom_call" | custom-call | tf_op jit(solution)/shard_map/rotate_far/pallas_call | solution.py:345
  8.4 2.1 %quantize_head.1 = (bf16[48,896]{1,0:T(8,128)(2,1)S(1)}, bf16[48,896]{1,0:T(8,128)(2,1)S(1)}, f32[96,128]{1,0:T(8,128)S(1)}, f32[32,128]{1,0:T(8,128)S(1)}) custom-call(f32[24,16,256]{2,1,0:T(8,128)S(1)} %bitcast.3, bf16[2,192,896]{2,1,0:T(8,128)(2,1)S(1)} %get-tuple-element.36.refs_1_, bf16[2,192,896]{2,1,0:T(8,128)(2,1)S(1)} %rotate_far.1.refs_2_), custom_call_target="tpu_custom_call" | custom-call | flops 396361728 | bytes 8388608 | tf_op jit(solution)/shard_map/quantize_head/pallas_call | solution.py:386
  10.5 9.1 %quantize_far.1 = (bf16[192,896]{1,0:T(8,128)(2,1)S(1)}, bf16[192,896]{1,0:T(8,128)(2,1)S(1)}, f32[576,128]{1,0:T(8,128)S(1)}, bf16[1136,128]{1,0:T(8,128)(2,1)S(1)}, f32[144,128]{1,0:T(8,128)S(1)}) custom-call(f32[12,16,256]{2,1,0:T(8,128)S(1)} %collective-permute-done.1.refs_0_, bf16[2,192,896]{2,1,0:T(8,128)(2,1)S(1)} %get-tuple-element.36.refs_1_, ...), custom_call_target="tpu_custom_call" | custom-call | flops 2113929216 | bytes 8388608 | tf_op jit(solution)/shard_map/quantize_far/pallas_call | solution.py:374
  19.6 1.4 %collective-permute-start.2 = (bf16[1136,128]{1,0:T(8,128)(2,1)S(1)}, bf16[1136,128]{1,0:T(8,128)(2,1)S(1)}, u32[]{:S(2)}, u32[]{:S(2)}) collective-permute-start(bf16[1136,128]{1,0:T(8,128)(2,1)S(1)} %get-tuple-element.46), channel_id=1, source_target_pairs={{0,2},{2,0},{1,3},{3,1},{4,6},{6,4},{5,7},{7,5},{8,10},{10,8},{9,1... | collective-permute-start | bytes 872456 | tf_op jit(solution)/shard_map/ppermute | solution.py:402
  21.0 6.5 %quantize_near.1 = (bf16[192,896]{1,0:T(8,128)(2,1)S(1)}, bf16[192,896]{1,0:T(8,128)(2,1)S(1)}, f32[992,128]{1,0:T(8,128)S(1)}, bf16[432,128]{1,0:T(8,128)(2,1)S(1)}) custom-call(f32[24,16,256]{2,1,0:T(8,128)S(1)} %bitcast.4, bf16[2,192,896]{2,1,0:T(8,128)(2,1)S(1)} %get-tuple-element.36.refs_1_, bf16[2,192,896]{2,1,0:T(8,128)(2,1)S(1)} %rotate_far.1.refs_2_, ...), custom_call_target="tpu_custom_call" | custom-call | flops 1717567488 | bytes 8388608 | tf_op jit(solution)/shard_map/quantize_near/pallas_call | solution.py:374
  27.6 0.7 %collective-permute-start.3 = (bf16[432,128]{1,0:T(8,128)(2,1)S(1)}, bf16[432,128]{1,0:T(8,128)(2,1)S(1)}, u32[]{:S(2)}, u32[]{:S(2)}) collective-permute-start(bf16[432,128]{1,0:T(8,128)(2,1)S(1)} %get-tuple-element.49), channel_id=1, source_target_pairs={{0,2},{2,0},{1,3},{3,1},{4,6},{6,4},{5,7},{7,5},{8,10},{10,8},{9,1... | collective-permute-start | bytes 331784 | tf_op jit(solution)/shard_map/ppermute | solution.py:405
  28.8 3.7 %collective-permute-start.5 = (bf16[248,128]{1,0:T(8,128)(2,1)S(1)}, bf16[248,128]{1,0:T(8,128)(2,1)S(1)}, u32[]{:S(2)}, u32[]{:S(2)}) collective-permute-start(bf16[248,128]{1,0:T(8,128)(2,1)S(1)} %get-tuple-element.52), channel_id=1, source_target_pairs={{0,12},{4,8},{8,4},{12,0},{1,13},{5,9},{9,5},{13,1},{2,14},{6,10},... | collective-permute-start | bytes 190472 | tf_op jit(solution)/shard_map/ppermute | solution.py:300
  32.4 0.8 %collective-permute-start.7 = (bf16[248,128]{1,0:T(8,128)(2,1)S(1)}, bf16[248,128]{1,0:T(8,128)(2,1)S(1)}, u32[]{:S(2)}, u32[]{:S(2)}) collective-permute-start(bf16[248,128]{1,0:T(8,128)(2,1)S(1)} %get-tuple-element.54), channel_id=1, source_target_pairs={{0,4},{4,0},{8,12},{12,8},{1,5},{5,1},{9,13},{13,9},{2,6},{6,2},{1... | collective-permute-start | bytes 190472 | tf_op jit(solution)/shard_map/ppermute | solution.py:300
  33.3 3.7 %collective-permute-start.8 = (bf16[144,128]{1,0:T(8,128)(2,1)S(1)}, bf16[144,128]{1,0:T(8,128)(2,1)S(1)}, u32[]{:S(2)}, u32[]{:S(2)}) collective-permute-start(bf16[144,128]{1,0:T(8,128)(2,1)S(1)} %get-tuple-element.58), channel_id=1, source_target_pairs={{0,12},{4,8},{8,4},{12,0},{1,13},{5,9},{9,5},{13,1},{2,14},{6,10},... | collective-permute-start | bytes 110600 | tf_op jit(solution)/shard_map/ppermute | solution.py:300
  36.9 1.4 %collective-permute-start.9 = (bf16[144,128]{1,0:T(8,128)(2,1)S(1)}, bf16[144,128]{1,0:T(8,128)(2,1)S(1)}, u32[]{:S(2)}, u32[]{:S(2)}) collective-permute-start(bf16[144,128]{1,0:T(8,128)(2,1)S(1)} %get-tuple-element.59), channel_id=1, source_target_pairs={{0,8},{4,12},{8,0},{12,4},{1,9},{5,13},{9,1},{13,5},{2,10},{6,14},... | collective-permute-start | bytes 110600 | tf_op jit(solution)/shard_map/ppermute | solution.py:300
  38.4 1.3 %collective-permute-start.10 = (bf16[144,128]{1,0:T(8,128)(2,1)S(1)}, bf16[144,128]{1,0:T(8,128)(2,1)S(1)}, u32[]{:S(2)}, u32[]{:S(2)}) collective-permute-start(bf16[144,128]{1,0:T(8,128)(2,1)S(1)} %get-tuple-element.60), channel_id=1, source_target_pairs={{0,4},{4,0},{8,12},{12,8},{1,5},{5,1},{9,13},{13,9},{2,6},{6,2},{1... | collective-permute-start | bytes 110600 | tf_op jit(solution)/shard_map/ppermute | solution.py:300
  40.0 1.9 %collective-permute-done.9 = bf16[144,128]{1,0:T(8,128)(2,1)S(1)} collective-permute-done((bf16[144,128]{1,0:T(8,128)(2,1)S(1)}, bf16[144,128]{1,0:T(8,128)(2,1)S(1)}, u32[]{:S(2)}, u32[]{:S(2)}) %collective-permute-start.9) | collective-permute-done | bytes 36896 | tf_op jit(solution)/shard_map/ppermute | solution.py:300
  42.4 1.4 %collective-permute-start.14 = (bf16[392,128]{1,0:T(8,128)(2,1)S(1)}, bf16[392,128]{1,0:T(8,128)(2,1)S(1)}, u32[]{:S(2)}, u32[]{:S(2)}) collective-permute-start(bf16[392,128]{1,0:T(8,128)(2,1)S(1)} %pad_maximum_fusion.refs_0_), channel_id=1, source_target_pairs={{0,4},{4,0},{8,12},{12,8},{1,5},{5,1},{9,13},{13,9},{2,6},{6,2},{1... | collective-permute-start | bytes 301064 | tf_op jit(solution)/shard_map/ppermute | solution.py:300
  43.8 1.8 %collective-permute-start.12 = (bf16[392,128]{1,0:T(8,128)(2,1)S(1)}, bf16[392,128]{1,0:T(8,128)(2,1)S(1)}, u32[]{:S(2)}, u32[]{:S(2)}) collective-permute-start(bf16[392,128]{1,0:T(8,128)(2,1)S(1)} %pad_maximum_fusion.refs_0_), channel_id=1, source_target_pairs={{0,8},{4,12},{8,0},{12,4},{1,9},{5,13},{9,1},{13,5},{2,10},{6,14},... | collective-permute-start | bytes 301064 | tf_op jit(solution)/shard_map/ppermute | solution.py:300
  45.6 1.2 %collective-permute-start.11 = (bf16[392,128]{1,0:T(8,128)(2,1)S(1)}, bf16[392,128]{1,0:T(8,128)(2,1)S(1)}, u32[]{:S(2)}, u32[]{:S(2)}) collective-permute-start(bf16[392,128]{1,0:T(8,128)(2,1)S(1)} %pad_maximum_fusion.refs_0_), channel_id=1, source_target_pairs={{0,12},{4,8},{8,4},{12,0},{1,13},{5,9},{9,5},{13,1},{2,14},{6,10},... | collective-permute-start | bytes 301064 | tf_op jit(solution)/shard_map/ppermute | solution.py:300
  47.4 1.6 %turn.1 = bf16[896,768]{1,0:T(8,128)(2,1)} custom-call(bf16[192,896]{1,0:T(8,128)(2,1)S(1)} %get-tuple-element.61.m0_ref, bf16[192,896]{1,0:T(8,128)(2,1)S(1)} %get-tuple-element.62.m1_ref, bf16[192,896]{1,0:T(8,128)(2,1)S(1)} %collective-permute-done.13.t0_ref, bf16[192,896]{1,0:T(8,128)(2,1)S(1)} %collective-permute-done.4.t1_ref), custom_call_target="tpu_custom_call" | custom-call | tf_op jit(solution)/shard_map/turn/pallas_call | solution.py:409
  49.0 3.6 %collective-permute-done.12.refs_3_ = bf16[392,128]{1,0:T(8,128)(2,1)S(1)} collective-permute-done((bf16[392,128]{1,0:T(8,128)(2,1)S(1)}, bf16[392,128]{1,0:T(8,128)(2,1)S(1)}, u32[]{:S(2)}, u32[]{:S(2)}) %collective-permute-start.12) | collective-permute-done | bytes 100384 | tf_op jit(solution)/shard_map/ppermute | solution.py:300
  52.6 0.5 collective-permute-start.18
  53.1 0.8 %collective-permute-done.17.refs_6_ = bf16[392,128]{1,0:T(8,128)(2,1)S(1)} collective-permute-done((bf16[392,128]{1,0:T(8,128)(2,1)S(1)}, bf16[392,128]{1,0:T(8,128)(2,1)S(1)}, u32[]{:S(2)}, u32[]{:S(2)}) %collective-permute-start.17) | collective-permute-done | bytes 100384 | tf_op jit(solution)/shard_map/ppermute | solution.py:440
  54.0 1.6 %final.1 = (f32[384,768]{1,0:T(8,128)}, f32[24,16,256]{2,1,0:T(8,128)}) custom-call(bf16[392,128]{1,0:T(8,128)(2,1)S(1)} %pad_maximum_fusion.refs_0_, bf16[392,128]{1,0:T(8,128)(2,1)S(1)} %collective-permute-done.14.refs_1_, bf16[392,128]{1,0:T(8,128)(2,1)S(1)} %collective-permute-done.11.refs_2_, bf16[392,128]{1,0:T(8,128)(2,1)S(1)} %collective-permute-done.12.refs_3_, ...), custom_call_target="tpu_custom_call" | custom-call | tf_op jit(solution)/shard_map/final/pallas_call | solution.py:443
  (29 shorter events, 1.9 us)
Async XLA Ops:
  0.6 6.7 %collective-permute-start = (bf16[896,768]{1,0:T(8,128)(2,1)}, bf16[896,768]{1,0:T(8,128)(2,1)S(1)}, u32[]{:S(2)}, u32[]{:S(2)}) collective-permute-start(bf16[896,768]{1,0:T(8,128)(2,1)} %vec_hbm.1), channel_id=1, source_target_pairs={{0,1},{1,0},{2,3},{3,2},{4,5},{5,4},{6,7},{7,6},{8,9},{9,8},{10,11... | collective-permute-start | bytes 4128776 | tf_op jit(solution)/shard_map/ppermute | solution.py:329
  2.1 8.5 %collective-permute-start.1 = (f32[12,16,256]{2,1,0:T(8,128)S(1)}, f32[12,16,256]{2,1,0:T(8,128)S(1)}, u32[]{:S(2)}, u32[]{:S(2)}) collective-permute-start(f32[12,16,256]{2,1,0:T(8,128)S(1)} %slice.1), channel_id=1, source_target_pairs={{0,2},{2,0},{1,3},{3,1},{4,6},{6,4},{5,7},{7,5},{8,10},{10,8},{9,1... | collective-permute-start | bytes 589832 | tf_op jit(solution)/shard_map/ppermute | solution.py:328
  7.4 1.0 %copy-start = (f32[24,256,16]{1,2,0:T(8,128)S(1)}, f32[24,256,16]{1,2,0:T(8,128)}, u32[]{:S(2)}) copy-start(f32[24,256,16]{1,2,0:T(8,128)} %param.5) | copy-start | bytes 1179652
  19.6 9.1 %collective-permute-start.2 = (bf16[1136,128]{1,0:T(8,128)(2,1)S(1)}, bf16[1136,128]{1,0:T(8,128)(2,1)S(1)}, u32[]{:S(2)}, u32[]{:S(2)}) collective-permute-start(bf16[1136,128]{1,0:T(8,128)(2,1)S(1)} %get-tuple-element.46), channel_id=1, source_target_pairs={{0,2},{2,0},{1,3},{3,1},{4,6},{6,4},{5,7},{7,5},{8,10},{10,8},{9,1... | collective-permute-start | bytes 872456 | tf_op jit(solution)/shard_map/ppermute | solution.py:402
  21.0 12.2 %collective-permute-start.4 = (bf16[192,896]{1,0:T(8,128)(2,1)S(1)}, bf16[192,896]{1,0:T(8,128)(2,1)S(1)}, u32[]{:S(2)}, u32[]{:S(2)}) collective-permute-start(bf16[192,896]{1,0:T(8,128)(2,1)S(1)} %get-tuple-element.50), channel_id=1, source_target_pairs={{0,1},{1,0},{2,3},{3,2},{4,5},{5,4},{6,7},{7,6},{8,9},{9,8},{10,11... | collective-permute-start | bytes 1032200 | tf_op jit(solution)/shard_map/ppermute | solution.py:403
  27.6 5.6 %collective-permute-start.3 = (bf16[432,128]{1,0:T(8,128)(2,1)S(1)}, bf16[432,128]{1,0:T(8,128)(2,1)S(1)}, u32[]{:S(2)}, u32[]{:S(2)}) collective-permute-start(bf16[432,128]{1,0:T(8,128)(2,1)S(1)} %get-tuple-element.49), channel_id=1, source_target_pairs={{0,2},{2,0},{1,3},{3,1},{4,6},{6,4},{5,7},{7,5},{8,10},{10,8},{9,1... | collective-permute-start | bytes 331784 | tf_op jit(solution)/shard_map/ppermute | solution.py:405
  28.8 8.2 %collective-permute-start.5 = (bf16[248,128]{1,0:T(8,128)(2,1)S(1)}, bf16[248,128]{1,0:T(8,128)(2,1)S(1)}, u32[]{:S(2)}, u32[]{:S(2)}) collective-permute-start(bf16[248,128]{1,0:T(8,128)(2,1)S(1)} %get-tuple-element.52), channel_id=1, source_target_pairs={{0,12},{4,8},{8,4},{12,0},{1,13},{5,9},{9,5},{13,1},{2,14},{6,10},... | collective-permute-start | bytes 190472 | tf_op jit(solution)/shard_map/ppermute | solution.py:300
  32.4 6.0 %collective-permute-start.6 = (bf16[248,128]{1,0:T(8,128)(2,1)S(1)}, bf16[248,128]{1,0:T(8,128)(2,1)S(1)}, u32[]{:S(2)}, u32[]{:S(2)}) collective-permute-start(bf16[248,128]{1,0:T(8,128)(2,1)S(1)} %get-tuple-element.53), channel_id=1, source_target_pairs={{0,8},{4,12},{8,0},{12,4},{1,9},{5,13},{9,1},{13,5},{2,10},{6,14},... | collective-permute-start | bytes 190472 | tf_op jit(solution)/shard_map/ppermute | solution.py:300
  32.4 7.3 %collective-permute-start.7 = (bf16[248,128]{1,0:T(8,128)(2,1)S(1)}, bf16[248,128]{1,0:T(8,128)(2,1)S(1)}, u32[]{:S(2)}, u32[]{:S(2)}) collective-permute-start(bf16[248,128]{1,0:T(8,128)(2,1)S(1)} %get-tuple-element.54), channel_id=1, source_target_pairs={{0,4},{4,0},{8,12},{12,8},{1,5},{5,1},{9,13},{13,9},{2,6},{6,2},{1... | collective-permute-start | bytes 190472 | tf_op jit(solution)/shard_map/ppermute | solution.py:300
  33.2 14.1 %collective-permute-start.13 = (bf16[192,896]{1,0:T(8,128)(2,1)S(1)}, bf16[192,896]{1,0:T(8,128)(2,1)S(1)}, u32[]{:S(2)}, u32[]{:S(2)}) collective-permute-start(bf16[192,896]{1,0:T(8,128)(2,1)S(1)} %get-tuple-element.63), channel_id=1, source_target_pairs={{0,1},{1,0},{2,3},{3,2},{4,5},{5,4},{6,7},{7,6},{8,9},{9,8},{10,11... | collective-permute-start | bytes 1032200 | tf_op jit(solution)/shard_map/ppermute | solution.py:407
  33.3 6.7 %collective-permute-start.8 = (bf16[144,128]{1,0:T(8,128)(2,1)S(1)}, bf16[144,128]{1,0:T(8,128)(2,1)S(1)}, u32[]{:S(2)}, u32[]{:S(2)}) collective-permute-start(bf16[144,128]{1,0:T(8,128)(2,1)S(1)} %get-tuple-element.58), channel_id=1, source_target_pairs={{0,12},{4,8},{8,4},{12,0},{1,13},{5,9},{9,5},{13,1},{2,14},{6,10},... | collective-permute-start | bytes 110600 | tf_op jit(solution)/shard_map/ppermute | solution.py:300
  36.9 5.0 %collective-permute-start.9 = (bf16[144,128]{1,0:T(8,128)(2,1)S(1)}, bf16[144,128]{1,0:T(8,128)(2,1)S(1)}, u32[]{:S(2)}, u32[]{:S(2)}) collective-permute-start(bf16[144,128]{1,0:T(8,128)(2,1)S(1)} %get-tuple-element.59), channel_id=1, source_target_pairs={{0,8},{4,12},{8,0},{12,4},{1,9},{5,13},{9,1},{13,5},{2,10},{6,14},... | collective-permute-start | bytes 110600 | tf_op jit(solution)/shard_map/ppermute | solution.py:300
  38.4 4.0 %collective-permute-start.10 = (bf16[144,128]{1,0:T(8,128)(2,1)S(1)}, bf16[144,128]{1,0:T(8,128)(2,1)S(1)}, u32[]{:S(2)}, u32[]{:S(2)}) collective-permute-start(bf16[144,128]{1,0:T(8,128)(2,1)S(1)} %get-tuple-element.60), channel_id=1, source_target_pairs={{0,4},{4,0},{8,12},{12,8},{1,5},{5,1},{9,13},{13,9},{2,6},{6,2},{1... | collective-permute-start | bytes 110600 | tf_op jit(solution)/shard_map/ppermute | solution.py:300
  42.4 4.7 %collective-permute-start.14 = (bf16[392,128]{1,0:T(8,128)(2,1)S(1)}, bf16[392,128]{1,0:T(8,128)(2,1)S(1)}, u32[]{:S(2)}, u32[]{:S(2)}) collective-permute-start(bf16[392,128]{1,0:T(8,128)(2,1)S(1)} %pad_maximum_fusion.refs_0_), channel_id=1, source_target_pairs={{0,4},{4,0},{8,12},{12,8},{1,5},{5,1},{9,13},{13,9},{2,6},{6,2},{1... | collective-permute-start | bytes 301064 | tf_op jit(solution)/shard_map/ppermute | solution.py:300
  43.8 8.8 %collective-permute-start.12 = (bf16[392,128]{1,0:T(8,128)(2,1)S(1)}, bf16[392,128]{1,0:T(8,128)(2,1)S(1)}, u32[]{:S(2)}, u32[]{:S(2)}) collective-permute-start(bf16[392,128]{1,0:T(8,128)(2,1)S(1)} %pad_maximum_fusion.refs_0_), channel_id=1, source_target_pairs={{0,8},{4,12},{8,0},{12,4},{1,9},{5,13},{9,1},{13,5},{2,10},{6,14},... | collective-permute-start | bytes 301064 | tf_op jit(solution)/shard_map/ppermute | solution.py:300
  45.6 7.0 %collective-permute-start.11 = (bf16[392,128]{1,0:T(8,128)(2,1)S(1)}, bf16[392,128]{1,0:T(8,128)(2,1)S(1)}, u32[]{:S(2)}, u32[]{:S(2)}) collective-permute-start(bf16[392,128]{1,0:T(8,128)(2,1)S(1)} %pad_maximum_fusion.refs_0_), channel_id=1, source_target_pairs={{0,12},{4,8},{8,4},{12,0},{1,13},{5,9},{9,5},{13,1},{2,14},{6,10},... | collective-permute-start | bytes 301064 | tf_op jit(solution)/shard_map/ppermute | solution.py:300
  46.8 6.3 %collective-permute-start.15 = (bf16[392,128]{1,0:T(8,128)(2,1)S(1)}, bf16[392,128]{1,0:T(8,128)(2,1)S(1)}, u32[]{:S(2)}, u32[]{:S(2)}) collective-permute-start(bf16[392,128]{1,0:T(8,128)(2,1)S(1)} %pad_maximum_fusion.refs_0_), channel_id=1, source_target_pairs={{0,1},{1,0},{2,3},{3,2},{4,5},{5,4},{6,7},{7,6},{8,9},{9,8},{10,11... | collective-permute-start | bytes 301064 | tf_op jit(solution)/shard_map/ppermute | solution.py:440
  47.1 6.0 %collective-permute-start.16 = (bf16[392,128]{1,0:T(8,128)(2,1)S(1)}, bf16[392,128]{1,0:T(8,128)(2,1)S(1)}, u32[]{:S(2)}, u32[]{:S(2)}) collective-permute-start(bf16[392,128]{1,0:T(8,128)(2,1)S(1)} %collective-permute-done.14.refs_1_), channel_id=1, source_target_pairs={{0,1},{1,0},{2,3},{3,2},{4,5},{5,4},{6,7},{7,6},{8,9},{9,8},{10,11... | collective-permute-start | bytes 301064 | tf_op jit(solution)/shard_map/ppermute | solution.py:440
  52.6 1.3 %collective-permute-start.17 = (bf16[392,128]{1,0:T(8,128)(2,1)S(1)}, bf16[392,128]{1,0:T(8,128)(2,1)S(1)}, u32[]{:S(2)}, u32[]{:S(2)}) collective-permute-start(bf16[392,128]{1,0:T(8,128)(2,1)S(1)} %collective-permute-done.11.refs_2_), channel_id=1, source_target_pairs={{0,1},{1,0},{2,3},{3,2},{4,5},{5,4},{6,7},{7,6},{8,9},{9,8},{10,11... | collective-permute-start | bytes 301064 | tf_op jit(solution)/shard_map/ppermute | solution.py:440
  52.6 1.5 %collective-permute-start.18 = (bf16[392,128]{1,0:T(8,128)(2,1)S(1)}, bf16[392,128]{1,0:T(8,128)(2,1)S(1)}, u32[]{:S(2)}, u32[]{:S(2)}) collective-permute-start(bf16[392,128]{1,0:T(8,128)(2,1)S(1)} %collective-permute-done.12.refs_3_), channel_id=1, source_target_pairs={{0,1},{1,0},{2,3},{3,2},{4,5},{5,4},{6,7},{7,6},{8,9},{9,8},{10,11... | collective-permute-start | bytes 301064 | tf_op jit(solution)/shard_map/ppermute | solution.py:440

commit v10 on v9

--- a/solution.py
+++ b/solution.py
@@ -13,7 +13,7 @@
 LOG2E = math.log2(math.e)
 F32, BF16 = jnp.float32, jnp.bfloat16
 VMEM_BYTES = 24 * 2**20
-HEAD = 3
+HEAD = 4
 FETCHES = 4
 SCATTER = (3, 2, 1)
 GATHER = (1, 3, 2)
@@ -63,12 +63,14 @@
             copies[-1].start()
     for copy in copies[:FETCHES]:
         copy.wait()
-    turned = rot[...].T
     for h in range(n):
         for q in range(2):
             @pl.when(r == q)
             def _():
-                rott_ref[(h + n - s) % n] = turned[(2 * h + q) * w : (2 * h + q + 1) * w]
+                at = (2 * h + q) * w
+                start = at // 128 * 128
+                turned = rot[:, start : start + 256].T
+                rott_ref[(h + n - s) % n] = turned[at - start : at - start + w]
     for copy in copies[FETCHES:]:
         copy.wait()
     for k in range(n):
@@ -119,10 +121,7 @@
         v0_ref, v1_ref, *refs = refs
         part = v0_ref.shape[1] // 2
         p_rows = (part // lanes) * w
-        if k == 1:
-            head0_ref, head1_ref, rec0_ref, rec1_ref, keep_ref, send_ref, also_ref, cnt = refs
-        else:
-            *head, rec0_ref, rec1_ref, keep_ref, send_ref, cnt = refs
+        *head, rec0_ref, rec1_ref, keep_ref, send_ref, cnt = refs
         sums_ref = keep_ref if k == 0 else send_ref
     stride = w if whole else last * SUBDIM
     ones = jnp.ones((SUBDIM, cols), BF16)
@@ -179,31 +178,17 @@
 
     at = p_rows + halves * w
     sums_ref[at : at + cnt.shape[0], :] = cnt[...].astype(sums_ref.dtype)
-    at_head = at + cnt.shape[0]
-    done = first * SUBDIM
-    early = HEAD * SUBDIM
-    cross = jnp.dot(rec0_ref[done:, :], v0_ref[...], preferred_element_type=F32) + jnp.dot(
-        rec1_ref[done:, :], v1_ref[...], preferred_element_type=F32
+    cross = jnp.dot(rec0_ref[...], v0_ref[...], preferred_element_type=F32) + jnp.dot(
+        rec1_ref[...], v1_ref[...], preferred_element_type=F32
     )
-    if k == 1:
-        ahead = jnp.dot(head0_ref[...], v0_ref[...], preferred_element_type=F32) + jnp.dot(
-            head1_ref[...], v1_ref[...], preferred_element_type=F32
-        )
-    size = w - done
     for h in range(2):
         @pl.when(s == h)
         def _():
             for g in range(part // lanes):
-                near = slice(h * part + g * lanes, h * part + (g + 1) * lanes)
-                away = slice((1 - h) * part + g * lanes, (1 - h) * part + (g + 1) * lanes)
-                keep_ref[g * w + done : (g + 1) * w, :] = cross[:, near]
-                send_ref[g * size : (g + 1) * size, :] = cross[:, away].astype(BF16)
-                if k == 1:
-                    at = at_head + g * early
-                    also_ref[g * early : (g + 1) * early, :] = ahead[:, near]
-                    send_ref[at : at + early, :] = ahead[:, away].astype(BF16)
-                elif done:
-                    keep_ref[g * w : g * w + done, :] = head[4][g * early : (g + 1) * early, :]
+                near = h * part + g * lanes
+                far = (1 - h) * part + g * lanes
+                keep_ref[g * w : (g + 1) * w, :] = cross[:, near : near + lanes]
+                send_ref[g * w : (g + 1) * w, :] = cross[:, far : far + lanes].astype(BF16)
 
 
 def slice_kernel(cb_hbm, out_ref, sems, *, per):
@@ -273,24 +258,10 @@
         copy.wait()
 
 
-def pieces_kernel(kept_ref, got_ref, *refs, n, late):
-    if late:
-        first_ref, *refs = refs
+def pieces_kernel(kept_ref, got_ref, *refs, n):
     outs, total = refs[:n], refs[n]
     z = lax.axis_index("row")
-    rows = kept_ref.shape[0]
-    if late:
-        early = HEAD * SUBDIM
-        groups = (first_ref.shape[0] - late) // early
-        w = rows // groups
-        for g in range(groups):
-            a, b = g * w, g * w + early
-            c = late + g * early
-            total[a:b, :] = kept_ref[a:b, :] + first_ref[c : c + early, :].astype(F32)
-            c = g * (w - early)
-            total[b : a + w, :] = kept_ref[b : a + w, :] + got_ref[c : c + w - early, :].astype(F32)
-    else:
-        total[...] = kept_ref[...] + got_ref[:rows, :].astype(F32)
+    total[...] = kept_ref[...] + got_ref[...].astype(F32)
     size = outs[0].shape[0]
     for out, d in zip(outs, (0,) + SCATTER):
         out[...] = total[pl.ds(pl.multiple_of((z ^ d) * size, 8), size), :].astype(out.dtype)
@@ -359,17 +330,16 @@
             bytes_accessed=2**23,
         )
 
-    groups = part // lanes
     early = HEAD * SUBDIM
 
     def quantize(k, cb_k, *head):
-        n_keep, n_send = (p_rows + s_rows, p_rows - groups * early) if k == 0 else (p_rows, p_rows + s_rows + groups * early)
+        n_keep, n_send = (p_rows + s_rows, p_rows) if k == 0 else (p_rows, p_rows + s_rows)
         out_shape = [
             rec_shape,
             rec_shape,
             jax.ShapeDtypeStruct((n_keep, lanes), F32),
             jax.ShapeDtypeStruct((n_send, lanes), BF16),
-        ] + [jax.ShapeDtypeStruct((groups * early, lanes), F32)] * k
+        ]
         first = 0 if k else HEAD
         return pl.pallas_call(
             functools.partial(quantize_kernel, k=k, per=per, first=first, last=per),
@@ -398,10 +368,12 @@
         name="quantize_head",
     )(cb, y0, y1)
 
-    mine1, other1, keep1, send1, ahead = quantize(1, cb_far, *head[:2])
+    cb_far, *head = lax.optimization_barrier((cb_far, *head))
+
+    mine1, other1, keep1, send1 = quantize(1, cb_far)
     got1 = lax.ppermute(send1, "sub", swap)
     theirs1 = lax.ppermute(other1, "rep", swap)
-    mine0, other0, keep0, send0 = quantize(0, cb, *head, ahead)
+    mine0, other0, keep0, send0 = quantize(0, cb, *head)
     got0 = lax.ppermute(send0, "sub", swap)
     other0, got1 = lax.optimization_barrier((other0, got1))
     theirs0 = lax.ppermute(other0, "rep", swap)
@@ -416,17 +388,17 @@
         name="turn",
     )(mine0, mine1, theirs0, theirs1)
 
-    def scatter(kept, got, *more):
+    def scatter(kept, got):
         size = (kept.shape[0] // rows_n, lanes)
         own, *sent = pl.pallas_call(
-            functools.partial(pieces_kernel, n=rows_n, late=p_rows + s_rows if more else 0),
+            functools.partial(pieces_kernel, n=rows_n),
             out_shape=[jax.ShapeDtypeStruct(size, F32)] + [jax.ShapeDtypeStruct(size, BF16)] * (rows_n - 1),
-            in_specs=[vmem] * (2 + len(more)),
+            in_specs=[vmem] * 2,
             out_specs=[vmem] * rows_n,
             scratch_shapes=[pltpu.VMEM(kept.shape, F32)],
             compiler_params=small,
             name="pieces",
-        )(kept, got, *more)
+        )(kept, got)
         return [own] + [exchange(x, rows_n, d) for x, d in zip(sent, SCATTER)]
 
     def add_up(parts):
@@ -434,7 +406,7 @@
 
     near = scatter(keep0, got1)
     near[0], got0, theirs1 = lax.optimization_barrier((near[0], got0, theirs1))
-    summed = jnp.concatenate([add_up(near), add_up(scatter(keep1, got0, got1))], axis=0)
+    summed = jnp.concatenate([add_up(near), add_up(scatter(keep1, got0))], axis=0)
     mine = [summed] + [exchange(summed, rows_n, d) for d in GATHER]
     mine[2], mine[3], reconstruction = lax.optimization_barrier((mine[2], mine[3], reconstruction))
     theirs = [lax.ppermute(x, "rep", swap) for x in mine]

time: 56 us -> 56 us (level)
  waiting for transfers between devices: 7.78 us -> 8.42 us
    pallas_call x2, Pallas kernels: 15.6 us -> 14.6 us  [quantize(): pl.pallas_call(functools.partial(quantize_kernel, k=k, per=per, first=fir...]
    ppermute x9, waiting for transfers between devices: 6.44 us -> 7.22 us  [exchange(): return lax.ppermute(x, 'row', [(i, i ^ d) for i in range(n)])]
    ppermute x1, starting transfers between devices: 1.44 us -> 0.69 us  [on_device(): got1 = lax.ppermute(send1, 'sub', swap)]
    ppermute x1, starting transfers between devices: 0.72 us -> 1.4 us  [on_device(): got0 = lax.ppermute(send0, 'sub', swap)]
    pallas_call x1, Pallas kernels: 2.13 us -> 2.7 us  [on_device(): pl.pallas_call(functools.partial(quantize_kernel, k=0, per=per, first=0,...]
  transfers between devices with their start and end apart: 19 -> 19, of which waited for: 8 -> 9; matrix products, arithmetic and copies ran while one was open for 0% -> 0% of each run, Pallas kernels for 27% -> 27%
where the time goes in v10:
time: 56 us; the launch traced here: 55.8 us
  Pallas kernels  25.2 us (45%)
  starting transfers between devices  21.1 us (38%)
  waiting for transfers between devices  8.42 us (15%)
  between operations  0.91 us (2%)
    ppermute x9, starting transfers between devices, exchange(): return lax.ppermute(x, 'row', [(i, i ^ d) for i in range(n)])  15.2 us
    pallas_call x2, Pallas kernels, quantize(): pl.pallas_call(functools.partial(quantize_kernel, k=k, per=per, first=fir...  14.6 us
    ppermute x9, waiting for transfers between devices, exchange(): return lax.ppermute(x, 'row', [(i, i ^ d) for i in range(n)])  7.22 us
    pallas_call x1, Pallas kernels, on_device(): pl.pallas_call(rotate_kernel, out_shape=(y_shape, jax.ShapeDtypeStruct((s...  2.71 us
    pallas_call x1, Pallas kernels, on_device(): pl.pallas_call(functools.partial(quantize_kernel, k=0, per=per, first=0,...  2.7 us
    ppermute x1, starting transfers between devices, on_device(): cb_far = lax.ppermute(cb_sent, 'sub', swap)  2.58 us
    pallas_call x1, Pallas kernels, on_device(): pl.pallas_call(turn_kernel, out_shape=jax.ShapeDtypeStruct((rows, width),...  1.61 us
    pallas_call x1, Pallas kernels, on_device(): pl.pallas_call(functools.partial(final_kernel, n=rows_n, per=per, total=t...  1.57 us
  transfers between devices with their start and end apart: 19, of which 9 were waited for; matrix products, arithmetic and copies ran while one was open for 0% of the time, Pallas kernels for 27%

profile of v10, /device:TPU:0, one launch (start us, length us, event | category | flops | bytes accessed | tf_op | source)
XLA Modules:
  0.0 55.8 jit_solution(8351512058351255744)
XLA Ops:
  0.6 0.5 collective-permute-start
  1.1 0.9 %slice.1 = f32[12,16,256]{2,1,0:T(8,128)S(1)} custom-call(f32[24,16,256]{2,1,0:T(8,128)} %bitcast.2), custom_call_target="tpu_custom_call" | custom-call | tf_op jit(solution)/shard_map/slice/pallas_call | solution.py:290
  2.1 2.6 %collective-permute-start.1 = (f32[12,16,256]{2,1,0:T(8,128)S(1)}, f32[12,16,256]{2,1,0:T(8,128)S(1)}, u32[]{:S(2)}, u32[]{:S(2)}) collective-permute-start(f32[12,16,256]{2,1,0:T(8,128)S(1)} %slice.1), channel_id=1, source_target_pairs={{0,2},{2,0},{1,3},{3,1},{4,6},{6,4},{5,7},{7,5},{8,10},{10,8},{9,1... | collective-permute-start | bytes 589832 | tf_op jit(solution)/shard_map/ppermute | solution.py:299
  4.6 2.7 %rotate.1 = (bf16[2,192,896]{2,1,0:T(8,128)(2,1)S(1)}, bf16[2,192,768]{2,1,0:T(8,128)(2,1)S(1)}, bf16[896,768]{1,0:T(8,128)(2,1)S(1)}) custom-call(bf16[896,768]{1,0:T(8,128)(2,1)} %vec_hbm.1, bf16[768,768]{1,0:T(8,128)(2,1)} %rot_hbm.1), custom_call_target="tpu_custom_call" | custom-call | tf_op jit(solution)/shard_map/rotate/pallas_call | solution.py:303
  7.4 1.0 %rotate_far.1.refs_2_ = bf16[2,192,896]{2,1,0:T(8,128)(2,1)S(1)} custom-call(bf16[896,768]{1,0:T(8,128)(2,1)S(1)} %collective-permute-done.vec_ref.refs_4_, bf16[2,192,768]{2,1,0:T(8,128)(2,1)S(1)} %get-tuple-element.41.rott_ref), custom_call_target="tpu_custom_call" | custom-call | tf_op jit(solution)/shard_map/rotate_far/pallas_call | solution.py:316
  8.4 2.7 %quantize_head.1 = (bf16[64,896]{1,0:T(8,128)(2,1)S(1)}, bf16[64,896]{1,0:T(8,128)(2,1)S(1)}, f32[128,128]{1,0:T(8,128)S(1)}, f32[32,128]{1,0:T(8,128)S(1)}) custom-call(f32[24,16,256]{2,1,0:T(8,128)S(1)} %bitcast.3, bf16[2,192,896]{2,1,0:T(8,128)(2,1)S(1)} %get-tuple-element.40.refs_1_, bf16[2,192,896]{2,1,0:T(8,128)(2,1)S(1)} %rotate_far.1.refs_2_), custom_call_target="tpu_custom_call" | custom-call | flops 528482304 | bytes 8388608 | tf_op jit(solution)/shard_map/quantize_head/pallas_call | solution.py:356
  11.1 8.6 %quantize_far.1 = (bf16[192,896]{1,0:T(8,128)(2,1)S(1)}, bf16[192,896]{1,0:T(8,128)(2,1)S(1)}, f32[576,128]{1,0:T(8,128)S(1)}, bf16[992,128]{1,0:T(8,128)(2,1)S(1)}) custom-call(f32[12,16,256]{2,1,0:T(8,128)S(1)} %collective-permute-done.1.refs_0_, bf16[2,192,896]{2,1,0:T(8,128)(2,1)S(1)} %get-tuple-element.40.refs_1_, ...), custom_call_target="tpu_custom_call" | custom-call | flops 2113929216 | bytes 8388608 | tf_op jit(solution)/shard_map/quantize_far/pallas_call | solution.py:344
  20.0 0.7 %collective-permute-start.2 = (bf16[992,128]{1,0:T(8,128)(2,1)S(1)}, bf16[992,128]{1,0:T(8,128)(2,1)S(1)}, u32[]{:S(2)}, u32[]{:S(2)}) collective-permute-start(bf16[992,128]{1,0:T(8,128)(2,1)S(1)} %get-tuple-element.54), channel_id=1, source_target_pairs={{0,2},{2,0},{1,3},{3,1},{4,6},{6,4},{5,7},{7,5},{8,10},{10,8},{9,1... | collective-permute-start | bytes 761864 | tf_op jit(solution)/shard_map/ppermute | solution.py:374
  20.7 6.0 %quantize_near.1 = (bf16[192,896]{1,0:T(8,128)(2,1)S(1)}, bf16[192,896]{1,0:T(8,128)(2,1)S(1)}, f32[992,128]{1,0:T(8,128)S(1)}, bf16[576,128]{1,0:T(8,128)(2,1)S(1)}) custom-call(f32[24,16,256]{2,1,0:T(8,128)S(1)} %bitcast.4, bf16[2,192,896]{2,1,0:T(8,128)(2,1)S(1)} %get-tuple-element.40.refs_1_, bf16[2,192,896]{2,1,0:T(8,128)(2,1)S(1)} %rotate_far.1.refs_2_, ...), custom_call_target="tpu_custom_call" | custom-call | flops 1585446912 | bytes 8388608 | tf_op jit(solution)/shard_map/quantize_near/pallas_call | solution.py:344
  26.7 1.4 %collective-permute-start.3 = (bf16[576,128]{1,0:T(8,128)(2,1)S(1)}, bf16[576,128]{1,0:T(8,128)(2,1)S(1)}, u32[]{:S(2)}, u32[]{:S(2)}) collective-permute-start(bf16[576,128]{1,0:T(8,128)(2,1)S(1)} %get-tuple-element.57), channel_id=1, source_target_pairs={{0,2},{2,0},{1,3},{3,1},{4,6},{6,4},{5,7},{7,5},{8,10},{10,8},{9,1... | collective-permute-start | bytes 442376 | tf_op jit(solution)/shard_map/ppermute | solution.py:377
  28.4 3.7 %collective-permute-start.5 = (bf16[248,128]{1,0:T(8,128)(2,1)S(1)}, bf16[248,128]{1,0:T(8,128)(2,1)S(1)}, u32[]{:S(2)}, u32[]{:S(2)}) collective-permute-start(bf16[248,128]{1,0:T(8,128)(2,1)S(1)} %get-tuple-element.60), channel_id=1, source_target_pairs={{0,12},{4,8},{8,4},{12,0},{1,13},{5,9},{9,5},{13,1},{2,14},{6,10},... | collective-permute-start | bytes 190472 | tf_op jit(solution)/shard_map/ppermute | solution.py:271
  32.1 0.8 %collective-permute-start.7 = (bf16[248,128]{1,0:T(8,128)(2,1)S(1)}, bf16[248,128]{1,0:T(8,128)(2,1)S(1)}, u32[]{:S(2)}, u32[]{:S(2)}) collective-permute-start(bf16[248,128]{1,0:T(8,128)(2,1)S(1)} %get-tuple-element.62), channel_id=1, source_target_pairs={{0,4},{4,0},{8,12},{12,8},{1,5},{5,1},{9,13},{13,9},{2,6},{6,2},{1... | collective-permute-start | bytes 190472 | tf_op jit(solution)/shard_map/ppermute | solution.py:271
  32.9 3.7 %collective-permute-start.8 = (bf16[144,128]{1,0:T(8,128)(2,1)S(1)}, bf16[144,128]{1,0:T(8,128)(2,1)S(1)}, u32[]{:S(2)}, u32[]{:S(2)}) collective-permute-start(bf16[144,128]{1,0:T(8,128)(2,1)S(1)} %get-tuple-element.66), channel_id=1, source_target_pairs={{0,12},{4,8},{8,4},{12,0},{1,13},{5,9},{9,5},{13,1},{2,14},{6,10},... | collective-permute-start | bytes 110600 | tf_op jit(solution)/shard_map/ppermute | solution.py:271
  36.6 0.8 %collective-permute-start.9 = (bf16[144,128]{1,0:T(8,128)(2,1)S(1)}, bf16[144,128]{1,0:T(8,128)(2,1)S(1)}, u32[]{:S(2)}, u32[]{:S(2)}) collective-permute-start(bf16[144,128]{1,0:T(8,128)(2,1)S(1)} %get-tuple-element.67), channel_id=1, source_target_pairs={{0,8},{4,12},{8,0},{12,4},{1,9},{5,13},{9,1},{13,5},{2,10},{6,14},... | collective-permute-start | bytes 110600 | tf_op jit(solution)/shard_map/ppermute | solution.py:271
  37.6 1.8 %collective-permute-start.10 = (bf16[144,128]{1,0:T(8,128)(2,1)S(1)}, bf16[144,128]{1,0:T(8,128)(2,1)S(1)}, u32[]{:S(2)}, u32[]{:S(2)}) collective-permute-start(bf16[144,128]{1,0:T(8,128)(2,1)S(1)} %get-tuple-element.68), channel_id=1, source_target_pairs={{0,4},{4,0},{8,12},{12,8},{1,5},{5,1},{9,13},{13,9},{2,6},{6,2},{1... | collective-permute-start | bytes 110600 | tf_op jit(solution)/shard_map/ppermute | solution.py:271
  39.8 1.8 %collective-permute-done.9 = bf16[144,128]{1,0:T(8,128)(2,1)S(1)} collective-permute-done((bf16[144,128]{1,0:T(8,128)(2,1)S(1)}, bf16[144,128]{1,0:T(8,128)(2,1)S(1)}, u32[]{:S(2)}, u32[]{:S(2)}) %collective-permute-start.9) | collective-permute-done | bytes 36896 | tf_op jit(solution)/shard_map/ppermute | solution.py:271
  42.0 1.5 %collective-permute-start.14 = (bf16[392,128]{1,0:T(8,128)(2,1)S(1)}, bf16[392,128]{1,0:T(8,128)(2,1)S(1)}, u32[]{:S(2)}, u32[]{:S(2)}) collective-permute-start(bf16[392,128]{1,0:T(8,128)(2,1)S(1)} %pad_maximum_fusion.refs_0_), channel_id=1, source_target_pairs={{0,4},{4,0},{8,12},{12,8},{1,5},{5,1},{9,13},{13,9},{2,6},{6,2},{1... | collective-permute-start | bytes 301064 | tf_op jit(solution)/shard_map/ppermute | solution.py:271
  43.5 1.5 %collective-permute-start.12 = (bf16[392,128]{1,0:T(8,128)(2,1)S(1)}, bf16[392,128]{1,0:T(8,128)(2,1)S(1)}, u32[]{:S(2)}, u32[]{:S(2)}) collective-permute-start(bf16[392,128]{1,0:T(8,128)(2,1)S(1)} %pad_maximum_fusion.refs_0_), channel_id=1, source_target_pairs={{0,8},{4,12},{8,0},{12,4},{1,9},{5,13},{9,1},{13,5},{2,10},{6,14},... | collective-permute-start | bytes 301064 | tf_op jit(solution)/shard_map/ppermute | solution.py:271
  45.0 1.4 %collective-permute-start.11 = (bf16[392,128]{1,0:T(8,128)(2,1)S(1)}, bf16[392,128]{1,0:T(8,128)(2,1)S(1)}, u32[]{:S(2)}, u32[]{:S(2)}) collective-permute-start(bf16[392,128]{1,0:T(8,128)(2,1)S(1)} %pad_maximum_fusion.refs_0_), channel_id=1, source_target_pairs={{0,12},{4,8},{8,4},{12,0},{1,13},{5,9},{9,5},{13,1},{2,14},{6,10},... | collective-permute-start | bytes 301064 | tf_op jit(solution)/shard_map/ppermute | solution.py:271
  46.4 0.8 %collective-permute-done.14.refs_1_ = bf16[392,128]{1,0:T(8,128)(2,1)S(1)} collective-permute-done((bf16[392,128]{1,0:T(8,128)(2,1)S(1)}, bf16[392,128]{1,0:T(8,128)(2,1)S(1)}, u32[]{:S(2)}, u32[]{:S(2)}) %collective-permute-start.14) | collective-permute-done | bytes 100384 | tf_op jit(solution)/shard_map/ppermute | solution.py:271
  47.3 1.6 %turn.1 = bf16[896,768]{1,0:T(8,128)(2,1)} custom-call(bf16[192,896]{1,0:T(8,128)(2,1)S(1)} %get-tuple-element.69.m0_ref, bf16[192,896]{1,0:T(8,128)(2,1)S(1)} %get-tuple-element.70.m1_ref, bf16[192,896]{1,0:T(8,128)(2,1)S(1)} %collective-permute-done.13.t0_ref, bf16[192,896]{1,0:T(8,128)(2,1)S(1)} %collective-permute-done.4.t1_ref), custom_call_target="tpu_custom_call" | custom-call | tf_op jit(solution)/shard_map/turn/pallas_call | solution.py:381
  48.9 3.7 %collective-permute-done.12.refs_3_ = bf16[392,128]{1,0:T(8,128)(2,1)S(1)} collective-permute-done((bf16[392,128]{1,0:T(8,128)(2,1)S(1)}, bf16[392,128]{1,0:T(8,128)(2,1)S(1)}, u32[]{:S(2)}, u32[]{:S(2)}) %collective-permute-start.12) | collective-permute-done | bytes 100384 | tf_op jit(solution)/shard_map/ppermute | solution.py:271
  53.1 0.8 %collective-permute-done.17.refs_6_ = bf16[392,128]{1,0:T(8,128)(2,1)S(1)} collective-permute-done((bf16[392,128]{1,0:T(8,128)(2,1)S(1)}, bf16[392,128]{1,0:T(8,128)(2,1)S(1)}, u32[]{:S(2)}, u32[]{:S(2)}) %collective-permute-start.17) | collective-permute-done | bytes 100384 | tf_op jit(solution)/shard_map/ppermute | solution.py:412
  54.0 1.6 %final.1 = (f32[384,768]{1,0:T(8,128)}, f32[24,16,256]{2,1,0:T(8,128)}) custom-call(bf16[392,128]{1,0:T(8,128)(2,1)S(1)} %pad_maximum_fusion.refs_0_, bf16[392,128]{1,0:T(8,128)(2,1)S(1)} %collective-permute-done.14.refs_1_, bf16[392,128]{1,0:T(8,128)(2,1)S(1)} %collective-permute-done.11.refs_2_, bf16[392,128]{1,0:T(8,128)(2,1)S(1)} %collective-permute-done.12.refs_3_, ...), custom_call_target="tpu_custom_call" | custom-call | tf_op jit(solution)/shard_map/final/pallas_call | solution.py:415
  (29 shorter events, 2.3 us)
Async XLA Ops:
  0.6 6.7 %collective-permute-start = (bf16[896,768]{1,0:T(8,128)(2,1)}, bf16[896,768]{1,0:T(8,128)(2,1)S(1)}, u32[]{:S(2)}, u32[]{:S(2)}) collective-permute-start(bf16[896,768]{1,0:T(8,128)(2,1)} %vec_hbm.1), channel_id=1, source_target_pairs={{0,1},{1,0},{2,3},{3,2},{4,5},{5,4},{6,7},{7,6},{8,9},{9,8},{10,11... | collective-permute-start | bytes 4128776 | tf_op jit(solution)/shard_map/ppermute | solution.py:300
  2.1 9.0 %collective-permute-start.1 = (f32[12,16,256]{2,1,0:T(8,128)S(1)}, f32[12,16,256]{2,1,0:T(8,128)S(1)}, u32[]{:S(2)}, u32[]{:S(2)}) collective-permute-start(f32[12,16,256]{2,1,0:T(8,128)S(1)} %slice.1), channel_id=1, source_target_pairs={{0,2},{2,0},{1,3},{3,1},{4,6},{6,4},{5,7},{7,5},{8,10},{10,8},{9,1... | collective-permute-start | bytes 589832 | tf_op jit(solution)/shard_map/ppermute | solution.py:299
  7.4 1.0 %copy-start = (f32[24,256,16]{1,2,0:T(8,128)S(1)}, f32[24,256,16]{1,2,0:T(8,128)}, u32[]{:S(2)}) copy-start(f32[24,256,16]{1,2,0:T(8,128)} %param.5) | copy-start | bytes 1179652
  19.7 13.2 %collective-permute-start.4 = (bf16[192,896]{1,0:T(8,128)(2,1)S(1)}, bf16[192,896]{1,0:T(8,128)(2,1)S(1)}, u32[]{:S(2)}, u32[]{:S(2)}) collective-permute-start(bf16[192,896]{1,0:T(8,128)(2,1)S(1)} %get-tuple-element.58), channel_id=1, source_target_pairs={{0,1},{1,0},{2,3},{3,2},{4,5},{5,4},{6,7},{7,6},{8,9},{9,8},{10,11... | collective-permute-start | bytes 1032200 | tf_op jit(solution)/shard_map/ppermute | solution.py:375
  20.0 8.3 %collective-permute-start.2 = (bf16[992,128]{1,0:T(8,128)(2,1)S(1)}, bf16[992,128]{1,0:T(8,128)(2,1)S(1)}, u32[]{:S(2)}, u32[]{:S(2)}) collective-permute-start(bf16[992,128]{1,0:T(8,128)(2,1)S(1)} %get-tuple-element.54), channel_id=1, source_target_pairs={{0,2},{2,0},{1,3},{3,1},{4,6},{6,4},{5,7},{7,5},{8,10},{10,8},{9,1... | collective-permute-start | bytes 761864 | tf_op jit(solution)/shard_map/ppermute | solution.py:374
  26.7 6.2 %collective-permute-start.3 = (bf16[576,128]{1,0:T(8,128)(2,1)S(1)}, bf16[576,128]{1,0:T(8,128)(2,1)S(1)}, u32[]{:S(2)}, u32[]{:S(2)}) collective-permute-start(bf16[576,128]{1,0:T(8,128)(2,1)S(1)} %get-tuple-element.57), channel_id=1, source_target_pairs={{0,2},{2,0},{1,3},{3,1},{4,6},{6,4},{5,7},{7,5},{8,10},{10,8},{9,1... | collective-permute-start | bytes 442376 | tf_op jit(solution)/shard_map/ppermute | solution.py:377
  28.4 8.2 %collective-permute-start.5 = (bf16[248,128]{1,0:T(8,128)(2,1)S(1)}, bf16[248,128]{1,0:T(8,128)(2,1)S(1)}, u32[]{:S(2)}, u32[]{:S(2)}) collective-permute-start(bf16[248,128]{1,0:T(8,128)(2,1)S(1)} %get-tuple-element.60), channel_id=1, source_target_pairs={{0,12},{4,8},{8,4},{12,0},{1,13},{5,9},{9,5},{13,1},{2,14},{6,10},... | collective-permute-start | bytes 190472 | tf_op jit(solution)/shard_map/ppermute | solution.py:271
  32.1 5.5 %collective-permute-start.6 = (bf16[248,128]{1,0:T(8,128)(2,1)S(1)}, bf16[248,128]{1,0:T(8,128)(2,1)S(1)}, u32[]{:S(2)}, u32[]{:S(2)}) collective-permute-start(bf16[248,128]{1,0:T(8,128)(2,1)S(1)} %get-tuple-element.61), channel_id=1, source_target_pairs={{0,8},{4,12},{8,0},{12,4},{1,9},{5,13},{9,1},{13,5},{2,10},{6,14},... | collective-permute-start | bytes 190472 | tf_op jit(solution)/shard_map/ppermute | solution.py:271
  32.1 7.3 %collective-permute-start.7 = (bf16[248,128]{1,0:T(8,128)(2,1)S(1)}, bf16[248,128]{1,0:T(8,128)(2,1)S(1)}, u32[]{:S(2)}, u32[]{:S(2)}) collective-permute-start(bf16[248,128]{1,0:T(8,128)(2,1)S(1)} %get-tuple-element.62), channel_id=1, source_target_pairs={{0,4},{4,0},{8,12},{12,8},{1,5},{5,1},{9,13},{13,9},{2,6},{6,2},{1... | collective-permute-start | bytes 190472 | tf_op jit(solution)/shard_map/ppermute | solution.py:271
  32.9 14.4 %collective-permute-start.13 = (bf16[192,896]{1,0:T(8,128)(2,1)S(1)}, bf16[192,896]{1,0:T(8,128)(2,1)S(1)}, u32[]{:S(2)}, u32[]{:S(2)}) collective-permute-start(bf16[192,896]{1,0:T(8,128)(2,1)S(1)} %get-tuple-element.71), channel_id=1, source_target_pairs={{0,1},{1,0},{2,3},{3,2},{4,5},{5,4},{6,7},{7,6},{8,9},{9,8},{10,11... | collective-permute-start | bytes 1032200 | tf_op jit(solution)/shard_map/ppermute | solution.py:379
  32.9 6.8 %collective-permute-start.8 = (bf16[144,128]{1,0:T(8,128)(2,1)S(1)}, bf16[144,128]{1,0:T(8,128)(2,1)S(1)}, u32[]{:S(2)}, u32[]{:S(2)}) collective-permute-start(bf16[144,128]{1,0:T(8,128)(2,1)S(1)} %get-tuple-element.66), channel_id=1, source_target_pairs={{0,12},{4,8},{8,4},{12,0},{1,13},{5,9},{9,5},{13,1},{2,14},{6,10},... | collective-permute-start | bytes 110600 | tf_op jit(solution)/shard_map/ppermute | solution.py:271
  36.6 4.9 %collective-permute-start.9 = (bf16[144,128]{1,0:T(8,128)(2,1)S(1)}, bf16[144,128]{1,0:T(8,128)(2,1)S(1)}, u32[]{:S(2)}, u32[]{:S(2)}) collective-permute-start(bf16[144,128]{1,0:T(8,128)(2,1)S(1)} %get-tuple-element.67), channel_id=1, source_target_pairs={{0,8},{4,12},{8,0},{12,4},{1,9},{5,13},{9,1},{13,5},{2,10},{6,14},... | collective-permute-start | bytes 110600 | tf_op jit(solution)/shard_map/ppermute | solution.py:271
  37.6 4.3 %collective-permute-start.10 = (bf16[144,128]{1,0:T(8,128)(2,1)S(1)}, bf16[144,128]{1,0:T(8,128)(2,1)S(1)}, u32[]{:S(2)}, u32[]{:S(2)}) collective-permute-start(bf16[144,128]{1,0:T(8,128)(2,1)S(1)} %get-tuple-element.68), channel_id=1, source_target_pairs={{0,4},{4,0},{8,12},{12,8},{1,5},{5,1},{9,13},{13,9},{2,6},{6,2},{1... | collective-permute-start | bytes 110600 | tf_op jit(solution)/shard_map/ppermute | solution.py:271
  42.0 5.3 %collective-permute-start.14 = (bf16[392,128]{1,0:T(8,128)(2,1)S(1)}, bf16[392,128]{1,0:T(8,128)(2,1)S(1)}, u32[]{:S(2)}, u32[]{:S(2)}) collective-permute-start(bf16[392,128]{1,0:T(8,128)(2,1)S(1)} %pad_maximum_fusion.refs_0_), channel_id=1, source_target_pairs={{0,4},{4,0},{8,12},{12,8},{1,5},{5,1},{9,13},{13,9},{2,6},{6,2},{1... | collective-permute-start | bytes 301064 | tf_op jit(solution)/shard_map/ppermute | solution.py:271
  43.5 9.1 %collective-permute-start.12 = (bf16[392,128]{1,0:T(8,128)(2,1)S(1)}, bf16[392,128]{1,0:T(8,128)(2,1)S(1)}, u32[]{:S(2)}, u32[]{:S(2)}) collective-permute-start(bf16[392,128]{1,0:T(8,128)(2,1)S(1)} %pad_maximum_fusion.refs_0_), channel_id=1, source_target_pairs={{0,8},{4,12},{8,0},{12,4},{1,9},{5,13},{9,1},{13,5},{2,10},{6,14},... | collective-permute-start | bytes 301064 | tf_op jit(solution)/shard_map/ppermute | solution.py:271
  45.0 7.6 %collective-permute-start.11 = (bf16[392,128]{1,0:T(8,128)(2,1)S(1)}, bf16[392,128]{1,0:T(8,128)(2,1)S(1)}, u32[]{:S(2)}, u32[]{:S(2)}) collective-permute-start(bf16[392,128]{1,0:T(8,128)(2,1)S(1)} %pad_maximum_fusion.refs_0_), channel_id=1, source_target_pairs={{0,12},{4,8},{8,4},{12,0},{1,13},{5,9},{9,5},{13,1},{2,14},{6,10},... | collective-permute-start | bytes 301064 | tf_op jit(solution)/shard_map/ppermute | solution.py:271
  46.4 6.7 %collective-permute-start.15 = (bf16[392,128]{1,0:T(8,128)(2,1)S(1)}, bf16[392,128]{1,0:T(8,128)(2,1)S(1)}, u32[]{:S(2)}, u32[]{:S(2)}) collective-permute-start(bf16[392,128]{1,0:T(8,128)(2,1)S(1)} %pad_maximum_fusion.refs_0_), channel_id=1, source_target_pairs={{0,1},{1,0},{2,3},{3,2},{4,5},{5,4},{6,7},{7,6},{8,9},{9,8},{10,11... | collective-permute-start | bytes 301064 | tf_op jit(solution)/shard_map/ppermute | solution.py:412
  47.3 5.8 %collective-permute-start.16 = (bf16[392,128]{1,0:T(8,128)(2,1)S(1)}, bf16[392,128]{1,0:T(8,128)(2,1)S(1)}, u32[]{:S(2)}, u32[]{:S(2)}) collective-permute-start(bf16[392,128]{1,0:T(8,128)(2,1)S(1)} %collective-permute-done.14.refs_1_), channel_id=1, source_target_pairs={{0,1},{1,0},{2,3},{3,2},{4,5},{5,4},{6,7},{7,6},{8,9},{9,8},{10,11... | collective-permute-start | bytes 301064 | tf_op jit(solution)/shard_map/ppermute | solution.py:412
  52.6 1.3 %collective-permute-start.17 = (bf16[392,128]{1,0:T(8,128)(2,1)S(1)}, bf16[392,128]{1,0:T(8,128)(2,1)S(1)}, u32[]{:S(2)}, u32[]{:S(2)}) collective-permute-start(bf16[392,128]{1,0:T(8,128)(2,1)S(1)} %collective-permute-done.11.refs_2_), channel_id=1, source_target_pairs={{0,1},{1,0},{2,3},{3,2},{4,5},{5,4},{6,7},{7,6},{8,9},{9,8},{10,11... | collective-permute-start | bytes 301064 | tf_op jit(solution)/shard_map/ppermute | solution.py:412
  52.6 1.5 %collective-permute-start.18 = (bf16[392,128]{1,0:T(8,128)(2,1)S(1)}, bf16[392,128]{1,0:T(8,128)(2,1)S(1)}, u32[]{:S(2)}, u32[]{:S(2)}) collective-permute-start(bf16[392,128]{1,0:T(8,128)(2,1)S(1)} %collective-permute-done.12.refs_3_), channel_id=1, source_target_pairs={{0,1},{1,0},{2,3},{3,2},{4,5},{5,4},{6,7},{7,6},{8,9},{9,8},{10,11... | collective-permute-start | bytes 301064 | tf_op jit(solution)/shard_map/ppermute | solution.py:412

commit v11 on v10

--- a/solution.py
+++ b/solution.py
@@ -229,6 +229,18 @@
             buf[side, pl.ds(pl.multiple_of(near_rows + source * far, 8), far), :] = ref[near:].astype(F32)
 
     copies = []
+    first = groups * w
+    for side in range(2):
+        part = r if side == 0 else 1 - r
+        for m in range(per):
+            c = cb_ref[part * per + m]
+            rows = [first + hf * w + m * SUBDIM for hf in range(halves)]
+            sums = jnp.concatenate([buf[side, a : a + SUBDIM, :] for a in rows], axis=1)
+            rows = [first + halves * w + hf * SUBDIM + m for hf in range(halves)]
+            count = jnp.concatenate([buf[side, a : a + 1, :] for a in rows], axis=1)
+            new[part * per + m] = (sums + c) / (count + 1.0)
+    copies.append(pltpu.make_async_copy(new, new_hbm, sems.at[groups]))
+    copies[-1].start()
     for g in range(groups):
         for h in range(2):
             for q in range(2):
@@ -242,18 +254,6 @@
         block = pl.ds(g * lanes, lanes)
         copies.append(pltpu.make_async_copy(cross.at[block], cross_hbm.at[block], sems.at[g]))
         copies[-1].start()
-    first = groups * w
-    for side in range(2):
-        part = r if side == 0 else 1 - r
-        for m in range(per):
-            c = cb_ref[part * per + m]
-            rows = [first + hf * w + m * SUBDIM for hf in range(halves)]
-            sums = jnp.concatenate([buf[side, a : a + SUBDIM, :] for a in rows], axis=1)
-            rows = [first + halves * w + hf * SUBDIM + m for hf in range(halves)]
-            count = jnp.concatenate([buf[side, a : a + 1, :] for a in rows], axis=1)
-            new[part * per + m] = (sums + c) / (count + 1.0)
-    copies.append(pltpu.make_async_copy(new, new_hbm, sems.at[groups]))
-    copies[-1].start()
     for copy in copies:
         copy.wait()
 

time: 56 us -> 55.9 us (level)
  no operation moved by 1% of the time
where the time goes in v11:
time: 55.9 us; the launch traced here: 55.7 us
  Pallas kernels  25.2 us (45%)
  starting transfers between devices  21.1 us (38%)
  waiting for transfers between devices  8.42 us (15%)
  between operations  0.91 us (2%)
    ppermute x9, starting transfers between devices, exchange(): return lax.ppermute(x, 'row', [(i, i ^ d) for i in range(n)])  15.2 us
    pallas_call x2, Pallas kernels, quantize(): pl.pallas_call(functools.partial(quantize_kernel, k=k, per=per, first=fir...  14.6 us
    ppermute x9, waiting for transfers between devices, exchange(): return lax.ppermute(x, 'row', [(i, i ^ d) for i in range(n)])  7.22 us
    pallas_call x1, Pallas kernels, on_device(): pl.pallas_call(rotate_kernel, out_shape=(y_shape, jax.ShapeDtypeStruct((s...  2.71 us
    pallas_call x1, Pallas kernels, on_device(): pl.pallas_call(functools.partial(quantize_kernel, k=0, per=per, first=0,...  2.7 us
    ppermute x1, starting transfers between devices, on_device(): cb_far = lax.ppermute(cb_sent, 'sub', swap)  2.58 us
    pallas_call x1, Pallas kernels, on_device(): pl.pallas_call(turn_kernel, out_shape=jax.ShapeDtypeStruct((rows, width),...  1.61 us
    pallas_call x1, Pallas kernels, on_device(): pl.pallas_call(functools.partial(final_kernel, n=rows_n, per=per, total=t...  1.48 us
  transfers between devices with their start and end apart: 19, of which 9 were waited for; matrix products, arithmetic and copies ran while one was open for 0% of the time, Pallas kernels for 27%

profile of v11, /device:TPU:0, one launch (start us, length us, event | category | flops | bytes accessed | tf_op | source)
XLA Modules:
  0.0 55.7 jit_solution(8262511574372840460)
XLA Ops:
  0.6 0.5 collective-permute-start
  1.1 0.9 %slice.1 = f32[12,16,256]{2,1,0:T(8,128)S(1)} custom-call(f32[24,16,256]{2,1,0:T(8,128)} %bitcast.2), custom_call_target="tpu_custom_call" | custom-call | tf_op jit(solution)/shard_map/slice/pallas_call | solution.py:290
  2.1 2.6 %collective-permute-start.1 = (f32[12,16,256]{2,1,0:T(8,128)S(1)}, f32[12,16,256]{2,1,0:T(8,128)S(1)}, u32[]{:S(2)}, u32[]{:S(2)}) collective-permute-start(f32[12,16,256]{2,1,0:T(8,128)S(1)} %slice.1), channel_id=1, source_target_pairs={{0,2},{2,0},{1,3},{3,1},{4,6},{6,4},{5,7},{7,5},{8,10},{10,8},{9,1... | collective-permute-start | bytes 589832 | tf_op jit(solution)/shard_map/ppermute | solution.py:299
  4.6 2.7 %rotate.1 = (bf16[2,192,896]{2,1,0:T(8,128)(2,1)S(1)}, bf16[2,192,768]{2,1,0:T(8,128)(2,1)S(1)}, bf16[896,768]{1,0:T(8,128)(2,1)S(1)}) custom-call(bf16[896,768]{1,0:T(8,128)(2,1)} %vec_hbm.1, bf16[768,768]{1,0:T(8,128)(2,1)} %rot_hbm.1), custom_call_target="tpu_custom_call" | custom-call | tf_op jit(solution)/shard_map/rotate/pallas_call | solution.py:303
  7.4 1.0 %rotate_far.1.refs_2_ = bf16[2,192,896]{2,1,0:T(8,128)(2,1)S(1)} custom-call(bf16[896,768]{1,0:T(8,128)(2,1)S(1)} %collective-permute-done.vec_ref.refs_4_, bf16[2,192,768]{2,1,0:T(8,128)(2,1)S(1)} %get-tuple-element.41.rott_ref), custom_call_target="tpu_custom_call" | custom-call | tf_op jit(solution)/shard_map/rotate_far/pallas_call | solution.py:316
  8.4 2.7 %quantize_head.1 = (bf16[64,896]{1,0:T(8,128)(2,1)S(1)}, bf16[64,896]{1,0:T(8,128)(2,1)S(1)}, f32[128,128]{1,0:T(8,128)S(1)}, f32[32,128]{1,0:T(8,128)S(1)}) custom-call(f32[24,16,256]{2,1,0:T(8,128)S(1)} %bitcast.3, bf16[2,192,896]{2,1,0:T(8,128)(2,1)S(1)} %get-tuple-element.40.refs_1_, bf16[2,192,896]{2,1,0:T(8,128)(2,1)S(1)} %rotate_far.1.refs_2_), custom_call_target="tpu_custom_call" | custom-call | flops 528482304 | bytes 8388608 | tf_op jit(solution)/shard_map/quantize_head/pallas_call | solution.py:356
  11.1 8.6 %quantize_far.1 = (bf16[192,896]{1,0:T(8,128)(2,1)S(1)}, bf16[192,896]{1,0:T(8,128)(2,1)S(1)}, f32[576,128]{1,0:T(8,128)S(1)}, bf16[992,128]{1,0:T(8,128)(2,1)S(1)}) custom-call(f32[12,16,256]{2,1,0:T(8,128)S(1)} %collective-permute-done.1.refs_0_, bf16[2,192,896]{2,1,0:T(8,128)(2,1)S(1)} %get-tuple-element.40.refs_1_, ...), custom_call_target="tpu_custom_call" | custom-call | flops 2113929216 | bytes 8388608 | tf_op jit(solution)/shard_map/quantize_far/pallas_call | solution.py:344
  20.0 0.7 %collective-permute-start.2 = (bf16[992,128]{1,0:T(8,128)(2,1)S(1)}, bf16[992,128]{1,0:T(8,128)(2,1)S(1)}, u32[]{:S(2)}, u32[]{:S(2)}) collective-permute-start(bf16[992,128]{1,0:T(8,128)(2,1)S(1)} %get-tuple-element.54), channel_id=1, source_target_pairs={{0,2},{2,0},{1,3},{3,1},{4,6},{6,4},{5,7},{7,5},{8,10},{10,8},{9,1... | collective-permute-start | bytes 761864 | tf_op jit(solution)/shard_map/ppermute | solution.py:374
  20.7 6.0 %quantize_near.1 = (bf16[192,896]{1,0:T(8,128)(2,1)S(1)}, bf16[192,896]{1,0:T(8,128)(2,1)S(1)}, f32[992,128]{1,0:T(8,128)S(1)}, bf16[576,128]{1,0:T(8,128)(2,1)S(1)}) custom-call(f32[24,16,256]{2,1,0:T(8,128)S(1)} %bitcast.4, bf16[2,192,896]{2,1,0:T(8,128)(2,1)S(1)} %get-tuple-element.40.refs_1_, bf16[2,192,896]{2,1,0:T(8,128)(2,1)S(1)} %rotate_far.1.refs_2_, ...), custom_call_target="tpu_custom_call" | custom-call | flops 1585446912 | bytes 8388608 | tf_op jit(solution)/shard_map/quantize_near/pallas_call | solution.py:344
  26.7 1.4 %collective-permute-start.3 = (bf16[576,128]{1,0:T(8,128)(2,1)S(1)}, bf16[576,128]{1,0:T(8,128)(2,1)S(1)}, u32[]{:S(2)}, u32[]{:S(2)}) collective-permute-start(bf16[576,128]{1,0:T(8,128)(2,1)S(1)} %get-tuple-element.57), channel_id=1, source_target_pairs={{0,2},{2,0},{1,3},{3,1},{4,6},{6,4},{5,7},{7,5},{8,10},{10,8},{9,1... | collective-permute-start | bytes 442376 | tf_op jit(solution)/shard_map/ppermute | solution.py:377
  28.4 3.7 %collective-permute-start.5 = (bf16[248,128]{1,0:T(8,128)(2,1)S(1)}, bf16[248,128]{1,0:T(8,128)(2,1)S(1)}, u32[]{:S(2)}, u32[]{:S(2)}) collective-permute-start(bf16[248,128]{1,0:T(8,128)(2,1)S(1)} %get-tuple-element.60), channel_id=1, source_target_pairs={{0,12},{4,8},{8,4},{12,0},{1,13},{5,9},{9,5},{13,1},{2,14},{6,10},... | collective-permute-start | bytes 190472 | tf_op jit(solution)/shard_map/ppermute | solution.py:271
  32.1 0.8 %collective-permute-start.7 = (bf16[248,128]{1,0:T(8,128)(2,1)S(1)}, bf16[248,128]{1,0:T(8,128)(2,1)S(1)}, u32[]{:S(2)}, u32[]{:S(2)}) collective-permute-start(bf16[248,128]{1,0:T(8,128)(2,1)S(1)} %get-tuple-element.62), channel_id=1, source_target_pairs={{0,4},{4,0},{8,12},{12,8},{1,5},{5,1},{9,13},{13,9},{2,6},{6,2},{1... | collective-permute-start | bytes 190472 | tf_op jit(solution)/shard_map/ppermute | solution.py:271
  32.9 3.7 %collective-permute-start.8 = (bf16[144,128]{1,0:T(8,128)(2,1)S(1)}, bf16[144,128]{1,0:T(8,128)(2,1)S(1)}, u32[]{:S(2)}, u32[]{:S(2)}) collective-permute-start(bf16[144,128]{1,0:T(8,128)(2,1)S(1)} %get-tuple-element.66), channel_id=1, source_target_pairs={{0,12},{4,8},{8,4},{12,0},{1,13},{5,9},{9,5},{13,1},{2,14},{6,10},... | collective-permute-start | bytes 110600 | tf_op jit(solution)/shard_map/ppermute | solution.py:271
  36.6 0.8 %collective-permute-start.9 = (bf16[144,128]{1,0:T(8,128)(2,1)S(1)}, bf16[144,128]{1,0:T(8,128)(2,1)S(1)}, u32[]{:S(2)}, u32[]{:S(2)}) collective-permute-start(bf16[144,128]{1,0:T(8,128)(2,1)S(1)} %get-tuple-element.67), channel_id=1, source_target_pairs={{0,8},{4,12},{8,0},{12,4},{1,9},{5,13},{9,1},{13,5},{2,10},{6,14},... | collective-permute-start | bytes 110600 | tf_op jit(solution)/shard_map/ppermute | solution.py:271
  37.6 1.8 %collective-permute-start.10 = (bf16[144,128]{1,0:T(8,128)(2,1)S(1)}, bf16[144,128]{1,0:T(8,128)(2,1)S(1)}, u32[]{:S(2)}, u32[]{:S(2)}) collective-permute-start(bf16[144,128]{1,0:T(8,128)(2,1)S(1)} %get-tuple-element.68), channel_id=1, source_target_pairs={{0,4},{4,0},{8,12},{12,8},{1,5},{5,1},{9,13},{13,9},{2,6},{6,2},{1... | collective-permute-start | bytes 110600 | tf_op jit(solution)/shard_map/ppermute | solution.py:271
  39.8 1.8 %collective-permute-done.9 = bf16[144,128]{1,0:T(8,128)(2,1)S(1)} collective-permute-done((bf16[144,128]{1,0:T(8,128)(2,1)S(1)}, bf16[144,128]{1,0:T(8,128)(2,1)S(1)}, u32[]{:S(2)}, u32[]{:S(2)}) %collective-permute-start.9) | collective-permute-done | bytes 36896 | tf_op jit(solution)/shard_map/ppermute | solution.py:271
  42.0 1.5 %collective-permute-start.14 = (bf16[392,128]{1,0:T(8,128)(2,1)S(1)}, bf16[392,128]{1,0:T(8,128)(2,1)S(1)}, u32[]{:S(2)}, u32[]{:S(2)}) collective-permute-start(bf16[392,128]{1,0:T(8,128)(2,1)S(1)} %pad_maximum_fusion.refs_0_), channel_id=1, source_target_pairs={{0,4},{4,0},{8,12},{12,8},{1,5},{5,1},{9,13},{13,9},{2,6},{6,2},{1... | collective-permute-start | bytes 301064 | tf_op jit(solution)/shard_map/ppermute | solution.py:271
  43.5 1.5 %collective-permute-start.12 = (bf16[392,128]{1,0:T(8,128)(2,1)S(1)}, bf16[392,128]{1,0:T(8,128)(2,1)S(1)}, u32[]{:S(2)}, u32[]{:S(2)}) collective-permute-start(bf16[392,128]{1,0:T(8,128)(2,1)S(1)} %pad_maximum_fusion.refs_0_), channel_id=1, source_target_pairs={{0,8},{4,12},{8,0},{12,4},{1,9},{5,13},{9,1},{13,5},{2,10},{6,14},... | collective-permute-start | bytes 301064 | tf_op jit(solution)/shard_map/ppermute | solution.py:271
  45.0 1.4 %collective-permute-start.11 = (bf16[392,128]{1,0:T(8,128)(2,1)S(1)}, bf16[392,128]{1,0:T(8,128)(2,1)S(1)}, u32[]{:S(2)}, u32[]{:S(2)}) collective-permute-start(bf16[392,128]{1,0:T(8,128)(2,1)S(1)} %pad_maximum_fusion.refs_0_), channel_id=1, source_target_pairs={{0,12},{4,8},{8,4},{12,0},{1,13},{5,9},{9,5},{13,1},{2,14},{6,10},... | collective-permute-start | bytes 301064 | tf_op jit(solution)/shard_map/ppermute | solution.py:271
  46.4 0.8 %collective-permute-done.14.refs_1_ = bf16[392,128]{1,0:T(8,128)(2,1)S(1)} collective-permute-done((bf16[392,128]{1,0:T(8,128)(2,1)S(1)}, bf16[392,128]{1,0:T(8,128)(2,1)S(1)}, u32[]{:S(2)}, u32[]{:S(2)}) %collective-permute-start.14) | collective-permute-done | bytes 100384 | tf_op jit(solution)/shard_map/ppermute | solution.py:271
  47.3 1.6 %turn.1 = bf16[896,768]{1,0:T(8,128)(2,1)} custom-call(bf16[192,896]{1,0:T(8,128)(2,1)S(1)} %get-tuple-element.69.m0_ref, bf16[192,896]{1,0:T(8,128)(2,1)S(1)} %get-tuple-element.70.m1_ref, bf16[192,896]{1,0:T(8,128)(2,1)S(1)} %collective-permute-done.13.t0_ref, bf16[192,896]{1,0:T(8,128)(2,1)S(1)} %collective-permute-done.4.t1_ref), custom_call_target="tpu_custom_call" | custom-call | tf_op jit(solution)/shard_map/turn/pallas_call | solution.py:381
  48.9 3.7 %collective-permute-done.12.refs_3_ = bf16[392,128]{1,0:T(8,128)(2,1)S(1)} collective-permute-done((bf16[392,128]{1,0:T(8,128)(2,1)S(1)}, bf16[392,128]{1,0:T(8,128)(2,1)S(1)}, u32[]{:S(2)}, u32[]{:S(2)}) %collective-permute-start.12) | collective-permute-done | bytes 100384 | tf_op jit(solution)/shard_map/ppermute | solution.py:271
  53.1 0.8 %collective-permute-done.17.refs_6_ = bf16[392,128]{1,0:T(8,128)(2,1)S(1)} collective-permute-done((bf16[392,128]{1,0:T(8,128)(2,1)S(1)}, bf16[392,128]{1,0:T(8,128)(2,1)S(1)}, u32[]{:S(2)}, u32[]{:S(2)}) %collective-permute-start.17) | collective-permute-done | bytes 100384 | tf_op jit(solution)/shard_map/ppermute | solution.py:412
  54.0 1.5 %final.1 = (f32[384,768]{1,0:T(8,128)}, f32[24,16,256]{2,1,0:T(8,128)}) custom-call(bf16[392,128]{1,0:T(8,128)(2,1)S(1)} %pad_maximum_fusion.refs_0_, bf16[392,128]{1,0:T(8,128)(2,1)S(1)} %collective-permute-done.14.refs_1_, bf16[392,128]{1,0:T(8,128)(2,1)S(1)} %collective-permute-done.11.refs_2_, bf16[392,128]{1,0:T(8,128)(2,1)S(1)} %collective-permute-done.12.refs_3_, ...), custom_call_target="tpu_custom_call" | custom-call | tf_op jit(solution)/shard_map/final/pallas_call | solution.py:415
  (29 shorter events, 2.3 us)
Async XLA Ops:
  0.6 6.7 %collective-permute-start = (bf16[896,768]{1,0:T(8,128)(2,1)}, bf16[896,768]{1,0:T(8,128)(2,1)S(1)}, u32[]{:S(2)}, u32[]{:S(2)}) collective-permute-start(bf16[896,768]{1,0:T(8,128)(2,1)} %vec_hbm.1), channel_id=1, source_target_pairs={{0,1},{1,0},{2,3},{3,2},{4,5},{5,4},{6,7},{7,6},{8,9},{9,8},{10,11... | collective-permute-start | bytes 4128776 | tf_op jit(solution)/shard_map/ppermute | solution.py:300
  2.1 9.0 %collective-permute-start.1 = (f32[12,16,256]{2,1,0:T(8,128)S(1)}, f32[12,16,256]{2,1,0:T(8,128)S(1)}, u32[]{:S(2)}, u32[]{:S(2)}) collective-permute-start(f32[12,16,256]{2,1,0:T(8,128)S(1)} %slice.1), channel_id=1, source_target_pairs={{0,2},{2,0},{1,3},{3,1},{4,6},{6,4},{5,7},{7,5},{8,10},{10,8},{9,1... | collective-permute-start | bytes 589832 | tf_op jit(solution)/shard_map/ppermute | solution.py:299
  7.4 1.0 %copy-start = (f32[24,256,16]{1,2,0:T(8,128)S(1)}, f32[24,256,16]{1,2,0:T(8,128)}, u32[]{:S(2)}) copy-start(f32[24,256,16]{1,2,0:T(8,128)} %param.5) | copy-start | bytes 1179652
  19.7 13.2 %collective-permute-start.4 = (bf16[192,896]{1,0:T(8,128)(2,1)S(1)}, bf16[192,896]{1,0:T(8,128)(2,1)S(1)}, u32[]{:S(2)}, u32[]{:S(2)}) collective-permute-start(bf16[192,896]{1,0:T(8,128)(2,1)S(1)} %get-tuple-element.58), channel_id=1, source_target_pairs={{0,1},{1,0},{2,3},{3,2},{4,5},{5,4},{6,7},{7,6},{8,9},{9,8},{10,11... | collective-permute-start | bytes 1032200 | tf_op jit(solution)/shard_map/ppermute | solution.py:375
  20.0 8.3 %collective-permute-start.2 = (bf16[992,128]{1,0:T(8,128)(2,1)S(1)}, bf16[992,128]{1,0:T(8,128)(2,1)S(1)}, u32[]{:S(2)}, u32[]{:S(2)}) collective-permute-start(bf16[992,128]{1,0:T(8,128)(2,1)S(1)} %get-tuple-element.54), channel_id=1, source_target_pairs={{0,2},{2,0},{1,3},{3,1},{4,6},{6,4},{5,7},{7,5},{8,10},{10,8},{9,1... | collective-permute-start | bytes 761864 | tf_op jit(solution)/shard_map/ppermute | solution.py:374
  26.7 6.2 %collective-permute-start.3 = (bf16[576,128]{1,0:T(8,128)(2,1)S(1)}, bf16[576,128]{1,0:T(8,128)(2,1)S(1)}, u32[]{:S(2)}, u32[]{:S(2)}) collective-permute-start(bf16[576,128]{1,0:T(8,128)(2,1)S(1)} %get-tuple-element.57), channel_id=1, source_target_pairs={{0,2},{2,0},{1,3},{3,1},{4,6},{6,4},{5,7},{7,5},{8,10},{10,8},{9,1... | collective-permute-start | bytes 442376 | tf_op jit(solution)/shard_map/ppermute | solution.py:377
  28.4 8.2 %collective-permute-start.5 = (bf16[248,128]{1,0:T(8,128)(2,1)S(1)}, bf16[248,128]{1,0:T(8,128)(2,1)S(1)}, u32[]{:S(2)}, u32[]{:S(2)}) collective-permute-start(bf16[248,128]{1,0:T(8,128)(2,1)S(1)} %get-tuple-element.60), channel_id=1, source_target_pairs={{0,12},{4,8},{8,4},{12,0},{1,13},{5,9},{9,5},{13,1},{2,14},{6,10},... | collective-permute-start | bytes 190472 | tf_op jit(solution)/shard_map/ppermute | solution.py:271
  32.1 5.5 %collective-permute-start.6 = (bf16[248,128]{1,0:T(8,128)(2,1)S(1)}, bf16[248,128]{1,0:T(8,128)(2,1)S(1)}, u32[]{:S(2)}, u32[]{:S(2)}) collective-permute-start(bf16[248,128]{1,0:T(8,128)(2,1)S(1)} %get-tuple-element.61), channel_id=1, source_target_pairs={{0,8},{4,12},{8,0},{12,4},{1,9},{5,13},{9,1},{13,5},{2,10},{6,14},... | collective-permute-start | bytes 190472 | tf_op jit(solution)/shard_map/ppermute | solution.py:271
  32.1 7.3 %collective-permute-start.7 = (bf16[248,128]{1,0:T(8,128)(2,1)S(1)}, bf16[248,128]{1,0:T(8,128)(2,1)S(1)}, u32[]{:S(2)}, u32[]{:S(2)}) collective-permute-start(bf16[248,128]{1,0:T(8,128)(2,1)S(1)} %get-tuple-element.62), channel_id=1, source_target_pairs={{0,4},{4,0},{8,12},{12,8},{1,5},{5,1},{9,13},{13,9},{2,6},{6,2},{1... | collective-permute-start | bytes 190472 | tf_op jit(solution)/shard_map/ppermute | solution.py:271
  32.9 14.4 %collective-permute-start.13 = (bf16[192,896]{1,0:T(8,128)(2,1)S(1)}, bf16[192,896]{1,0:T(8,128)(2,1)S(1)}, u32[]{:S(2)}, u32[]{:S(2)}) collective-permute-start(bf16[192,896]{1,0:T(8,128)(2,1)S(1)} %get-tuple-element.71), channel_id=1, source_target_pairs={{0,1},{1,0},{2,3},{3,2},{4,5},{5,4},{6,7},{7,6},{8,9},{9,8},{10,11... | collective-permute-start | bytes 1032200 | tf_op jit(solution)/shard_map/ppermute | solution.py:379
  32.9 6.8 %collective-permute-start.8 = (bf16[144,128]{1,0:T(8,128)(2,1)S(1)}, bf16[144,128]{1,0:T(8,128)(2,1)S(1)}, u32[]{:S(2)}, u32[]{:S(2)}) collective-permute-start(bf16[144,128]{1,0:T(8,128)(2,1)S(1)} %get-tuple-element.66), channel_id=1, source_target_pairs={{0,12},{4,8},{8,4},{12,0},{1,13},{5,9},{9,5},{13,1},{2,14},{6,10},... | collective-permute-start | bytes 110600 | tf_op jit(solution)/shard_map/ppermute | solution.py:271
  36.6 4.9 %collective-permute-start.9 = (bf16[144,128]{1,0:T(8,128)(2,1)S(1)}, bf16[144,128]{1,0:T(8,128)(2,1)S(1)}, u32[]{:S(2)}, u32[]{:S(2)}) collective-permute-start(bf16[144,128]{1,0:T(8,128)(2,1)S(1)} %get-tuple-element.67), channel_id=1, source_target_pairs={{0,8},{4,12},{8,0},{12,4},{1,9},{5,13},{9,1},{13,5},{2,10},{6,14},... | collective-permute-start | bytes 110600 | tf_op jit(solution)/shard_map/ppermute | solution.py:271
  37.6 4.3 %collective-permute-start.10 = (bf16[144,128]{1,0:T(8,128)(2,1)S(1)}, bf16[144,128]{1,0:T(8,128)(2,1)S(1)}, u32[]{:S(2)}, u32[]{:S(2)}) collective-permute-start(bf16[144,128]{1,0:T(8,128)(2,1)S(1)} %get-tuple-element.68), channel_id=1, source_target_pairs={{0,4},{4,0},{8,12},{12,8},{1,5},{5,1},{9,13},{13,9},{2,6},{6,2},{1... | collective-permute-start | bytes 110600 | tf_op jit(solution)/shard_map/ppermute | solution.py:271
  42.0 5.3 %collective-permute-start.14 = (bf16[392,128]{1,0:T(8,128)(2,1)S(1)}, bf16[392,128]{1,0:T(8,128)(2,1)S(1)}, u32[]{:S(2)}, u32[]{:S(2)}) collective-permute-start(bf16[392,128]{1,0:T(8,128)(2,1)S(1)} %pad_maximum_fusion.refs_0_), channel_id=1, source_target_pairs={{0,4},{4,0},{8,12},{12,8},{1,5},{5,1},{9,13},{13,9},{2,6},{6,2},{1... | collective-permute-start | bytes 301064 | tf_op jit(solution)/shard_map/ppermute | solution.py:271
  43.5 9.1 %collective-permute-start.12 = (bf16[392,128]{1,0:T(8,128)(2,1)S(1)}, bf16[392,128]{1,0:T(8,128)(2,1)S(1)}, u32[]{:S(2)}, u32[]{:S(2)}) collective-permute-start(bf16[392,128]{1,0:T(8,128)(2,1)S(1)} %pad_maximum_fusion.refs_0_), channel_id=1, source_target_pairs={{0,8},{4,12},{8,0},{12,4},{1,9},{5,13},{9,1},{13,5},{2,10},{6,14},... | collective-permute-start | bytes 301064 | tf_op jit(solution)/shard_map/ppermute | solution.py:271
  45.0 7.6 %collective-permute-start.11 = (bf16[392,128]{1,0:T(8,128)(2,1)S(1)}, bf16[392,128]{1,0:T(8,128)(2,1)S(1)}, u32[]{:S(2)}, u32[]{:S(2)}) collective-permute-start(bf16[392,128]{1,0:T(8,128)(2,1)S(1)} %pad_maximum_fusion.refs_0_), channel_id=1, source_target_pairs={{0,12},{4,8},{8,4},{12,0},{1,13},{5,9},{9,5},{13,1},{2,14},{6,10},... | collective-permute-start | bytes 301064 | tf_op jit(solution)/shard_map/ppermute | solution.py:271
  46.4 6.7 %collective-permute-start.15 = (bf16[392,128]{1,0:T(8,128)(2,1)S(1)}, bf16[392,128]{1,0:T(8,128)(2,1)S(1)}, u32[]{:S(2)}, u32[]{:S(2)}) collective-permute-start(bf16[392,128]{1,0:T(8,128)(2,1)S(1)} %pad_maximum_fusion.refs_0_), channel_id=1, source_target_pairs={{0,1},{1,0},{2,3},{3,2},{4,5},{5,4},{6,7},{7,6},{8,9},{9,8},{10,11... | collective-permute-start | bytes 301064 | tf_op jit(solution)/shard_map/ppermute | solution.py:412
  47.3 5.8 %collective-permute-start.16 = (bf16[392,128]{1,0:T(8,128)(2,1)S(1)}, bf16[392,128]{1,0:T(8,128)(2,1)S(1)}, u32[]{:S(2)}, u32[]{:S(2)}) collective-permute-start(bf16[392,128]{1,0:T(8,128)(2,1)S(1)} %collective-permute-done.14.refs_1_), channel_id=1, source_target_pairs={{0,1},{1,0},{2,3},{3,2},{4,5},{5,4},{6,7},{7,6},{8,9},{9,8},{10,11... | collective-permute-start | bytes 301064 | tf_op jit(solution)/shard_map/ppermute | solution.py:412
  52.6 1.3 %collective-permute-start.17 = (bf16[392,128]{1,0:T(8,128)(2,1)S(1)}, bf16[392,128]{1,0:T(8,128)(2,1)S(1)}, u32[]{:S(2)}, u32[]{:S(2)}) collective-permute-start(bf16[392,128]{1,0:T(8,128)(2,1)S(1)} %collective-permute-done.11.refs_2_), channel_id=1, source_target_pairs={{0,1},{1,0},{2,3},{3,2},{4,5},{5,4},{6,7},{7,6},{8,9},{9,8},{10,11... | collective-permute-start | bytes 301064 | tf_op jit(solution)/shard_map/ppermute | solution.py:412
  52.6 1.5 %collective-permute-start.18 = (bf16[392,128]{1,0:T(8,128)(2,1)S(1)}, bf16[392,128]{1,0:T(8,128)(2,1)S(1)}, u32[]{:S(2)}, u32[]{:S(2)}) collective-permute-start(bf16[392,128]{1,0:T(8,128)(2,1)S(1)} %collective-permute-done.12.refs_3_), channel_id=1, source_target_pairs={{0,1},{1,0},{2,3},{3,2},{4,5},{5,4},{6,7},{7,6},{8,9},{9,8},{10,11... | collective-permute-start | bytes 301064 | tf_op jit(solution)/shard_map/ppermute | solution.py:412

commit v12 on v11

--- a/solution.py
+++ b/solution.py
@@ -15,7 +15,7 @@
 VMEM_BYTES = 24 * 2**20
 HEAD = 4
 FETCHES = 4
-SCATTER = (3, 2, 1)
+SCATTER = (2, 3, 1)
 GATHER = (1, 3, 2)
 
 
@@ -79,13 +79,6 @@
         ).astype(BF16)
 
 
-def rotate_more_kernel(vec_ref, rott_ref, y_ref):
-    for k in range(y_ref.shape[0]):
-        y_ref[k] = lax.dot_general(
-            rott_ref[k], vec_ref[...], (((1,), (1,)), ((), ())), preferred_element_type=F32
-        ).astype(BF16)
-
-
 def operands(c):
     codes = c.shape[1]
     scaled = c * (2.0 / SOFTNESS * LOG2E)
@@ -104,8 +97,7 @@
 
 
 def quantize_kernel(*refs, k, per, first, last):
-    cb_ref, y0_ref, y1_ref = refs[:3]
-    refs = refs[3:]
+    cb_ref, y0_ref, y1_ref, *refs = refs
     s, r = lax.axis_index("sub"), lax.axis_index("rep")
     codes = cb_ref.shape[2]
     cols = y0_ref.shape[2]
@@ -115,7 +107,12 @@
     whole = last == per
     base = r * per if k == 0 else 0
     if not whole:
-        rec0_ref, rec1_ref, sums_ref, cnt = refs
+        vec_ref = y1_ref
+        rott_ref, rec0_ref, rec1_ref, sums_ref, cnt, y1_ref = refs
+        for half in range(y1_ref.shape[0]):
+            y1_ref[half] = lax.dot_general(
+                rott_ref[half], vec_ref[...], (((1,), (1,)), ((), ())), preferred_element_type=F32
+            ).astype(BF16)
         p_rows = 0
     else:
         v0_ref, v1_ref, *refs = refs
@@ -313,10 +310,6 @@
         compiler_params=small,
         name="rotate",
     )(*(pltpu.with_memory_space_constraint(x, pltpu.HBM) for x in (vectors, rotation)))
-    y1 = pl.pallas_call(
-        rotate_more_kernel, out_shape=y_shape, in_specs=[vmem] * 2, out_specs=vmem, compiler_params=small, name="rotate_far"
-    )(vec_far, rott)
-
     p_rows = (part // lanes) * w
     s_rows = (codes // lanes) * (w + SUBDIM)
     rec_shape = jax.ShapeDtypeStruct((w, rows), BF16)
@@ -332,7 +325,7 @@
 
     early = HEAD * SUBDIM
 
-    def quantize(k, cb_k, *head):
+    def quantize(k, cb_k, y1, *head):
         n_keep, n_send = (p_rows + s_rows, p_rows) if k == 0 else (p_rows, p_rows + s_rows)
         out_shape = [
             rec_shape,
@@ -353,27 +346,28 @@
         )(cb_k, y0, y1, v0, vec_far, *head)
 
     early_shape = jax.ShapeDtypeStruct((early, rows), BF16)
-    head = pl.pallas_call(
+    *head, y1 = pl.pallas_call(
         functools.partial(quantize_kernel, k=0, per=per, first=0, last=HEAD),
-        in_specs=[vmem] * 3,
-        out_specs=[vmem] * 4,
+        in_specs=[vmem] * 4,
+        out_specs=[vmem] * 5,
         out_shape=[
             early_shape,
             early_shape,
             jax.ShapeDtypeStruct(((codes // lanes) * early, lanes), F32),
             jax.ShapeDtypeStruct(cnt_shape, F32),
+            y_shape,
         ],
         compiler_params=params,
         cost_estimate=cost(HEAD, 0),
         name="quantize_head",
-    )(cb, y0, y1)
+    )(cb, y0, vec_far, rott)
 
     cb_far, *head = lax.optimization_barrier((cb_far, *head))
 
-    mine1, other1, keep1, send1 = quantize(1, cb_far)
+    mine1, other1, keep1, send1 = quantize(1, cb_far, y1)
     got1 = lax.ppermute(send1, "sub", swap)
     theirs1 = lax.ppermute(other1, "rep", swap)
-    mine0, other0, keep0, send0 = quantize(0, cb, *head)
+    mine0, other0, keep0, send0 = quantize(0, cb, y1, *head)
     got0 = lax.ppermute(send0, "sub", swap)
     other0, got1 = lax.optimization_barrier((other0, got1))
     theirs0 = lax.ppermute(other0, "rep", swap)

time: 55.9 us -> 55.8 us (level)
    pallas_call x1 -> x0, Pallas kernels: 0.99 us -> none  [on_device(): pl.pallas_call(rotate_more_kernel, out_shape=y_shape, in_specs=[vmem] * 2...]
    pallas_call x1, Pallas kernels: 2.7 us -> 3.53 us  [on_device(): pl.pallas_call(functools.partial(quantize_kernel, k=0, per=per, first=0,...]
where the time goes in v12:
time: 55.8 us; the launch traced here: 55.5 us
  Pallas kernels  25.1 us (45%)
  starting transfers between devices  21.3 us (38%)
  waiting for transfers between devices  8.17 us (15%)
  between operations  0.91 us (2%)
    ppermute x9, starting transfers between devices, exchange(): return lax.ppermute(x, 'row', [(i, i ^ d) for i in range(n)])  15.3 us
    pallas_call x2, Pallas kernels, quantize(): pl.pallas_call(functools.partial(quantize_kernel, k=k, per=per, first=fir...  14.7 us
    ppermute x9, waiting for transfers between devices, exchange(): return lax.ppermute(x, 'row', [(i, i ^ d) for i in range(n)])  6.8 us
    pallas_call x1, Pallas kernels, on_device(): pl.pallas_call(functools.partial(quantize_kernel, k=0, per=per, first=0,...  3.53 us
    pallas_call x1, Pallas kernels, on_device(): pl.pallas_call(rotate_kernel, out_shape=(y_shape, jax.ShapeDtypeStruct((s...  2.71 us
    ppermute x1, starting transfers between devices, on_device(): cb_far = lax.ppermute(cb_sent, 'sub', swap)  2.58 us
    pallas_call x1, Pallas kernels, on_device(): pl.pallas_call(turn_kernel, out_shape=jax.ShapeDtypeStruct((rows, width),...  1.61 us
    pallas_call x1, Pallas kernels, on_device(): pl.pallas_call(functools.partial(final_kernel, n=rows_n, per=per, total=t...  1.48 us
  transfers between devices with their start and end apart: 19, of which 9 were waited for; matrix products, arithmetic and copies ran while one was open for 0% of the time, Pallas kernels for 27%

profile of v12, /device:TPU:0, one launch (start us, length us, event | category | flops | bytes accessed | tf_op | source)
XLA Modules:
  0.0 55.5 jit_solution(9062340749567316291)
XLA Ops:
  0.6 0.5 collective-permute-start
  1.1 0.9 %slice.1 = f32[12,16,256]{2,1,0:T(8,128)S(1)} custom-call(f32[24,16,256]{2,1,0:T(8,128)} %bitcast.2), custom_call_target="tpu_custom_call" | custom-call | tf_op jit(solution)/shard_map/slice/pallas_call | solution.py:287
  2.1 2.6 %collective-permute-start.1 = (f32[12,16,256]{2,1,0:T(8,128)S(1)}, f32[12,16,256]{2,1,0:T(8,128)S(1)}, u32[]{:S(2)}, u32[]{:S(2)}) collective-permute-start(f32[12,16,256]{2,1,0:T(8,128)S(1)} %slice.1), channel_id=1, source_target_pairs={{0,2},{2,0},{1,3},{3,1},{4,6},{6,4},{5,7},{7,5},{8,10},{10,8},{9,1... | collective-permute-start | bytes 589832 | tf_op jit(solution)/shard_map/ppermute | solution.py:296
  4.6 2.7 %rotate.1 = (bf16[2,192,896]{2,1,0:T(8,128)(2,1)S(1)}, bf16[2,192,768]{2,1,0:T(8,128)(2,1)S(1)}, bf16[896,768]{1,0:T(8,128)(2,1)S(1)}) custom-call(bf16[896,768]{1,0:T(8,128)(2,1)} %vec_hbm.1, bf16[768,768]{1,0:T(8,128)(2,1)} %rot_hbm.1), custom_call_target="tpu_custom_call" | custom-call | tf_op jit(solution)/shard_map/rotate/pallas_call | solution.py:300
  7.4 3.5 %quantize_head.1 = (bf16[64,896]{1,0:T(8,128)(2,1)S(1)}, bf16[64,896]{1,0:T(8,128)(2,1)S(1)}, f32[128,128]{1,0:T(8,128)S(1)}, f32[32,128]{1,0:T(8,128)S(1)}, bf16[2,192,896]{2,1,0:T(8,128)(2,1)S(1)}) custom-call(f32[24,16,256]{2,1,0:T(8,128)S(1)} %bitcast.3, bf16[2,192,896]{2,1,0:T(8,128)(2,1)S(1)} %get-tuple-element.41.refs_1_, ...), custom_call_target="tpu_custom_call" | custom-call | flops 528482304 | bytes 8388608 | tf_op jit(solution)/shard_map/quantize_head/pallas_call | solution.py:349
  10.9 8.7 %quantize_far.1 = (bf16[192,896]{1,0:T(8,128)(2,1)S(1)}, bf16[192,896]{1,0:T(8,128)(2,1)S(1)}, f32[576,128]{1,0:T(8,128)S(1)}, bf16[992,128]{1,0:T(8,128)(2,1)S(1)}) custom-call(f32[12,16,256]{2,1,0:T(8,128)S(1)} %collective-permute-done.1.refs_0_, bf16[2,192,896]{2,1,0:T(8,128)(2,1)S(1)} %get-tuple-element.41.refs_1_, ...), custom_call_target="tpu_custom_call" | custom-call | flops 2113929216 | bytes 8388608 | tf_op jit(solution)/shard_map/quantize_far/pallas_call | solution.py:337
  19.9 0.8 %collective-permute-start.2 = (bf16[992,128]{1,0:T(8,128)(2,1)S(1)}, bf16[992,128]{1,0:T(8,128)(2,1)S(1)}, u32[]{:S(2)}, u32[]{:S(2)}) collective-permute-start(bf16[992,128]{1,0:T(8,128)(2,1)S(1)} %get-tuple-element.56), channel_id=1, source_target_pairs={{0,2},{2,0},{1,3},{3,1},{4,6},{6,4},{5,7},{7,5},{8,10},{10,8},{9,1... | collective-permute-start | bytes 761864 | tf_op jit(solution)/shard_map/ppermute | solution.py:368
  20.7 6.0 %quantize_near.1 = (bf16[192,896]{1,0:T(8,128)(2,1)S(1)}, bf16[192,896]{1,0:T(8,128)(2,1)S(1)}, f32[992,128]{1,0:T(8,128)S(1)}, bf16[576,128]{1,0:T(8,128)(2,1)S(1)}) custom-call(f32[24,16,256]{2,1,0:T(8,128)S(1)} %bitcast.4, bf16[2,192,896]{2,1,0:T(8,128)(2,1)S(1)} %get-tuple-element.41.refs_1_, bf16[2,192,896]{2,1,0:T(8,128)(2,1)S(1)} %get-tuple-element.43.refs_2_, ...), custom_call_target="tpu_custom_call" | custom-call | flops 1585446912 | bytes 8388608 | tf_op jit(solution)/shard_map/quantize_near/pallas_call | solution.py:337
  26.8 1.2 %collective-permute-start.3 = (bf16[576,128]{1,0:T(8,128)(2,1)S(1)}, bf16[576,128]{1,0:T(8,128)(2,1)S(1)}, u32[]{:S(2)}, u32[]{:S(2)}) collective-permute-start(bf16[576,128]{1,0:T(8,128)(2,1)S(1)} %get-tuple-element.59), channel_id=1, source_target_pairs={{0,2},{2,0},{1,3},{3,1},{4,6},{6,4},{5,7},{7,5},{8,10},{10,8},{9,1... | collective-permute-start | bytes 442376 | tf_op jit(solution)/shard_map/ppermute | solution.py:371
  28.3 2.7 %collective-permute-start.5 = (bf16[248,128]{1,0:T(8,128)(2,1)S(1)}, bf16[248,128]{1,0:T(8,128)(2,1)S(1)}, u32[]{:S(2)}, u32[]{:S(2)}) collective-permute-start(bf16[248,128]{1,0:T(8,128)(2,1)S(1)} %get-tuple-element.62), channel_id=1, source_target_pairs={{0,8},{4,12},{8,0},{12,4},{1,9},{5,13},{9,1},{13,5},{2,10},{6,14},... | collective-permute-start | bytes 190472 | tf_op jit(solution)/shard_map/ppermute | solution.py:268
  31.0 1.3 %collective-permute-start.6 = (bf16[248,128]{1,0:T(8,128)(2,1)S(1)}, bf16[248,128]{1,0:T(8,128)(2,1)S(1)}, u32[]{:S(2)}, u32[]{:S(2)}) collective-permute-start(bf16[248,128]{1,0:T(8,128)(2,1)S(1)} %get-tuple-element.63), channel_id=1, source_target_pairs={{0,12},{4,8},{8,4},{12,0},{1,13},{5,9},{9,5},{13,1},{2,14},{6,10},... | collective-permute-start | bytes 190472 | tf_op jit(solution)/shard_map/ppermute | solution.py:268
  32.8 2.7 %collective-permute-start.8 = (bf16[144,128]{1,0:T(8,128)(2,1)S(1)}, bf16[144,128]{1,0:T(8,128)(2,1)S(1)}, u32[]{:S(2)}, u32[]{:S(2)}) collective-permute-start(bf16[144,128]{1,0:T(8,128)(2,1)S(1)} %get-tuple-element.68), channel_id=1, source_target_pairs={{0,8},{4,12},{8,0},{12,4},{1,9},{5,13},{9,1},{13,5},{2,10},{6,14},... | collective-permute-start | bytes 110600 | tf_op jit(solution)/shard_map/ppermute | solution.py:268
  35.5 4.0 %collective-permute-start.9 = (bf16[144,128]{1,0:T(8,128)(2,1)S(1)}, bf16[144,128]{1,0:T(8,128)(2,1)S(1)}, u32[]{:S(2)}, u32[]{:S(2)}) collective-permute-start(bf16[144,128]{1,0:T(8,128)(2,1)S(1)} %get-tuple-element.69), channel_id=1, source_target_pairs={{0,12},{4,8},{8,4},{12,0},{1,13},{5,9},{9,5},{13,1},{2,14},{6,10},... | collective-permute-start | bytes 110600 | tf_op jit(solution)/shard_map/ppermute | solution.py:268
  39.5 2.1 %collective-permute-done.9 = bf16[144,128]{1,0:T(8,128)(2,1)S(1)} collective-permute-done((bf16[144,128]{1,0:T(8,128)(2,1)S(1)}, bf16[144,128]{1,0:T(8,128)(2,1)S(1)}, u32[]{:S(2)}, u32[]{:S(2)}) %collective-permute-start.9) | collective-permute-done | bytes 36896 | tf_op jit(solution)/shard_map/ppermute | solution.py:268
  41.7 1.8 %collective-permute-done.10 = bf16[144,128]{1,0:T(8,128)(2,1)S(1)} collective-permute-done((bf16[144,128]{1,0:T(8,128)(2,1)S(1)}, bf16[144,128]{1,0:T(8,128)(2,1)S(1)}, u32[]{:S(2)}, u32[]{:S(2)}) %collective-permute-start.10) | collective-permute-done | bytes 36896 | tf_op jit(solution)/shard_map/ppermute | solution.py:268
  43.5 0.5 collective-permute-start.14
  43.9 2.0 %collective-permute-start.12 = (bf16[392,128]{1,0:T(8,128)(2,1)S(1)}, bf16[392,128]{1,0:T(8,128)(2,1)S(1)}, u32[]{:S(2)}, u32[]{:S(2)}) collective-permute-start(bf16[392,128]{1,0:T(8,128)(2,1)S(1)} %pad_maximum_fusion.refs_0_), channel_id=1, source_target_pairs={{0,8},{4,12},{8,0},{12,4},{1,9},{5,13},{9,1},{13,5},{2,10},{6,14},... | collective-permute-start | bytes 301064 | tf_op jit(solution)/shard_map/ppermute | solution.py:268
  45.9 2.0 %collective-permute-start.11 = (bf16[392,128]{1,0:T(8,128)(2,1)S(1)}, bf16[392,128]{1,0:T(8,128)(2,1)S(1)}, u32[]{:S(2)}, u32[]{:S(2)}) collective-permute-start(bf16[392,128]{1,0:T(8,128)(2,1)S(1)} %pad_maximum_fusion.refs_0_), channel_id=1, source_target_pairs={{0,12},{4,8},{8,4},{12,0},{1,13},{5,9},{9,5},{13,1},{2,14},{6,10},... | collective-permute-start | bytes 301064 | tf_op jit(solution)/shard_map/ppermute | solution.py:268
  47.9 1.6 %collective-permute-done.14.refs_1_ = bf16[392,128]{1,0:T(8,128)(2,1)S(1)} collective-permute-done((bf16[392,128]{1,0:T(8,128)(2,1)S(1)}, bf16[392,128]{1,0:T(8,128)(2,1)S(1)}, u32[]{:S(2)}, u32[]{:S(2)}) %collective-permute-start.14) | collective-permute-done | bytes 100384 | tf_op jit(solution)/shard_map/ppermute | solution.py:268
  49.6 1.6 %turn.1 = bf16[896,768]{1,0:T(8,128)(2,1)} custom-call(bf16[192,896]{1,0:T(8,128)(2,1)S(1)} %get-tuple-element.71.m0_ref, bf16[192,896]{1,0:T(8,128)(2,1)S(1)} %get-tuple-element.72.m1_ref, bf16[192,896]{1,0:T(8,128)(2,1)S(1)} %collective-permute-done.13.t0_ref, bf16[192,896]{1,0:T(8,128)(2,1)S(1)} %collective-permute-done.4.t1_ref), custom_call_target="tpu_custom_call" | custom-call | tf_op jit(solution)/shard_map/turn/pallas_call | solution.py:375
  51.3 1.1 %collective-permute-done.11.refs_2_ = bf16[392,128]{1,0:T(8,128)(2,1)S(1)} collective-permute-done((bf16[392,128]{1,0:T(8,128)(2,1)S(1)}, bf16[392,128]{1,0:T(8,128)(2,1)S(1)}, u32[]{:S(2)}, u32[]{:S(2)}) %collective-permute-start.11) | collective-permute-done | bytes 100384 | tf_op jit(solution)/shard_map/ppermute | solution.py:268
  52.4 0.5 collective-permute-start.18
  53.0 0.8 %collective-permute-done.17.refs_6_ = bf16[392,128]{1,0:T(8,128)(2,1)S(1)} collective-permute-done((bf16[392,128]{1,0:T(8,128)(2,1)S(1)}, bf16[392,128]{1,0:T(8,128)(2,1)S(1)}, u32[]{:S(2)}, u32[]{:S(2)}) %collective-permute-start.17) | collective-permute-done | bytes 100384 | tf_op jit(solution)/shard_map/ppermute | solution.py:406
  53.9 1.5 %final.1 = (f32[384,768]{1,0:T(8,128)}, f32[24,16,256]{2,1,0:T(8,128)}) custom-call(bf16[392,128]{1,0:T(8,128)(2,1)S(1)} %pad_maximum_fusion.refs_0_, bf16[392,128]{1,0:T(8,128)(2,1)S(1)} %collective-permute-done.14.refs_1_, bf16[392,128]{1,0:T(8,128)(2,1)S(1)} %collective-permute-done.11.refs_2_, bf16[392,128]{1,0:T(8,128)(2,1)S(1)} %collective-permute-done.12.refs_3_, ...), custom_call_target="tpu_custom_call" | custom-call | tf_op jit(solution)/shard_map/final/pallas_call | solution.py:409
  (28 shorter events, 1.5 us)
Async XLA Ops:
  0.6 6.7 %collective-permute-start = (bf16[896,768]{1,0:T(8,128)(2,1)}, bf16[896,768]{1,0:T(8,128)(2,1)S(1)}, u32[]{:S(2)}, u32[]{:S(2)}) collective-permute-start(bf16[896,768]{1,0:T(8,128)(2,1)} %vec_hbm.1), channel_id=1, source_target_pairs={{0,1},{1,0},{2,3},{3,2},{4,5},{5,4},{6,7},{7,6},{8,9},{9,8},{10,11... | collective-permute-start | bytes 4128776 | tf_op jit(solution)/shard_map/ppermute | solution.py:297
  2.1 5.3 %copy-start = (f32[24,256,16]{1,2,0:T(8,128)S(1)}, f32[24,256,16]{1,2,0:T(8,128)}, u32[]{:S(2)}) copy-start(f32[24,256,16]{1,2,0:T(8,128)} %param.5) | copy-start | bytes 1179652
  2.1 8.9 %collective-permute-start.1 = (f32[12,16,256]{2,1,0:T(8,128)S(1)}, f32[12,16,256]{2,1,0:T(8,128)S(1)}, u32[]{:S(2)}, u32[]{:S(2)}) collective-permute-start(f32[12,16,256]{2,1,0:T(8,128)S(1)} %slice.1), channel_id=1, source_target_pairs={{0,2},{2,0},{1,3},{3,1},{4,6},{6,4},{5,7},{7,5},{8,10},{10,8},{9,1... | collective-permute-start | bytes 589832 | tf_op jit(solution)/shard_map/ppermute | solution.py:296
  19.6 13.2 %collective-permute-start.4 = (bf16[192,896]{1,0:T(8,128)(2,1)S(1)}, bf16[192,896]{1,0:T(8,128)(2,1)S(1)}, u32[]{:S(2)}, u32[]{:S(2)}) collective-permute-start(bf16[192,896]{1,0:T(8,128)(2,1)S(1)} %get-tuple-element.60), channel_id=1, source_target_pairs={{0,1},{1,0},{2,3},{3,2},{4,5},{5,4},{6,7},{7,6},{8,9},{9,8},{10,11... | collective-permute-start | bytes 1032200 | tf_op jit(solution)/shard_map/ppermute | solution.py:369
  19.9 8.3 %collective-permute-start.2 = (bf16[992,128]{1,0:T(8,128)(2,1)S(1)}, bf16[992,128]{1,0:T(8,128)(2,1)S(1)}, u32[]{:S(2)}, u32[]{:S(2)}) collective-permute-start(bf16[992,128]{1,0:T(8,128)(2,1)S(1)} %get-tuple-element.56), channel_id=1, source_target_pairs={{0,2},{2,0},{1,3},{3,1},{4,6},{6,4},{5,7},{7,5},{8,10},{10,8},{9,1... | collective-permute-start | bytes 761864 | tf_op jit(solution)/shard_map/ppermute | solution.py:368
  26.8 6.0 %collective-permute-start.3 = (bf16[576,128]{1,0:T(8,128)(2,1)S(1)}, bf16[576,128]{1,0:T(8,128)(2,1)S(1)}, u32[]{:S(2)}, u32[]{:S(2)}) collective-permute-start(bf16[576,128]{1,0:T(8,128)(2,1)S(1)} %get-tuple-element.59), channel_id=1, source_target_pairs={{0,2},{2,0},{1,3},{3,1},{4,6},{6,4},{5,7},{7,5},{8,10},{10,8},{9,1... | collective-permute-start | bytes 442376 | tf_op jit(solution)/shard_map/ppermute | solution.py:371
  28.3 7.2 %collective-permute-start.5 = (bf16[248,128]{1,0:T(8,128)(2,1)S(1)}, bf16[248,128]{1,0:T(8,128)(2,1)S(1)}, u32[]{:S(2)}, u32[]{:S(2)}) collective-permute-start(bf16[248,128]{1,0:T(8,128)(2,1)S(1)} %get-tuple-element.62), channel_id=1, source_target_pairs={{0,8},{4,12},{8,0},{12,4},{1,9},{5,13},{9,1},{13,5},{2,10},{6,14},... | collective-permute-start | bytes 190472 | tf_op jit(solution)/shard_map/ppermute | solution.py:268
  31.0 8.5 %collective-permute-start.6 = (bf16[248,128]{1,0:T(8,128)(2,1)S(1)}, bf16[248,128]{1,0:T(8,128)(2,1)S(1)}, u32[]{:S(2)}, u32[]{:S(2)}) collective-permute-start(bf16[248,128]{1,0:T(8,128)(2,1)S(1)} %get-tuple-element.63), channel_id=1, source_target_pairs={{0,12},{4,8},{8,4},{12,0},{1,13},{5,9},{9,5},{13,1},{2,14},{6,10},... | collective-permute-start | bytes 190472 | tf_op jit(solution)/shard_map/ppermute | solution.py:268
  32.3 7.1 %collective-permute-start.7 = (bf16[248,128]{1,0:T(8,128)(2,1)S(1)}, bf16[248,128]{1,0:T(8,128)(2,1)S(1)}, u32[]{:S(2)}, u32[]{:S(2)}) collective-permute-start(bf16[248,128]{1,0:T(8,128)(2,1)S(1)} %get-tuple-element.64), channel_id=1, source_target_pairs={{0,4},{4,0},{8,12},{12,8},{1,5},{5,1},{9,13},{13,9},{2,6},{6,2},{1... | collective-permute-start | bytes 190472 | tf_op jit(solution)/shard_map/ppermute | solution.py:268
  32.8 16.8 %collective-permute-start.13 = (bf16[192,896]{1,0:T(8,128)(2,1)S(1)}, bf16[192,896]{1,0:T(8,128)(2,1)S(1)}, u32[]{:S(2)}, u32[]{:S(2)}) collective-permute-start(bf16[192,896]{1,0:T(8,128)(2,1)S(1)} %get-tuple-element.73), channel_id=1, source_target_pairs={{0,1},{1,0},{2,3},{3,2},{4,5},{5,4},{6,7},{7,6},{8,9},{9,8},{10,11... | collective-permute-start | bytes 1032200 | tf_op jit(solution)/shard_map/ppermute | solution.py:373
  32.8 6.7 %collective-permute-start.8 = (bf16[144,128]{1,0:T(8,128)(2,1)S(1)}, bf16[144,128]{1,0:T(8,128)(2,1)S(1)}, u32[]{:S(2)}, u32[]{:S(2)}) collective-permute-start(bf16[144,128]{1,0:T(8,128)(2,1)S(1)} %get-tuple-element.68), channel_id=1, source_target_pairs={{0,8},{4,12},{8,0},{12,4},{1,9},{5,13},{9,1},{13,5},{2,10},{6,14},... | collective-permute-start | bytes 110600 | tf_op jit(solution)/shard_map/ppermute | solution.py:268
  35.5 6.2 %collective-permute-start.9 = (bf16[144,128]{1,0:T(8,128)(2,1)S(1)}, bf16[144,128]{1,0:T(8,128)(2,1)S(1)}, u32[]{:S(2)}, u32[]{:S(2)}) collective-permute-start(bf16[144,128]{1,0:T(8,128)(2,1)S(1)} %get-tuple-element.69), channel_id=1, source_target_pairs={{0,12},{4,8},{8,4},{12,0},{1,13},{5,9},{9,5},{13,1},{2,14},{6,10},... | collective-permute-start | bytes 110600 | tf_op jit(solution)/shard_map/ppermute | solution.py:268
  39.5 4.0 %collective-permute-start.10 = (bf16[144,128]{1,0:T(8,128)(2,1)S(1)}, bf16[144,128]{1,0:T(8,128)(2,1)S(1)}, u32[]{:S(2)}, u32[]{:S(2)}) collective-permute-start(bf16[144,128]{1,0:T(8,128)(2,1)S(1)} %get-tuple-element.70), channel_id=1, source_target_pairs={{0,4},{4,0},{8,12},{12,8},{1,5},{5,1},{9,13},{13,9},{2,6},{6,2},{1... | collective-permute-start | bytes 110600 | tf_op jit(solution)/shard_map/ppermute | solution.py:268
  43.5 6.1 %collective-permute-start.14 = (bf16[392,128]{1,0:T(8,128)(2,1)S(1)}, bf16[392,128]{1,0:T(8,128)(2,1)S(1)}, u32[]{:S(2)}, u32[]{:S(2)}) collective-permute-start(bf16[392,128]{1,0:T(8,128)(2,1)S(1)} %pad_maximum_fusion.refs_0_), channel_id=1, source_target_pairs={{0,4},{4,0},{8,12},{12,8},{1,5},{5,1},{9,13},{13,9},{2,6},{6,2},{1... | collective-permute-start | bytes 301064 | tf_op jit(solution)/shard_map/ppermute | solution.py:268
  43.9 7.4 %collective-permute-start.12 = (bf16[392,128]{1,0:T(8,128)(2,1)S(1)}, bf16[392,128]{1,0:T(8,128)(2,1)S(1)}, u32[]{:S(2)}, u32[]{:S(2)}) collective-permute-start(bf16[392,128]{1,0:T(8,128)(2,1)S(1)} %pad_maximum_fusion.refs_0_), channel_id=1, source_target_pairs={{0,8},{4,12},{8,0},{12,4},{1,9},{5,13},{9,1},{13,5},{2,10},{6,14},... | collective-permute-start | bytes 301064 | tf_op jit(solution)/shard_map/ppermute | solution.py:268
  45.9 6.5 %collective-permute-start.11 = (bf16[392,128]{1,0:T(8,128)(2,1)S(1)}, bf16[392,128]{1,0:T(8,128)(2,1)S(1)}, u32[]{:S(2)}, u32[]{:S(2)}) collective-permute-start(bf16[392,128]{1,0:T(8,128)(2,1)S(1)} %pad_maximum_fusion.refs_0_), channel_id=1, source_target_pairs={{0,12},{4,8},{8,4},{12,0},{1,13},{5,9},{9,5},{13,1},{2,14},{6,10},... | collective-permute-start | bytes 301064 | tf_op jit(solution)/shard_map/ppermute | solution.py:268
  47.9 5.0 %collective-permute-start.15 = (bf16[392,128]{1,0:T(8,128)(2,1)S(1)}, bf16[392,128]{1,0:T(8,128)(2,1)S(1)}, u32[]{:S(2)}, u32[]{:S(2)}) collective-permute-start(bf16[392,128]{1,0:T(8,128)(2,1)S(1)} %pad_maximum_fusion.refs_0_), channel_id=1, source_target_pairs={{0,1},{1,0},{2,3},{3,2},{4,5},{5,4},{6,7},{7,6},{8,9},{9,8},{10,11... | collective-permute-start | bytes 301064 | tf_op jit(solution)/shard_map/ppermute | solution.py:406
  49.6 3.4 %collective-permute-start.16 = (bf16[392,128]{1,0:T(8,128)(2,1)S(1)}, bf16[392,128]{1,0:T(8,128)(2,1)S(1)}, u32[]{:S(2)}, u32[]{:S(2)}) collective-permute-start(bf16[392,128]{1,0:T(8,128)(2,1)S(1)} %collective-permute-done.14.refs_1_), channel_id=1, source_target_pairs={{0,1},{1,0},{2,3},{3,2},{4,5},{5,4},{6,7},{7,6},{8,9},{9,8},{10,11... | collective-permute-start | bytes 301064 | tf_op jit(solution)/shard_map/ppermute | solution.py:406
  52.4 1.3 %collective-permute-start.17 = (bf16[392,128]{1,0:T(8,128)(2,1)S(1)}, bf16[392,128]{1,0:T(8,128)(2,1)S(1)}, u32[]{:S(2)}, u32[]{:S(2)}) collective-permute-start(bf16[392,128]{1,0:T(8,128)(2,1)S(1)} %collective-permute-done.11.refs_2_), channel_id=1, source_target_pairs={{0,1},{1,0},{2,3},{3,2},{4,5},{5,4},{6,7},{7,6},{8,9},{9,8},{10,11... | collective-permute-start | bytes 301064 | tf_op jit(solution)/shard_map/ppermute | solution.py:406
  52.4 1.5 %collective-permute-start.18 = (bf16[392,128]{1,0:T(8,128)(2,1)S(1)}, bf16[392,128]{1,0:T(8,128)(2,1)S(1)}, u32[]{:S(2)}, u32[]{:S(2)}) collective-permute-start(bf16[392,128]{1,0:T(8,128)(2,1)S(1)} %collective-permute-done.12.refs_3_), channel_id=1, source_target_pairs={{0,1},{1,0},{2,3},{3,2},{4,5},{5,4},{6,7},{7,6},{8,9},{9,8},{10,11... | collective-permute-start | bytes 301064 | tf_op jit(solution)/shard_map/ppermute | solution.py:406

commit v13 on v12

--- a/solution.py
+++ b/solution.py
@@ -236,8 +236,10 @@
             rows = [first + halves * w + hf * SUBDIM + m for hf in range(halves)]
             count = jnp.concatenate([buf[side, a : a + 1, :] for a in rows], axis=1)
             new[part * per + m] = (sums + c) / (count + 1.0)
-    copies.append(pltpu.make_async_copy(new, new_hbm, sems.at[groups]))
-    copies[-1].start()
+    for q in range(2):
+        block = pl.ds(q * per, per)
+        copies.append(pltpu.make_async_copy(new.at[block], new_hbm.at[block], sems.at[2 * groups + q]))
+        copies[-1].start()
     for g in range(groups):
         for h in range(2):
             for q in range(2):
@@ -248,9 +250,10 @@
                         start = (col ^ h) * near_rows + g * w
                         parts += [buf[rep ^ q, start : start + w, :] for rep in range(2)]
                     cross[g * lanes : (g + 1) * lanes, :] = jnp.concatenate(parts, axis=0).T * (1.0 / total)
-        block = pl.ds(g * lanes, lanes)
-        copies.append(pltpu.make_async_copy(cross.at[block], cross_hbm.at[block], sems.at[g]))
-        copies[-1].start()
+        for q in range(2):
+            block = pl.ds(g * lanes + q * (lanes // 2), lanes // 2)
+            copies.append(pltpu.make_async_copy(cross.at[block], cross_hbm.at[block], sems.at[2 * g + q]))
+            copies[-1].start()
     for copy in copies:
         copy.wait()
 
@@ -415,7 +418,7 @@
             pltpu.VMEM((2, 2 * p_rows + s_rows, lanes), F32),
             pltpu.VMEM((part, width), F32),
             pltpu.VMEM(cb.shape, F32),
-            pltpu.SemaphoreType.DMA((part // lanes + 1,)),
+            pltpu.SemaphoreType.DMA((2 * (part // lanes) + 2,)),
         ],
         compiler_params=small,
         name="final",

time: 55.8 us -> 55.8 us (level)
  no operation moved by 1% of the time
where the time goes in v13:
time: 55.8 us; the launch traced here: 55.6 us
  Pallas kernels  25.1 us (45%)
  starting transfers between devices  21.3 us (38%)
  waiting for transfers between devices  8.17 us (15%)
  between operations  0.91 us (2%)
    ppermute x9, starting transfers between devices, exchange(): return lax.ppermute(x, 'row', [(i, i ^ d) for i in range(n)])  15.3 us
    pallas_call x2, Pallas kernels, quantize(): pl.pallas_call(functools.partial(quantize_kernel, k=k, per=per, first=fir...  14.7 us
    ppermute x9, waiting for transfers between devices, exchange(): return lax.ppermute(x, 'row', [(i, i ^ d) for i in range(n)])  6.8 us
    pallas_call x1, Pallas kernels, on_device(): pl.pallas_call(functools.partial(quantize_kernel, k=0, per=per, first=0,...  3.53 us
    pallas_call x1, Pallas kernels, on_device(): pl.pallas_call(rotate_kernel, out_shape=(y_shape, jax.ShapeDtypeStruct((s...  2.71 us
    ppermute x1, starting transfers between devices, on_device(): cb_far = lax.ppermute(cb_sent, 'sub', swap)  2.58 us
    pallas_call x1, Pallas kernels, on_device(): pl.pallas_call(turn_kernel, out_shape=jax.ShapeDtypeStruct((rows, width),...  1.61 us
    pallas_call x1, Pallas kernels, on_device(): pl.pallas_call(functools.partial(final_kernel, n=rows_n, per=per, total=t...  1.51 us
  transfers between devices with their start and end apart: 19, of which 9 were waited for; matrix products, arithmetic and copies ran while one was open for 0% of the time, Pallas kernels for 27%

profile of v13, /device:TPU:0, one launch (start us, length us, event | category | flops | bytes accessed | tf_op | source)
XLA Modules:
  0.0 55.6 jit_solution(12444705514607134422)
XLA Ops:
  0.6 0.5 collective-permute-start
  1.1 0.9 %slice.1 = f32[12,16,256]{2,1,0:T(8,128)S(1)} custom-call(f32[24,16,256]{2,1,0:T(8,128)} %bitcast.2), custom_call_target="tpu_custom_call" | custom-call | tf_op jit(solution)/shard_map/slice/pallas_call | solution.py:290
  2.1 2.6 %collective-permute-start.1 = (f32[12,16,256]{2,1,0:T(8,128)S(1)}, f32[12,16,256]{2,1,0:T(8,128)S(1)}, u32[]{:S(2)}, u32[]{:S(2)}) collective-permute-start(f32[12,16,256]{2,1,0:T(8,128)S(1)} %slice.1), channel_id=1, source_target_pairs={{0,2},{2,0},{1,3},{3,1},{4,6},{6,4},{5,7},{7,5},{8,10},{10,8},{9,1... | collective-permute-start | bytes 589832 | tf_op jit(solution)/shard_map/ppermute | solution.py:299
  4.6 2.7 %rotate.1 = (bf16[2,192,896]{2,1,0:T(8,128)(2,1)S(1)}, bf16[2,192,768]{2,1,0:T(8,128)(2,1)S(1)}, bf16[896,768]{1,0:T(8,128)(2,1)S(1)}) custom-call(bf16[896,768]{1,0:T(8,128)(2,1)} %vec_hbm.1, bf16[768,768]{1,0:T(8,128)(2,1)} %rot_hbm.1), custom_call_target="tpu_custom_call" | custom-call | tf_op jit(solution)/shard_map/rotate/pallas_call | solution.py:303
  7.4 3.5 %quantize_head.1 = (bf16[64,896]{1,0:T(8,128)(2,1)S(1)}, bf16[64,896]{1,0:T(8,128)(2,1)S(1)}, f32[128,128]{1,0:T(8,128)S(1)}, f32[32,128]{1,0:T(8,128)S(1)}, bf16[2,192,896]{2,1,0:T(8,128)(2,1)S(1)}) custom-call(f32[24,16,256]{2,1,0:T(8,128)S(1)} %bitcast.3, bf16[2,192,896]{2,1,0:T(8,128)(2,1)S(1)} %get-tuple-element.41.refs_1_, ...), custom_call_target="tpu_custom_call" | custom-call | flops 528482304 | bytes 8388608 | tf_op jit(solution)/shard_map/quantize_head/pallas_call | solution.py:352
  10.9 8.7 %quantize_far.1 = (bf16[192,896]{1,0:T(8,128)(2,1)S(1)}, bf16[192,896]{1,0:T(8,128)(2,1)S(1)}, f32[576,128]{1,0:T(8,128)S(1)}, bf16[992,128]{1,0:T(8,128)(2,1)S(1)}) custom-call(f32[12,16,256]{2,1,0:T(8,128)S(1)} %collective-permute-done.1.refs_0_, bf16[2,192,896]{2,1,0:T(8,128)(2,1)S(1)} %get-tuple-element.41.refs_1_, ...), custom_call_target="tpu_custom_call" | custom-call | flops 2113929216 | bytes 8388608 | tf_op jit(solution)/shard_map/quantize_far/pallas_call | solution.py:340
  19.9 0.8 %collective-permute-start.2 = (bf16[992,128]{1,0:T(8,128)(2,1)S(1)}, bf16[992,128]{1,0:T(8,128)(2,1)S(1)}, u32[]{:S(2)}, u32[]{:S(2)}) collective-permute-start(bf16[992,128]{1,0:T(8,128)(2,1)S(1)} %get-tuple-element.56), channel_id=1, source_target_pairs={{0,2},{2,0},{1,3},{3,1},{4,6},{6,4},{5,7},{7,5},{8,10},{10,8},{9,1... | collective-permute-start | bytes 761864 | tf_op jit(solution)/shard_map/ppermute | solution.py:371
  20.7 6.0 %quantize_near.1 = (bf16[192,896]{1,0:T(8,128)(2,1)S(1)}, bf16[192,896]{1,0:T(8,128)(2,1)S(1)}, f32[992,128]{1,0:T(8,128)S(1)}, bf16[576,128]{1,0:T(8,128)(2,1)S(1)}) custom-call(f32[24,16,256]{2,1,0:T(8,128)S(1)} %bitcast.4, bf16[2,192,896]{2,1,0:T(8,128)(2,1)S(1)} %get-tuple-element.41.refs_1_, bf16[2,192,896]{2,1,0:T(8,128)(2,1)S(1)} %get-tuple-element.43.refs_2_, ...), custom_call_target="tpu_custom_call" | custom-call | flops 1585446912 | bytes 8388608 | tf_op jit(solution)/shard_map/quantize_near/pallas_call | solution.py:340
  26.8 1.2 %collective-permute-start.3 = (bf16[576,128]{1,0:T(8,128)(2,1)S(1)}, bf16[576,128]{1,0:T(8,128)(2,1)S(1)}, u32[]{:S(2)}, u32[]{:S(2)}) collective-permute-start(bf16[576,128]{1,0:T(8,128)(2,1)S(1)} %get-tuple-element.59), channel_id=1, source_target_pairs={{0,2},{2,0},{1,3},{3,1},{4,6},{6,4},{5,7},{7,5},{8,10},{10,8},{9,1... | collective-permute-start | bytes 442376 | tf_op jit(solution)/shard_map/ppermute | solution.py:374
  28.3 2.7 %collective-permute-start.5 = (bf16[248,128]{1,0:T(8,128)(2,1)S(1)}, bf16[248,128]{1,0:T(8,128)(2,1)S(1)}, u32[]{:S(2)}, u32[]{:S(2)}) collective-permute-start(bf16[248,128]{1,0:T(8,128)(2,1)S(1)} %get-tuple-element.62), channel_id=1, source_target_pairs={{0,8},{4,12},{8,0},{12,4},{1,9},{5,13},{9,1},{13,5},{2,10},{6,14},... | collective-permute-start | bytes 190472 | tf_op jit(solution)/shard_map/ppermute | solution.py:271
  31.0 1.3 %collective-permute-start.6 = (bf16[248,128]{1,0:T(8,128)(2,1)S(1)}, bf16[248,128]{1,0:T(8,128)(2,1)S(1)}, u32[]{:S(2)}, u32[]{:S(2)}) collective-permute-start(bf16[248,128]{1,0:T(8,128)(2,1)S(1)} %get-tuple-element.63), channel_id=1, source_target_pairs={{0,12},{4,8},{8,4},{12,0},{1,13},{5,9},{9,5},{13,1},{2,14},{6,10},... | collective-permute-start | bytes 190472 | tf_op jit(solution)/shard_map/ppermute | solution.py:271
  32.8 2.7 %collective-permute-start.8 = (bf16[144,128]{1,0:T(8,128)(2,1)S(1)}, bf16[144,128]{1,0:T(8,128)(2,1)S(1)}, u32[]{:S(2)}, u32[]{:S(2)}) collective-permute-start(bf16[144,128]{1,0:T(8,128)(2,1)S(1)} %get-tuple-element.68), channel_id=1, source_target_pairs={{0,8},{4,12},{8,0},{12,4},{1,9},{5,13},{9,1},{13,5},{2,10},{6,14},... | collective-permute-start | bytes 110600 | tf_op jit(solution)/shard_map/ppermute | solution.py:271
  35.5 4.0 %collective-permute-start.9 = (bf16[144,128]{1,0:T(8,128)(2,1)S(1)}, bf16[144,128]{1,0:T(8,128)(2,1)S(1)}, u32[]{:S(2)}, u32[]{:S(2)}) collective-permute-start(bf16[144,128]{1,0:T(8,128)(2,1)S(1)} %get-tuple-element.69), channel_id=1, source_target_pairs={{0,12},{4,8},{8,4},{12,0},{1,13},{5,9},{9,5},{13,1},{2,14},{6,10},... | collective-permute-start | bytes 110600 | tf_op jit(solution)/shard_map/ppermute | solution.py:271
  39.5 2.1 %collective-permute-done.9 = bf16[144,128]{1,0:T(8,128)(2,1)S(1)} collective-permute-done((bf16[144,128]{1,0:T(8,128)(2,1)S(1)}, bf16[144,128]{1,0:T(8,128)(2,1)S(1)}, u32[]{:S(2)}, u32[]{:S(2)}) %collective-permute-start.9) | collective-permute-done | bytes 36896 | tf_op jit(solution)/shard_map/ppermute | solution.py:271
  41.7 1.8 %collective-permute-done.10 = bf16[144,128]{1,0:T(8,128)(2,1)S(1)} collective-permute-done((bf16[144,128]{1,0:T(8,128)(2,1)S(1)}, bf16[144,128]{1,0:T(8,128)(2,1)S(1)}, u32[]{:S(2)}, u32[]{:S(2)}) %collective-permute-start.10) | collective-permute-done | bytes 36896 | tf_op jit(solution)/shard_map/ppermute | solution.py:271
  43.5 0.5 collective-permute-start.14
  43.9 2.0 %collective-permute-start.12 = (bf16[392,128]{1,0:T(8,128)(2,1)S(1)}, bf16[392,128]{1,0:T(8,128)(2,1)S(1)}, u32[]{:S(2)}, u32[]{:S(2)}) collective-permute-start(bf16[392,128]{1,0:T(8,128)(2,1)S(1)} %pad_maximum_fusion.refs_0_), channel_id=1, source_target_pairs={{0,8},{4,12},{8,0},{12,4},{1,9},{5,13},{9,1},{13,5},{2,10},{6,14},... | collective-permute-start | bytes 301064 | tf_op jit(solution)/shard_map/ppermute | solution.py:271
  45.9 2.0 %collective-permute-start.11 = (bf16[392,128]{1,0:T(8,128)(2,1)S(1)}, bf16[392,128]{1,0:T(8,128)(2,1)S(1)}, u32[]{:S(2)}, u32[]{:S(2)}) collective-permute-start(bf16[392,128]{1,0:T(8,128)(2,1)S(1)} %pad_maximum_fusion.refs_0_), channel_id=1, source_target_pairs={{0,12},{4,8},{8,4},{12,0},{1,13},{5,9},{9,5},{13,1},{2,14},{6,10},... | collective-permute-start | bytes 301064 | tf_op jit(solution)/shard_map/ppermute | solution.py:271
  47.9 1.6 %collective-permute-done.14.refs_1_ = bf16[392,128]{1,0:T(8,128)(2,1)S(1)} collective-permute-done((bf16[392,128]{1,0:T(8,128)(2,1)S(1)}, bf16[392,128]{1,0:T(8,128)(2,1)S(1)}, u32[]{:S(2)}, u32[]{:S(2)}) %collective-permute-start.14) | collective-permute-done | bytes 100384 | tf_op jit(solution)/shard_map/ppermute | solution.py:271
  49.6 1.6 %turn.1 = bf16[896,768]{1,0:T(8,128)(2,1)} custom-call(bf16[192,896]{1,0:T(8,128)(2,1)S(1)} %get-tuple-element.71.m0_ref, bf16[192,896]{1,0:T(8,128)(2,1)S(1)} %get-tuple-element.72.m1_ref, bf16[192,896]{1,0:T(8,128)(2,1)S(1)} %collective-permute-done.13.t0_ref, bf16[192,896]{1,0:T(8,128)(2,1)S(1)} %collective-permute-done.4.t1_ref), custom_call_target="tpu_custom_call" | custom-call | tf_op jit(solution)/shard_map/turn/pallas_call | solution.py:378
  51.3 1.1 %collective-permute-done.11.refs_2_ = bf16[392,128]{1,0:T(8,128)(2,1)S(1)} collective-permute-done((bf16[392,128]{1,0:T(8,128)(2,1)S(1)}, bf16[392,128]{1,0:T(8,128)(2,1)S(1)}, u32[]{:S(2)}, u32[]{:S(2)}) %collective-permute-start.11) | collective-permute-done | bytes 100384 | tf_op jit(solution)/shard_map/ppermute | solution.py:271
  52.4 0.5 collective-permute-start.18
  53.0 0.8 %collective-permute-done.17.refs_6_ = bf16[392,128]{1,0:T(8,128)(2,1)S(1)} collective-permute-done((bf16[392,128]{1,0:T(8,128)(2,1)S(1)}, bf16[392,128]{1,0:T(8,128)(2,1)S(1)}, u32[]{:S(2)}, u32[]{:S(2)}) %collective-permute-start.17) | collective-permute-done | bytes 100384 | tf_op jit(solution)/shard_map/ppermute | solution.py:409
  53.9 1.5 %final.1 = (f32[384,768]{1,0:T(8,128)}, f32[24,16,256]{2,1,0:T(8,128)}) custom-call(bf16[392,128]{1,0:T(8,128)(2,1)S(1)} %pad_maximum_fusion.refs_0_, bf16[392,128]{1,0:T(8,128)(2,1)S(1)} %collective-permute-done.14.refs_1_, bf16[392,128]{1,0:T(8,128)(2,1)S(1)} %collective-permute-done.11.refs_2_, bf16[392,128]{1,0:T(8,128)(2,1)S(1)} %collective-permute-done.12.refs_3_, ...), custom_call_target="tpu_custom_call" | custom-call | tf_op jit(solution)/shard_map/final/pallas_call | solution.py:412
  (28 shorter events, 1.5 us)
Async XLA Ops:
  0.6 6.7 %collective-permute-start = (bf16[896,768]{1,0:T(8,128)(2,1)}, bf16[896,768]{1,0:T(8,128)(2,1)S(1)}, u32[]{:S(2)}, u32[]{:S(2)}) collective-permute-start(bf16[896,768]{1,0:T(8,128)(2,1)} %vec_hbm.1), channel_id=1, source_target_pairs={{0,1},{1,0},{2,3},{3,2},{4,5},{5,4},{6,7},{7,6},{8,9},{9,8},{10,11... | collective-permute-start | bytes 4128776 | tf_op jit(solution)/shard_map/ppermute | solution.py:300
  2.1 5.3 %copy-start = (f32[24,256,16]{1,2,0:T(8,128)S(1)}, f32[24,256,16]{1,2,0:T(8,128)}, u32[]{:S(2)}) copy-start(f32[24,256,16]{1,2,0:T(8,128)} %param.5) | copy-start | bytes 1179652
  2.1 8.9 %collective-permute-start.1 = (f32[12,16,256]{2,1,0:T(8,128)S(1)}, f32[12,16,256]{2,1,0:T(8,128)S(1)}, u32[]{:S(2)}, u32[]{:S(2)}) collective-permute-start(f32[12,16,256]{2,1,0:T(8,128)S(1)} %slice.1), channel_id=1, source_target_pairs={{0,2},{2,0},{1,3},{3,1},{4,6},{6,4},{5,7},{7,5},{8,10},{10,8},{9,1... | collective-permute-start | bytes 589832 | tf_op jit(solution)/shard_map/ppermute | solution.py:299
  19.6 13.2 %collective-permute-start.4 = (bf16[192,896]{1,0:T(8,128)(2,1)S(1)}, bf16[192,896]{1,0:T(8,128)(2,1)S(1)}, u32[]{:S(2)}, u32[]{:S(2)}) collective-permute-start(bf16[192,896]{1,0:T(8,128)(2,1)S(1)} %get-tuple-element.60), channel_id=1, source_target_pairs={{0,1},{1,0},{2,3},{3,2},{4,5},{5,4},{6,7},{7,6},{8,9},{9,8},{10,11... | collective-permute-start | bytes 1032200 | tf_op jit(solution)/shard_map/ppermute | solution.py:372
  19.9 8.3 %collective-permute-start.2 = (bf16[992,128]{1,0:T(8,128)(2,1)S(1)}, bf16[992,128]{1,0:T(8,128)(2,1)S(1)}, u32[]{:S(2)}, u32[]{:S(2)}) collective-permute-start(bf16[992,128]{1,0:T(8,128)(2,1)S(1)} %get-tuple-element.56), channel_id=1, source_target_pairs={{0,2},{2,0},{1,3},{3,1},{4,6},{6,4},{5,7},{7,5},{8,10},{10,8},{9,1... | collective-permute-start | bytes 761864 | tf_op jit(solution)/shard_map/ppermute | solution.py:371
  26.8 6.0 %collective-permute-start.3 = (bf16[576,128]{1,0:T(8,128)(2,1)S(1)}, bf16[576,128]{1,0:T(8,128)(2,1)S(1)}, u32[]{:S(2)}, u32[]{:S(2)}) collective-permute-start(bf16[576,128]{1,0:T(8,128)(2,1)S(1)} %get-tuple-element.59), channel_id=1, source_target_pairs={{0,2},{2,0},{1,3},{3,1},{4,6},{6,4},{5,7},{7,5},{8,10},{10,8},{9,1... | collective-permute-start | bytes 442376 | tf_op jit(solution)/shard_map/ppermute | solution.py:374
  28.3 7.2 %collective-permute-start.5 = (bf16[248,128]{1,0:T(8,128)(2,1)S(1)}, bf16[248,128]{1,0:T(8,128)(2,1)S(1)}, u32[]{:S(2)}, u32[]{:S(2)}) collective-permute-start(bf16[248,128]{1,0:T(8,128)(2,1)S(1)} %get-tuple-element.62), channel_id=1, source_target_pairs={{0,8},{4,12},{8,0},{12,4},{1,9},{5,13},{9,1},{13,5},{2,10},{6,14},... | collective-permute-start | bytes 190472 | tf_op jit(solution)/shard_map/ppermute | solution.py:271
  31.0 8.5 %collective-permute-start.6 = (bf16[248,128]{1,0:T(8,128)(2,1)S(1)}, bf16[248,128]{1,0:T(8,128)(2,1)S(1)}, u32[]{:S(2)}, u32[]{:S(2)}) collective-permute-start(bf16[248,128]{1,0:T(8,128)(2,1)S(1)} %get-tuple-element.63), channel_id=1, source_target_pairs={{0,12},{4,8},{8,4},{12,0},{1,13},{5,9},{9,5},{13,1},{2,14},{6,10},... | collective-permute-start | bytes 190472 | tf_op jit(solution)/shard_map/ppermute | solution.py:271
  32.3 7.1 %collective-permute-start.7 = (bf16[248,128]{1,0:T(8,128)(2,1)S(1)}, bf16[248,128]{1,0:T(8,128)(2,1)S(1)}, u32[]{:S(2)}, u32[]{:S(2)}) collective-permute-start(bf16[248,128]{1,0:T(8,128)(2,1)S(1)} %get-tuple-element.64), channel_id=1, source_target_pairs={{0,4},{4,0},{8,12},{12,8},{1,5},{5,1},{9,13},{13,9},{2,6},{6,2},{1... | collective-permute-start | bytes 190472 | tf_op jit(solution)/shard_map/ppermute | solution.py:271
  32.8 16.8 %collective-permute-start.13 = (bf16[192,896]{1,0:T(8,128)(2,1)S(1)}, bf16[192,896]{1,0:T(8,128)(2,1)S(1)}, u32[]{:S(2)}, u32[]{:S(2)}) collective-permute-start(bf16[192,896]{1,0:T(8,128)(2,1)S(1)} %get-tuple-element.73), channel_id=1, source_target_pairs={{0,1},{1,0},{2,3},{3,2},{4,5},{5,4},{6,7},{7,6},{8,9},{9,8},{10,11... | collective-permute-start | bytes 1032200 | tf_op jit(solution)/shard_map/ppermute | solution.py:376
  32.8 6.7 %collective-permute-start.8 = (bf16[144,128]{1,0:T(8,128)(2,1)S(1)}, bf16[144,128]{1,0:T(8,128)(2,1)S(1)}, u32[]{:S(2)}, u32[]{:S(2)}) collective-permute-start(bf16[144,128]{1,0:T(8,128)(2,1)S(1)} %get-tuple-element.68), channel_id=1, source_target_pairs={{0,8},{4,12},{8,0},{12,4},{1,9},{5,13},{9,1},{13,5},{2,10},{6,14},... | collective-permute-start | bytes 110600 | tf_op jit(solution)/shard_map/ppermute | solution.py:271
  35.5 6.2 %collective-permute-start.9 = (bf16[144,128]{1,0:T(8,128)(2,1)S(1)}, bf16[144,128]{1,0:T(8,128)(2,1)S(1)}, u32[]{:S(2)}, u32[]{:S(2)}) collective-permute-start(bf16[144,128]{1,0:T(8,128)(2,1)S(1)} %get-tuple-element.69), channel_id=1, source_target_pairs={{0,12},{4,8},{8,4},{12,0},{1,13},{5,9},{9,5},{13,1},{2,14},{6,10},... | collective-permute-start | bytes 110600 | tf_op jit(solution)/shard_map/ppermute | solution.py:271
  39.5 4.0 %collective-permute-start.10 = (bf16[144,128]{1,0:T(8,128)(2,1)S(1)}, bf16[144,128]{1,0:T(8,128)(2,1)S(1)}, u32[]{:S(2)}, u32[]{:S(2)}) collective-permute-start(bf16[144,128]{1,0:T(8,128)(2,1)S(1)} %get-tuple-element.70), channel_id=1, source_target_pairs={{0,4},{4,0},{8,12},{12,8},{1,5},{5,1},{9,13},{13,9},{2,6},{6,2},{1... | collective-permute-start | bytes 110600 | tf_op jit(solution)/shard_map/ppermute | solution.py:271
  43.5 6.1 %collective-permute-start.14 = (bf16[392,128]{1,0:T(8,128)(2,1)S(1)}, bf16[392,128]{1,0:T(8,128)(2,1)S(1)}, u32[]{:S(2)}, u32[]{:S(2)}) collective-permute-start(bf16[392,128]{1,0:T(8,128)(2,1)S(1)} %pad_maximum_fusion.refs_0_), channel_id=1, source_target_pairs={{0,4},{4,0},{8,12},{12,8},{1,5},{5,1},{9,13},{13,9},{2,6},{6,2},{1... | collective-permute-start | bytes 301064 | tf_op jit(solution)/shard_map/ppermute | solution.py:271
  43.9 7.4 %collective-permute-start.12 = (bf16[392,128]{1,0:T(8,128)(2,1)S(1)}, bf16[392,128]{1,0:T(8,128)(2,1)S(1)}, u32[]{:S(2)}, u32[]{:S(2)}) collective-permute-start(bf16[392,128]{1,0:T(8,128)(2,1)S(1)} %pad_maximum_fusion.refs_0_), channel_id=1, source_target_pairs={{0,8},{4,12},{8,0},{12,4},{1,9},{5,13},{9,1},{13,5},{2,10},{6,14},... | collective-permute-start | bytes 301064 | tf_op jit(solution)/shard_map/ppermute | solution.py:271
  45.9 6.5 %collective-permute-start.11 = (bf16[392,128]{1,0:T(8,128)(2,1)S(1)}, bf16[392,128]{1,0:T(8,128)(2,1)S(1)}, u32[]{:S(2)}, u32[]{:S(2)}) collective-permute-start(bf16[392,128]{1,0:T(8,128)(2,1)S(1)} %pad_maximum_fusion.refs_0_), channel_id=1, source_target_pairs={{0,12},{4,8},{8,4},{12,0},{1,13},{5,9},{9,5},{13,1},{2,14},{6,10},... | collective-permute-start | bytes 301064 | tf_op jit(solution)/shard_map/ppermute | solution.py:271
  47.9 5.0 %collective-permute-start.15 = (bf16[392,128]{1,0:T(8,128)(2,1)S(1)}, bf16[392,128]{1,0:T(8,128)(2,1)S(1)}, u32[]{:S(2)}, u32[]{:S(2)}) collective-permute-start(bf16[392,128]{1,0:T(8,128)(2,1)S(1)} %pad_maximum_fusion.refs_0_), channel_id=1, source_target_pairs={{0,1},{1,0},{2,3},{3,2},{4,5},{5,4},{6,7},{7,6},{8,9},{9,8},{10,11... | collective-permute-start | bytes 301064 | tf_op jit(solution)/shard_map/ppermute | solution.py:409
  49.6 3.4 %collective-permute-start.16 = (bf16[392,128]{1,0:T(8,128)(2,1)S(1)}, bf16[392,128]{1,0:T(8,128)(2,1)S(1)}, u32[]{:S(2)}, u32[]{:S(2)}) collective-permute-start(bf16[392,128]{1,0:T(8,128)(2,1)S(1)} %collective-permute-done.14.refs_1_), channel_id=1, source_target_pairs={{0,1},{1,0},{2,3},{3,2},{4,5},{5,4},{6,7},{7,6},{8,9},{9,8},{10,11... | collective-permute-start | bytes 301064 | tf_op jit(solution)/shard_map/ppermute | solution.py:409
  52.4 1.3 %collective-permute-start.17 = (bf16[392,128]{1,0:T(8,128)(2,1)S(1)}, bf16[392,128]{1,0:T(8,128)(2,1)S(1)}, u32[]{:S(2)}, u32[]{:S(2)}) collective-permute-start(bf16[392,128]{1,0:T(8,128)(2,1)S(1)} %collective-permute-done.11.refs_2_), channel_id=1, source_target_pairs={{0,1},{1,0},{2,3},{3,2},{4,5},{5,4},{6,7},{7,6},{8,9},{9,8},{10,11... | collective-permute-start | bytes 301064 | tf_op jit(solution)/shard_map/ppermute | solution.py:409
  52.4 1.5 %collective-permute-start.18 = (bf16[392,128]{1,0:T(8,128)(2,1)S(1)}, bf16[392,128]{1,0:T(8,128)(2,1)S(1)}, u32[]{:S(2)}, u32[]{:S(2)}) collective-permute-start(bf16[392,128]{1,0:T(8,128)(2,1)S(1)} %collective-permute-done.12.refs_3_), channel_id=1, source_target_pairs={{0,1},{1,0},{2,3},{3,2},{4,5},{5,4},{6,7},{7,6},{8,9},{9,8},{10,11... | collective-permute-start | bytes 301064 | tf_op jit(solution)/shard_map/ppermute | solution.py:409

commit v14 on v12

--- a/solution.py
+++ b/solution.py
@@ -16,6 +16,7 @@
 HEAD = 4
 FETCHES = 4
 SCATTER = (2, 3, 1)
+LATER = (3, 2, 1)
 GATHER = (1, 3, 2)
 
 
@@ -255,12 +256,12 @@
         copy.wait()
 
 
-def pieces_kernel(kept_ref, got_ref, *refs, n):
+def pieces_kernel(kept_ref, got_ref, *refs, n, order):
     outs, total = refs[:n], refs[n]
     z = lax.axis_index("row")
     total[...] = kept_ref[...] + got_ref[...].astype(F32)
     size = outs[0].shape[0]
-    for out, d in zip(outs, (0,) + SCATTER):
+    for out, d in zip(outs, (0,) + order):
         out[...] = total[pl.ds(pl.multiple_of((z ^ d) * size, 8), size), :].astype(out.dtype)
 
 
@@ -382,10 +383,10 @@
         name="turn",
     )(mine0, mine1, theirs0, theirs1)
 
-    def scatter(kept, got):
+    def scatter(kept, got, order):
         size = (kept.shape[0] // rows_n, lanes)
         own, *sent = pl.pallas_call(
-            functools.partial(pieces_kernel, n=rows_n),
+            functools.partial(pieces_kernel, n=rows_n, order=order),
             out_shape=[jax.ShapeDtypeStruct(size, F32)] + [jax.ShapeDtypeStruct(size, BF16)] * (rows_n - 1),
             in_specs=[vmem] * 2,
             out_specs=[vmem] * rows_n,
@@ -393,14 +394,14 @@
             compiler_params=small,
             name="pieces",
         )(kept, got)
-        return [own] + [exchange(x, rows_n, d) for x, d in zip(sent, SCATTER)]
+        return [own] + [exchange(x, rows_n, d) for x, d in zip(sent, order)]
 
     def add_up(parts):
         return functools.reduce(lambda a, b: a + b.astype(F32), parts[1:], parts[0]).astype(BF16)
 
-    near = scatter(keep0, got1)
+    near = scatter(keep0, got1, SCATTER)
     near[0], got0, theirs1 = lax.optimization_barrier((near[0], got0, theirs1))
-    summed = jnp.concatenate([add_up(near), add_up(scatter(keep1, got0))], axis=0)
+    summed = jnp.concatenate([add_up(near), add_up(scatter(keep1, got0, LATER))], axis=0)
     mine = [summed] + [exchange(summed, rows_n, d) for d in GATHER]
     mine[2], mine[3], reconstruction = lax.optimization_barrier((mine[2], mine[3], reconstruction))
     theirs = [lax.ppermute(x, "rep", swap) for x in mine]

time: 55.8 us -> 55.9 us (level)
  no operation moved by 1% of the time
where the time goes in v14:
time: 55.9 us; the launch traced here: 55.6 us
  Pallas kernels  25.1 us (45%)
  starting transfers between devices  21.5 us (38%)
  waiting for transfers between devices  8.09 us (14%)
  between operations  0.9 us (2%)
    ppermute x9, starting transfers between devices, exchange(): return lax.ppermute(x, 'row', [(i, i ^ d) for i in range(n)])  15.5 us
    pallas_call x2, Pallas kernels, quantize(): pl.pallas_call(functools.partial(quantize_kernel, k=k, per=per, first=fir...  14.7 us
    ppermute x9, waiting for transfers between devices, exchange(): return lax.ppermute(x, 'row', [(i, i ^ d) for i in range(n)])  6.72 us
    pallas_call x1, Pallas kernels, on_device(): pl.pallas_call(functools.partial(quantize_kernel, k=0, per=per, first=0,...  3.53 us
    pallas_call x1, Pallas kernels, on_device(): pl.pallas_call(rotate_kernel, out_shape=(y_shape, jax.ShapeDtypeStruct((s...  2.71 us
    ppermute x1, starting transfers between devices, on_device(): cb_far = lax.ppermute(cb_sent, 'sub', swap)  2.58 us
    pallas_call x1, Pallas kernels, on_device(): pl.pallas_call(turn_kernel, out_shape=jax.ShapeDtypeStruct((rows, width),...  1.61 us
    pallas_call x1, Pallas kernels, on_device(): pl.pallas_call(functools.partial(final_kernel, n=rows_n, per=per, total=t...  1.48 us
  transfers between devices with their start and end apart: 19, of which 9 were waited for; matrix products, arithmetic and copies ran while one was open for 0% of the time, Pallas kernels for 27%

profile of v14, /device:TPU:0, one launch (start us, length us, event | category | flops | bytes accessed | tf_op | source)
XLA Modules:
  0.0 55.6 jit_solution(14647306203826691772)
XLA Ops:
  0.6 0.5 collective-permute-start
  1.1 0.9 %slice.1 = f32[12,16,256]{2,1,0:T(8,128)S(1)} custom-call(f32[24,16,256]{2,1,0:T(8,128)} %bitcast.2), custom_call_target="tpu_custom_call" | custom-call | tf_op jit(solution)/shard_map/slice/pallas_call | solution.py:288
  2.1 2.6 %collective-permute-start.1 = (f32[12,16,256]{2,1,0:T(8,128)S(1)}, f32[12,16,256]{2,1,0:T(8,128)S(1)}, u32[]{:S(2)}, u32[]{:S(2)}) collective-permute-start(f32[12,16,256]{2,1,0:T(8,128)S(1)} %slice.1), channel_id=1, source_target_pairs={{0,2},{2,0},{1,3},{3,1},{4,6},{6,4},{5,7},{7,5},{8,10},{10,8},{9,1... | collective-permute-start | bytes 589832 | tf_op jit(solution)/shard_map/ppermute | solution.py:297
  4.6 2.7 %rotate.1 = (bf16[2,192,896]{2,1,0:T(8,128)(2,1)S(1)}, bf16[2,192,768]{2,1,0:T(8,128)(2,1)S(1)}, bf16[896,768]{1,0:T(8,128)(2,1)S(1)}) custom-call(bf16[896,768]{1,0:T(8,128)(2,1)} %vec_hbm.1, bf16[768,768]{1,0:T(8,128)(2,1)} %rot_hbm.1), custom_call_target="tpu_custom_call" | custom-call | tf_op jit(solution)/shard_map/rotate/pallas_call | solution.py:301
  7.4 3.5 %quantize_head.1 = (bf16[64,896]{1,0:T(8,128)(2,1)S(1)}, bf16[64,896]{1,0:T(8,128)(2,1)S(1)}, f32[128,128]{1,0:T(8,128)S(1)}, f32[32,128]{1,0:T(8,128)S(1)}, bf16[2,192,896]{2,1,0:T(8,128)(2,1)S(1)}) custom-call(f32[24,16,256]{2,1,0:T(8,128)S(1)} %bitcast.3, bf16[2,192,896]{2,1,0:T(8,128)(2,1)S(1)} %get-tuple-element.41.refs_1_, ...), custom_call_target="tpu_custom_call" | custom-call | flops 528482304 | bytes 8388608 | tf_op jit(solution)/shard_map/quantize_head/pallas_call | solution.py:350
  10.9 8.7 %quantize_far.1 = (bf16[192,896]{1,0:T(8,128)(2,1)S(1)}, bf16[192,896]{1,0:T(8,128)(2,1)S(1)}, f32[576,128]{1,0:T(8,128)S(1)}, bf16[992,128]{1,0:T(8,128)(2,1)S(1)}) custom-call(f32[12,16,256]{2,1,0:T(8,128)S(1)} %collective-permute-done.1.refs_0_, bf16[2,192,896]{2,1,0:T(8,128)(2,1)S(1)} %get-tuple-element.41.refs_1_, ...), custom_call_target="tpu_custom_call" | custom-call | flops 2113929216 | bytes 8388608 | tf_op jit(solution)/shard_map/quantize_far/pallas_call | solution.py:338
  19.9 0.8 %collective-permute-start.2 = (bf16[992,128]{1,0:T(8,128)(2,1)S(1)}, bf16[992,128]{1,0:T(8,128)(2,1)S(1)}, u32[]{:S(2)}, u32[]{:S(2)}) collective-permute-start(bf16[992,128]{1,0:T(8,128)(2,1)S(1)} %get-tuple-element.56), channel_id=1, source_target_pairs={{0,2},{2,0},{1,3},{3,1},{4,6},{6,4},{5,7},{7,5},{8,10},{10,8},{9,1... | collective-permute-start | bytes 761864 | tf_op jit(solution)/shard_map/ppermute | solution.py:369
  20.7 6.0 %quantize_near.1 = (bf16[192,896]{1,0:T(8,128)(2,1)S(1)}, bf16[192,896]{1,0:T(8,128)(2,1)S(1)}, f32[992,128]{1,0:T(8,128)S(1)}, bf16[576,128]{1,0:T(8,128)(2,1)S(1)}) custom-call(f32[24,16,256]{2,1,0:T(8,128)S(1)} %bitcast.4, bf16[2,192,896]{2,1,0:T(8,128)(2,1)S(1)} %get-tuple-element.41.refs_1_, bf16[2,192,896]{2,1,0:T(8,128)(2,1)S(1)} %get-tuple-element.43.refs_2_, ...), custom_call_target="tpu_custom_call" | custom-call | flops 1585446912 | bytes 8388608 | tf_op jit(solution)/shard_map/quantize_near/pallas_call | solution.py:338
  26.8 1.2 %collective-permute-start.3 = (bf16[576,128]{1,0:T(8,128)(2,1)S(1)}, bf16[576,128]{1,0:T(8,128)(2,1)S(1)}, u32[]{:S(2)}, u32[]{:S(2)}) collective-permute-start(bf16[576,128]{1,0:T(8,128)(2,1)S(1)} %get-tuple-element.59), channel_id=1, source_target_pairs={{0,2},{2,0},{1,3},{3,1},{4,6},{6,4},{5,7},{7,5},{8,10},{10,8},{9,1... | collective-permute-start | bytes 442376 | tf_op jit(solution)/shard_map/ppermute | solution.py:372
  28.3 2.7 %collective-permute-start.5 = (bf16[248,128]{1,0:T(8,128)(2,1)S(1)}, bf16[248,128]{1,0:T(8,128)(2,1)S(1)}, u32[]{:S(2)}, u32[]{:S(2)}) collective-permute-start(bf16[248,128]{1,0:T(8,128)(2,1)S(1)} %get-tuple-element.62), channel_id=1, source_target_pairs={{0,8},{4,12},{8,0},{12,4},{1,9},{5,13},{9,1},{13,5},{2,10},{6,14},... | collective-permute-start | bytes 190472 | tf_op jit(solution)/shard_map/ppermute | solution.py:269
  31.0 1.3 %collective-permute-start.6 = (bf16[248,128]{1,0:T(8,128)(2,1)S(1)}, bf16[248,128]{1,0:T(8,128)(2,1)S(1)}, u32[]{:S(2)}, u32[]{:S(2)}) collective-permute-start(bf16[248,128]{1,0:T(8,128)(2,1)S(1)} %get-tuple-element.63), channel_id=1, source_target_pairs={{0,12},{4,8},{8,4},{12,0},{1,13},{5,9},{9,5},{13,1},{2,14},{6,10},... | collective-permute-start | bytes 190472 | tf_op jit(solution)/shard_map/ppermute | solution.py:269
  32.8 3.7 %collective-permute-start.8 = (bf16[144,128]{1,0:T(8,128)(2,1)S(1)}, bf16[144,128]{1,0:T(8,128)(2,1)S(1)}, u32[]{:S(2)}, u32[]{:S(2)}) collective-permute-start(bf16[144,128]{1,0:T(8,128)(2,1)S(1)} %get-tuple-element.68), channel_id=1, source_target_pairs={{0,12},{4,8},{8,4},{12,0},{1,13},{5,9},{9,5},{13,1},{2,14},{6,10},... | collective-permute-start | bytes 110600 | tf_op jit(solution)/shard_map/ppermute | solution.py:269
  36.8 0.4 collective-permute-done.6
  37.2 2.9 %collective-permute-start.10 = (bf16[144,128]{1,0:T(8,128)(2,1)S(1)}, bf16[144,128]{1,0:T(8,128)(2,1)S(1)}, u32[]{:S(2)}, u32[]{:S(2)}) collective-permute-start(bf16[144,128]{1,0:T(8,128)(2,1)S(1)} %get-tuple-element.70), channel_id=1, source_target_pairs={{0,4},{4,0},{8,12},{12,8},{1,5},{5,1},{9,13},{13,9},{2,6},{6,2},{1... | collective-permute-start | bytes 110600 | tf_op jit(solution)/shard_map/ppermute | solution.py:269
  40.1 1.7 %collective-permute-done.9 = bf16[144,128]{1,0:T(8,128)(2,1)S(1)} collective-permute-done((bf16[144,128]{1,0:T(8,128)(2,1)S(1)}, bf16[144,128]{1,0:T(8,128)(2,1)S(1)}, u32[]{:S(2)}, u32[]{:S(2)}) %collective-permute-start.9) | collective-permute-done | bytes 36896 | tf_op jit(solution)/shard_map/ppermute | solution.py:269
  42.2 1.9 %collective-permute-start.14 = (bf16[392,128]{1,0:T(8,128)(2,1)S(1)}, bf16[392,128]{1,0:T(8,128)(2,1)S(1)}, u32[]{:S(2)}, u32[]{:S(2)}) collective-permute-start(bf16[392,128]{1,0:T(8,128)(2,1)S(1)} %pad_maximum_fusion.refs_0_), channel_id=1, source_target_pairs={{0,4},{4,0},{8,12},{12,8},{1,5},{5,1},{9,13},{13,9},{2,6},{6,2},{1... | collective-permute-start | bytes 301064 | tf_op jit(solution)/shard_map/ppermute | solution.py:269
  44.1 0.9 %collective-permute-start.12 = (bf16[392,128]{1,0:T(8,128)(2,1)S(1)}, bf16[392,128]{1,0:T(8,128)(2,1)S(1)}, u32[]{:S(2)}, u32[]{:S(2)}) collective-permute-start(bf16[392,128]{1,0:T(8,128)(2,1)S(1)} %pad_maximum_fusion.refs_0_), channel_id=1, source_target_pairs={{0,8},{4,12},{8,0},{12,4},{1,9},{5,13},{9,1},{13,5},{2,10},{6,14},... | collective-permute-start | bytes 301064 | tf_op jit(solution)/shard_map/ppermute | solution.py:269
  45.0 1.7 %collective-permute-start.11 = (bf16[392,128]{1,0:T(8,128)(2,1)S(1)}, bf16[392,128]{1,0:T(8,128)(2,1)S(1)}, u32[]{:S(2)}, u32[]{:S(2)}) collective-permute-start(bf16[392,128]{1,0:T(8,128)(2,1)S(1)} %pad_maximum_fusion.refs_0_), channel_id=1, source_target_pairs={{0,12},{4,8},{8,4},{12,0},{1,13},{5,9},{9,5},{13,1},{2,14},{6,10},... | collective-permute-start | bytes 301064 | tf_op jit(solution)/shard_map/ppermute | solution.py:269
  46.7 0.6 %collective-permute-done.14.refs_1_ = bf16[392,128]{1,0:T(8,128)(2,1)S(1)} collective-permute-done((bf16[392,128]{1,0:T(8,128)(2,1)S(1)}, bf16[392,128]{1,0:T(8,128)(2,1)S(1)}, u32[]{:S(2)}, u32[]{:S(2)}) %collective-permute-start.14) | collective-permute-done | bytes 100384 | tf_op jit(solution)/shard_map/ppermute | solution.py:269
  47.3 1.6 %turn.1 = bf16[896,768]{1,0:T(8,128)(2,1)} custom-call(bf16[192,896]{1,0:T(8,128)(2,1)S(1)} %get-tuple-element.71.m0_ref, bf16[192,896]{1,0:T(8,128)(2,1)S(1)} %get-tuple-element.72.m1_ref, bf16[192,896]{1,0:T(8,128)(2,1)S(1)} %collective-permute-done.13.t0_ref, bf16[192,896]{1,0:T(8,128)(2,1)S(1)} %collective-permute-done.4.t1_ref), custom_call_target="tpu_custom_call" | custom-call | tf_op jit(solution)/shard_map/turn/pallas_call | solution.py:376
  48.9 3.6 %collective-permute-done.12.refs_3_ = bf16[392,128]{1,0:T(8,128)(2,1)S(1)} collective-permute-done((bf16[392,128]{1,0:T(8,128)(2,1)S(1)}, bf16[392,128]{1,0:T(8,128)(2,1)S(1)}, u32[]{:S(2)}, u32[]{:S(2)}) %collective-permute-start.12) | collective-permute-done | bytes 100384 | tf_op jit(solution)/shard_map/ppermute | solution.py:269
  52.5 0.5 collective-permute-start.18
  53.1 0.8 %collective-permute-done.17.refs_6_ = bf16[392,128]{1,0:T(8,128)(2,1)S(1)} collective-permute-done((bf16[392,128]{1,0:T(8,128)(2,1)S(1)}, bf16[392,128]{1,0:T(8,128)(2,1)S(1)}, u32[]{:S(2)}, u32[]{:S(2)}) %collective-permute-start.17) | collective-permute-done | bytes 100384 | tf_op jit(solution)/shard_map/ppermute | solution.py:407
  54.0 1.5 %final.1 = (f32[384,768]{1,0:T(8,128)}, f32[24,16,256]{2,1,0:T(8,128)}) custom-call(bf16[392,128]{1,0:T(8,128)(2,1)S(1)} %pad_maximum_fusion.refs_0_, bf16[392,128]{1,0:T(8,128)(2,1)S(1)} %collective-permute-done.14.refs_1_, bf16[392,128]{1,0:T(8,128)(2,1)S(1)} %collective-permute-done.11.refs_2_, bf16[392,128]{1,0:T(8,128)(2,1)S(1)} %collective-permute-done.12.refs_3_, ...), custom_call_target="tpu_custom_call" | custom-call | tf_op jit(solution)/shard_map/final/pallas_call | solution.py:410
  (28 shorter events, 2.0 us)
Async XLA Ops:
  0.6 6.7 %collective-permute-start = (bf16[896,768]{1,0:T(8,128)(2,1)}, bf16[896,768]{1,0:T(8,128)(2,1)S(1)}, u32[]{:S(2)}, u32[]{:S(2)}) collective-permute-start(bf16[896,768]{1,0:T(8,128)(2,1)} %vec_hbm.1), channel_id=1, source_target_pairs={{0,1},{1,0},{2,3},{3,2},{4,5},{5,4},{6,7},{7,6},{8,9},{9,8},{10,11... | collective-permute-start | bytes 4128776 | tf_op jit(solution)/shard_map/ppermute | solution.py:298
  2.1 5.3 %copy-start = (f32[24,256,16]{1,2,0:T(8,128)S(1)}, f32[24,256,16]{1,2,0:T(8,128)}, u32[]{:S(2)}) copy-start(f32[24,256,16]{1,2,0:T(8,128)} %param.5) | copy-start | bytes 1179652
  2.1 8.9 %collective-permute-start.1 = (f32[12,16,256]{2,1,0:T(8,128)S(1)}, f32[12,16,256]{2,1,0:T(8,128)S(1)}, u32[]{:S(2)}, u32[]{:S(2)}) collective-permute-start(f32[12,16,256]{2,1,0:T(8,128)S(1)} %slice.1), channel_id=1, source_target_pairs={{0,2},{2,0},{1,3},{3,1},{4,6},{6,4},{5,7},{7,5},{8,10},{10,8},{9,1... | collective-permute-start | bytes 589832 | tf_op jit(solution)/shard_map/ppermute | solution.py:297
  19.6 13.2 %collective-permute-start.4 = (bf16[192,896]{1,0:T(8,128)(2,1)S(1)}, bf16[192,896]{1,0:T(8,128)(2,1)S(1)}, u32[]{:S(2)}, u32[]{:S(2)}) collective-permute-start(bf16[192,896]{1,0:T(8,128)(2,1)S(1)} %get-tuple-element.60), channel_id=1, source_target_pairs={{0,1},{1,0},{2,3},{3,2},{4,5},{5,4},{6,7},{7,6},{8,9},{9,8},{10,11... | collective-permute-start | bytes 1032200 | tf_op jit(solution)/shard_map/ppermute | solution.py:370
  19.9 8.3 %collective-permute-start.2 = (bf16[992,128]{1,0:T(8,128)(2,1)S(1)}, bf16[992,128]{1,0:T(8,128)(2,1)S(1)}, u32[]{:S(2)}, u32[]{:S(2)}) collective-permute-start(bf16[992,128]{1,0:T(8,128)(2,1)S(1)} %get-tuple-element.56), channel_id=1, source_target_pairs={{0,2},{2,0},{1,3},{3,1},{4,6},{6,4},{5,7},{7,5},{8,10},{10,8},{9,1... | collective-permute-start | bytes 761864 | tf_op jit(solution)/shard_map/ppermute | solution.py:369
  26.8 6.0 %collective-permute-start.3 = (bf16[576,128]{1,0:T(8,128)(2,1)S(1)}, bf16[576,128]{1,0:T(8,128)(2,1)S(1)}, u32[]{:S(2)}, u32[]{:S(2)}) collective-permute-start(bf16[576,128]{1,0:T(8,128)(2,1)S(1)} %get-tuple-element.59), channel_id=1, source_target_pairs={{0,2},{2,0},{1,3},{3,1},{4,6},{6,4},{5,7},{7,5},{8,10},{10,8},{9,1... | collective-permute-start | bytes 442376 | tf_op jit(solution)/shard_map/ppermute | solution.py:372
  28.3 8.2 %collective-permute-start.5 = (bf16[248,128]{1,0:T(8,128)(2,1)S(1)}, bf16[248,128]{1,0:T(8,128)(2,1)S(1)}, u32[]{:S(2)}, u32[]{:S(2)}) collective-permute-start(bf16[248,128]{1,0:T(8,128)(2,1)S(1)} %get-tuple-element.62), channel_id=1, source_target_pairs={{0,8},{4,12},{8,0},{12,4},{1,9},{5,13},{9,1},{13,5},{2,10},{6,14},... | collective-permute-start | bytes 190472 | tf_op jit(solution)/shard_map/ppermute | solution.py:269
  31.0 6.2 %collective-permute-start.6 = (bf16[248,128]{1,0:T(8,128)(2,1)S(1)}, bf16[248,128]{1,0:T(8,128)(2,1)S(1)}, u32[]{:S(2)}, u32[]{:S(2)}) collective-permute-start(bf16[248,128]{1,0:T(8,128)(2,1)S(1)} %get-tuple-element.63), channel_id=1, source_target_pairs={{0,12},{4,8},{8,4},{12,0},{1,13},{5,9},{9,5},{13,1},{2,14},{6,10},... | collective-permute-start | bytes 190472 | tf_op jit(solution)/shard_map/ppermute | solution.py:269
  32.3 7.7 %collective-permute-start.7 = (bf16[248,128]{1,0:T(8,128)(2,1)S(1)}, bf16[248,128]{1,0:T(8,128)(2,1)S(1)}, u32[]{:S(2)}, u32[]{:S(2)}) collective-permute-start(bf16[248,128]{1,0:T(8,128)(2,1)S(1)} %get-tuple-element.64), channel_id=1, source_target_pairs={{0,4},{4,0},{8,12},{12,8},{1,5},{5,1},{9,13},{13,9},{2,6},{6,2},{1... | collective-permute-start | bytes 190472 | tf_op jit(solution)/shard_map/ppermute | solution.py:269
  32.8 14.5 %collective-permute-start.13 = (bf16[192,896]{1,0:T(8,128)(2,1)S(1)}, bf16[192,896]{1,0:T(8,128)(2,1)S(1)}, u32[]{:S(2)}, u32[]{:S(2)}) collective-permute-start(bf16[192,896]{1,0:T(8,128)(2,1)S(1)} %get-tuple-element.73), channel_id=1, source_target_pairs={{0,1},{1,0},{2,3},{3,2},{4,5},{5,4},{6,7},{7,6},{8,9},{9,8},{10,11... | collective-permute-start | bytes 1032200 | tf_op jit(solution)/shard_map/ppermute | solution.py:374
  32.8 7.2 %collective-permute-start.8 = (bf16[144,128]{1,0:T(8,128)(2,1)S(1)}, bf16[144,128]{1,0:T(8,128)(2,1)S(1)}, u32[]{:S(2)}, u32[]{:S(2)}) collective-permute-start(bf16[144,128]{1,0:T(8,128)(2,1)S(1)} %get-tuple-element.68), channel_id=1, source_target_pairs={{0,12},{4,8},{8,4},{12,0},{1,13},{5,9},{9,5},{13,1},{2,14},{6,10},... | collective-permute-start | bytes 110600 | tf_op jit(solution)/shard_map/ppermute | solution.py:269
  36.5 5.3 %collective-permute-start.9 = (bf16[144,128]{1,0:T(8,128)(2,1)S(1)}, bf16[144,128]{1,0:T(8,128)(2,1)S(1)}, u32[]{:S(2)}, u32[]{:S(2)}) collective-permute-start(bf16[144,128]{1,0:T(8,128)(2,1)S(1)} %get-tuple-element.69), channel_id=1, source_target_pairs={{0,8},{4,12},{8,0},{12,4},{1,9},{5,13},{9,1},{13,5},{2,10},{6,14},... | collective-permute-start | bytes 110600 | tf_op jit(solution)/shard_map/ppermute | solution.py:269
  37.2 5.0 %collective-permute-start.10 = (bf16[144,128]{1,0:T(8,128)(2,1)S(1)}, bf16[144,128]{1,0:T(8,128)(2,1)S(1)}, u32[]{:S(2)}, u32[]{:S(2)}) collective-permute-start(bf16[144,128]{1,0:T(8,128)(2,1)S(1)} %get-tuple-element.70), channel_id=1, source_target_pairs={{0,4},{4,0},{8,12},{12,8},{1,5},{5,1},{9,13},{13,9},{2,6},{6,2},{1... | collective-permute-start | bytes 110600 | tf_op jit(solution)/shard_map/ppermute | solution.py:269
  42.2 5.1 %collective-permute-start.14 = (bf16[392,128]{1,0:T(8,128)(2,1)S(1)}, bf16[392,128]{1,0:T(8,128)(2,1)S(1)}, u32[]{:S(2)}, u32[]{:S(2)}) collective-permute-start(bf16[392,128]{1,0:T(8,128)(2,1)S(1)} %pad_maximum_fusion.refs_0_), channel_id=1, source_target_pairs={{0,4},{4,0},{8,12},{12,8},{1,5},{5,1},{9,13},{13,9},{2,6},{6,2},{1... | collective-permute-start | bytes 301064 | tf_op jit(solution)/shard_map/ppermute | solution.py:269
  44.1 8.4 %collective-permute-start.12 = (bf16[392,128]{1,0:T(8,128)(2,1)S(1)}, bf16[392,128]{1,0:T(8,128)(2,1)S(1)}, u32[]{:S(2)}, u32[]{:S(2)}) collective-permute-start(bf16[392,128]{1,0:T(8,128)(2,1)S(1)} %pad_maximum_fusion.refs_0_), channel_id=1, source_target_pairs={{0,8},{4,12},{8,0},{12,4},{1,9},{5,13},{9,1},{13,5},{2,10},{6,14},... | collective-permute-start | bytes 301064 | tf_op jit(solution)/shard_map/ppermute | solution.py:269
  45.0 7.5 %collective-permute-start.11 = (bf16[392,128]{1,0:T(8,128)(2,1)S(1)}, bf16[392,128]{1,0:T(8,128)(2,1)S(1)}, u32[]{:S(2)}, u32[]{:S(2)}) collective-permute-start(bf16[392,128]{1,0:T(8,128)(2,1)S(1)} %pad_maximum_fusion.refs_0_), channel_id=1, source_target_pairs={{0,12},{4,8},{8,4},{12,0},{1,13},{5,9},{9,5},{13,1},{2,14},{6,10},... | collective-permute-start | bytes 301064 | tf_op jit(solution)/shard_map/ppermute | solution.py:269
  46.7 6.4 %collective-permute-start.15 = (bf16[392,128]{1,0:T(8,128)(2,1)S(1)}, bf16[392,128]{1,0:T(8,128)(2,1)S(1)}, u32[]{:S(2)}, u32[]{:S(2)}) collective-permute-start(bf16[392,128]{1,0:T(8,128)(2,1)S(1)} %pad_maximum_fusion.refs_0_), channel_id=1, source_target_pairs={{0,1},{1,0},{2,3},{3,2},{4,5},{5,4},{6,7},{7,6},{8,9},{9,8},{10,11... | collective-permute-start | bytes 301064 | tf_op jit(solution)/shard_map/ppermute | solution.py:407
  47.3 5.8 %collective-permute-start.16 = (bf16[392,128]{1,0:T(8,128)(2,1)S(1)}, bf16[392,128]{1,0:T(8,128)(2,1)S(1)}, u32[]{:S(2)}, u32[]{:S(2)}) collective-permute-start(bf16[392,128]{1,0:T(8,128)(2,1)S(1)} %collective-permute-done.14.refs_1_), channel_id=1, source_target_pairs={{0,1},{1,0},{2,3},{3,2},{4,5},{5,4},{6,7},{7,6},{8,9},{9,8},{10,11... | collective-permute-start | bytes 301064 | tf_op jit(solution)/shard_map/ppermute | solution.py:407
  52.5 1.3 %collective-permute-start.17 = (bf16[392,128]{1,0:T(8,128)(2,1)S(1)}, bf16[392,128]{1,0:T(8,128)(2,1)S(1)}, u32[]{:S(2)}, u32[]{:S(2)}) collective-permute-start(bf16[392,128]{1,0:T(8,128)(2,1)S(1)} %collective-permute-done.11.refs_2_), channel_id=1, source_target_pairs={{0,1},{1,0},{2,3},{3,2},{4,5},{5,4},{6,7},{7,6},{8,9},{9,8},{10,11... | collective-permute-start | bytes 301064 | tf_op jit(solution)/shard_map/ppermute | solution.py:407
  52.5 1.5 %collective-permute-start.18 = (bf16[392,128]{1,0:T(8,128)(2,1)S(1)}, bf16[392,128]{1,0:T(8,128)(2,1)S(1)}, u32[]{:S(2)}, u32[]{:S(2)}) collective-permute-start(bf16[392,128]{1,0:T(8,128)(2,1)S(1)} %collective-permute-done.12.refs_3_), channel_id=1, source_target_pairs={{0,1},{1,0},{2,3},{3,2},{4,5},{5,4},{6,7},{7,6},{8,9},{9,8},{10,11... | collective-permute-start | bytes 301064 | tf_op jit(solution)/shard_map/ppermute | solution.py:407
